TPU v7x, 32 devices: a whole 2x2x4 slice. The times are simulated.
32 devices in a mesh: epi: 2 (over y), space: 4 (over z), draw: 4 (over x, core).
Axes of the slice: x: 2, y: 2, z: 4, core: 2. Of those that a mesh axis runs over, the one named last changes fastest.
Arguments:
- log_perm: float32 [64, 64, 384], P(('epi', 'space')), parts along dimension 0, may hold values from -4 to 4
- noise: float32 [4, 64, 64, 384], P('draw', ('epi', 'space')), parts along dimension 1, may hold values from -3.5 to 3.5
- source: float32 [64, 64, 384], P(('epi', 'space')), parts along dimension 0, may hold values from -24 to 24
- start_pressure: float32 [64, 64, 384], P(('epi', 'space')), parts along dimension 0, may hold values from -18 to 18
- observe: float32 [64, 64, 384], P(('epi', 'space')), parts along dimension 0, may hold values from -12 to 12
Outputs:
- pressure: float32 [4, 64, 64, 384], P('draw', ('epi', 'space')), parts along dimension 1
- log_perm_grad: float32 [64, 64, 384], P(('epi', 'space'), 'draw'), parts along dimension 0
There are 2 independent parts, one for each index of `epi`. A program takes and returns all parts, laid end to end along the dimension named above; each array names one. Nothing has to cross between parts.
All inputs are finite; a program needn't handle non-finite values.
Results may differ from a plain program's by a relative error of at most 0.00002.
Values sent between devices are 32-bit elements; how exact they have to be, the bound alone decides.
No kernel may reach another device: no remote copies, remote signals or barrier semaphores. Data moves between devices by JAX's collectives and lax.ppermute only.
A program may use at most 64 MiB of HBM per device.

v0:
```python
import jax
import jax.numpy as jnp
from jax import lax
from jax.sharding import PartitionSpec as P

SWEEPS = 3


def extended(shard, sides, width):
    for axis, dim in sides:
        size, length = (lax.axis_size(axis), shard.shape[dim])
        up = [(i, (i + 1) % size) for i in range(size - 1)]
        down = [(j, i) for i, j in up]
        last = lax.slice_in_dim(shard, length - width, length, axis=dim)
        initial = lax.slice_in_dim(shard, 0, width, axis=dim)
        before = lax.ppermute(last, axis, up)
        after = lax.ppermute(initial, axis, down)
        shard = jnp.concatenate([before, shard, after], axis=dim)
    return shard


def pad_plane(value):
    widths = ((0, 0),) * (value.ndim - 2) + ((1, 1), (1, 1))
    return jnp.pad(value, widths)


def face_weights(padded_k):
    face_z = 0.5 * (padded_k[..., :-1, 1:-1, 1:-1] + padded_k[..., 1:, 1:-1, 1:-1])
    face_x = 0.5 * (padded_k[..., 1:-1, :-1, 1:-1] + padded_k[..., 1:-1, 1:, 1:-1])
    face_y = 0.5 * (padded_k[..., 1:-1, 1:-1, :-1] + padded_k[..., 1:-1, 1:-1, 1:])
    diag = (
        0.5
        + face_z[..., :-1, :, :]
        + face_z[..., 1:, :, :]
        + face_x[..., :, :-1, :]
        + face_x[..., :, 1:, :]
        + face_y[..., :-1]
        + face_y[..., 1:]
    )
    return ((face_z, face_x, face_y), diag)


def apply_faces(weights, padded_v):
    face_z, face_x, face_y = weights
    total = (
        face_z[..., :-1, :, :] * padded_v[..., :-2, 1:-1, 1:-1]
        + face_z[..., 1:, :, :] * padded_v[..., 2:, 1:-1, 1:-1]
    )
    total = (
        total
        + face_x[..., :, :-1, :] * padded_v[..., 1:-1, :-2, 1:-1]
        + face_x[..., :, 1:, :] * padded_v[..., 1:-1, 2:, 1:-1]
    )
    total = (
        total
        + face_y[..., :-1] * padded_v[..., 1:-1, 1:-1, :-2]
        + face_y[..., 1:] * padded_v[..., 1:-1, 1:-1, 2:]
    )
    return total


def face_terms(padded_u, padded_q, padded_e):
    grad_z = (
        padded_u[..., :-1, 1:-1, 1:-1] * padded_q[..., 1:, 1:-1, 1:-1]
        + padded_u[..., 1:, 1:-1, 1:-1] * padded_q[..., :-1, 1:-1, 1:-1]
        + padded_e[..., :-1, 1:-1, 1:-1]
        + padded_e[..., 1:, 1:-1, 1:-1]
    )
    grad_x = (
        padded_u[..., 1:-1, :-1, 1:-1] * padded_q[..., 1:-1, 1:, 1:-1]
        + padded_u[..., 1:-1, 1:, 1:-1] * padded_q[..., 1:-1, :-1, 1:-1]
        + padded_e[..., 1:-1, :-1, 1:-1]
        + padded_e[..., 1:-1, 1:, 1:-1]
    )
    grad_y = (
        padded_u[..., 1:-1, 1:-1, :-1] * padded_q[..., 1:-1, 1:-1, 1:]
        + padded_u[..., 1:-1, 1:-1, 1:] * padded_q[..., 1:-1, 1:-1, :-1]
        + padded_e[..., 1:-1, 1:-1, :-1]
        + padded_e[..., 1:-1, 1:-1, 1:]
    )
    return 0.5 * (
        grad_z[..., :-1, :, :]
        + grad_z[..., 1:, :, :]
        + grad_x[..., :, :-1, :]
        + grad_x[..., :, 1:, :]
        + grad_y[..., :-1]
        + grad_y[..., 1:]
    )


def adjoint_pass(observe, conduct, weights, diag, rims, current):
    adjoint = jnp.broadcast_to(observe, conduct.shape)
    grad = jnp.zeros(conduct.shape, jnp.float32)
    for step in reversed(range(SWEEPS)):
        mult = adjoint / diag
        if step + 1 < SWEEPS:
            later = rims[step + 1][..., 1:-1, 1:-1, 1:-1]
        else:
            later = current
        term = -mult * later
        both = pad_plane(extended(jnp.stack([mult, term]), (("space", 2),), 1))
        grad = grad + face_terms(both[0], rims[step], both[1])
        if step > 0:
            adjoint = apply_faces(weights, both[0])
    return grad


def local(log_perm, noise, source, start_pressure, observe):
    conduct = jnp.exp(log_perm[None] + noise)
    start_full = jnp.broadcast_to(start_pressure, conduct.shape)
    rims = []
    joined = pad_plane(extended(jnp.stack([conduct, start_full]), (("space", 2),), 1))
    weights, diag = face_weights(joined[0])
    padded = joined[1]
    current = start_full
    for step in range(SWEEPS):
        if step > 0:
            padded = pad_plane(extended(current, (("space", 1),), 1))
        rims.append(padded)
        current = (source + apply_faces(weights, padded)) / diag
    grad = adjoint_pass(observe, conduct, weights, diag, rims, current)
    local_grad = jnp.sum(conduct * grad, axis=0)
    summed = lax.psum_scatter(local_grad, "draw", scatter_dimension=1, tiled=True)
    return (current, summed)


def solution(mesh):
    return jax.shard_map(
        local,
        mesh=mesh,
        in_specs=(
            P(("epi", "space"), None, None),
            P("draw", ("epi", "space"), None, None),
            P(("epi", "space"), None, None),
            P(("epi", "space"), None, None),
            P(("epi", "space"), None, None),
        ),
        out_specs=(P("draw", ("epi", "space"), None, None), P(("epi", "space"), "draw", None)),
        check_vma=False,
    )
```

profile of v0, /device:TPU:0, one launch (start us, length us, event | category | flops | bytes accessed | tf_op | source)
XLA Modules:
  0.0 132.2 jit_solution(8687566363700270305)
XLA Ops:
  7.2 0.0 copy-start.3
  7.2 0.0 reduce-scatter.2.cloned.1.call-start
  7.2 1.6 %fusion.73 = f32[1,1,8,64,384]{4,3,2,1,0:T(8,128)S(1)} fusion(f32[1,8,64,384]{3,2,1,0:T(8,128)} %param.6, f32[8,64,384]{2,1,0:T(8,128)} %param.5), kind=kLoop, calls=%fused_computation.196 | loop fusion | flops 196608 | bytes 2359296 | tf_op jit(solution)/shard_map/stack | solution.py:112
  8.8 1.0 pad_maximum_fusion.11
  9.7 4.9 %collective-permute-start = (f32[2,1,1,64,384]{4,3,2,1,0:T(8,128)S(1)}, f32[2,1,1,64,384]{4,3,2,1,0:T(8,128)S(1)}, u32[]{:S(2)}, u32[]{:S(2)}) collective-permute-start(f32[2,1,1,64,384]{4,3,2,1,0:T(8,128)S(1)} %get-tuple-element.23), channel_id=1, source_target_pairs={{0,4},{4,8},{8,12},{1,5},{5,9},{9,13},{2,6},{6,10},{10,14},{3,7},{... | collective-permute-start | bytes 589832 | tf_op jit(solution)/shard_map/ppermute | solution.py:16
  14.7 1.3 collective-permute-start.1
  16.0 2.8 %collective-permute-done = f32[2,1,1,64,384]{4,3,2,1,0:T(8,128)S(1)} collective-permute-done((f32[2,1,1,64,384]{4,3,2,1,0:T(8,128)S(1)}, f32[2,1,1,64,384]{4,3,2,1,0:T(8,128)S(1)}, u32[]{:S(2)}, u32[]{:S(2)}) %collective-permute-start) | collective-permute-done | bytes 196640 | tf_op jit(solution)/shard_map/ppermute | solution.py:16
  18.8 4.1 %collective-permute-done.1 = f32[2,1,1,64,384]{4,3,2,1,0:T(8,128)S(1)} collective-permute-done((f32[2,1,1,64,384]{4,3,2,1,0:T(8,128)S(1)}, f32[2,1,1,64,384]{4,3,2,1,0:T(8,128)S(1)}, u32[]{:S(2)}, u32[]{:S(2)}) %collective-permute-start.1) | collective-permute-done | bytes 196640 | tf_op jit(solution)/shard_map/ppermute | solution.py:17
  23.0 0.0 copy-done.3
  23.0 2.4 %select_maximum_fusion.9 = f32[2,1,10,66,386]{4,3,2,1,0:T(8,128)S(1)} fusion(f32[2,1,1,64,384]{4,3,2,1,0:T(8,128)S(1)} %collective-permute-done.1, f32[2,1,1,64,384]{4,3,2,1,0:T(8,128)S(1)} %collective-permute-done, f32[1,1,8,64,384]{4,3,2,1,0:T(8,128)S(1)} %bitcast.53, f32[1,1,8,64,384]{4,3,2,1,0:T(8,128)S(1)} %fusion.73), kind=kLoop, calls=%fused_computation.13 | loop fusion | flops 9171360 | bytes 4004160 | tf_op jit(solution)/shard_map/concatenate | solution.py:18
  25.3 0.3 slice_bitcast_fusion.6
  25.6 0.5 fusion.25
  26.2 0.0 copy-start
  26.2 0.5 fusion.24
  26.7 0.4 fusion.9
  27.1 0.2 copy-done
  27.3 1.5 %fusion.67 = f32[1,8,64,384]{3,2,1,0:T(8,128)S(1)} fusion(f32[1,10,66,386]{3,2,1,0:T(8,128)S(1)} %get-tuple-element.15, f32[8,64,384]{2,1,0:T(8,128)S(1)} %copy-done, f32[1,8,64,385]{3,2,1,0:T(8,128)S(1)} %fusion.9, f32[1,8,65,384]{3,2,1,0:T(8,128)S(1)} %fusion.24, f32[1,9,64,384]{3,2,1,0:T(8,128)S(1)} %fusion.25), kind=kLoop, calls=%fused_computation.178 | loop fusion | flops 3735552 | bytes 11010048 | tf_op jit(solution)/shard_map/div | solution.py:120
  28.9 3.5 %collective-permute-start.2 = (f32[1,1,64,384]{3,2,1,0:T(8,128)S(1)}, f32[1,1,64,384]{3,2,1,0:T(8,128)S(1)}, u32[]{:S(2)}, u32[]{:S(2)}) collective-permute-start(f32[1,1,64,384]{3,2,1,0:T(8,128)S(1)} %get-tuple-element.27), channel_id=1, source_target_pairs={{0,4},{4,8},{8,12},{1,5},{5,9},{9,13},{2,6},{6,10},{10,14},{3,7},{... | collective-permute-start | bytes 294920 | tf_op jit(solution)/shard_map/ppermute | solution.py:16
  32.4 1.3 collective-permute-start.3
  33.7 0.9 collective-permute-done.2
  34.6 4.3 %collective-permute-done.3 = f32[1,1,64,384]{3,2,1,0:T(8,128)S(1)} collective-permute-done((f32[1,1,64,384]{3,2,1,0:T(8,128)S(1)}, f32[1,1,64,384]{3,2,1,0:T(8,128)S(1)}, u32[]{:S(2)}, u32[]{:S(2)}) %collective-permute-start.3) | collective-permute-done | bytes 98336 | tf_op jit(solution)/shard_map/ppermute | solution.py:17
  38.9 0.5 select_maximum_fusion.14
  39.4 1.3 fusion.45
  40.7 0.0 copy-start.4
  40.7 3.6 %collective-permute-start.4 = (f32[1,1,64,384]{3,2,1,0:T(8,128)S(1)}, f32[1,1,64,384]{3,2,1,0:T(8,128)S(1)}, u32[]{:S(2)}, u32[]{:S(2)}) collective-permute-start(f32[1,1,64,384]{3,2,1,0:T(8,128)S(1)} %get-tuple-element.25), channel_id=1, source_target_pairs={{0,4},{4,8},{8,12},{1,5},{5,9},{9,13},{2,6},{6,10},{10,14},{3,7},{... | collective-permute-start | bytes 294920 | tf_op jit(solution)/shard_map/ppermute | solution.py:16
  44.4 1.3 collective-permute-start.5
  45.6 0.9 collective-permute-done.4
  46.5 4.3 %collective-permute-done.5 = f32[1,1,64,384]{3,2,1,0:T(8,128)S(1)} collective-permute-done((f32[1,1,64,384]{3,2,1,0:T(8,128)S(1)}, f32[1,1,64,384]{3,2,1,0:T(8,128)S(1)}, u32[]{:S(2)}, u32[]{:S(2)}) %collective-permute-start.5) | collective-permute-done | bytes 98336 | tf_op jit(solution)/shard_map/ppermute | solution.py:17
  50.9 0.5 select_maximum_fusion.12
  51.3 0.0 copy-done.4
  51.4 2.1 %multiply_bitcast_fusion.2 = (f32[1,1,8,64,384]{4,3,2,1,0:T(8,128)S(1)}, f32[1,8,64,384]{3,2,1,0:T(8,128)S(1)}, f32[1,8,64,384]{3,2,1,0:T(8,128)}) fusion(f32[1,8,64,385]{3,2,1,0:T(8,128)S(1)} %fusion.9, f32[1,8,65,384]{3,2,1,0:T(8,128)S(1)} %fusion.24, f32[1,9,64,384]{3,2,1,0:T(8,128)S(1)} %fusion.25, f32[8,64,384]{2,1,0:T(8,128)S(1)} %copy-done.4, ...), kind=kLoop, calls=%fused_computation.193 | loop fusion | flops 4718592 | bytes 12779520 | tf_op jit(solution)/shard_map/stack | solution.py:101
  53.5 1.9 %collective-permute-start.6 = (f32[2,1,1,64,384]{4,3,2,1,0:T(8,128)S(1)}, f32[2,1,1,64,384]{4,3,2,1,0:T(8,128)S(1)}, u32[]{:S(2)}, u32[]{:S(2)}) collective-permute-start(f32[2,1,1,64,384]{4,3,2,1,0:T(8,128)S(1)} %get-tuple-element.21), channel_id=1, source_target_pairs={{0,4},{4,8},{8,12},{1,5},{5,9},{9,13},{2,6},{6,10},{10,14},{3,7},{... | collective-permute-start | bytes 589832 | tf_op jit(solution)/shard_map/ppermute | solution.py:16
  55.4 1.5 %collective-permute-start.7 = (f32[2,1,1,64,384]{4,3,2,1,0:T(8,128)S(1)}, f32[2,1,1,64,384]{4,3,2,1,0:T(8,128)S(1)}, u32[]{:S(2)}, u32[]{:S(2)}) collective-permute-start(f32[2,1,1,64,384]{4,3,2,1,0:T(8,128)S(1)} %get-tuple-element.22), channel_id=1, source_target_pairs={{4,0},{8,4},{12,8},{5,1},{9,5},{13,9},{6,2},{10,6},{14,10},{7,3},{... | collective-permute-start | bytes 589832 | tf_op jit(solution)/shard_map/ppermute | solution.py:17
  56.9 1.7 %collective-permute-done.6 = f32[2,1,1,64,384]{4,3,2,1,0:T(8,128)S(1)} collective-permute-done((f32[2,1,1,64,384]{4,3,2,1,0:T(8,128)S(1)}, f32[2,1,1,64,384]{4,3,2,1,0:T(8,128)S(1)}, u32[]{:S(2)}, u32[]{:S(2)}) %collective-permute-start.6) | collective-permute-done | bytes 196640 | tf_op jit(solution)/shard_map/ppermute | solution.py:16
  58.6 4.4 %collective-permute-done.7 = f32[2,1,1,64,384]{4,3,2,1,0:T(8,128)S(1)} collective-permute-done((f32[2,1,1,64,384]{4,3,2,1,0:T(8,128)S(1)}, f32[2,1,1,64,384]{4,3,2,1,0:T(8,128)S(1)}, u32[]{:S(2)}, u32[]{:S(2)}) %collective-permute-start.7) | collective-permute-done | bytes 196640 | tf_op jit(solution)/shard_map/ppermute | solution.py:17
  63.0 2.4 %select_maximum_fusion.6 = f32[2,1,10,66,386]{4,3,2,1,0:T(8,128)S(1)} fusion(f32[2,1,1,64,384]{4,3,2,1,0:T(8,128)S(1)} %collective-permute-done.7, f32[2,1,1,64,384]{4,3,2,1,0:T(8,128)S(1)} %collective-permute-done.6, f32[1,1,8,64,384]{4,3,2,1,0:T(8,128)S(1)} %get-tuple-element.6, f32[1,1,8,64,384]{4,3,2,1,0:T(8,128)S(1)} %bitcast.51), kind=kLoop, calls=%fused_computation.10 | loop fusion | flops 9171360 | bytes 4004160 | tf_op jit(solution)/shard_map/concatenate | solution.py:18
  65.4 0.3 slice_bitcast_fusion.4
  65.7 1.6 %multiply_bitcast_fusion.1 = (f32[1,1,8,64,384]{4,3,2,1,0:T(8,128)S(1)}, f32[1,8,64,384]{3,2,1,0:T(8,128)S(1)}) fusion(f32[1,8,64,384]{3,2,1,0:T(8,128)S(1)} %fusion.45, f32[1,10,66,386]{3,2,1,0:T(8,128)S(1)} %get-tuple-element.10, f32[1,8,64,385]{3,2,1,0:T(8,128)S(1)} %fusion.9, f32[1,8,65,384]{3,2,1,0:T(8,128)S(1)} %fusion.24, ...), kind=kLoop, calls=%fused_computation.192 | loop fusion | flops 3932160 | bytes 11796480 | tf_op jit(solution)/shard_map/stack | solution.py:101
  67.3 1.2 slice_add_fusion.4
  68.5 1.9 %collective-permute-start.8 = (f32[2,1,1,64,384]{4,3,2,1,0:T(8,128)S(1)}, f32[2,1,1,64,384]{4,3,2,1,0:T(8,128)S(1)}, u32[]{:S(2)}, u32[]{:S(2)}) collective-permute-start(f32[2,1,1,64,384]{4,3,2,1,0:T(8,128)S(1)} %get-tuple-element.19), channel_id=1, source_target_pairs={{0,4},{4,8},{8,12},{1,5},{5,9},{9,13},{2,6},{6,10},{10,14},{3,7},{... | collective-permute-start | bytes 589832 | tf_op jit(solution)/shard_map/ppermute | solution.py:16
  70.4 1.3 collective-permute-start.9
  71.7 1.5 %slice_add_fusion.13 = f32[1,8,65,384]{3,2,1,0:T(8,128)S(1)} fusion(f32[1,10,66,386]{3,2,1,0:T(8,128)S(1)} %get-tuple-element.9, f32[1,10,66,386]{3,2,1,0:T(8,128)S(1)} %select_maximum_fusion.12, f32[1,10,66,386]{3,2,1,0:T(8,128)S(1)} %get-tuple-element.10), kind=kLoop, calls=%fused_computation.88 | loop fusion | flops 998400 | bytes 5591040 | tf_op jit(solution)/shard_map/add | solution.py:70
  73.2 0.3 collective-permute-done.8
  73.6 4.4 %collective-permute-done.9 = f32[2,1,1,64,384]{4,3,2,1,0:T(8,128)S(1)} collective-permute-done((f32[2,1,1,64,384]{4,3,2,1,0:T(8,128)S(1)}, f32[2,1,1,64,384]{4,3,2,1,0:T(8,128)S(1)}, u32[]{:S(2)}, u32[]{:S(2)}) %collective-permute-start.9) | collective-permute-done | bytes 196640 | tf_op jit(solution)/shard_map/ppermute | solution.py:17
  78.0 2.4 %select_maximum_fusion.3 = f32[2,1,10,66,386]{4,3,2,1,0:T(8,128)S(1)} fusion(f32[2,1,1,64,384]{4,3,2,1,0:T(8,128)S(1)} %collective-permute-done.9, f32[2,1,1,64,384]{4,3,2,1,0:T(8,128)S(1)} %collective-permute-done.8, f32[1,1,8,64,384]{4,3,2,1,0:T(8,128)S(1)} %get-tuple-element.4, f32[1,1,8,64,384]{4,3,2,1,0:T(8,128)S(1)} %bitcast.49), kind=kLoop, calls=%fused_computation.7 | loop fusion | flops 9171360 | bytes 4004160 | tf_op jit(solution)/shard_map/concatenate | solution.py:18
  80.4 0.3 slice_bitcast_fusion.2
  80.7 1.6 %multiply_bitcast_fusion = (f32[1,1,8,64,384]{4,3,2,1,0:T(8,128)S(1)}, f32[1,8,64,384]{3,2,1,0:T(8,128)S(1)}) fusion(f32[1,8,64,384]{3,2,1,0:T(8,128)S(1)} %fusion.67, f32[1,10,66,386]{3,2,1,0:T(8,128)S(1)} %get-tuple-element.12, f32[1,8,64,385]{3,2,1,0:T(8,128)S(1)} %fusion.9, f32[1,8,65,384]{3,2,1,0:T(8,128)S(1)} %fusion.24, f32[1,9,64,384]{3,2,1,0:T(8,128)S(1)} %fusion.25), kind=kLoop, calls=%fused_computation.191 | loop fusion | flops 3932160 | bytes 11796480 | tf_op jit(solution)/shard_map/stack | solution.py:101
  82.3 1.9 %collective-permute-start.10 = (f32[2,1,1,64,384]{4,3,2,1,0:T(8,128)S(1)}, f32[2,1,1,64,384]{4,3,2,1,0:T(8,128)S(1)}, u32[]{:S(2)}, u32[]{:S(2)}) collective-permute-start(f32[2,1,1,64,384]{4,3,2,1,0:T(8,128)S(1)} %get-tuple-element.17), channel_id=1, source_target_pairs={{0,4},{4,8},{8,12},{1,5},{5,9},{9,13},{2,6},{6,10},{10,14},{3,7},{... | collective-permute-start | bytes 589832 | tf_op jit(solution)/shard_map/ppermute | solution.py:16
  84.2 1.5 %collective-permute-start.11 = (f32[2,1,1,64,384]{4,3,2,1,0:T(8,128)S(1)}, f32[2,1,1,64,384]{4,3,2,1,0:T(8,128)S(1)}, u32[]{:S(2)}, u32[]{:S(2)}) collective-permute-start(f32[2,1,1,64,384]{4,3,2,1,0:T(8,128)S(1)} %get-tuple-element.18), channel_id=1, source_target_pairs={{4,0},{8,4},{12,8},{5,1},{9,5},{13,9},{6,2},{10,6},{14,10},{7,3},{... | collective-permute-start | bytes 589832 | tf_op jit(solution)/shard_map/ppermute | solution.py:17
  85.7 2.0 %fusion.13 = (f32[1,9,64,384]{3,2,1,0:T(8,128)S(1)}, f32[1,9,64,384]{3,2,1,0:T(8,128)S(1)}) fusion(f32[1,1,64,384]{3,2,1,0:T(8,128)S(1)} %collective-permute-done.5, f32[1,1,64,384]{3,2,1,0:T(8,128)S(1)} %collective-permute-done.4, f32[1,10,66,386]{3,2,1,0:T(8,128)S(1)} %get-tuple-element.9, f32[1,10,66,386]{3,2,1,0:T(8,128)S(1)} %get-tuple-element.10, ...), kind=kLoop, calls=%fused_computation.66 | loop fusion | flops 3096576 | bytes 10813440 | tf_op jit(solution)/shard_map/add | solution.py:64
  87.7 0.0 collective-permute-done.10
  87.7 4.0 %collective-permute-done.11 = f32[2,1,1,64,384]{4,3,2,1,0:T(8,128)S(1)} collective-permute-done((f32[2,1,1,64,384]{4,3,2,1,0:T(8,128)S(1)}, f32[2,1,1,64,384]{4,3,2,1,0:T(8,128)S(1)}, u32[]{:S(2)}, u32[]{:S(2)}) %collective-permute-start.11) | collective-permute-done | bytes 196640 | tf_op jit(solution)/shard_map/ppermute | solution.py:17
  91.8 2.4 %select_maximum_fusion = f32[2,1,10,66,386]{4,3,2,1,0:T(8,128)S(1)} fusion(f32[2,1,1,64,384]{4,3,2,1,0:T(8,128)S(1)} %collective-permute-done.11, f32[2,1,1,64,384]{4,3,2,1,0:T(8,128)S(1)} %collective-permute-done.10, f32[1,1,8,64,384]{4,3,2,1,0:T(8,128)S(1)} %get-tuple-element.2, f32[1,1,8,64,384]{4,3,2,1,0:T(8,128)S(1)} %bitcast.47), kind=kLoop, calls=%fused_computation.4 | loop fusion | flops 9171360 | bytes 4004160 | tf_op jit(solution)/shard_map/concatenate | solution.py:18
  94.2 0.3 slice_bitcast_fusion.1
  94.5 1.5 %slice_add_fusion.9 = f32[1,9,64,384]{3,2,1,0:T(8,128)S(1)} fusion(f32[1,10,66,386]{3,2,1,0:T(8,128)S(1)} %get-tuple-element.14, f32[1,10,66,386]{3,2,1,0:T(8,128)S(1)} %get-tuple-element.15, f32[1,10,66,386]{3,2,1,0:T(8,128)S(1)} %get-tuple-element.13), kind=kLoop, calls=%fused_computation.78 | loop fusion | flops 1105920 | bytes 6193152 | tf_op jit(solution)/shard_map/add | solution.py:64
  96.0 3.0 %slice_add_fusion.7 = (f32[1,8,65,384]{3,2,1,0:T(8,128)S(1)}, f32[1,8,65,384]{3,2,1,0:T(8,128)S(1)}) fusion(f32[1,10,66,386]{3,2,1,0:T(8,128)S(1)} %get-tuple-element.14, f32[1,10,66,386]{3,2,1,0:T(8,128)S(1)} %get-tuple-element.15, f32[1,10,66,386]{3,2,1,0:T(8,128)S(1)} %get-tuple-element.13, f32[1,10,66,386]{3,2,1,0:T(8,128)S(1)} %get-tuple-element.11, ...), kind=kLoop, calls=%fused_computation.73 | loop fusion | flops 1996800 | bytes 11182080 | tf_op jit(solution)/shard_map/add | solution.py:70
  99.0 0.0 copy-start.1
  99.1 0.0 copy-start.2
  99.1 2.7 %slice_add_fusion = (f32[1,8,64,385]{3,2,1,0:T(8,128)S(1)}, f32[1,8,64,385]{3,2,1,0:T(8,128)S(1)}) fusion(f32[1,10,66,386]{3,2,1,0:T(8,128)S(1)} %get-tuple-element.14, f32[1,10,66,386]{3,2,1,0:T(8,128)S(1)} %get-tuple-element.15, f32[1,10,66,386]{3,2,1,0:T(8,128)S(1)} %get-tuple-element.13, f32[1,10,66,386]{3,2,1,0:T(8,128)S(1)} %get-tuple-element.11, ...), kind=kLoop, calls=%fused_computation.46 | loop fusion | flops 1971200 | bytes 11038720 | tf_op jit(solution)/shard_map/add | solution.py:76
  101.8 0.0 copy-done.1
  101.8 0.0 copy-done.2
  101.8 1.9 %fusion.51 = f32[8,64,384]{2,1,0:T(8,128)} fusion(f32[1,8,64,385]{3,2,1,0:T(8,128)S(1)} %get-tuple-element.29, f32[1,8,65,384]{3,2,1,0:T(8,128)S(1)} %get-tuple-element.33, f32[1,9,64,384]{3,2,1,0:T(8,128)S(1)} %slice_add_fusion.9, f32[1,8,64,385]{3,2,1,0:T(8,128)S(1)} %get-tuple-element.30, f32[1,8,65,384]{3,2,1,0:T(8,128)S(1)} %get-tuple-element.34, ...), kind=kLoop, calls=%fused_computation.127 | loop fusion | flops 3932160 | bytes 16515072 | tf_op jit(solution)/shard_map/reduce_sum | solution.py:122
  103.7 0.0 reduce-scatter.2.cloned.1.call-update
  103.7 21.6 %reduce-scatter.2.cloned.1.call-done = f32[8,16,384]{2,1,0:T(8,128)} async-done(((f32[8,64,384]{2,1,0:T(8,128)}), f32[8,16,384]{2,1,0:T(8,128)}) %reduce-scatter.2.cloned.1.call-update) | async-done | bytes 196624 | tf_op jit(solution)/shard_map/reduce_scatter | solution.py:123
  (5 shorter events, 0.1 us)
Async XLA Ops:
  7.2 15.8 %copy-start.3 = (f32[8,64,384]{2,1,0:T(8,128)S(1)}, f32[8,64,384]{2,1,0:T(8,128)}, u32[]{:S(2)}) copy-start(f32[8,64,384]{2,1,0:T(8,128)} %param.8) | copy-start | bytes 2359300
  7.2 118.2 %reduce-scatter.2.cloned.1.call-start = ((), (), s32[]{:S(2)}) async-start(), calls=%async_computation.1 | async-start | bytes 983040 | tf_op jit(solution)/shard_map/reduce_scatter | solution.py:123
  9.7 9.1 %collective-permute-start = (f32[2,1,1,64,384]{4,3,2,1,0:T(8,128)S(1)}, f32[2,1,1,64,384]{4,3,2,1,0:T(8,128)S(1)}, u32[]{:S(2)}, u32[]{:S(2)}) collective-permute-start(f32[2,1,1,64,384]{4,3,2,1,0:T(8,128)S(1)} %get-tuple-element.23), channel_id=1, source_target_pairs={{0,4},{4,8},{8,12},{1,5},{5,9},{9,13},{2,6},{6,10},{10,14},{3,7},{... | collective-permute-start | bytes 589832 | tf_op jit(solution)/shard_map/ppermute | solution.py:16
  14.7 8.3 %collective-permute-start.1 = (f32[2,1,1,64,384]{4,3,2,1,0:T(8,128)S(1)}, f32[2,1,1,64,384]{4,3,2,1,0:T(8,128)S(1)}, u32[]{:S(2)}, u32[]{:S(2)}) collective-permute-start(f32[2,1,1,64,384]{4,3,2,1,0:T(8,128)S(1)} %get-tuple-element.24), channel_id=1, source_target_pairs={{4,0},{8,4},{12,8},{5,1},{9,5},{13,9},{6,2},{10,6},{14,10},{7,3},{... | collective-permute-start | bytes 589832 | tf_op jit(solution)/shard_map/ppermute | solution.py:17
  26.2 1.1 copy-start
  28.9 5.7 %collective-permute-start.2 = (f32[1,1,64,384]{3,2,1,0:T(8,128)S(1)}, f32[1,1,64,384]{3,2,1,0:T(8,128)S(1)}, u32[]{:S(2)}, u32[]{:S(2)}) collective-permute-start(f32[1,1,64,384]{3,2,1,0:T(8,128)S(1)} %get-tuple-element.27), channel_id=1, source_target_pairs={{0,4},{4,8},{8,12},{1,5},{5,9},{9,13},{2,6},{6,10},{10,14},{3,7},{... | collective-permute-start | bytes 294920 | tf_op jit(solution)/shard_map/ppermute | solution.py:16
  32.4 6.5 %collective-permute-start.3 = (f32[1,1,64,384]{3,2,1,0:T(8,128)S(1)}, f32[1,1,64,384]{3,2,1,0:T(8,128)S(1)}, u32[]{:S(2)}, u32[]{:S(2)}) collective-permute-start(f32[1,1,64,384]{3,2,1,0:T(8,128)S(1)} %get-tuple-element.28), channel_id=1, source_target_pairs={{4,0},{8,4},{12,8},{5,1},{9,5},{13,9},{6,2},{10,6},{14,10},{7,3},{... | collective-permute-start | bytes 294920 | tf_op jit(solution)/shard_map/ppermute | solution.py:17
  40.7 10.7 %copy-start.4 = (f32[8,64,384]{2,1,0:T(8,128)S(1)}, f32[8,64,384]{2,1,0:T(8,128)}, u32[]{:S(2)}) copy-start(f32[8,64,384]{2,1,0:T(8,128)} %param.9) | copy-start | bytes 2359300
  40.7 5.8 %collective-permute-start.4 = (f32[1,1,64,384]{3,2,1,0:T(8,128)S(1)}, f32[1,1,64,384]{3,2,1,0:T(8,128)S(1)}, u32[]{:S(2)}, u32[]{:S(2)}) collective-permute-start(f32[1,1,64,384]{3,2,1,0:T(8,128)S(1)} %get-tuple-element.25), channel_id=1, source_target_pairs={{0,4},{4,8},{8,12},{1,5},{5,9},{9,13},{2,6},{6,10},{10,14},{3,7},{... | collective-permute-start | bytes 294920 | tf_op jit(solution)/shard_map/ppermute | solution.py:16
  44.4 6.5 %collective-permute-start.5 = (f32[1,1,64,384]{3,2,1,0:T(8,128)S(1)}, f32[1,1,64,384]{3,2,1,0:T(8,128)S(1)}, u32[]{:S(2)}, u32[]{:S(2)}) collective-permute-start(f32[1,1,64,384]{3,2,1,0:T(8,128)S(1)} %get-tuple-element.26), channel_id=1, source_target_pairs={{4,0},{8,4},{12,8},{5,1},{9,5},{13,9},{6,2},{10,6},{14,10},{7,3},{... | collective-permute-start | bytes 294920 | tf_op jit(solution)/shard_map/ppermute | solution.py:17
  53.5 5.1 %collective-permute-start.6 = (f32[2,1,1,64,384]{4,3,2,1,0:T(8,128)S(1)}, f32[2,1,1,64,384]{4,3,2,1,0:T(8,128)S(1)}, u32[]{:S(2)}, u32[]{:S(2)}) collective-permute-start(f32[2,1,1,64,384]{4,3,2,1,0:T(8,128)S(1)} %get-tuple-element.21), channel_id=1, source_target_pairs={{0,4},{4,8},{8,12},{1,5},{5,9},{9,13},{2,6},{6,10},{10,14},{3,7},{... | collective-permute-start | bytes 589832 | tf_op jit(solution)/shard_map/ppermute | solution.py:16
  55.4 7.6 %collective-permute-start.7 = (f32[2,1,1,64,384]{4,3,2,1,0:T(8,128)S(1)}, f32[2,1,1,64,384]{4,3,2,1,0:T(8,128)S(1)}, u32[]{:S(2)}, u32[]{:S(2)}) collective-permute-start(f32[2,1,1,64,384]{4,3,2,1,0:T(8,128)S(1)} %get-tuple-element.22), channel_id=1, source_target_pairs={{4,0},{8,4},{12,8},{5,1},{9,5},{13,9},{6,2},{10,6},{14,10},{7,3},{... | collective-permute-start | bytes 589832 | tf_op jit(solution)/shard_map/ppermute | solution.py:17
  68.5 5.1 %collective-permute-start.8 = (f32[2,1,1,64,384]{4,3,2,1,0:T(8,128)S(1)}, f32[2,1,1,64,384]{4,3,2,1,0:T(8,128)S(1)}, u32[]{:S(2)}, u32[]{:S(2)}) collective-permute-start(f32[2,1,1,64,384]{4,3,2,1,0:T(8,128)S(1)} %get-tuple-element.19), channel_id=1, source_target_pairs={{0,4},{4,8},{8,12},{1,5},{5,9},{9,13},{2,6},{6,10},{10,14},{3,7},{... | collective-permute-start | bytes 589832 | tf_op jit(solution)/shard_map/ppermute | solution.py:16
  70.4 7.6 %collective-permute-start.9 = (f32[2,1,1,64,384]{4,3,2,1,0:T(8,128)S(1)}, f32[2,1,1,64,384]{4,3,2,1,0:T(8,128)S(1)}, u32[]{:S(2)}, u32[]{:S(2)}) collective-permute-start(f32[2,1,1,64,384]{4,3,2,1,0:T(8,128)S(1)} %get-tuple-element.20), channel_id=1, source_target_pairs={{4,0},{8,4},{12,8},{5,1},{9,5},{13,9},{6,2},{10,6},{14,10},{7,3},{... | collective-permute-start | bytes 589832 | tf_op jit(solution)/shard_map/ppermute | solution.py:17
  82.3 5.4 %collective-permute-start.10 = (f32[2,1,1,64,384]{4,3,2,1,0:T(8,128)S(1)}, f32[2,1,1,64,384]{4,3,2,1,0:T(8,128)S(1)}, u32[]{:S(2)}, u32[]{:S(2)}) collective-permute-start(f32[2,1,1,64,384]{4,3,2,1,0:T(8,128)S(1)} %get-tuple-element.17), channel_id=1, source_target_pairs={{0,4},{4,8},{8,12},{1,5},{5,9},{9,13},{2,6},{6,10},{10,14},{3,7},{... | collective-permute-start | bytes 589832 | tf_op jit(solution)/shard_map/ppermute | solution.py:16
  84.2 7.6 %collective-permute-start.11 = (f32[2,1,1,64,384]{4,3,2,1,0:T(8,128)S(1)}, f32[2,1,1,64,384]{4,3,2,1,0:T(8,128)S(1)}, u32[]{:S(2)}, u32[]{:S(2)}) collective-permute-start(f32[2,1,1,64,384]{4,3,2,1,0:T(8,128)S(1)} %get-tuple-element.18), channel_id=1, source_target_pairs={{4,0},{8,4},{12,8},{5,1},{9,5},{13,9},{6,2},{10,6},{14,10},{7,3},{... | collective-permute-start | bytes 589832 | tf_op jit(solution)/shard_map/ppermute | solution.py:17
  99.0 2.7 %copy-start.1 = (f32[1,8,64,384]{3,2,1,0:T(8,128)S(1)}, f32[1,8,64,384]{3,2,1,0:T(8,128)}, u32[]{:S(2)}) copy-start(f32[1,8,64,384]{3,2,1,0:T(8,128)} %param.6) | copy-start | bytes 2359300
  99.1 2.7 %copy-start.2 = (f32[8,64,384]{2,1,0:T(8,128)S(1)}, f32[8,64,384]{2,1,0:T(8,128)}, u32[]{:S(2)}) copy-start(f32[8,64,384]{2,1,0:T(8,128)} %param.5) | copy-start | bytes 2359300
Sparse Core Ops, SparseCore 0:
  103.8 21.4 reduce-scatter.1
where the time goes:
time: 133 us; the launch traced here: 132 us
  waiting for transfers between devices  53.9 us (41%)
  other arithmetic  36.5 us (27%)
  starting transfers between devices  26 us (20%)
  between operations  14.4 us (11%)
  local copies, waits for them, and re-layouts  1.43 us (1%)
    ppermute x6, waiting for transfers between devices, extended(): after = lax.ppermute(initial, axis, down)  25.6 us
    reduce_scatter x1, waiting for transfers between devices, local(): lax.psum_scatter(local_grad, 'draw', scatter_dimension=1, tiled=True)  21.6 us
    ppermute x6, starting transfers between devices, extended(): before = lax.ppermute(last, axis, up)  17.8 us
    concatenate x6, other arithmetic, extended(): shard = jnp.concatenate([before, shard, after], axis=dim)  10.5 us
    ppermute x6, starting transfers between devices, extended(): after = lax.ppermute(initial, axis, down)  8.15 us
    ppermute x6, waiting for transfers between devices, extended(): before = lax.ppermute(last, axis, up)  6.63 us
    another operation x3, other arithmetic, adjoint_pass(): both = pad_plane(extended(jnp.stack([mult, term]), (('space', 2),), 1))  5.29 us
    add x2, other arithmetic, face_terms(): padded_u[..., 1:-1, :-1, 1:-1] * padded_q[..., 1:-1, 1:, 1:-1]  4.56 us
  transfers between devices with their start and end apart: 13, of which 12 were waited for; matrix products, arithmetic and copies ran while one was open for 3% of the time, Pallas kernels for 0%

commit v1 on v0

v1 whole, which is shorter than its diff:
```python
import functools

import jax
import jax.numpy as jnp
from jax import lax
from jax.experimental import pallas as pl
from jax.experimental.pallas import tpu as pltpu
from jax.sharding import PartitionSpec as P

SWEEPS = 3
HALO = SWEEPS + 1
LANES = 128
SUB = 8


def neighbours(ref, zz, r, rows):
    tiles = ref.shape[1]
    lane = lax.broadcasted_iota(jnp.int32, (SUB, LANES), 1)
    sub = lax.broadcasted_iota(jnp.int32, (SUB, LANES), 0)
    zero = jnp.zeros((SUB, LANES), jnp.float32)
    here = pl.ds(SUB * r, SUB)
    own = [ref[zz, c, here, :] for c in range(tiles)]
    fwd = [pltpu.roll(v, 1, 1) for v in own]
    bwd = [pltpu.roll(v, LANES - 1, 1) for v in own]
    out = []
    for c in range(tiles):
        left = jnp.where(lane == 0, fwd[c - 1] if c > 0 else zero, fwd[c])
        right = jnp.where(lane == LANES - 1, bwd[c + 1] if c + 1 < tiles else zero, bwd[c])
        if r > 0:
            north = ref[zz, c, pl.ds(SUB * r - 1, SUB), :]
        else:
            north = jnp.where(sub == 0, zero, pltpu.roll(own[c], 1, 0))
        if r + 1 < rows:
            south = ref[zz, c, pl.ds(SUB * r + 1, SUB), :]
        else:
            south = jnp.where(sub == SUB - 1, zero, pltpu.roll(own[c], SUB - 1, 0))
        out.append((left, right, north, south, ref[zz - 1, c, here, :], ref[zz + 1, c, here, :]))
    return own, out


def six(parts):
    a, b, c, d, e, f = parts
    return ((a + b) + (c + d)) + (e + f)


def kernel(
    k_in, klo_in, khi_in, p0_in, src_in, obs_in, alo_in, ahi_in, blo_in, bhi_in,
    press_out, keep_out, send_out,
    K, P0, P1, P2, P3, U1, U2, U3, X, Y, X2, Y2, E, G, NP0, RINV, SRC, OBS, sems,
):
    slab = p0_in.shape[0]
    nx = p0_in.shape[1]
    half = nx // 2
    rows, tiles = nx // SUB, p0_in.shape[2] // LANES
    top = HALO + slab
    depth = top + HALO
    draw, draws = lax.axis_index("draw"), lax.axis_size("draw")
    space, spaces = lax.axis_index("space"), lax.axis_size("space")
    par, group = draw % 2, draw // 2
    groups = draws // 2
    block = nx // draws

    copies = []

    def copy(src, dst):
        cp = pltpu.make_async_copy(src, dst, sems.at[len(copies)])
        cp.start()
        copies.append(cp)

    mine = pl.ds(pl.multiple_of(half * par, half), half)
    other = pl.ds(pl.multiple_of(half * (1 - par), half), half)
    for c in range(tiles):
        cols = pl.ds(c * LANES, LANES)
        copy(k_in.at[:, :, cols], K.at[pl.ds(HALO, slab), c])
        copy(klo_in.at[:, :, cols], K.at[pl.ds(0, HALO), c])
        copy(khi_in.at[:, :, cols], K.at[pl.ds(top, HALO), c])
        copy(p0_in.at[:, :, cols], P0.at[pl.ds(HALO, slab), c])
        for lo, hi, at in ((alo_in, ahi_in, mine), (blo_in, bhi_in, other)):
            copy(lo.at[pl.ds(0, HALO), :, cols], P0.at[pl.ds(0, HALO), c, at])
            copy(hi.at[pl.ds(0, HALO), :, cols], P0.at[pl.ds(top, HALO), c, at])
    copy(src_in, SRC.at[pl.ds(HALO, slab)])
    copy(obs_in, OBS.at[pl.ds(HALO, slab)])
    for lo, hi, at in ((alo_in, ahi_in, mine), (blo_in, bhi_in, other)):
        copy(lo.at[pl.ds(HALO, SWEEPS)], SRC.at[pl.ds(1, SWEEPS), at])
        copy(lo.at[pl.ds(HALO + SWEEPS, SWEEPS)], OBS.at[pl.ds(1, SWEEPS), at])
        copy(hi.at[pl.ds(HALO, SWEEPS)], SRC.at[pl.ds(top, SWEEPS), at])
        copy(hi.at[pl.ds(HALO + SWEEPS, SWEEPS)], OBS.at[pl.ds(top, SWEEPS), at])
    for cp in copies:
        cp.wait()

    low_in = jnp.where(space > 0, 1.0, 0.0).astype(jnp.float32)
    high_in = jnp.where(space + 1 < spaces, 1.0, 0.0).astype(jnp.float32)

    def at(r):
        return pl.ds(SUB * r, SUB)

    def cl(c):
        return pl.ds(c * LANES, LANES)

    def stage1(zz, _):
        inside = jnp.where(zz < HALO, low_in, jnp.where(zz >= top, high_in, jnp.float32(1.0)))
        for r in range(rows):
            k, kn = neighbours(K, zz, r, rows)
            p, pn = neighbours(P0, zz, r, rows)
            for c in range(tiles):
                rinv = inside / (0.5 + 0.5 * (6.0 * k[c] + six(kn[c])))
                flow = six([(k[c] + a) * b for a, b in zip(kn[c], pn[c])])
                p1 = (SRC[zz, at(r), cl(c)] + 0.5 * flow) * rinv
                u3 = OBS[zz, at(r), cl(c)] * rinv
                RINV[zz, c, at(r), :] = rinv
                NP0[zz, c, at(r), :] = six(pn[c])
                P1[zz, c, at(r), :] = p1
                U3[zz, c, at(r), :] = u3
                X[zz, c, at(r), :] = k[c] * p1
                Y[zz, c, at(r), :] = k[c] * u3
        return 0

    lax.fori_loop(1, depth - 1, stage1, 0)

    def stage2(zz, _):
        for r in range(rows):
            _, a = neighbours(P1, zz, r, rows)
            _, b = neighbours(X, zz, r, rows)
            _, v = neighbours(U3, zz, r, rows)
            _, w = neighbours(Y, zz, r, rows)
            for c in range(tiles):
                k, rinv = K[zz, c, at(r), :], RINV[zz, c, at(r), :]
                np1, nu3 = six(a[c]), six(v[c])
                p2 = (SRC[zz, at(r), cl(c)] + 0.5 * (k * np1 + six(b[c]))) * rinv
                u2 = (0.5 * (k * nu3 + six(w[c]))) * rinv
                P2[zz, c, at(r), :] = p2
                U2[zz, c, at(r), :] = u2
                X2[zz, c, at(r), :] = k * p2
                Y2[zz, c, at(r), :] = k * u2
                G[zz, c, at(r), :] = u2 * np1 + p2 * nu3
        return 0

    lax.fori_loop(2, depth - 2, stage2, 0)

    def stage3(zz, _):
        for r in range(rows):
            p2, a = neighbours(P2, zz, r, rows)
            _, b = neighbours(X2, zz, r, rows)
            u2, v = neighbours(U2, zz, r, rows)
            _, w = neighbours(Y2, zz, r, rows)
            for c in range(tiles):
                k, rinv = K[zz, c, at(r), :], RINV[zz, c, at(r), :]
                p1, u3 = P1[zz, c, at(r), :], U3[zz, c, at(r), :]
                np2, nu2 = six(a[c]), six(v[c])
                p3 = (SRC[zz, at(r), cl(c)] + 0.5 * (k * np2 + six(b[c]))) * rinv
                u1 = (0.5 * (k * nu2 + six(w[c]))) * rinv
                e = -(u1 * p1 + u2[c] * p2[c] + u3 * p3)
                g = G[zz, c, at(r), :] + u3 * np2 + p1 * nu2 + u1 * NP0[zz, c, at(r), :]
                P3[zz, at(r), cl(c)] = p3
                U1[zz, c, at(r), :] = u1
                E[zz, c, at(r), :] = e
                G[zz, c, at(r), :] = g + 6.0 * e
        return 0

    lax.fori_loop(3, depth - 3, stage3, 0)
    out = pltpu.make_async_copy(P3.at[pl.ds(HALO, slab)], press_out, sems.at[0])
    out.start()

    def gradient(zz, r):
        _, v = neighbours(U1, zz, r, rows)
        _, w = neighbours(E, zz, r, rows)
        return [
            0.5 * K[zz, c, at(r), :] * (G[zz, c, at(r), :] + P0[zz, c, at(r), :] * six(v[c]) + six(w[c]))
            for c in range(tiles)
        ]

    def stage4(z, _):
        zz = z + HALO
        for h in range(groups):
            slot = (h - group + groups) % groups
            for q in range(block // SUB):
                even = gradient(zz, (2 * h * block) // SUB + q)
                odd = gradient(zz, ((2 * h + 1) * block) // SUB + q)
                for c in range(tiles):
                    keep_out[slot, z, pl.ds(SUB * q, SUB), cl(c)] = jnp.where(par == 0, even[c], odd[c])
                    send_out[slot, z, pl.ds(SUB * q, SUB), cl(c)] = jnp.where(par == 0, odd[c], even[c])
        return 0

    lax.fori_loop(0, slab, stage4, 0)
    out.wait()


def solve(k, klo, khi, p0, src, obs, alo, ahi, blo, bhi, draws):
    slab, nx, ny = p0.shape
    tiles = ny // LANES
    depth = slab + 2 * HALO
    field = pltpu.VMEM((depth, tiles, nx, LANES), jnp.float32)
    plain = pltpu.VMEM((depth, nx, ny), jnp.float32)
    part = jax.ShapeDtypeStruct((draws // 2, slab, nx // draws, ny), jnp.float32)
    anywhere = pl.BlockSpec(memory_space=pl.ANY)
    whole = pl.BlockSpec(memory_space=pltpu.VMEM)
    return pl.pallas_call(
        kernel,
        out_shape=(jax.ShapeDtypeStruct((slab, nx, ny), jnp.float32), part, part),
        in_specs=[anywhere] * 10,
        out_specs=(anywhere, whole, whole),
        scratch_shapes=[
            field, field, field, field, plain, field, field, field, field, field, field, field, field, field, field,
            field, plain, plain, pltpu.SemaphoreType.DMA((8 * tiles + 10,)),
        ],
        compiler_params=pltpu.CompilerParams(vmem_limit_bytes=56 * 2**20),
        cost_estimate=pl.CostEstimate(flops=200 * depth * nx * ny, bytes_accessed=40 * slab * nx * ny, transcendentals=0),
    )(k, klo, khi, p0, src, obs, alo, ahi, blo, bhi)


def local(log_perm, noise, source, start_pressure, observe):
    draws, spaces = lax.axis_size("draw"), lax.axis_size("space")
    draw = lax.axis_index("draw")
    nx = log_perm.shape[1]
    half = nx // 2
    up = [(i, i + 1) for i in range(spaces - 1)]
    down = [(j, i) for i, j in up]
    pair = [(i, i ^ 1) for i in range(draws)]

    def edge(start):
        pick = (lambda a, w: a[a.shape[0] - w :]) if start is None else (lambda a, w: a[:w])
        joined = [pick(start_pressure, HALO), pick(source, SWEEPS), pick(observe, SWEEPS)]
        cut = [lax.dynamic_slice_in_dim(a, (draw % 2) * half, half, axis=1) for a in joined]
        return jnp.concatenate(cut, axis=0)

    alo = lax.ppermute(edge(None), "space", up)
    ahi = lax.ppermute(edge(0), "space", down)
    k = jnp.exp(log_perm + noise[0])
    klo = lax.ppermute(k[k.shape[0] - HALO :], "space", up)
    khi = lax.ppermute(k[:HALO], "space", down)
    blo = lax.ppermute(alo, "draw", pair)
    bhi = lax.ppermute(ahi, "draw", pair)
    press, keep, send = solve(k, klo, khi, start_pressure, source, observe, alo, ahi, blo, bhi, draws)
    both = keep + lax.ppermute(send, "draw", pair)
    total = both[0]
    for s in range(1, draws // 2):
        total = total + lax.ppermute(both[s], "draw", [(j, (j + 2 * s) % draws) for j in range(draws)])
    return press[None], total


def solution(mesh):
    return jax.shard_map(
        local,
        mesh=mesh,
        in_specs=(
            P(("epi", "space"), None, None),
            P("draw", ("epi", "space"), None, None),
            P(("epi", "space"), None, None),
            P(("epi", "space"), None, None),
            P(("epi", "space"), None, None),
        ),
        out_specs=(P("draw", ("epi", "space"), None, None), P(("epi", "space"), "draw", None)),
        check_vma=False,
    )
```

time: 133 us -> 63.8 us (0.48)
  other arithmetic: 36.5 us -> 1.94 us
  waiting for transfers between devices: 53.9 us -> 26.5 us
  Pallas kernels: 0 us -> 14.7 us
  between operations: 14.4 us -> 0.87 us
  starting transfers between devices: 26 us -> 15.1 us
  local copies, waits for them, and re-layouts: 1.43 us -> 4.37 us
    reduce_scatter x1 -> x0, waiting for transfers between devices: 21.6 us -> none  [local(): lax.psum_scatter(local_grad, 'draw', scatter_dimension=1, tiled=True)]
    pallas_call x0 -> x1, Pallas kernels: none -> 14.7 us  [solve(): pl.pallas_call(kernel, out_shape=(jax.ShapeDtypeStruct((slab, nx, ny), jn...]
    ppermute x12 -> x8, starting transfers between devices: 26 us -> 15.1 us  [the longest x1 5.72 us: local(): alo = lax.ppermute(edge(None), 'space', up)]
    concatenate x6 -> x2, other arithmetic: 10.5 us -> 0.07 us  [edge(): return jnp.concatenate(cut, axis=0)]
    add x6 -> x2, other arithmetic: 11.9 us -> 1.75 us  [the longest x1 1.05 us: local(): both = keep + lax.ppermute(send, 'draw', pair)]
    another operation x4 -> x0, other arithmetic: 6.84 us -> none  [the longest x3 5.29 us: adjoint_pass(): both = pad_plane(extended(jnp.stack([mult, term]), (('space', 2),), 1))]
    ppermute x12 -> x8, waiting for transfers between devices: 32.2 us -> 26.5 us  [the longest x1 8.83 us: local(): ahi = lax.ppermute(edge(0), 'space', down)]
    div x2 -> x0, other arithmetic: 2.86 us -> none  [local(): current = (source + apply_faces(weights, padded)) / diag]
  transfers between devices with their start and end apart: 13 -> 8, of which waited for: 12 -> 6; matrix products, arithmetic and copies ran while one was open for 3% -> 0% of each run, Pallas kernels for 0% -> 0%
where the time goes in v1:
time: 63.8 us; the launch traced here: 63.5 us
  waiting for transfers between devices  26.5 us (42%)
  starting transfers between devices  15.1 us (24%)
  Pallas kernels  14.7 us (23%)
  local copies, waits for them, and re-layouts  4.37 us (7%)
  other arithmetic  1.94 us (3%)
  between operations  0.87 us (1%)
    pallas_call x1, Pallas kernels, solve(): pl.pallas_call(kernel, out_shape=(jax.ShapeDtypeStruct((slab, nx, ny), jn...  14.7 us
    ppermute x1, waiting for transfers between devices, local(): ahi = lax.ppermute(edge(0), 'space', down)  8.83 us
    ppermute x1, waiting for transfers between devices, local(): khi = lax.ppermute(k[:HALO], 'space', down)  7.82 us
    ppermute x1, starting transfers between devices, local(): alo = lax.ppermute(edge(None), 'space', up)  5.72 us
    ppermute x1, waiting for transfers between devices, local(): lax.ppermute(both[s], 'draw', [(j, (j + 2 * s) % draws) for j in range(dr...  5.29 us
    ppermute x1, starting transfers between devices, local(): klo = lax.ppermute(k[k.shape[0] - HALO:], 'space', up)  5.04 us
    unnamed x22, local copies, waits for them, and re-layouts  2.94 us
    ppermute x1, waiting for transfers between devices, local(): both = keep + lax.ppermute(send, 'draw', pair)  1.92 us
  transfers between devices with their start and end apart: 8, of which 6 were waited for; matrix products, arithmetic and copies ran while one was open for 0% of the time, Pallas kernels for 0%

profile of v1, /device:TPU:0, one launch (start us, length us, event | category | flops | bytes accessed | tf_op | source)
XLA Modules:
  0.0 63.5 jit_solution(8251443866410865579)
XLA Ops:
  0.6 0.0 copy-start.2
  0.7 1.2 %fusion.3 = (f32[3,64,384]{2,1,0:T(8,128)S(1)}, f32[3,64,384]{2,1,0:T(8,128)S(1)}) fusion(f32[8,64,384]{2,1,0:T(8,128)} %src_in.1), kind=kLoop, calls=%fused_computation.14 | loop fusion | bytes 1179648 | tf_op jit(solution)/shard_map/slice | solution.py:221
  1.8 0.1 copy-done.2
  1.9 0.0 copy-start.1
  2.0 1.1 %copy-done.1 = f32[8,64,384]{2,1,0:T(8,128)S(1)} copy-done((f32[8,64,384]{2,1,0:T(8,128)S(1)}, f32[8,64,384]{2,1,0:T(8,128)}, u32[]{:S(2)}) %copy-start.1) | copy-done | bytes 786456
  3.1 0.1 fusion.2
  3.2 1.3 %collective-permute-start.3 = (f32[10,32,384]{2,1,0:T(8,128)S(1)}, f32[10,32,384]{2,1,0:T(8,128)S(1)}, u32[]{:S(2)}, u32[]{:S(2)}) collective-permute-start(f32[10,32,384]{2,1,0:T(8,128)S(1)} %pad_maximum_fusion.1), channel_id=1, source_target_pairs={{4,0},{8,4},{12,8},{5,1},{9,5},{13,9},{6,2},{10,6},{14,10},{7,3},{... | collective-permute-start | bytes 1474568 | tf_op jit(solution)/shard_map/ppermute | solution.py:227
  4.6 0.0 copy-start.3
  4.6 0.0 copy-start.4
  4.7 5.7 %collective-permute-start.2 = (f32[10,32,384]{2,1,0:T(8,128)S(1)}, f32[10,32,384]{2,1,0:T(8,128)S(1)}, u32[]{:S(2)}, u32[]{:S(2)}) collective-permute-start(f32[10,32,384]{2,1,0:T(8,128)S(1)} %pad_maximum_fusion), channel_id=1, source_target_pairs={{0,4},{4,8},{8,12},{1,5},{5,9},{9,13},{2,6},{6,10},{10,14},{3,7},{... | collective-permute-start | bytes 1474568 | tf_op jit(solution)/shard_map/ppermute | solution.py:226
  10.4 0.0 copy-done.3
  10.4 0.0 copy-done.4
  10.4 0.1 fusion.k_in
  10.6 0.0 copy-start
  10.6 8.8 %collective-permute-done.3.ahi_in = f32[10,32,384]{2,1,0:T(8,128)S(1)} collective-permute-done((f32[10,32,384]{2,1,0:T(8,128)S(1)}, f32[10,32,384]{2,1,0:T(8,128)S(1)}, u32[]{:S(2)}, u32[]{:S(2)}) %collective-permute-start.3) | collective-permute-done | bytes 491552 | tf_op jit(solution)/shard_map/ppermute | solution.py:227
  19.4 0.0 copy-start.5
  19.4 0.0 collective-permute-start.5
  19.4 1.4 %collective-permute-done.2.alo_in = f32[10,32,384]{2,1,0:T(8,128)S(1)} collective-permute-done((f32[10,32,384]{2,1,0:T(8,128)S(1)}, f32[10,32,384]{2,1,0:T(8,128)S(1)}, u32[]{:S(2)}, u32[]{:S(2)}) %collective-permute-start.2) | collective-permute-done | bytes 491552 | tf_op jit(solution)/shard_map/ppermute | solution.py:226
  20.8 0.0 copy-start.6
  20.8 0.0 collective-permute-start.4
  20.8 0.1 fusion.5
  20.9 0.0 copy-done
  20.9 0.0 copy-done.5
  20.9 1.3 %collective-permute-start.1 = (f32[4,64,384]{2,1,0:T(8,128)S(1)}, f32[4,64,384]{2,1,0:T(8,128)S(1)}, u32[]{:S(2)}, u32[]{:S(2)}) collective-permute-start(f32[4,64,384]{2,1,0:T(8,128)S(1)} %get-tuple-element.14), channel_id=1, source_target_pairs={{4,0},{8,4},{12,8},{5,1},{9,5},{13,9},{6,2},{10,6},{14,10},{7,3},{... | collective-permute-start | bytes 1179656 | tf_op jit(solution)/shard_map/ppermute | solution.py:230
  22.2 5.0 %collective-permute-start = (f32[4,64,384]{2,1,0:T(8,128)S(1)}, f32[4,64,384]{2,1,0:T(8,128)S(1)}, u32[]{:S(2)}, u32[]{:S(2)}) collective-permute-start(f32[4,64,384]{2,1,0:T(8,128)S(1)} %get-tuple-element.15), channel_id=1, source_target_pairs={{0,4},{4,8},{8,12},{1,5},{5,9},{9,13},{2,6},{6,10},{10,14},{3,7},{... | collective-permute-start | bytes 1179656 | tf_op jit(solution)/shard_map/ppermute | solution.py:229
  27.3 7.8 %collective-permute-done.1.khi_in = f32[4,64,384]{2,1,0:T(8,128)S(1)} collective-permute-done((f32[4,64,384]{2,1,0:T(8,128)S(1)}, f32[4,64,384]{2,1,0:T(8,128)S(1)}, u32[]{:S(2)}, u32[]{:S(2)}) %collective-permute-start.1) | collective-permute-done | bytes 393248 | tf_op jit(solution)/shard_map/ppermute | solution.py:230
  35.1 0.0 copy-start.9
  35.1 1.2 %collective-permute-done.klo_in = f32[4,64,384]{2,1,0:T(8,128)S(1)} collective-permute-done((f32[4,64,384]{2,1,0:T(8,128)S(1)}, f32[4,64,384]{2,1,0:T(8,128)S(1)}, u32[]{:S(2)}, u32[]{:S(2)}) %collective-permute-start) | collective-permute-done | bytes 393248 | tf_op jit(solution)/shard_map/ppermute | solution.py:229
  36.3 0.0 copy-start.10
  36.3 0.0 collective-permute-done.5.bhi_in
  36.3 0.0 copy-start.7
  36.3 0.0 collective-permute-done.4.blo_in
  36.3 0.0 copy-done.6
  36.3 0.0 copy-done.9
  36.3 0.7 %copy-done.10 = f32[4,64,384]{2,1,0:T(8,128)} copy-done((f32[4,64,384]{2,1,0:T(8,128)}, f32[4,64,384]{2,1,0:T(8,128)S(1)}, u32[]{:S(2)}) %copy-start.10) | copy-done | bytes 393240
  37.0 0.2 copy-done.7
  37.2 0.0 copy-start.8
  37.2 0.8 %copy-done.8 = f32[10,32,384]{2,1,0:T(8,128)} copy-done((f32[10,32,384]{2,1,0:T(8,128)}, f32[10,32,384]{2,1,0:T(8,128)S(1)}, u32[]{:S(2)}) %copy-start.8) | copy-done | bytes 491544
  38.0 14.7 %shard_map.68 = (f32[8,64,384]{2,1,0:T(8,128)}, f32[2,8,16,384]{3,2,1,0:T(8,128)}, f32[2,8,16,384]{3,2,1,0:T(8,128)}) custom-call(f32[8,64,384]{2,1,0:T(8,128)} %copy-done, f32[4,64,384]{2,1,0:T(8,128)} %copy-done.10, f32[4,64,384]{2,1,0:T(8,128)} %copy-done.9, f32[8,64,384]{2,1,0:T(8,128)} %p0_in.1, f32[8,64,384]{2,1,0:T(8,128)} %src_in.1, ...), custom_call_target="tpu_custom_call" | custom-call | flops 78643200 | bytes 7864320 | tf_op jit(solution)/shard_map/pallas_call | solution.py:197
  52.7 0.1 collective-permute-start.6
  52.8 1.9 %collective-permute-done.6 = f32[2,8,16,384]{3,2,1,0:T(8,128)S(1)} collective-permute-done((f32[2,8,16,384]{3,2,1,0:T(8,128)}, f32[2,8,16,384]{3,2,1,0:T(8,128)S(1)}, u32[]{:S(2)}, u32[]{:S(2)}) %collective-permute-start.6) | collective-permute-done | bytes 393248 | tf_op jit(solution)/shard_map/ppermute | solution.py:234
  54.7 1.0 %add.29 = f32[2,8,16,384]{3,2,1,0:T(8,128)S(1)} add(f32[2,8,16,384]{3,2,1,0:T(8,128)} %get-tuple-element.6, f32[2,8,16,384]{3,2,1,0:T(8,128)S(1)} %collective-permute-done.6) | non-fusion elementwise | flops 98304 | bytes 1179648 | tf_op jit(solution)/shard_map/add | solution.py:234
  55.8 1.7 %collective-permute-start.7 = (f32[8,16,384]{2,1,0:T(8,128)S(1)}, f32[8,16,384]{2,1,0:T(8,128)S(1)}, u32[]{:S(2)}, u32[]{:S(2)}) collective-permute-start(f32[8,16,384]{2,1,0:T(8,128)S(1)} %slice_bitcast_fusion), channel_id=1, source_target_pairs={{0,2},{1,3},{2,0},{3,1},{4,6},{5,7},{6,4},{7,5},{8,10},{9,11},{10,... | collective-permute-start | bytes 589832 | tf_op jit(solution)/shard_map/ppermute | solution.py:237
  57.5 5.3 %collective-permute-done.7 = f32[8,16,384]{2,1,0:T(8,128)S(1)} collective-permute-done((f32[8,16,384]{2,1,0:T(8,128)S(1)}, f32[8,16,384]{2,1,0:T(8,128)S(1)}, u32[]{:S(2)}, u32[]{:S(2)}) %collective-permute-start.7) | collective-permute-done | bytes 196640 | tf_op jit(solution)/shard_map/ppermute | solution.py:237
  62.8 0.7 %fusion.1 = f32[8,16,384]{2,1,0:T(8,128)} fusion(f32[8,16,384]{2,1,0:T(8,128)S(1)} %collective-permute-done.7, f32[2,8,16,384]{3,2,1,0:T(8,128)S(1)} %add.29), kind=kLoop, calls=%fused_computation.6 | loop fusion | flops 49152 | bytes 589824 | tf_op jit(solution)/shard_map/add | solution.py:237
  (8 shorter events, 0.2 us)
Async XLA Ops:
  0.6 1.3 %copy-start.2 = (f32[8,64,384]{2,1,0:T(8,128)S(1)}, f32[8,64,384]{2,1,0:T(8,128)}, u32[]{:S(2)}) copy-start(f32[8,64,384]{2,1,0:T(8,128)} %obs_in.1) | copy-start | bytes 2359300
  1.9 1.1 %copy-start.1 = (f32[8,64,384]{2,1,0:T(8,128)S(1)}, f32[8,64,384]{2,1,0:T(8,128)}, u32[]{:S(2)}) copy-start(f32[8,64,384]{2,1,0:T(8,128)} %p0_in.1) | copy-start | bytes 2359300
  3.2 16.1 %collective-permute-start.3 = (f32[10,32,384]{2,1,0:T(8,128)S(1)}, f32[10,32,384]{2,1,0:T(8,128)S(1)}, u32[]{:S(2)}, u32[]{:S(2)}) collective-permute-start(f32[10,32,384]{2,1,0:T(8,128)S(1)} %pad_maximum_fusion.1), channel_id=1, source_target_pairs={{4,0},{8,4},{12,8},{5,1},{9,5},{13,9},{6,2},{10,6},{14,10},{7,3},{... | collective-permute-start | bytes 1474568 | tf_op jit(solution)/shard_map/ppermute | solution.py:227
  4.6 5.8 %copy-start.3 = (f32[8,64,384]{2,1,0:T(8,128)S(1)}, f32[8,64,384]{2,1,0:T(8,128)}, u32[]{:S(2)}) copy-start(f32[8,64,384]{2,1,0:T(8,128)} %param.5) | copy-start | bytes 2359300
  4.6 5.8 %copy-start.4 = (f32[1,8,64,384]{3,2,1,0:T(8,128)S(1)}, f32[1,8,64,384]{3,2,1,0:T(8,128)}, u32[]{:S(2)}) copy-start(f32[1,8,64,384]{3,2,1,0:T(8,128)} %param.6) | copy-start | bytes 2359300
  4.7 16.2 %collective-permute-start.2 = (f32[10,32,384]{2,1,0:T(8,128)S(1)}, f32[10,32,384]{2,1,0:T(8,128)S(1)}, u32[]{:S(2)}, u32[]{:S(2)}) collective-permute-start(f32[10,32,384]{2,1,0:T(8,128)S(1)} %pad_maximum_fusion), channel_id=1, source_target_pairs={{0,4},{4,8},{8,12},{1,5},{5,9},{9,13},{2,6},{6,10},{10,14},{3,7},{... | collective-permute-start | bytes 1474568 | tf_op jit(solution)/shard_map/ppermute | solution.py:226
  10.6 10.3 %copy-start = (f32[8,64,384]{2,1,0:T(8,128)}, f32[8,64,384]{2,1,0:T(8,128)S(1)}, u32[]{:S(2)}) copy-start(f32[8,64,384]{2,1,0:T(8,128)S(1)} %fusion.k_in) | copy-start | bytes 2359300
  19.4 1.5 %copy-start.5 = (f32[10,32,384]{2,1,0:T(8,128)}, f32[10,32,384]{2,1,0:T(8,128)S(1)}, u32[]{:S(2)}) copy-start(f32[10,32,384]{2,1,0:T(8,128)S(1)} %collective-permute-done.3.ahi_in) | copy-start | bytes 1474564
  19.4 16.9 %collective-permute-start.5 = (f32[10,32,384]{2,1,0:T(8,128)S(1)}, f32[10,32,384]{2,1,0:T(8,128)S(1)}, u32[]{:S(2)}, u32[]{:S(2)}) collective-permute-start(f32[10,32,384]{2,1,0:T(8,128)S(1)} %collective-permute-done.3.ahi_in), channel_id=1, source_target_pairs={{0,1},{1,0},{2,3},{3,2},{4,5},{5,4},{6,7},{7,6},{8,9},{9,8},{10,11... | collective-permute-start | bytes 1474568 | tf_op jit(solution)/shard_map/ppermute | solution.py:232
  20.8 15.4 %copy-start.6 = (f32[10,32,384]{2,1,0:T(8,128)}, f32[10,32,384]{2,1,0:T(8,128)S(1)}, u32[]{:S(2)}) copy-start(f32[10,32,384]{2,1,0:T(8,128)S(1)} %collective-permute-done.2.alo_in) | copy-start | bytes 1474564
  20.8 15.4 %collective-permute-start.4 = (f32[10,32,384]{2,1,0:T(8,128)S(1)}, f32[10,32,384]{2,1,0:T(8,128)S(1)}, u32[]{:S(2)}, u32[]{:S(2)}) collective-permute-start(f32[10,32,384]{2,1,0:T(8,128)S(1)} %collective-permute-done.2.alo_in), channel_id=1, source_target_pairs={{0,1},{1,0},{2,3},{3,2},{4,5},{5,4},{6,7},{7,6},{8,9},{9,8},{10,11... | collective-permute-start | bytes 1474568 | tf_op jit(solution)/shard_map/ppermute | solution.py:231
  20.9 14.2 %collective-permute-start.1 = (f32[4,64,384]{2,1,0:T(8,128)S(1)}, f32[4,64,384]{2,1,0:T(8,128)S(1)}, u32[]{:S(2)}, u32[]{:S(2)}) collective-permute-start(f32[4,64,384]{2,1,0:T(8,128)S(1)} %get-tuple-element.14), channel_id=1, source_target_pairs={{4,0},{8,4},{12,8},{5,1},{9,5},{13,9},{6,2},{10,6},{14,10},{7,3},{... | collective-permute-start | bytes 1179656 | tf_op jit(solution)/shard_map/ppermute | solution.py:230
  22.2 14.0 %collective-permute-start = (f32[4,64,384]{2,1,0:T(8,128)S(1)}, f32[4,64,384]{2,1,0:T(8,128)S(1)}, u32[]{:S(2)}, u32[]{:S(2)}) collective-permute-start(f32[4,64,384]{2,1,0:T(8,128)S(1)} %get-tuple-element.15), channel_id=1, source_target_pairs={{0,4},{4,8},{8,12},{1,5},{5,9},{9,13},{2,6},{6,10},{10,14},{3,7},{... | collective-permute-start | bytes 1179656 | tf_op jit(solution)/shard_map/ppermute | solution.py:229
  35.1 1.2 %copy-start.9 = (f32[4,64,384]{2,1,0:T(8,128)}, f32[4,64,384]{2,1,0:T(8,128)S(1)}, u32[]{:S(2)}) copy-start(f32[4,64,384]{2,1,0:T(8,128)S(1)} %collective-permute-done.1.khi_in) | copy-start | bytes 1179652
  36.3 0.8 %copy-start.10 = (f32[4,64,384]{2,1,0:T(8,128)}, f32[4,64,384]{2,1,0:T(8,128)S(1)}, u32[]{:S(2)}) copy-start(f32[4,64,384]{2,1,0:T(8,128)S(1)} %collective-permute-done.klo_in) | copy-start | bytes 1179652
  36.3 0.9 %copy-start.7 = (f32[10,32,384]{2,1,0:T(8,128)}, f32[10,32,384]{2,1,0:T(8,128)S(1)}, u32[]{:S(2)}) copy-start(f32[10,32,384]{2,1,0:T(8,128)S(1)} %collective-permute-done.5.bhi_in) | copy-start | bytes 1474564
  37.2 0.8 %copy-start.8 = (f32[10,32,384]{2,1,0:T(8,128)}, f32[10,32,384]{2,1,0:T(8,128)S(1)}, u32[]{:S(2)}) copy-start(f32[10,32,384]{2,1,0:T(8,128)S(1)} %collective-permute-done.4.blo_in) | copy-start | bytes 1474564
  52.7 2.0 %collective-permute-start.6 = (f32[2,8,16,384]{3,2,1,0:T(8,128)}, f32[2,8,16,384]{3,2,1,0:T(8,128)S(1)}, u32[]{:S(2)}, u32[]{:S(2)}) collective-permute-start(f32[2,8,16,384]{3,2,1,0:T(8,128)} %get-tuple-element.7), channel_id=1, source_target_pairs={{0,1},{1,0},{2,3},{3,2},{4,5},{5,4},{6,7},{7,6},{8,9},{9,8},{10,11... | collective-permute-start | bytes 1179656 | tf_op jit(solution)/shard_map/ppermute | solution.py:234
  55.8 7.0 %collective-permute-start.7 = (f32[8,16,384]{2,1,0:T(8,128)S(1)}, f32[8,16,384]{2,1,0:T(8,128)S(1)}, u32[]{:S(2)}, u32[]{:S(2)}) collective-permute-start(f32[8,16,384]{2,1,0:T(8,128)S(1)} %slice_bitcast_fusion), channel_id=1, source_target_pairs={{0,2},{1,3},{2,0},{3,1},{4,6},{5,7},{6,4},{7,5},{8,10},{9,11},{10,... | collective-permute-start | bytes 589832 | tf_op jit(solution)/shard_map/ppermute | solution.py:237

commit v2 on v0

v2 whole, which is shorter than its diff:
```python
import jax
import jax.numpy as jnp
from jax import lax
from jax.experimental import pallas as pl
from jax.experimental.pallas import tpu as pltpu
from jax.sharding import PartitionSpec as P

SWEEPS = 3
HALO = SWEEPS + 1
EDGE = HALO + 2 * SWEEPS
LANES = 128
SUB = 8
ANYWHERE = pl.BlockSpec(memory_space=pl.ANY)
OFFCHIP = pl.BlockSpec(memory_space=pltpu.HBM)
ONCHIP = pl.BlockSpec(memory_space=pltpu.VMEM)


def around(ref, zz, r, rows):
    tiles = ref.shape[1]
    lane = lax.broadcasted_iota(jnp.int32, (SUB, LANES), 1)
    sub = lax.broadcasted_iota(jnp.int32, (SUB, LANES), 0)
    zero = jnp.zeros((SUB, LANES), jnp.float32)
    here = pl.ds(SUB * r, SUB)
    own = [ref[zz, c, here, :] for c in range(tiles)]
    fwd = [pltpu.roll(v, 1, 1) for v in own]
    bwd = [pltpu.roll(v, LANES - 1, 1) for v in own]
    out = []
    for c in range(tiles):
        left = jnp.where(lane == 0, fwd[c - 1] if c > 0 else zero, fwd[c])
        right = jnp.where(lane == LANES - 1, bwd[c + 1] if c + 1 < tiles else zero, bwd[c])
        out.append((left, right) + cross(ref, zz, c, r, rows, own[c], sub, zero))
    return own, out


def cross(ref, zz, c, r, rows, own, sub, zero):
    if r > 0:
        north = ref[zz, c, pl.ds(SUB * r - 1, SUB), :]
    else:
        north = jnp.where(sub == 0, zero, pltpu.roll(own, 1, 0))
    if r + 1 < rows:
        south = ref[zz, c, pl.ds(SUB * r + 1, SUB), :]
    else:
        south = jnp.where(sub == SUB - 1, zero, pltpu.roll(own, SUB - 1, 0))
    here = pl.ds(SUB * r, SUB)
    return north, south, ref[zz - 1, c, here, :], ref[zz + 1, c, here, :]


def faces(K, WL, WR, zz, c, r, rows):
    sub = lax.broadcasted_iota(jnp.int32, (SUB, LANES), 0)
    zero = jnp.zeros((SUB, LANES), jnp.float32)
    here = pl.ds(SUB * r, SUB)
    k = K[zz, c, here, :]
    rest = [k + v for v in cross(K, zz, c, r, rows, k, sub, zero)]
    return (WL[zz, c, here, :], WR[zz, c, here, :], *rest)


def six(parts):
    a, b, c, d, e, f = parts
    return ((a + b) + (c + d)) + (e + f)


def weighted(weights, parts):
    return six([w * v for w, v in zip(weights, parts)])


def sweeps(refs, ranges, inside, press):
    K, P0, SRC, OBS, P1, P2, U1, U2, U3, HR, SR, NP0, WL, WR, G, E = refs
    tiles, rows = K.shape[1], K.shape[2] // SUB

    def at(r):
        return pl.ds(SUB * r, SUB)

    def first(zz):
        valid = inside(zz)
        for r in range(rows):
            k, kn = around(K, zz, r, rows)
            _, pn = around(P0, zz, r, rows)
            for c in range(tiles):
                w = [k[c] + v for v in kn[c]]
                rinv = valid / (0.5 + 0.5 * six(w))
                hr = 0.5 * rinv
                sr = SRC[zz, c, at(r), :] * rinv
                HR[zz, c, at(r), :] = hr
                SR[zz, c, at(r), :] = sr
                WL[zz, c, at(r), :] = w[0]
                WR[zz, c, at(r), :] = w[1]
                NP0[zz, c, at(r), :] = six(pn[c])
                P1[zz, c, at(r), :] = sr + weighted(w, pn[c]) * hr
                U3[zz, c, at(r), :] = OBS[zz, c, at(r), :] * rinv

    def second(zz):
        for r in range(rows):
            _, a = around(P1, zz, r, rows)
            _, v = around(U3, zz, r, rows)
            for c in range(tiles):
                w = faces(K, WL, WR, zz, c, r, rows)
                hr = HR[zz, c, at(r), :]
                p2 = SR[zz, c, at(r), :] + weighted(w, a[c]) * hr
                u2 = weighted(w, v[c]) * hr
                P2[zz, c, at(r), :] = p2
                U2[zz, c, at(r), :] = u2
                G[zz, c, at(r), :] = u2 * six(a[c]) + p2 * six(v[c])

    def third(zz, own):
        for r in range(rows):
            p2, a = around(P2, zz, r, rows)
            u2, v = around(U2, zz, r, rows)
            for c in range(tiles):
                w = faces(K, WL, WR, zz, c, r, rows)
                hr = HR[zz, c, at(r), :]
                p1, u3 = P1[zz, c, at(r), :], U3[zz, c, at(r), :]
                p3 = SR[zz, c, at(r), :] + weighted(w, a[c]) * hr
                u1 = weighted(w, v[c]) * hr
                e = -(u1 * p1 + u2[c] * p2[c] + u3 * p3)
                U1[zz, c, at(r), :] = u1
                E[zz, c, at(r), :] = e
                if own:
                    g = u3 * six(a[c]) + p1 * six(v[c]) + u1 * NP0[zz, c, at(r), :]
                    press(zz)[at(r), pl.ds(c * LANES, LANES)] = p3
                    G[zz, c, at(r), :] = (G[zz, c, at(r), :] + 6.0 * e) + g

    for body, spans in zip((first, second, third), ranges):
        for span in spans:
            lo, hi, *own = span
            lax.fori_loop(lo, hi, lambda zz, _, body=body, own=own: body(zz, *own) or 0, 0)


def edges_kernel(p0, src, obs, up, down, sems):
    nx, ny = p0.shape[1:]
    slab, half = p0.shape[0], nx // 2
    rows = pl.ds(pl.multiple_of(half * (lax.axis_index("draw") % 2), half), half)
    copies = []
    for c in range(ny // LANES):
        cols = pl.ds(c * LANES, LANES)
        at = 0
        for ref, width in ((p0, HALO), (src, SWEEPS), (obs, SWEEPS)):
            for start, out in ((slab - width, up), (0, down)):
                copies.append(
                    pltpu.make_async_copy(
                        ref.at[pl.ds(start, width), rows, cols], out.at[pl.ds(at, width), c], sems.at[len(copies)]
                    )
                )
            at += width
    for cp in copies:
        cp.start()
    for cp in copies:
        cp.wait()


def conduct_kernel(log_perm, noise, K, top, bottom):
    slab, nx, ny = log_perm.shape

    def plane(z, _):
        for r in range(nx // SUB):
            for c in range(ny // LANES):
                here, cols = pl.ds(SUB * r, SUB), pl.ds(c * LANES, LANES)
                K[z + HALO, c, here, :] = jnp.exp(log_perm[z, here, cols] + noise[z, here, cols])
        return 0

    lax.fori_loop(0, slab, plane, 0)

    def edge(z, _):
        top[z] = K[slab + z]
        bottom[z] = K[HALO + z]
        return 0

    lax.fori_loop(0, HALO, edge, 0)


def inner_kernel(K, p0, src, obs, P0, SRC, OBS, P1, P2, U1, U2, U3, HR, SR, NP0, WL, WR, G, E, mid, sems):
    slab = p0.shape[0]
    top = HALO + slab
    copies = []
    for c in range(K.shape[1]):
        for ref, out in ((p0, P0), (src, SRC), (obs, OBS)):
            copies.append(
                pltpu.make_async_copy(
                    ref.at[:, :, pl.ds(c * LANES, LANES)], out.at[pl.ds(HALO, slab), c], sems.at[len(copies)]
                )
            )
    for cp in copies:
        cp.start()
    for cp in copies:
        cp.wait()
    refs = (K, P0, SRC, OBS, P1, P2, U1, U2, U3, HR, SR, NP0, WL, WR, G, E)
    ranges = [[(HALO + n, top - n)] for n in (1, 2)] + [[(HALO + 3, top - 3, True)]]
    sweeps(refs, ranges, lambda zz: jnp.float32(1.0), lambda zz: mid.at[zz - HALO - SWEEPS])


def outer_kernel(*args):
    klo, khi, alo, ahi, blo, bhi, mid = args[:7]
    refs, (press_out, keep_out, send_out, press, sems) = args[-21:-5], args[-5:]
    K, P0, SRC, OBS, P1, P2, U1, U2, U3, HR, SR, NP0, WL, WR, G, E = refs
    slab, nx = press.shape[:2]
    half, top, depth = nx // 2, HALO + slab, slab + 2 * HALO
    tiles, rows = K.shape[1], nx // SUB
    draw, draws = lax.axis_index("draw"), lax.axis_size("draw")
    space, spaces = lax.axis_index("space"), lax.axis_size("space")
    par, group, groups = draw % 2, draw // 2, draws // 2
    block = nx // draws

    pairs = [(klo, K.at[pl.ds(0, HALO)]), (khi, K.at[pl.ds(top, HALO)])]
    mine = pl.ds(pl.multiple_of(half * par, half), half)
    other = pl.ds(pl.multiple_of(half * (1 - par), half), half)
    for lo, hi, at in ((alo, ahi, mine), (blo, bhi, other)):
        first = 0
        for field, width in ((P0, HALO), (SRC, SWEEPS), (OBS, SWEEPS)):
            span = pl.ds(first, width)
            pairs.append((lo.at[span], field.at[pl.ds(HALO - width, width), :, at]))
            pairs.append((hi.at[span], field.at[pl.ds(top, width), :, at]))
            first += width
    copies = [pltpu.make_async_copy(a, b, sems.at[i]) for i, (a, b) in enumerate(pairs)]
    for cp in copies:
        cp.start()
    for cp in copies:
        cp.wait()

    low = jnp.where(space > 0, 1.0, 0.0).astype(jnp.float32)
    high = jnp.where(space + 1 < spaces, 1.0, 0.0).astype(jnp.float32)

    def inside(zz):
        return jnp.where(zz < HALO, low, jnp.where(zz >= top, high, jnp.float32(1.0)))

    ranges = [
        [(1, HALO + 1), (top - 1, depth - 1)],
        [(2, HALO + 2), (top - 2, depth - 2)],
        [(3, HALO, False), (HALO, HALO + 3, True), (top - 3, top, True), (top, depth - 3, False)],
    ]
    sweeps(refs, ranges, inside, lambda zz: press.at[zz - HALO])
    done = [
        pltpu.make_async_copy(press.at[span], press_out.at[span], sems.at[i])
        for i, span in enumerate((pl.ds(0, SWEEPS), pl.ds(slab - SWEEPS, SWEEPS)))
    ]
    middle = pl.ds(SWEEPS, slab - 2 * SWEEPS)
    done.append(pltpu.make_async_copy(mid, press_out.at[middle], sems.at[len(done)]))
    for cp in done:
        cp.start()

    def at(r):
        return pl.ds(SUB * r, SUB)

    def gradient(zz, r):
        _, v = around(U1, zz, r, rows)
        _, w = around(E, zz, r, rows)
        return [
            0.5 * K[zz, c, at(r), :] * (G[zz, c, at(r), :] + P0[zz, c, at(r), :] * six(v[c]) + six(w[c]))
            for c in range(tiles)
        ]

    def last(z, _):
        zz = z + HALO
        for h in range(groups):
            slot = (h - group + groups) % groups
            for q in range(block // SUB):
                even = gradient(zz, (2 * h * block) // SUB + q)
                odd = gradient(zz, ((2 * h + 1) * block) // SUB + q)
                for c in range(tiles):
                    cols = pl.ds(c * LANES, LANES)
                    keep_out[slot, z, pl.ds(SUB * q, SUB), cols] = jnp.where(par == 0, even[c], odd[c])
                    send_out[slot, z, pl.ds(SUB * q, SUB), cols] = jnp.where(par == 0, odd[c], even[c])
        return 0

    lax.fori_loop(0, slab, last, 0)
    for cp in done:
        cp.wait()


def local(log_perm, noise, source, start_pressure, observe):
    draws, spaces = lax.axis_size("draw"), lax.axis_size("space")
    slab, nx, ny = log_perm.shape
    tiles, depth, half = ny // LANES, slab + 2 * HALO, nx // 2
    up = [(i, i + 1) for i in range(spaces - 1)]
    down = [(j, i) for i, j in up]
    pair = [(i, i ^ 1) for i in range(draws)]
    f32 = jnp.float32
    field = pltpu.VMEM((depth, tiles, nx, LANES), f32)
    edge = jax.ShapeDtypeStruct((EDGE, tiles, half, LANES), f32)
    rim = jax.ShapeDtypeStruct((HALO, tiles, nx, LANES), f32)
    whole = jax.ShapeDtypeStruct((slab, nx, ny), f32)
    mid = jax.ShapeDtypeStruct((slab - 2 * SWEEPS, nx, ny), f32)
    part = jax.ShapeDtypeStruct((draws // 2, slab, nx // draws, ny), f32)
    params = pltpu.CompilerParams(vmem_limit_bytes=8 * 2**20)
    cells = slab * nx * ny

    aup, adown = pl.pallas_call(
        edges_kernel,
        out_shape=(edge, edge),
        in_specs=[OFFCHIP] * 3,
        out_specs=(ONCHIP, ONCHIP),
        scratch_shapes=[pltpu.SemaphoreType.DMA((6 * tiles,))],
        compiler_params=params,
        cost_estimate=pl.CostEstimate(flops=cells, bytes_accessed=20 * cells, transcendentals=0),
    )(start_pressure, source, observe)
    alo = lax.ppermute(aup, "space", up)
    ahi = lax.ppermute(adown, "space", down)
    K, top, bottom = pl.pallas_call(
        conduct_kernel,
        out_shape=(field, rim, rim),
        in_specs=[ONCHIP] * 2,
        out_specs=(ONCHIP,) * 3,
        compiler_params=params,
        cost_estimate=pl.CostEstimate(flops=cells, bytes_accessed=12 * cells, transcendentals=cells),
    )(log_perm, noise[0])
    klo = lax.ppermute(top, "space", up)
    khi = lax.ppermute(bottom, "space", down)
    state = pl.pallas_call(
        inner_kernel,
        out_shape=(field,) * 15 + (mid,),
        in_specs=[ONCHIP] + [ANYWHERE] * 3,
        out_specs=(ONCHIP,) * 16,
        scratch_shapes=[pltpu.SemaphoreType.DMA((3 * tiles,))],
        compiler_params=params,
        cost_estimate=pl.CostEstimate(flops=200 * cells, bytes_accessed=60 * cells, transcendentals=0),
    )(K, start_pressure, source, observe)
    alo, ahi, klo, khi, last = lax.optimization_barrier((alo, ahi, klo, khi, state[-2]))
    state = (*state[:-2], last, state[-1])
    blo = lax.ppermute(alo, "draw", pair)
    bhi = lax.ppermute(ahi, "draw", pair)
    fields = (K, *state[:-1])
    n = len(fields)
    *_, press, keep, send = pl.pallas_call(
        outer_kernel,
        out_shape=(field,) * n + (whole, part, part),
        in_specs=[ONCHIP] * (7 + n),
        out_specs=(ONCHIP,) * n + (OFFCHIP, ONCHIP, ONCHIP),
        scratch_shapes=[pltpu.VMEM((slab, nx, ny), f32), pltpu.SemaphoreType.DMA((14,))],
        input_output_aliases={7 + i: i for i in range(n)},
        compiler_params=params,
        cost_estimate=pl.CostEstimate(flops=200 * cells, bytes_accessed=60 * cells, transcendentals=0),
    )(klo, khi, alo, ahi, blo, bhi, state[-1], *fields)
    got = lax.ppermute(send, "draw", pair)
    moved = [
        lax.ppermute(keep[s] + got[s], "draw", [(j, (j + 2 * s) % draws) for j in range(draws)])
        for s in range(1, draws // 2)
    ]
    total = keep[0] + got[0]
    for part_sum in moved:
        total = total + part_sum
    return press[None], total


def solution(mesh):
    return jax.shard_map(
        local,
        mesh=mesh,
        in_specs=(
            P(("epi", "space"), None, None),
            P("draw", ("epi", "space"), None, None),
            P(("epi", "space"), None, None),
            P(("epi", "space"), None, None),
            P(("epi", "space"), None, None),
        ),
        out_specs=(P("draw", ("epi", "space"), None, None), P(("epi", "space"), "draw", None)),
        check_vma=False,
    )
```

time: 133 us -> 52.3 us (0.39)
  other arithmetic: 36.5 us -> 0.73 us
  waiting for transfers between devices: 53.9 us -> 20.7 us
  between operations: 14.4 us -> 0.75 us
  starting transfers between devices: 26 us -> 14.5 us
  Pallas kernels: 0 us -> 10.7 us
  local copies, waits for them, and re-layouts: 1.43 us -> 4.53 us
    reduce_scatter x1 -> x0, waiting for transfers between devices: 21.6 us -> none  [local(): lax.psum_scatter(local_grad, 'draw', scatter_dimension=1, tiled=True)]
    ppermute x12 -> x8, waiting for transfers between devices: 32.2 us -> 20.7 us  [the longest x1 7.44 us: local(): klo = lax.ppermute(top, 'space', up)]
    ppermute x12 -> x8, starting transfers between devices: 26 us -> 14.5 us  [the longest x1 5.09 us: local(): alo = lax.ppermute(aup, 'space', up)]
    add x6 -> x2, other arithmetic: 11.9 us -> 0.73 us  [the longest x1 0.71 us: local(): total = total + part_sum]
    pallas_call x0 -> x4, Pallas kernels: none -> 10.7 us  [the longest x1 7.37 us: local(): pl.pallas_call(outer_kernel, out_shape=(field,) * n + (whole, part, part)...]
    concatenate x6 -> x0, other arithmetic: 10.5 us -> none  [extended(): shard = jnp.concatenate([before, shard, after], axis=dim)]
    another operation x4 -> x0, other arithmetic: 6.84 us -> none  [the longest x3 5.29 us: adjoint_pass(): both = pad_plane(extended(jnp.stack([mult, term]), (('space', 2),), 1))]
    unnamed x10 -> x14, local copies, waits for them, and re-layouts: 0.22 us -> 4.53 us
  transfers between devices with their start and end apart: 13 -> 8, of which waited for: 12 -> 6; matrix products, arithmetic and copies ran while one was open for 3% -> 0% of each run, Pallas kernels for 0% -> 6%
where the time goes in v2:
time: 52.3 us; the launch traced here: 51.9 us
  waiting for transfers between devices  20.7 us (40%)
  starting transfers between devices  14.5 us (28%)
  Pallas kernels  10.7 us (20%)
  local copies, waits for them, and re-layouts  4.53 us (9%)
  between operations  0.75 us (1%)
  other arithmetic  0.73 us (1%)
    ppermute x1, waiting for transfers between devices, local(): klo = lax.ppermute(top, 'space', up)  7.44 us
    pallas_call x1, Pallas kernels, local(): pl.pallas_call(outer_kernel, out_shape=(field,) * n + (whole, part, part)...  7.37 us
    ppermute x1, waiting for transfers between devices, local(): lax.ppermute(keep[s] + got[s], 'draw', [(j, (j + 2 * s) % draws) for j in...  5.45 us
    ppermute x1, starting transfers between devices, local(): alo = lax.ppermute(aup, 'space', up)  5.09 us
    ppermute x1, starting transfers between devices, local(): klo = lax.ppermute(top, 'space', up)  4.57 us
    unnamed x14, local copies, waits for them, and re-layouts  4.53 us
    ppermute x1, waiting for transfers between devices, local(): khi = lax.ppermute(bottom, 'space', down)  4.14 us
    pallas_call x1, Pallas kernels, local(): pl.pallas_call(inner_kernel, out_shape=(field,) * 15 + (mid,), in_specs=[...  2.82 us
  transfers between devices with their start and end apart: 8, of which 6 were waited for; matrix products, arithmetic and copies ran while one was open for 0% of the time, Pallas kernels for 6%

profile of v2, /device:TPU:0, one launch (start us, length us, event | category | flops | bytes accessed | tf_op | source)
XLA Modules:
  0.0 51.9 jit_solution(8562682289066124696)
XLA Ops:
  0.6 0.0 copy-start
  0.6 1.1 %copy-done = f32[8,64,384]{2,1,0:T(8,128)S(1)} copy-done((f32[8,64,384]{2,1,0:T(8,128)S(1)}, f32[8,64,384]{2,1,0:T(8,128)}, u32[]{:S(2)}) %copy-start) | copy-done | bytes 786456
  1.8 0.0 copy-start.2
  1.8 1.1 %copy-done.2 = f32[8,64,384]{2,1,0:T(8,128)S(1)} copy-done((f32[8,64,384]{2,1,0:T(8,128)S(1)}, f32[8,64,384]{2,1,0:T(8,128)}, u32[]{:S(2)}) %copy-start.2) | copy-done | bytes 786456
  2.9 0.0 copy-start.4
  2.9 1.1 %copy-done.4 = f32[8,64,384]{2,1,0:T(8,128)S(1)} copy-done((f32[8,64,384]{2,1,0:T(8,128)S(1)}, f32[8,64,384]{2,1,0:T(8,128)}, u32[]{:S(2)}) %copy-start.4) | copy-done | bytes 786456
  4.0 0.0 copy-start.5
  4.0 0.0 copy-start.1
  4.0 0.0 copy-start.3
  4.0 0.3 shard_map.68
  4.3 5.1 %collective-permute-start = (f32[10,3,32,128]{3,2,1,0:T(8,128)S(1)}, f32[10,3,32,128]{3,2,1,0:T(8,128)S(1)}, u32[]{:S(2)}, u32[]{:S(2)}) collective-permute-start(f32[10,3,32,128]{3,2,1,0:T(8,128)S(1)} %get-tuple-element.31), channel_id=1, source_target_pairs={{0,4},{4,8},{8,12},{1,5},{5,9},{9,13},{2,6},{6,10},{10,14},{3,7},{... | collective-permute-start | bytes 1474568 | tf_op jit(solution)/shard_map/ppermute | solution.py:294
  9.4 1.3 %collective-permute-start.1 = (f32[10,3,32,128]{3,2,1,0:T(8,128)S(1)}, f32[10,3,32,128]{3,2,1,0:T(8,128)S(1)}, u32[]{:S(2)}, u32[]{:S(2)}) collective-permute-start(f32[10,3,32,128]{3,2,1,0:T(8,128)S(1)} %get-tuple-element.32), channel_id=1, source_target_pairs={{4,0},{8,4},{12,8},{5,1},{9,5},{13,9},{6,2},{10,6},{14,10},{7,3},{... | collective-permute-start | bytes 1474568 | tf_op jit(solution)/shard_map/ppermute | solution.py:295
  10.7 0.0 copy-done.5
  10.7 0.0 copy-start.6
  10.8 1.1 %copy-done.6 = f32[1,8,64,384]{3,2,1,0:T(8,128)S(1)} copy-done((f32[1,8,64,384]{3,2,1,0:T(8,128)S(1)}, f32[1,8,64,384]{3,2,1,0:T(8,128)}, u32[]{:S(2)}) %copy-start.6) | copy-done | bytes 786456
  11.9 0.2 shard_map.69
  12.1 4.6 %collective-permute-start.2 = (f32[4,3,64,128]{3,2,1,0:T(8,128)S(1)}, f32[4,3,64,128]{3,2,1,0:T(8,128)S(1)}, u32[]{:S(2)}, u32[]{:S(2)}) collective-permute-start(f32[4,3,64,128]{3,2,1,0:T(8,128)S(1)} %get-tuple-element.33), channel_id=1, source_target_pairs={{0,4},{4,8},{8,12},{1,5},{5,9},{9,13},{2,6},{6,10},{10,14},{3,7},{... | collective-permute-start | bytes 1179656 | tf_op jit(solution)/shard_map/ppermute | solution.py:304
  16.7 1.3 %collective-permute-start.3 = (f32[4,3,64,128]{3,2,1,0:T(8,128)S(1)}, f32[4,3,64,128]{3,2,1,0:T(8,128)S(1)}, u32[]{:S(2)}, u32[]{:S(2)}) collective-permute-start(f32[4,3,64,128]{3,2,1,0:T(8,128)S(1)} %get-tuple-element.34), channel_id=1, source_target_pairs={{4,0},{8,4},{12,8},{5,1},{9,5},{13,9},{6,2},{10,6},{14,10},{7,3},{... | collective-permute-start | bytes 1179656 | tf_op jit(solution)/shard_map/ppermute | solution.py:305
  18.0 0.0 copy-done.1
  18.0 0.0 copy-done.3
  18.0 2.8 %shard_map.70 = (f32[16,3,64,128]{3,2,1,0:T(8,128)S(1)}, f32[16,3,64,128]{3,2,1,0:T(8,128)S(1)}, f32[16,3,64,128]{3,2,1,0:T(8,128)S(1)}, f32[16,3,64,128]{3,2,1,...) custom-call(f32[16,3,64,128]{3,2,1,0:T(8,128)S(1)} %get-tuple-elemen, ...), custom_call_target="tpu_custom_call" | custom-call | flops 39321600 | bytes 11796480 | tf_op jit(solution)/shard_map/pallas_call | solution.py:306
  20.8 7.4 %collective-permute-done.2.args_0_ = f32[4,3,64,128]{3,2,1,0:T(8,128)S(1)} collective-permute-done((f32[4,3,64,128]{3,2,1,0:T(8,128)S(1)}, f32[4,3,64,128]{3,2,1,0:T(8,128)S(1)}, u32[]{:S(2)}, u32[]{:S(2)}) %collective-permute-start.2) | collective-permute-done | bytes 393248 | tf_op jit(solution)/shard_map/ppermute | solution.py:304
  28.3 4.1 %collective-permute-done.3.args_1_ = f32[4,3,64,128]{3,2,1,0:T(8,128)S(1)} collective-permute-done((f32[4,3,64,128]{3,2,1,0:T(8,128)S(1)}, f32[4,3,64,128]{3,2,1,0:T(8,128)S(1)}, u32[]{:S(2)}, u32[]{:S(2)}) %collective-permute-start.3) | collective-permute-done | bytes 393248 | tf_op jit(solution)/shard_map/ppermute | solution.py:305
  32.4 0.0 collective-permute-done.args_2_
  32.4 0.0 collective-permute-done.1.args_3_
  32.4 0.0 collective-permute-start.4
  32.4 0.5 collective-permute-start.5
  33.0 1.4 %collective-permute-done.4.args_4_ = f32[10,3,32,128]{3,2,1,0:T(8,128)S(1)} collective-permute-done((f32[10,3,32,128]{3,2,1,0:T(8,128)S(1)}, f32[10,3,32,128]{3,2,1,0:T(8,128)S(1)}, u32[]{:S(2)}, u32[]{:S(2)}) %collective-permute-start.4) | collective-permute-done | bytes 491552 | tf_op jit(solution)/shard_map/ppermute | solution.py:317
  34.3 0.7 %collective-permute-done.5.args_5_ = f32[10,3,32,128]{3,2,1,0:T(8,128)S(1)} collective-permute-done((f32[10,3,32,128]{3,2,1,0:T(8,128)S(1)}, f32[10,3,32,128]{3,2,1,0:T(8,128)S(1)}, u32[]{:S(2)}, u32[]{:S(2)}) %collective-permute-start.5) | collective-permute-done | bytes 491552 | tf_op jit(solution)/shard_map/ppermute | solution.py:318
  35.0 7.4 %shard_map.71 = (f32[16,3,64,128]{3,2,1,0:T(8,128)S(1)}, f32[16,3,64,128]{3,2,1,0:T(8,128)S(1)}, f32[16,3,64,128]{3,2,1,0:T(8,128)S(1)}, f32[16,3,64,128]{3,2,1,...) custom-call(f32[4,3,64,128]{3,2,1,0:T(8,128)S(1)} %collective-permut, ...), custom_call_target="tpu_custom_call", output_to_operand_aliasing={{0}: (7, {}), {1}: (8, {}), {2}: (9, {}), {3}: (10, {}), {4... | custom-call | flops 39321600 | bytes 11796480 | tf_op jit(solution)/shard_map/pallas_call | solution.py:321
  42.4 0.2 collective-permute-start.6
  42.6 1.6 %collective-permute-done.6 = f32[2,8,16,384]{3,2,1,0:T(8,128)S(1)} collective-permute-done((f32[2,8,16,384]{3,2,1,0:T(8,128)S(1)}, f32[2,8,16,384]{3,2,1,0:T(8,128)S(1)}, u32[]{:S(2)}, u32[]{:S(2)}) %collective-permute-start.6) | collective-permute-done | bytes 393248 | tf_op jit(solution)/shard_map/ppermute | solution.py:331
  44.2 1.6 %collective-permute-start.7 = (f32[8,16,384]{2,1,0:T(8,128)S(1)}, f32[8,16,384]{2,1,0:T(8,128)S(1)}, u32[]{:S(2)}, u32[]{:S(2)}) collective-permute-start(f32[8,16,384]{2,1,0:T(8,128)S(1)} %fusion), channel_id=1, source_target_pairs={{0,2},{1,3},{2,0},{3,1},{4,6},{5,7},{6,4},{7,5},{8,10},{9,11},{10,... | collective-permute-start | bytes 589832 | tf_op jit(solution)/shard_map/ppermute | solution.py:333
  45.8 5.5 %collective-permute-done.7 = f32[8,16,384]{2,1,0:T(8,128)S(1)} collective-permute-done((f32[8,16,384]{2,1,0:T(8,128)S(1)}, f32[8,16,384]{2,1,0:T(8,128)S(1)}, u32[]{:S(2)}, u32[]{:S(2)}) %collective-permute-start.7) | collective-permute-done | bytes 196640 | tf_op jit(solution)/shard_map/ppermute | solution.py:333
  51.2 0.7 %fusion.2 = f32[8,16,384]{2,1,0:T(8,128)} fusion(f32[8,16,384]{2,1,0:T(8,128)S(1)} %collective-permute-done.7, f32[2,8,16,384]{3,2,1,0:T(8,128)S(1)} %collective-permute-done.6, f32[2,8,16,384]{3,2,1,0:T(8,128)S(1)} %get-tuple-element.58), kind=kLoop, calls=%fused_computation.4 | loop fusion | flops 98304 | bytes 786432 | tf_op jit(solution)/shard_map/add | solution.py:338
  (1 shorter events, 0.0 us)
Async XLA Ops:
  0.6 1.1 %copy-start = (f32[8,64,384]{2,1,0:T(8,128)S(1)}, f32[8,64,384]{2,1,0:T(8,128)}, u32[]{:S(2)}) copy-start(f32[8,64,384]{2,1,0:T(8,128)} %p0.3) | copy-start | bytes 2359300
  1.8 1.1 %copy-start.2 = (f32[8,64,384]{2,1,0:T(8,128)S(1)}, f32[8,64,384]{2,1,0:T(8,128)}, u32[]{:S(2)}) copy-start(f32[8,64,384]{2,1,0:T(8,128)} %src.3) | copy-start | bytes 2359300
  2.9 1.1 %copy-start.4 = (f32[8,64,384]{2,1,0:T(8,128)S(1)}, f32[8,64,384]{2,1,0:T(8,128)}, u32[]{:S(2)}) copy-start(f32[8,64,384]{2,1,0:T(8,128)} %obs.3) | copy-start | bytes 2359300
  4.0 6.7 %copy-start.5 = (f32[8,64,384]{2,1,0:T(8,128)S(1)}, f32[8,64,384]{2,1,0:T(8,128)}, u32[]{:S(2)}) copy-start(f32[8,64,384]{2,1,0:T(8,128)} %log_perm.1) | copy-start | bytes 2359300
  4.0 14.0 %copy-start.1 = (f32[8,64,384]{2,1,0:T(8,128)S(1)}, f32[8,64,384]{2,1,0:T(8,128)}, u32[]{:S(2)}) copy-start(f32[8,64,384]{2,1,0:T(8,128)} %p0.3) | copy-start | bytes 2359300
  4.0 14.0 %copy-start.3 = (f32[8,64,384]{2,1,0:T(8,128)S(1)}, f32[8,64,384]{2,1,0:T(8,128)}, u32[]{:S(2)}) copy-start(f32[8,64,384]{2,1,0:T(8,128)} %src.3) | copy-start | bytes 2359300
  4.3 28.1 %collective-permute-start = (f32[10,3,32,128]{3,2,1,0:T(8,128)S(1)}, f32[10,3,32,128]{3,2,1,0:T(8,128)S(1)}, u32[]{:S(2)}, u32[]{:S(2)}) collective-permute-start(f32[10,3,32,128]{3,2,1,0:T(8,128)S(1)} %get-tuple-element.31), channel_id=1, source_target_pairs={{0,4},{4,8},{8,12},{1,5},{5,9},{9,13},{2,6},{6,10},{10,14},{3,7},{... | collective-permute-start | bytes 1474568 | tf_op jit(solution)/shard_map/ppermute | solution.py:294
  9.4 23.0 %collective-permute-start.1 = (f32[10,3,32,128]{3,2,1,0:T(8,128)S(1)}, f32[10,3,32,128]{3,2,1,0:T(8,128)S(1)}, u32[]{:S(2)}, u32[]{:S(2)}) collective-permute-start(f32[10,3,32,128]{3,2,1,0:T(8,128)S(1)} %get-tuple-element.32), channel_id=1, source_target_pairs={{4,0},{8,4},{12,8},{5,1},{9,5},{13,9},{6,2},{10,6},{14,10},{7,3},{... | collective-permute-start | bytes 1474568 | tf_op jit(solution)/shard_map/ppermute | solution.py:295
  10.7 1.1 %copy-start.6 = (f32[1,8,64,384]{3,2,1,0:T(8,128)S(1)}, f32[1,8,64,384]{3,2,1,0:T(8,128)}, u32[]{:S(2)}) copy-start(f32[1,8,64,384]{3,2,1,0:T(8,128)} %param.6) | copy-start | bytes 2359300
  12.1 16.2 %collective-permute-start.2 = (f32[4,3,64,128]{3,2,1,0:T(8,128)S(1)}, f32[4,3,64,128]{3,2,1,0:T(8,128)S(1)}, u32[]{:S(2)}, u32[]{:S(2)}) collective-permute-start(f32[4,3,64,128]{3,2,1,0:T(8,128)S(1)} %get-tuple-element.33), channel_id=1, source_target_pairs={{0,4},{4,8},{8,12},{1,5},{5,9},{9,13},{2,6},{6,10},{10,14},{3,7},{... | collective-permute-start | bytes 1179656 | tf_op jit(solution)/shard_map/ppermute | solution.py:304
  16.7 15.7 %collective-permute-start.3 = (f32[4,3,64,128]{3,2,1,0:T(8,128)S(1)}, f32[4,3,64,128]{3,2,1,0:T(8,128)S(1)}, u32[]{:S(2)}, u32[]{:S(2)}) collective-permute-start(f32[4,3,64,128]{3,2,1,0:T(8,128)S(1)} %get-tuple-element.34), channel_id=1, source_target_pairs={{4,0},{8,4},{12,8},{5,1},{9,5},{13,9},{6,2},{10,6},{14,10},{7,3},{... | collective-permute-start | bytes 1179656 | tf_op jit(solution)/shard_map/ppermute | solution.py:305
  32.4 1.9 %collective-permute-start.4 = (f32[10,3,32,128]{3,2,1,0:T(8,128)S(1)}, f32[10,3,32,128]{3,2,1,0:T(8,128)S(1)}, u32[]{:S(2)}, u32[]{:S(2)}) collective-permute-start(f32[10,3,32,128]{3,2,1,0:T(8,128)S(1)} %collective-permute-done.args_2_), channel_id=1, source_target_pairs={{0,1},{1,0},{2,3},{3,2},{4,5},{5,4},{6,7},{7,6},{8,9},{9,8},{10,11... | collective-permute-start | bytes 1474568 | tf_op jit(solution)/shard_map/ppermute | solution.py:317
  32.4 2.6 %collective-permute-start.5 = (f32[10,3,32,128]{3,2,1,0:T(8,128)S(1)}, f32[10,3,32,128]{3,2,1,0:T(8,128)S(1)}, u32[]{:S(2)}, u32[]{:S(2)}) collective-permute-start(f32[10,3,32,128]{3,2,1,0:T(8,128)S(1)} %collective-permute-done.1.args_3_), channel_id=1, source_target_pairs={{0,1},{1,0},{2,3},{3,2},{4,5},{5,4},{6,7},{7,6},{8,9},{9,8},{10,11... | collective-permute-start | bytes 1474568 | tf_op jit(solution)/shard_map/ppermute | solution.py:318
  42.4 1.8 %collective-permute-start.6 = (f32[2,8,16,384]{3,2,1,0:T(8,128)S(1)}, f32[2,8,16,384]{3,2,1,0:T(8,128)S(1)}, u32[]{:S(2)}, u32[]{:S(2)}) collective-permute-start(f32[2,8,16,384]{3,2,1,0:T(8,128)S(1)} %get-tuple-element.59), channel_id=1, source_target_pairs={{0,1},{1,0},{2,3},{3,2},{4,5},{5,4},{6,7},{7,6},{8,9},{9,8},{10,11... | collective-permute-start | bytes 1179656 | tf_op jit(solution)/shard_map/ppermute | solution.py:331
  44.2 7.0 %collective-permute-start.7 = (f32[8,16,384]{2,1,0:T(8,128)S(1)}, f32[8,16,384]{2,1,0:T(8,128)S(1)}, u32[]{:S(2)}, u32[]{:S(2)}) collective-permute-start(f32[8,16,384]{2,1,0:T(8,128)S(1)} %fusion), channel_id=1, source_target_pairs={{0,2},{1,3},{2,0},{3,1},{4,6},{5,7},{6,4},{7,5},{8,10},{9,11},{10,... | collective-permute-start | bytes 589832 | tf_op jit(solution)/shard_map/ppermute | solution.py:333

commit v3 on v2

--- a/solution.py
+++ b/solution.py
@@ -1,3 +1,5 @@
+import functools
+
 import jax
 import jax.numpy as jnp
 from jax import lax
@@ -8,6 +10,7 @@
 SWEEPS = 3
 HALO = SWEEPS + 1
 EDGE = HALO + 2 * SWEEPS
+FIELDS = 16
 LANES = 128
 SUB = 8
 ANYWHERE = pl.BlockSpec(memory_space=pl.ANY)
@@ -15,21 +18,32 @@
 ONCHIP = pl.BlockSpec(memory_space=pltpu.VMEM)
 
 
+def lane_shifts(own):
+    lane = lax.broadcasted_iota(jnp.int32, (SUB, LANES), 1)
+    zero = jnp.zeros((SUB, LANES), jnp.float32)
+    fwd = [zero] + [pltpu.roll(v, 1, 1) for v in own]
+    bwd = [pltpu.roll(v, LANES - 1, 1) for v in own] + [zero]
+    return [
+        (jnp.where(lane == 0, fwd[c], fwd[c + 1]), jnp.where(lane == LANES - 1, bwd[c + 1], bwd[c]))
+        for c in range(len(own))
+    ]
+
+
 def around(ref, zz, r, rows):
-    tiles = ref.shape[1]
-    lane = lax.broadcasted_iota(jnp.int32, (SUB, LANES), 1)
     sub = lax.broadcasted_iota(jnp.int32, (SUB, LANES), 0)
     zero = jnp.zeros((SUB, LANES), jnp.float32)
-    here = pl.ds(SUB * r, SUB)
-    own = [ref[zz, c, here, :] for c in range(tiles)]
-    fwd = [pltpu.roll(v, 1, 1) for v in own]
-    bwd = [pltpu.roll(v, LANES - 1, 1) for v in own]
+    own = [ref[zz, c, pl.ds(SUB * r, SUB), :] for c in range(ref.shape[1])]
+    sides = lane_shifts(own)
+    return own, [sides[c] + cross(ref, zz, c, r, rows, own[c], sub, zero) for c in range(len(own))]
+
+
+def around_padded(ref, zz, start):
+    own = [ref[zz, c, pl.ds(start, SUB), :] for c in range(ref.shape[1])]
     out = []
-    for c in range(tiles):
-        left = jnp.where(lane == 0, fwd[c - 1] if c > 0 else zero, fwd[c])
-        right = jnp.where(lane == LANES - 1, bwd[c + 1] if c + 1 < tiles else zero, bwd[c])
-        out.append((left, right) + cross(ref, zz, c, r, rows, own[c], sub, zero))
-    return own, out
+    for c, pair in enumerate(lane_shifts(own)):
+        rest = [ref[zz, c, pl.ds(start + d, SUB), :] for d in (-1, 1)]
+        out.append(pair + tuple(rest) + tuple(ref[zz + d, c, pl.ds(start, SUB), :] for d in (-1, 1)))
+    return out
 
 
 def cross(ref, zz, c, r, rows, own, sub, zero):
@@ -112,8 +126,8 @@
                 p3 = SR[zz, c, at(r), :] + weighted(w, a[c]) * hr
                 u1 = weighted(w, v[c]) * hr
                 e = -(u1 * p1 + u2[c] * p2[c] + u3 * p3)
-                U1[zz, c, at(r), :] = u1
-                E[zz, c, at(r), :] = e
+                U1[zz, c, at(r + 1), :] = u1
+                E[zz, c, at(r + 1), :] = e
                 if own:
                     g = u3 * six(a[c]) + p1 * six(v[c]) + u1 * NP0[zz, c, at(r), :]
                     press(zz)[at(r), pl.ds(c * LANES, LANES)] = p3
@@ -182,32 +196,38 @@
         cp.start()
     for cp in copies:
         cp.wait()
+    rim = jnp.zeros((SUB, LANES), jnp.float32)
+
+    def clear(zz, _):
+        for ref in (U1, E):
+            for c in range(ref.shape[1]):
+                ref[zz, c, pl.ds(0, SUB), :] = rim
+                ref[zz, c, pl.ds(ref.shape[2] - SUB, SUB), :] = rim
+        return 0
+
+    lax.fori_loop(HALO, top, clear, 0)
     refs = (K, P0, SRC, OBS, P1, P2, U1, U2, U3, HR, SR, NP0, WL, WR, G, E)
     ranges = [[(HALO + n, top - n)] for n in (1, 2)] + [[(HALO + 3, top - 3, True)]]
     sweeps(refs, ranges, lambda zz: jnp.float32(1.0), lambda zz: mid.at[zz - HALO - SWEEPS])
 
 
-def outer_kernel(*args):
-    klo, khi, alo, ahi, blo, bhi, mid = args[:7]
-    refs, (press_out, keep_out, send_out, press, sems) = args[-21:-5], args[-5:]
-    K, P0, SRC, OBS, P1, P2, U1, U2, U3, HR, SR, NP0, WL, WR, G, E = refs
-    slab, nx = press.shape[:2]
-    half, top, depth = nx // 2, HALO + slab, slab + 2 * HALO
-    tiles, rows = K.shape[1], nx // SUB
-    draw, draws = lax.axis_index("draw"), lax.axis_size("draw")
-    space, spaces = lax.axis_index("space"), lax.axis_size("space")
-    par, group, groups = draw % 2, draw // 2, draws // 2
-    block = nx // draws
-
-    pairs = [(klo, K.at[pl.ds(0, HALO)]), (khi, K.at[pl.ds(top, HALO)])]
-    mine = pl.ds(pl.multiple_of(half * par, half), half)
-    other = pl.ds(pl.multiple_of(half * (1 - par), half), half)
-    for lo, hi, at in ((alo, ahi, mine), (blo, bhi, other)):
+def side_kernel(low, *args):
+    khalo, mine, theirs = args[:3]
+    refs, sems = args[3 + FIELDS : 3 + 2 * FIELDS], args[-1]
+    press, sends = args[3 + 2 * FIELDS], args[4 + 2 * FIELDS : -1]
+    K, P0, SRC, OBS = refs[:4]
+    nx = K.shape[2]
+    depth = K.shape[0]
+    half, top = nx // 2, depth - HALO
+    par = lax.axis_index("draw") % 2
+
+    pairs = [(khalo, K.at[pl.ds(0 if low else top, HALO)])]
+    for half_rows, which in ((mine, par), (theirs, 1 - par)):
+        rows = pl.ds(pl.multiple_of(half * which, half), half)
         first = 0
         for field, width in ((P0, HALO), (SRC, SWEEPS), (OBS, SWEEPS)):
-            span = pl.ds(first, width)
-            pairs.append((lo.at[span], field.at[pl.ds(HALO - width, width), :, at]))
-            pairs.append((hi.at[span], field.at[pl.ds(top, width), :, at]))
+            planes = pl.ds(HALO - width if low else top, width)
+            pairs.append((half_rows.at[pl.ds(first, width)], field.at[planes, :, rows]))
             first += width
     copies = [pltpu.make_async_copy(a, b, sems.at[i]) for i, (a, b) in enumerate(pairs)]
     for cp in copies:
@@ -215,53 +235,57 @@
     for cp in copies:
         cp.wait()
 
-    low = jnp.where(space > 0, 1.0, 0.0).astype(jnp.float32)
-    high = jnp.where(space + 1 < spaces, 1.0, 0.0).astype(jnp.float32)
+    space, spaces = lax.axis_index("space"), lax.axis_size("space")
+    met = jnp.where(space > 0 if low else space + 1 < spaces, 1.0, 0.0).astype(jnp.float32)
+    if low:
+        ranges = [[(1, HALO + 1)], [(2, HALO + 2)], [(3, HALO, False), (HALO, HALO + 3, True)]]
+        shift = HALO
+    else:
+        ranges = [[(top - 1, depth - 1)], [(top - 2, depth - 2)], [(top - 3, top, True), (top, depth - 3, False)]]
+        shift = top - 3
 
     def inside(zz):
-        return jnp.where(zz < HALO, low, jnp.where(zz >= top, high, jnp.float32(1.0)))
-
-    ranges = [
-        [(1, HALO + 1), (top - 1, depth - 1)],
-        [(2, HALO + 2), (top - 2, depth - 2)],
-        [(3, HALO, False), (HALO, HALO + 3, True), (top - 3, top, True), (top, depth - 3, False)],
-    ]
-    sweeps(refs, ranges, inside, lambda zz: press.at[zz - HALO])
-    done = [
-        pltpu.make_async_copy(press.at[span], press_out.at[span], sems.at[i])
-        for i, span in enumerate((pl.ds(0, SWEEPS), pl.ds(slab - SWEEPS, SWEEPS)))
-    ]
-    middle = pl.ds(SWEEPS, slab - 2 * SWEEPS)
-    done.append(pltpu.make_async_copy(mid, press_out.at[middle], sems.at[len(done)]))
-    for cp in done:
+        return jnp.where(zz < HALO if low else zz >= top, met, jnp.float32(1.0))
+
+    sweeps(refs, ranges, inside, lambda zz: press.at[zz - shift])
+    if sends:
+        gradients(K, P0, refs[6], refs[-2], refs[-1], [(sends[0], 1 - par, 1)])
+
+
+def gradients(K, P0, U1, G, E, parts):
+    tiles, nx, slab = K.shape[1], K.shape[2], K.shape[0] - 2 * HALO
+    draw, draws = lax.axis_index("draw"), lax.axis_size("draw")
+    block, groups = nx // draws, draws // 2
+
+    def plane(z, _):
+        zz = z + HALO
+        for out, parity, first in parts:
+            for s in range(out.shape[0]):
+                base = (2 * ((draw // 2 + first + s) % groups) + parity) * block
+                for q in range(block // SUB):
+                    start = pl.multiple_of(base + SUB * q, SUB)
+                    v = around_padded(U1, zz, pl.multiple_of(start + SUB, SUB))
+                    w = around_padded(E, zz, pl.multiple_of(start + SUB, SUB))
+                    at = pl.ds(start, SUB)
+                    for c in range(tiles):
+                        g = G[zz, c, at, :] + P0[zz, c, at, :] * six(v[c]) + six(w[c])
+                        out[s, z, pl.ds(SUB * q, SUB), pl.ds(c * LANES, LANES)] = 0.5 * K[zz, c, at, :] * g
+        return 0
+
+    lax.fori_loop(0, slab, plane, 0)
+
+
+def rest_kernel(low, mid, high, K, P0, U1, G, E, press, keep_near, keep_far, send_near, sems):
+    slab, nx = press.shape[:2]
+    par = lax.axis_index("draw") % 2
+    copies, at = [], 0
+    for ref in (low, mid, high):
+        copies.append(pltpu.make_async_copy(ref, press.at[pl.ds(at, ref.shape[0])], sems.at[len(copies)]))
+        at += ref.shape[0]
+    for cp in copies:
         cp.start()
-
-    def at(r):
-        return pl.ds(SUB * r, SUB)
-
-    def gradient(zz, r):
-        _, v = around(U1, zz, r, rows)
-        _, w = around(E, zz, r, rows)
-        return [
-            0.5 * K[zz, c, at(r), :] * (G[zz, c, at(r), :] + P0[zz, c, at(r), :] * six(v[c]) + six(w[c]))
-            for c in range(tiles)
-        ]
-
-    def last(z, _):
-        zz = z + HALO
-        for h in range(groups):
-            slot = (h - group + groups) % groups
-            for q in range(block // SUB):
-                even = gradient(zz, (2 * h * block) // SUB + q)
-                odd = gradient(zz, ((2 * h + 1) * block) // SUB + q)
-                for c in range(tiles):
-                    cols = pl.ds(c * LANES, LANES)
-                    keep_out[slot, z, pl.ds(SUB * q, SUB), cols] = jnp.where(par == 0, even[c], odd[c])
-                    send_out[slot, z, pl.ds(SUB * q, SUB), cols] = jnp.where(par == 0, odd[c], even[c])
-        return 0
-
-    lax.fori_loop(0, slab, last, 0)
-    for cp in done:
+    gradients(K, P0, U1, G, E, [(keep_far, par, 1), (keep_near, par, 0), (send_near, 1 - par, 0)])
+    for cp in copies:
         cp.wait()
 
 
@@ -274,11 +298,14 @@
     pair = [(i, i ^ 1) for i in range(draws)]
     f32 = jnp.float32
     field = pltpu.VMEM((depth, tiles, nx, LANES), f32)
+    padded = pltpu.VMEM((depth, tiles, nx + 2 * SUB, LANES), f32)
+    kinds = [field] * 6 + [padded] + [field] * 8 + [padded]
     edge = jax.ShapeDtypeStruct((EDGE, tiles, half, LANES), f32)
     rim = jax.ShapeDtypeStruct((HALO, tiles, nx, LANES), f32)
     whole = jax.ShapeDtypeStruct((slab, nx, ny), f32)
     mid = jax.ShapeDtypeStruct((slab - 2 * SWEEPS, nx, ny), f32)
-    part = jax.ShapeDtypeStruct((draws // 2, slab, nx // draws, ny), f32)
+    groups = draws // 2
+    near, far = [jax.ShapeDtypeStruct((n, slab, nx // draws, ny), f32) for n in (1, groups - 1)]
     params = pltpu.CompilerParams(vmem_limit_bytes=8 * 2**20)
     cells = slab * nx * ny
 
@@ -290,7 +317,7 @@
         scratch_shapes=[pltpu.SemaphoreType.DMA((6 * tiles,))],
         compiler_params=params,
         cost_estimate=pl.CostEstimate(flops=cells, bytes_accessed=20 * cells, transcendentals=0),
-    )(start_pressure, source, observe)
+    )(*[pltpu.with_memory_space_constraint(a, pltpu.HBM) for a in (start_pressure, source, observe)])
     alo = lax.ppermute(aup, "space", up)
     ahi = lax.ppermute(adown, "space", down)
     K, top, bottom = pl.pallas_call(
@@ -305,7 +332,7 @@
     khi = lax.ppermute(bottom, "space", down)
     state = pl.pallas_call(
         inner_kernel,
-        out_shape=(field,) * 15 + (mid,),
+        out_shape=(*kinds[1:], mid),
         in_specs=[ONCHIP] + [ANYWHERE] * 3,
         out_specs=(ONCHIP,) * 16,
         scratch_shapes=[pltpu.SemaphoreType.DMA((3 * tiles,))],
@@ -316,24 +343,39 @@
     state = (*state[:-2], last, state[-1])
     blo = lax.ppermute(alo, "draw", pair)
     bhi = lax.ppermute(ahi, "draw", pair)
-    fields = (K, *state[:-1])
-    n = len(fields)
-    *_, press, keep, send = pl.pallas_call(
-        outer_kernel,
-        out_shape=(field,) * n + (whole, part, part),
-        in_specs=[ONCHIP] * (7 + n),
-        out_specs=(ONCHIP,) * n + (OFFCHIP, ONCHIP, ONCHIP),
-        scratch_shapes=[pltpu.VMEM((slab, nx, ny), f32), pltpu.SemaphoreType.DMA((14,))],
-        input_output_aliases={7 + i: i for i in range(n)},
+    fields, centre = (K, *state[:-1]), state[-1]
+
+    def side(low, khalo, mine, theirs, fields):
+        ends = (jax.ShapeDtypeStruct((SWEEPS, nx, ny), f32),) + ((far,) if low else ())
+        out = pl.pallas_call(
+            functools.partial(side_kernel, low),
+            out_shape=(*kinds, *ends),
+            in_specs=[ONCHIP] * (3 + FIELDS),
+            out_specs=(ONCHIP,) * (FIELDS + len(ends)),
+            scratch_shapes=[pltpu.SemaphoreType.DMA((7,))],
+            input_output_aliases={3 + i: i for i in range(FIELDS)},
+            compiler_params=params,
+            cost_estimate=pl.CostEstimate(flops=100 * cells, bytes_accessed=30 * cells, transcendentals=0),
+        )(khalo, mine, theirs, *fields)
+        return out[:FIELDS], *out[FIELDS:]
+
+    fields, high = side(False, khi, ahi, bhi, fields)
+    fields, low, send_far = side(True, klo, alo, blo, fields)
+    got_far = lax.ppermute(send_far, "draw", pair)
+    press, keep_near, keep_far, send_near = pl.pallas_call(
+        rest_kernel,
+        out_shape=(whole, near, far, near),
+        in_specs=[ONCHIP] * 8,
+        out_specs=(OFFCHIP,) + (ONCHIP,) * 3,
+        scratch_shapes=[pltpu.SemaphoreType.DMA((3,))],
         compiler_params=params,
-        cost_estimate=pl.CostEstimate(flops=200 * cells, bytes_accessed=60 * cells, transcendentals=0),
-    )(klo, khi, alo, ahi, blo, bhi, state[-1], *fields)
-    got = lax.ppermute(send, "draw", pair)
+        cost_estimate=pl.CostEstimate(flops=30 * cells, bytes_accessed=30 * cells, transcendentals=0),
+    )(low, centre, high, fields[0], fields[1], fields[6], fields[14], fields[15])
     moved = [
-        lax.ppermute(keep[s] + got[s], "draw", [(j, (j + 2 * s) % draws) for j in range(draws)])
-        for s in range(1, draws // 2)
+        lax.ppermute(keep_far[s - 1] + got_far[s - 1], "draw", [(j, (j + 2 * s) % draws) for j in range(draws)])
+        for s in range(1, groups)
     ]
-    total = keep[0] + got[0]
+    total = keep_near[0] + lax.ppermute(send_near, "draw", pair)[0]
     for part_sum in moved:
         total = total + part_sum
     return press[None], total

time: 52.3 us -> 49 us (0.937)
  waiting for transfers between devices: 20.7 us -> 17.2 us
  local copies, waits for them, and re-layouts: 4.53 us -> 2.27 us
  Pallas kernels: 10.7 us -> 12.8 us
    unnamed x14 -> x10, local copies, waits for them, and re-layouts: 4.53 us -> 2.27 us
    ppermute x2 -> x3, waiting for transfers between devices: 7.04 us -> 5.45 us  [the longest x1 5.44 us: local(): lax.ppermute(keep_far[s - 1] + got_far[s - 1], 'draw', [(j, (j + 2 * s) %...]
    ppermute x1, waiting for transfers between devices: 1.35 us -> 0.01 us  [local(): blo = lax.ppermute(alo, 'draw', pair)]
    pallas_call x1, Pallas kernels: 0.29 us -> 1.52 us  [local(): pl.pallas_call(edges_kernel, out_shape=(edge, edge), in_specs=[OFFCHIP] *...]
    ppermute x1, waiting for transfers between devices: 7.44 us -> 6.27 us  [local(): klo = lax.ppermute(top, 'space', up)]
    pallas_call x2 -> x4, Pallas kernels: 10.2 us -> 11.1 us  [the longest x2 6.89 us: side(): pl.pallas_call(functools.partial(side_kernel, low), out_shape=(*kinds, *e...]
    ppermute x1, waiting for transfers between devices: 0.7 us -> 1.35 us  [local(): bhi = lax.ppermute(ahi, 'draw', pair)]
    ppermute x2 -> x3, starting transfers between devices: 1.76 us -> 2.2 us  [the longest x1 1.56 us: local(): lax.ppermute(keep_far[s - 1] + got_far[s - 1], 'draw', [(j, (j + 2 * s) %...]
  transfers between devices with their start and end apart: 8 -> 9, of which waited for: 6 -> 4; matrix products, arithmetic and copies ran while one was open for 0% -> 0% of each run, Pallas kernels for 6% -> 15%
where the time goes in v3:
time: 49 us; the launch traced here: 48.7 us
  waiting for transfers between devices  17.2 us (35%)
  starting transfers between devices  14.8 us (30%)
  Pallas kernels  12.8 us (26%)
  local copies, waits for them, and re-layouts  2.27 us (5%)
  between operations  0.79 us (2%)
  other arithmetic  0.74 us (2%)
    pallas_call x2, Pallas kernels, side(): pl.pallas_call(functools.partial(side_kernel, low), out_shape=(*kinds, *e...  6.89 us
    ppermute x1, waiting for transfers between devices, local(): klo = lax.ppermute(top, 'space', up)  6.27 us
    ppermute x1, waiting for transfers between devices, local(): lax.ppermute(keep_far[s - 1] + got_far[s - 1], 'draw', [(j, (j + 2 * s) %...  5.44 us
    ppermute x1, starting transfers between devices, local(): alo = lax.ppermute(aup, 'space', up)  4.96 us
    ppermute x1, starting transfers between devices, local(): klo = lax.ppermute(top, 'space', up)  4.57 us
    ppermute x1, waiting for transfers between devices, local(): khi = lax.ppermute(bottom, 'space', down)  4.14 us
    pallas_call x1, Pallas kernels, local(): pl.pallas_call(inner_kernel, out_shape=(*kinds[1:], mid), in_specs=[ONCHI...  2.86 us
    unnamed x10, local copies, waits for them, and re-layouts  2.27 us
  transfers between devices with their start and end apart: 9, of which 4 were waited for; matrix products, arithmetic and copies ran while one was open for 0% of the time, Pallas kernels for 15%

profile of v3, /device:TPU:0, one launch (start us, length us, event | category | flops | bytes accessed | tf_op | source)
XLA Modules:
  0.0 48.7 jit_solution(13825006653486507220)
XLA Ops:
  0.6 0.0 copy-start.1
  0.6 0.0 copy-start
  0.7 0.0 copy-start.2
  0.7 1.5 %shard_map.68 = (f32[10,3,32,128]{3,2,1,0:T(8,128)S(1)}, f32[10,3,32,128]{3,2,1,0:T(8,128)S(1)}) custom-call(f32[8,64,384]{2,1,0:T(8,128)} %p0.3, f32[8,64,384]{2,1,0:T(8,128)} %src.3, f32[8,64,384]{2,1,0:T(8,128)} %obs.3), custom_call_target="tpu_custom_call" | custom-call | flops 196608 | bytes 3932160 | tf_op jit(solution)/shard_map/pallas_call | solution.py:312
  2.2 5.0 %collective-permute-start = (f32[10,3,32,128]{3,2,1,0:T(8,128)S(1)}, f32[10,3,32,128]{3,2,1,0:T(8,128)S(1)}, u32[]{:S(2)}, u32[]{:S(2)}) collective-permute-start(f32[10,3,32,128]{3,2,1,0:T(8,128)S(1)} %get-tuple-element.56), channel_id=1, source_target_pairs={{0,4},{4,8},{8,12},{1,5},{5,9},{9,13},{2,6},{6,10},{10,14},{3,7},{... | collective-permute-start | bytes 1474568 | tf_op jit(solution)/shard_map/ppermute | solution.py:321
  7.2 1.3 %collective-permute-start.1 = (f32[10,3,32,128]{3,2,1,0:T(8,128)S(1)}, f32[10,3,32,128]{3,2,1,0:T(8,128)S(1)}, u32[]{:S(2)}, u32[]{:S(2)}) collective-permute-start(f32[10,3,32,128]{3,2,1,0:T(8,128)S(1)} %get-tuple-element.57), channel_id=1, source_target_pairs={{4,0},{8,4},{12,8},{5,1},{9,5},{13,9},{6,2},{10,6},{14,10},{7,3},{... | collective-permute-start | bytes 1474568 | tf_op jit(solution)/shard_map/ppermute | solution.py:322
  8.5 0.0 copy-start.3
  8.5 1.1 %copy-done.3 = f32[8,64,384]{2,1,0:T(8,128)S(1)} copy-done((f32[8,64,384]{2,1,0:T(8,128)S(1)}, f32[8,64,384]{2,1,0:T(8,128)}, u32[]{:S(2)}) %copy-start.3) | copy-done | bytes 786456
  9.6 0.0 copy-start.4
  9.6 1.1 %copy-done.4 = f32[1,8,64,384]{3,2,1,0:T(8,128)S(1)} copy-done((f32[1,8,64,384]{3,2,1,0:T(8,128)S(1)}, f32[1,8,64,384]{3,2,1,0:T(8,128)}, u32[]{:S(2)}) %copy-start.4) | copy-done | bytes 786456
  10.7 0.2 shard_map.69
  11.0 4.6 %collective-permute-start.2 = (f32[4,3,64,128]{3,2,1,0:T(8,128)S(1)}, f32[4,3,64,128]{3,2,1,0:T(8,128)S(1)}, u32[]{:S(2)}, u32[]{:S(2)}) collective-permute-start(f32[4,3,64,128]{3,2,1,0:T(8,128)S(1)} %get-tuple-element.58), channel_id=1, source_target_pairs={{0,4},{4,8},{8,12},{1,5},{5,9},{9,13},{2,6},{6,10},{10,14},{3,7},{... | collective-permute-start | bytes 1179656 | tf_op jit(solution)/shard_map/ppermute | solution.py:331
  15.6 1.3 %collective-permute-start.3 = (f32[4,3,64,128]{3,2,1,0:T(8,128)S(1)}, f32[4,3,64,128]{3,2,1,0:T(8,128)S(1)}, u32[]{:S(2)}, u32[]{:S(2)}) collective-permute-start(f32[4,3,64,128]{3,2,1,0:T(8,128)S(1)} %get-tuple-element.59), channel_id=1, source_target_pairs={{4,0},{8,4},{12,8},{5,1},{9,5},{13,9},{6,2},{10,6},{14,10},{7,3},{... | collective-permute-start | bytes 1179656 | tf_op jit(solution)/shard_map/ppermute | solution.py:332
  16.9 0.0 copy-done.1
  16.9 0.0 copy-done
  16.9 0.0 copy-done.2
  16.9 2.9 %shard_map.70 = (f32[16,3,64,128]{3,2,1,0:T(8,128)S(1)}, f32[16,3,64,128]{3,2,1,0:T(8,128)S(1)}, f32[16,3,64,128]{3,2,1,0:T(8,128)S(1)}, f32[16,3,64,128]{3,2,1,...) custom-call(f32[16,3,64,128]{3,2,1,0:T(8,128)S(1)} %get-tuple-elemen, ...), custom_call_target="tpu_custom_call" | custom-call | flops 39321600 | bytes 11796480 | tf_op jit(solution)/shard_map/pallas_call | solution.py:333
  19.7 6.3 %collective-permute-done.2.args_0_ = f32[4,3,64,128]{3,2,1,0:T(8,128)S(1)} collective-permute-done((f32[4,3,64,128]{3,2,1,0:T(8,128)S(1)}, f32[4,3,64,128]{3,2,1,0:T(8,128)S(1)}, u32[]{:S(2)}, u32[]{:S(2)}) %collective-permute-start.2) | collective-permute-done | bytes 393248 | tf_op jit(solution)/shard_map/ppermute | solution.py:331
  26.0 4.1 %collective-permute-done.3.args_0_ = f32[4,3,64,128]{3,2,1,0:T(8,128)S(1)} collective-permute-done((f32[4,3,64,128]{3,2,1,0:T(8,128)S(1)}, f32[4,3,64,128]{3,2,1,0:T(8,128)S(1)}, u32[]{:S(2)}, u32[]{:S(2)}) %collective-permute-start.3) | collective-permute-done | bytes 393248 | tf_op jit(solution)/shard_map/ppermute | solution.py:332
  30.2 0.0 collective-permute-done.args_1_
  30.2 0.0 collective-permute-done.1.args_1_
  30.2 0.0 collective-permute-start.5
  30.2 0.5 %collective-permute-start.4 = (f32[10,3,32,128]{3,2,1,0:T(8,128)S(1)}, f32[10,3,32,128]{3,2,1,0:T(8,128)S(1)}, u32[]{:S(2)}, u32[]{:S(2)}) collective-permute-start(f32[10,3,32,128]{3,2,1,0:T(8,128)S(1)} %collective-permute-done.args_1_), channel_id=1, source_target_pairs={{0,1},{1,0},{2,3},{3,2},{4,5},{5,4},{6,7},{7,6},{8,9},{9,8},{10,11... | collective-permute-start | bytes 1474568 | tf_op jit(solution)/shard_map/ppermute | solution.py:344
  30.7 1.4 %collective-permute-done.5.args_2_ = f32[10,3,32,128]{3,2,1,0:T(8,128)S(1)} collective-permute-done((f32[10,3,32,128]{3,2,1,0:T(8,128)S(1)}, f32[10,3,32,128]{3,2,1,0:T(8,128)S(1)}, u32[]{:S(2)}, u32[]{:S(2)}) %collective-permute-start.5) | collective-permute-done | bytes 491552 | tf_op jit(solution)/shard_map/ppermute | solution.py:345
  32.0 3.0 %shard_map.71 = (f32[16,3,64,128]{3,2,1,0:T(8,128)S(1)}, f32[16,3,64,128]{3,2,1,0:T(8,128)S(1)}, f32[16,3,64,128]{3,2,1,0:T(8,128)S(1)}, f32[16,3,64,128]{3,2,1,...) custom-call(f32[4,3,64,128]{3,2,1,0:T(8,128)S(1)} %collective-permut, ...), custom_call_target="tpu_custom_call", output_to_operand_aliasing={{0}: (3, {}), {1}: (4, {}), {2}: (5, {}), {3}: (6, {}), {4}... | custom-call | flops 19660800 | bytes 5898240 | tf_op jit(solution)/shard_map/pallas_call | solution.py:350
  35.0 0.0 collective-permute-done.4.args_2_
  35.0 3.9 %shard_map.72 = (f32[16,3,64,128]{3,2,1,0:T(8,128)S(1)}, f32[16,3,64,128]{3,2,1,0:T(8,128)S(1)}, f32[16,3,64,128]{3,2,1,0:T(8,128)S(1)}, f32[16,3,64,128]{3,2,1,...) custom-call(f32[4,3,64,128]{3,2,1,0:T(8,128)S(1)} %collective-permut, ...), custom_call_target="tpu_custom_call", output_to_operand_aliasing={{0}: (3, {}), {1}: (4, {}), {2}: (5, {}), {3}: (6, {}), {4}... | custom-call | flops 19660800 | bytes 5898240 | tf_op jit(solution)/shard_map/pallas_call | solution.py:350
  38.9 0.2 collective-permute-start.7
  39.1 1.3 %shard_map.73 = (f32[8,64,384]{2,1,0:T(8,128)}, f32[1,8,16,384]{3,2,1,0:T(8,128)S(1)}, f32[1,8,16,384]{3,2,1,0:T(8,128)S(1)}, f32[1,8,16,384]{3,2,1,0:T(8,128)S(1)}) custom-call(f32[3,64,384]{2,1,0:T(8,128)S(1)} %get-tuple-element.97.low, f32[2,64,384]{2,1,0:T(8,128)S(1)} %get-tuple-element.98.mid, f32[3,64,384]{2,1,0:T(8,128)S(1)} %get-tuple-element.99.high, ...), custom_call_target="tpu_custom_call" | custom-call | flops 5898240 | bytes 5898240 | tf_op jit(solution)/shard_map/pallas_call | solution.py:365
  40.5 0.4 collective-permute-start.6
  40.9 0.0 collective-permute-done.7
  41.0 1.6 %collective-permute-start.8 = (f32[8,16,384]{2,1,0:T(8,128)S(1)}, f32[8,16,384]{2,1,0:T(8,128)S(1)}, u32[]{:S(2)}, u32[]{:S(2)}) collective-permute-start(f32[8,16,384]{2,1,0:T(8,128)S(1)} %add_bitcast_fusion), channel_id=1, source_target_pairs={{0,2},{1,3},{2,0},{3,1},{4,6},{5,7},{6,4},{7,5},{8,10},{9,11},{10,... | collective-permute-start | bytes 589832 | tf_op jit(solution)/shard_map/ppermute | solution.py:375
  42.5 0.0 collective-permute-done.6
  42.5 5.4 %collective-permute-done.8 = f32[8,16,384]{2,1,0:T(8,128)S(1)} collective-permute-done((f32[8,16,384]{2,1,0:T(8,128)S(1)}, f32[8,16,384]{2,1,0:T(8,128)S(1)}, u32[]{:S(2)}, u32[]{:S(2)}) %collective-permute-start.8) | collective-permute-done | bytes 196640 | tf_op jit(solution)/shard_map/ppermute | solution.py:375
  48.0 0.7 %bitcast_add_fusion = f32[8,16,384]{2,1,0:T(8,128)} fusion(f32[8,16,384]{2,1,0:T(8,128)S(1)} %collective-permute-done.8, f32[1,8,16,384]{3,2,1,0:T(8,128)S(1)} %get-tuple-element.106, f32[1,8,16,384]{3,2,1,0:T(8,128)S(1)} %collective-permute-done.6), kind=kLoop, calls=%fused_computation | loop fusion | flops 98304 | bytes 786432 | tf_op jit(solution)/shard_map/add | solution.py:380
  (1 shorter events, 0.0 us)
Async XLA Ops:
  0.6 16.2 %copy-start.1 = (f32[8,64,384]{2,1,0:T(8,128)S(1)}, f32[8,64,384]{2,1,0:T(8,128)}, u32[]{:S(2)}) copy-start(f32[8,64,384]{2,1,0:T(8,128)} %src.3) | copy-start | bytes 2359300
  0.6 16.2 %copy-start = (f32[8,64,384]{2,1,0:T(8,128)S(1)}, f32[8,64,384]{2,1,0:T(8,128)}, u32[]{:S(2)}) copy-start(f32[8,64,384]{2,1,0:T(8,128)} %p0.3) | copy-start | bytes 2359300
  0.7 16.2 %copy-start.2 = (f32[8,64,384]{2,1,0:T(8,128)S(1)}, f32[8,64,384]{2,1,0:T(8,128)}, u32[]{:S(2)}) copy-start(f32[8,64,384]{2,1,0:T(8,128)} %obs.3) | copy-start | bytes 2359300
  2.2 28.0 %collective-permute-start = (f32[10,3,32,128]{3,2,1,0:T(8,128)S(1)}, f32[10,3,32,128]{3,2,1,0:T(8,128)S(1)}, u32[]{:S(2)}, u32[]{:S(2)}) collective-permute-start(f32[10,3,32,128]{3,2,1,0:T(8,128)S(1)} %get-tuple-element.56), channel_id=1, source_target_pairs={{0,4},{4,8},{8,12},{1,5},{5,9},{9,13},{2,6},{6,10},{10,14},{3,7},{... | collective-permute-start | bytes 1474568 | tf_op jit(solution)/shard_map/ppermute | solution.py:321
  7.2 23.0 %collective-permute-start.1 = (f32[10,3,32,128]{3,2,1,0:T(8,128)S(1)}, f32[10,3,32,128]{3,2,1,0:T(8,128)S(1)}, u32[]{:S(2)}, u32[]{:S(2)}) collective-permute-start(f32[10,3,32,128]{3,2,1,0:T(8,128)S(1)} %get-tuple-element.57), channel_id=1, source_target_pairs={{4,0},{8,4},{12,8},{5,1},{9,5},{13,9},{6,2},{10,6},{14,10},{7,3},{... | collective-permute-start | bytes 1474568 | tf_op jit(solution)/shard_map/ppermute | solution.py:322
  8.5 1.1 %copy-start.3 = (f32[8,64,384]{2,1,0:T(8,128)S(1)}, f32[8,64,384]{2,1,0:T(8,128)}, u32[]{:S(2)}) copy-start(f32[8,64,384]{2,1,0:T(8,128)} %log_perm.1) | copy-start | bytes 2359300
  9.6 1.1 %copy-start.4 = (f32[1,8,64,384]{3,2,1,0:T(8,128)S(1)}, f32[1,8,64,384]{3,2,1,0:T(8,128)}, u32[]{:S(2)}) copy-start(f32[1,8,64,384]{3,2,1,0:T(8,128)} %param.6) | copy-start | bytes 2359300
  11.0 15.0 %collective-permute-start.2 = (f32[4,3,64,128]{3,2,1,0:T(8,128)S(1)}, f32[4,3,64,128]{3,2,1,0:T(8,128)S(1)}, u32[]{:S(2)}, u32[]{:S(2)}) collective-permute-start(f32[4,3,64,128]{3,2,1,0:T(8,128)S(1)} %get-tuple-element.58), channel_id=1, source_target_pairs={{0,4},{4,8},{8,12},{1,5},{5,9},{9,13},{2,6},{6,10},{10,14},{3,7},{... | collective-permute-start | bytes 1179656 | tf_op jit(solution)/shard_map/ppermute | solution.py:331
  15.6 14.6 %collective-permute-start.3 = (f32[4,3,64,128]{3,2,1,0:T(8,128)S(1)}, f32[4,3,64,128]{3,2,1,0:T(8,128)S(1)}, u32[]{:S(2)}, u32[]{:S(2)}) collective-permute-start(f32[4,3,64,128]{3,2,1,0:T(8,128)S(1)} %get-tuple-element.59), channel_id=1, source_target_pairs={{4,0},{8,4},{12,8},{5,1},{9,5},{13,9},{6,2},{10,6},{14,10},{7,3},{... | collective-permute-start | bytes 1179656 | tf_op jit(solution)/shard_map/ppermute | solution.py:332
  30.2 1.9 %collective-permute-start.5 = (f32[10,3,32,128]{3,2,1,0:T(8,128)S(1)}, f32[10,3,32,128]{3,2,1,0:T(8,128)S(1)}, u32[]{:S(2)}, u32[]{:S(2)}) collective-permute-start(f32[10,3,32,128]{3,2,1,0:T(8,128)S(1)} %collective-permute-done.1.args_1_), channel_id=1, source_target_pairs={{0,1},{1,0},{2,3},{3,2},{4,5},{5,4},{6,7},{7,6},{8,9},{9,8},{10,11... | collective-permute-start | bytes 1474568 | tf_op jit(solution)/shard_map/ppermute | solution.py:345
  30.2 4.8 %collective-permute-start.4 = (f32[10,3,32,128]{3,2,1,0:T(8,128)S(1)}, f32[10,3,32,128]{3,2,1,0:T(8,128)S(1)}, u32[]{:S(2)}, u32[]{:S(2)}) collective-permute-start(f32[10,3,32,128]{3,2,1,0:T(8,128)S(1)} %collective-permute-done.args_1_), channel_id=1, source_target_pairs={{0,1},{1,0},{2,3},{3,2},{4,5},{5,4},{6,7},{7,6},{8,9},{9,8},{10,11... | collective-permute-start | bytes 1474568 | tf_op jit(solution)/shard_map/ppermute | solution.py:344
  38.9 2.0 %collective-permute-start.7 = (f32[1,8,16,384]{3,2,1,0:T(8,128)S(1)}, f32[1,8,16,384]{3,2,1,0:T(8,128)S(1)}, u32[]{:S(2)}, u32[]{:S(2)}) collective-permute-start(f32[1,8,16,384]{3,2,1,0:T(8,128)S(1)} %get-tuple-element.109), channel_id=1, source_target_pairs={{0,1},{1,0},{2,3},{3,2},{4,5},{5,4},{6,7},{7,6},{8,9},{9,8},{10,11... | collective-permute-start | bytes 589832 | tf_op jit(solution)/shard_map/ppermute | solution.py:364
  40.5 2.0 %collective-permute-start.6 = (f32[1,8,16,384]{3,2,1,0:T(8,128)S(1)}, f32[1,8,16,384]{3,2,1,0:T(8,128)S(1)}, u32[]{:S(2)}, u32[]{:S(2)}) collective-permute-start(f32[1,8,16,384]{3,2,1,0:T(8,128)S(1)} %get-tuple-element.107), channel_id=1, source_target_pairs={{0,1},{1,0},{2,3},{3,2},{4,5},{5,4},{6,7},{7,6},{8,9},{9,8},{10,11... | collective-permute-start | bytes 589832 | tf_op jit(solution)/shard_map/ppermute | solution.py:378
  41.0 7.0 %collective-permute-start.8 = (f32[8,16,384]{2,1,0:T(8,128)S(1)}, f32[8,16,384]{2,1,0:T(8,128)S(1)}, u32[]{:S(2)}, u32[]{:S(2)}) collective-permute-start(f32[8,16,384]{2,1,0:T(8,128)S(1)} %add_bitcast_fusion), channel_id=1, source_target_pairs={{0,2},{1,3},{2,0},{3,1},{4,6},{5,7},{6,4},{7,5},{8,10},{9,11},{10,... | collective-permute-start | bytes 589832 | tf_op jit(solution)/shard_map/ppermute | solution.py:375

commit v4 on v3

--- a/solution.py
+++ b/solution.py
@@ -139,46 +139,46 @@
             lax.fori_loop(lo, hi, lambda zz, _, body=body, own=own: body(zz, *own) or 0, 0)
 
 
-def edges_kernel(p0, src, obs, up, down, sems):
-    nx, ny = p0.shape[1:]
-    slab, half = p0.shape[0], nx // 2
+def first_kernel(log_perm, noise, p0, src, obs, K, up, down, means, draws, sems):
+    slab, nx, ny = log_perm.shape
+    tiles, half = ny // LANES, nx // 2
     rows = pl.ds(pl.multiple_of(half * (lax.axis_index("draw") % 2), half), half)
     copies = []
-    for c in range(ny // LANES):
+
+    def copy(src_ref, dst_ref):
+        copies.append(pltpu.make_async_copy(src_ref, dst_ref, sems.at[len(copies)]))
+
+    copy(log_perm, means)
+    copy(noise, draws)
+    for c in range(tiles):
         cols = pl.ds(c * LANES, LANES)
         at = 0
         for ref, width in ((p0, HALO), (src, SWEEPS), (obs, SWEEPS)):
             for start, out in ((slab - width, up), (0, down)):
-                copies.append(
-                    pltpu.make_async_copy(
-                        ref.at[pl.ds(start, width), rows, cols], out.at[pl.ds(at, width), c], sems.at[len(copies)]
-                    )
-                )
+                copy(ref.at[pl.ds(start, width), rows, cols], out.at[pl.ds(at, width), c])
             at += width
     for cp in copies:
         cp.start()
-    for cp in copies:
+    for cp in copies[:2]:
         cp.wait()
 
-
-def conduct_kernel(log_perm, noise, K, top, bottom):
-    slab, nx, ny = log_perm.shape
-
-    def plane(z, _):
+    def plane(z, _, out=None, first=0):
         for r in range(nx // SUB):
-            for c in range(ny // LANES):
+            for c in range(tiles):
                 here, cols = pl.ds(SUB * r, SUB), pl.ds(c * LANES, LANES)
-                K[z + HALO, c, here, :] = jnp.exp(log_perm[z, here, cols] + noise[z, here, cols])
+                k = jnp.exp(means[z, here, cols] + draws[z, here, cols])
+                K[z + HALO, c, here, :] = k
+                if out is not None:
+                    part, at = divmod(SUB * r, half)
+                    out[EDGE + part * HALO + z - first, c, pl.ds(at, SUB), :] = k
         return 0
 
-    lax.fori_loop(0, slab, plane, 0)
-
-    def edge(z, _):
-        top[z] = K[slab + z]
-        bottom[z] = K[HALO + z]
-        return 0
-
-    lax.fori_loop(0, HALO, edge, 0)
+    low, high = functools.partial(plane, out=down), functools.partial(plane, out=up, first=slab - HALO)
+    lax.fori_loop(0, HALO, low, 0)
+    lax.fori_loop(HALO, slab - HALO, plane, 0)
+    lax.fori_loop(slab - HALO, slab, high, 0)
+    for cp in copies[2:]:
+        cp.wait()
 
 
 def inner_kernel(K, p0, src, obs, P0, SRC, OBS, P1, P2, U1, U2, U3, HR, SR, NP0, WL, WR, G, E, mid, sems):
@@ -211,29 +211,34 @@
     sweeps(refs, ranges, lambda zz: jnp.float32(1.0), lambda zz: mid.at[zz - HALO - SWEEPS])
 
 
-def side_kernel(low, *args):
-    khalo, mine, theirs = args[:3]
-    refs, sems = args[3 + FIELDS : 3 + 2 * FIELDS], args[-1]
-    press, sends = args[3 + 2 * FIELDS], args[4 + 2 * FIELDS : -1]
+def side_kernel(low, stages, *args):
+    halos = args[: 2 if 0 in stages else 0]
+    refs = args[len(halos) + FIELDS : len(halos) + 2 * FIELDS]
+    ends = args[len(halos) + 2 * FIELDS :]
     K, P0, SRC, OBS = refs[:4]
-    nx = K.shape[2]
-    depth = K.shape[0]
+    nx, depth = K.shape[2], K.shape[0]
     half, top = nx // 2, depth - HALO
     par = lax.axis_index("draw") % 2
 
-    pairs = [(khalo, K.at[pl.ds(0 if low else top, HALO)])]
-    for half_rows, which in ((mine, par), (theirs, 1 - par)):
-        rows = pl.ds(pl.multiple_of(half * which, half), half)
-        first = 0
-        for field, width in ((P0, HALO), (SRC, SWEEPS), (OBS, SWEEPS)):
-            planes = pl.ds(HALO - width if low else top, width)
-            pairs.append((half_rows.at[pl.ds(first, width)], field.at[planes, :, rows]))
-            first += width
-    copies = [pltpu.make_async_copy(a, b, sems.at[i]) for i, (a, b) in enumerate(pairs)]
-    for cp in copies:
-        cp.start()
-    for cp in copies:
-        cp.wait()
+    if halos:
+        mine, theirs = halos
+        sems = ends[-1]
+        pairs = [
+            (mine.at[pl.ds(EDGE + h * HALO, HALO)], K.at[pl.ds(0 if low else top, HALO), :, pl.ds(h * half, half)])
+            for h in range(2)
+        ]
+        for half_rows, which in ((mine, par), (theirs, 1 - par)):
+            rows = pl.ds(pl.multiple_of(half * which, half), half)
+            first = 0
+            for field, width in ((P0, HALO), (SRC, SWEEPS), (OBS, SWEEPS)):
+                planes = pl.ds(HALO - width if low else top, width)
+                pairs.append((half_rows.at[pl.ds(first, width)], field.at[planes, :, rows]))
+                first += width
+        copies = [pltpu.make_async_copy(a, b, sems.at[i]) for i, (a, b) in enumerate(pairs)]
+        for cp in copies:
+            cp.start()
+        for cp in copies:
+            cp.wait()
 
     space, spaces = lax.axis_index("space"), lax.axis_size("space")
     met = jnp.where(space > 0 if low else space + 1 < spaces, 1.0, 0.0).astype(jnp.float32)
@@ -247,9 +252,10 @@
     def inside(zz):
         return jnp.where(zz < HALO if low else zz >= top, met, jnp.float32(1.0))
 
-    sweeps(refs, ranges, inside, lambda zz: press.at[zz - shift])
-    if sends:
-        gradients(K, P0, refs[6], refs[-2], refs[-1], [(sends[0], 1 - par, 1)])
+    ranges = [spans if n in stages else [] for n, spans in enumerate(ranges)]
+    sweeps(refs, ranges, inside, lambda zz: ends[0].at[zz - shift])
+    if not low:
+        gradients(K, P0, refs[6], refs[-2], refs[-1], [(ends[1], 1 - par, 1)])
 
 
 def gradients(K, P0, U1, G, E, parts):
@@ -300,8 +306,7 @@
     field = pltpu.VMEM((depth, tiles, nx, LANES), f32)
     padded = pltpu.VMEM((depth, tiles, nx + 2 * SUB, LANES), f32)
     kinds = [field] * 6 + [padded] + [field] * 8 + [padded]
-    edge = jax.ShapeDtypeStruct((EDGE, tiles, half, LANES), f32)
-    rim = jax.ShapeDtypeStruct((HALO, tiles, nx, LANES), f32)
+    edge = jax.ShapeDtypeStruct((EDGE + 2 * HALO, tiles, half, LANES), f32)
     whole = jax.ShapeDtypeStruct((slab, nx, ny), f32)
     mid = jax.ShapeDtypeStruct((slab - 2 * SWEEPS, nx, ny), f32)
     groups = draws // 2
@@ -309,27 +314,18 @@
     params = pltpu.CompilerParams(vmem_limit_bytes=8 * 2**20)
     cells = slab * nx * ny
 
-    aup, adown = pl.pallas_call(
-        edges_kernel,
-        out_shape=(edge, edge),
-        in_specs=[OFFCHIP] * 3,
-        out_specs=(ONCHIP, ONCHIP),
-        scratch_shapes=[pltpu.SemaphoreType.DMA((6 * tiles,))],
+    inputs = (log_perm, noise[0], start_pressure, source, observe)
+    K, to_up, to_down = pl.pallas_call(
+        first_kernel,
+        out_shape=(field, edge, edge),
+        in_specs=[OFFCHIP] * 5,
+        out_specs=(ONCHIP,) * 3,
+        scratch_shapes=[pltpu.VMEM((slab, nx, ny), f32)] * 2 + [pltpu.SemaphoreType.DMA((2 + 6 * tiles,))],
         compiler_params=params,
-        cost_estimate=pl.CostEstimate(flops=cells, bytes_accessed=20 * cells, transcendentals=0),
-    )(*[pltpu.with_memory_space_constraint(a, pltpu.HBM) for a in (start_pressure, source, observe)])
-    alo = lax.ppermute(aup, "space", up)
-    ahi = lax.ppermute(adown, "space", down)
-    K, top, bottom = pl.pallas_call(
-        conduct_kernel,
-        out_shape=(field, rim, rim),
-        in_specs=[ONCHIP] * 2,
-        out_specs=(ONCHIP,) * 3,
-        compiler_params=params,
-        cost_estimate=pl.CostEstimate(flops=cells, bytes_accessed=12 * cells, transcendentals=cells),
-    )(log_perm, noise[0])
-    klo = lax.ppermute(top, "space", up)
-    khi = lax.ppermute(bottom, "space", down)
+        cost_estimate=pl.CostEstimate(flops=cells, bytes_accessed=20 * cells, transcendentals=cells),
+    )(*[pltpu.with_memory_space_constraint(a, pltpu.HBM) for a in inputs])
+    alo = lax.ppermute(to_up, "space", up)
+    ahi = lax.ppermute(to_down, "space", down)
     state = pl.pallas_call(
         inner_kernel,
         out_shape=(*kinds[1:], mid),
@@ -339,28 +335,33 @@
         compiler_params=params,
         cost_estimate=pl.CostEstimate(flops=200 * cells, bytes_accessed=60 * cells, transcendentals=0),
     )(K, start_pressure, source, observe)
-    alo, ahi, klo, khi, last = lax.optimization_barrier((alo, ahi, klo, khi, state[-2]))
-    state = (*state[:-2], last, state[-1])
-    blo = lax.ppermute(alo, "draw", pair)
-    bhi = lax.ppermute(ahi, "draw", pair)
     fields, centre = (K, *state[:-1]), state[-1]
 
-    def side(low, khalo, mine, theirs, fields):
-        ends = (jax.ShapeDtypeStruct((SWEEPS, nx, ny), f32),) + ((far,) if low else ())
+    def side(low, stages, halos, fields):
+        ends = (jax.ShapeDtypeStruct((SWEEPS, nx, ny), f32),) if 2 in stages else ()
+        ends = ends if low else (*ends, far)
+        n = len(halos)
         out = pl.pallas_call(
-            functools.partial(side_kernel, low),
+            functools.partial(side_kernel, low, stages),
             out_shape=(*kinds, *ends),
-            in_specs=[ONCHIP] * (3 + FIELDS),
+            in_specs=[ONCHIP] * (n + FIELDS),
             out_specs=(ONCHIP,) * (FIELDS + len(ends)),
-            scratch_shapes=[pltpu.SemaphoreType.DMA((7,))],
-            input_output_aliases={3 + i: i for i in range(FIELDS)},
+            scratch_shapes=[pltpu.SemaphoreType.DMA((8,))] if n else [],
+            input_output_aliases={n + i: i for i in range(FIELDS)},
             compiler_params=params,
-            cost_estimate=pl.CostEstimate(flops=100 * cells, bytes_accessed=30 * cells, transcendentals=0),
-        )(khalo, mine, theirs, *fields)
+            cost_estimate=pl.CostEstimate(flops=60 * cells, bytes_accessed=20 * cells, transcendentals=0),
+        )(*halos, *fields)
         return out[:FIELDS], *out[FIELDS:]
 
-    fields, high = side(False, khi, ahi, bhi, fields)
-    fields, low, send_far = side(True, klo, alo, blo, fields)
+    def swapped(got, fields):
+        got, last = lax.optimization_barrier((got, fields[-1]))
+        return (got, lax.ppermute(got[:EDGE], "draw", pair)), (*fields[:-1], last)
+
+    halos, fields = swapped(alo, fields)
+    (fields,) = side(True, (0,), halos, fields)
+    halos, fields = swapped(ahi, fields)
+    fields, low = side(True, (1, 2), (), fields)
+    fields, high, send_far = side(False, (0, 1, 2), halos, fields)
     got_far = lax.ppermute(send_far, "draw", pair)
     press, keep_near, keep_far, send_near = pl.pallas_call(
         rest_kernel,

time: 49 us -> 47 us (0.959)
  starting transfers between devices: 14.8 us -> 8.62 us
  waiting for transfers between devices: 17.2 us -> 23.3 us
  local copies, waits for them, and re-layouts: 2.27 us -> 0.08 us
    ppermute x6 -> x4, starting transfers between devices: 12.6 us -> 6.42 us  [the longest x1 4.98 us: local(): alo = lax.ppermute(to_up, 'space', up)]
    ppermute x6 -> x4, waiting for transfers between devices: 11.8 us -> 17.6 us  [the longest x1 14.5 us: local(): alo = lax.ppermute(to_up, 'space', up)]
    unnamed x10 -> x6, local copies, waits for them, and re-layouts: 2.27 us -> 0.01 us
  transfers between devices with their start and end apart: 9 -> 7, of which waited for: 4 -> 4; matrix products, arithmetic and copies ran while one was open for 0% -> 0% of each run, Pallas kernels for 15% -> 16%
where the time goes in v4:
time: 47 us; the launch traced here: 46.8 us
  waiting for transfers between devices  23.3 us (50%)
  Pallas kernels  13.2 us (28%)
  starting transfers between devices  8.62 us (18%)
  between operations  0.78 us (2%)
  other arithmetic  0.74 us (2%)
    ppermute x1, waiting for transfers between devices, local(): alo = lax.ppermute(to_up, 'space', up)  14.5 us
    pallas_call x3, Pallas kernels, side(): pl.pallas_call(functools.partial(side_kernel, low, stages), out_shape=(*k...  7.04 us
    ppermute x1, waiting for transfers between devices, local(): lax.ppermute(keep_far[s - 1] + got_far[s - 1], 'draw', [(j, (j + 2 * s) %...  5.77 us
    ppermute x1, starting transfers between devices, local(): alo = lax.ppermute(to_up, 'space', up)  4.98 us
    pallas_call x1, Pallas kernels, local(): pl.pallas_call(inner_kernel, out_shape=(*kinds[1:], mid), in_specs=[ONCHI...  2.95 us
    pallas_call x1, Pallas kernels, local(): pl.pallas_call(first_kernel, out_shape=(field, edge, edge), in_specs=[OFF...  1.91 us
    ppermute x2, waiting for transfers between devices, swapped(): return ((got, lax.ppermute(got[:EDGE], 'draw', pair)), (*fields[:-1], last))  1.85 us
    ppermute x1, starting transfers between devices, local(): lax.ppermute(keep_far[s - 1] + got_far[s - 1], 'draw', [(j, (j + 2 * s) %...  1.56 us
  transfers between devices with their start and end apart: 7, of which 4 were waited for; matrix products, arithmetic and copies ran while one was open for 0% of the time, Pallas kernels for 16%

profile of v4, /device:TPU:0, one launch (start us, length us, event | category | flops | bytes accessed | tf_op | source)
XLA Modules:
  0.0 46.8 jit_solution(12951404216433283576)
XLA Ops:
  0.6 0.0 copy-start
  0.6 0.0 copy-start.1
  0.7 0.0 copy-start.2
  0.7 1.9 %shard_map.68 = (f32[16,3,64,128]{3,2,1,0:T(8,128)S(1)}, f32[18,3,32,128]{3,2,1,0:T(8,128)S(1)}, f32[18,3,32,128]{3,2,1,0:T(8,128)S(1)}) custom-call(f32[8,64,384]{2,1,0:T(8,128)} %log_perm.1, f32[8,64,384]{2,1,0:T(8,128)} %bitcast.6, f32[8,64,384]{2,1,0:T(8,128)} %p0.3, f32[8,64,384]{2,1,0:T(8,128)} %src.3, f32[8,64,384]{2,1,0:T(8,128)} %obs.3), custom_call_target="tpu_custom_call" | custom-call | flops 196608 | bytes 3932160 | tf_op jit(solution)/shard_map/pallas_call | solution.py:318
  2.6 5.0 %collective-permute-start = (f32[18,3,32,128]{3,2,1,0:T(8,128)S(1)}, f32[18,3,32,128]{3,2,1,0:T(8,128)S(1)}, u32[]{:S(2)}, u32[]{:S(2)}) collective-permute-start(f32[18,3,32,128]{3,2,1,0:T(8,128)S(1)} %get-tuple-element.69), channel_id=1, source_target_pairs={{0,4},{4,8},{8,12},{1,5},{5,9},{9,13},{2,6},{6,10},{10,14},{3,7},{... | collective-permute-start | bytes 2654216 | tf_op jit(solution)/shard_map/ppermute | solution.py:327
  7.6 1.3 %collective-permute-start.2 = (f32[18,3,32,128]{3,2,1,0:T(8,128)S(1)}, f32[18,3,32,128]{3,2,1,0:T(8,128)S(1)}, u32[]{:S(2)}, u32[]{:S(2)}) collective-permute-start(f32[18,3,32,128]{3,2,1,0:T(8,128)S(1)} %get-tuple-element.103), channel_id=1, source_target_pairs={{4,0},{8,4},{12,8},{5,1},{9,5},{13,9},{6,2},{10,6},{14,10},{7,3},{... | collective-permute-start | bytes 2654216 | tf_op jit(solution)/shard_map/ppermute | solution.py:328
  8.9 0.0 copy-done
  8.9 0.0 copy-done.1
  8.9 0.0 copy-done.2
  8.9 2.9 %shard_map.69 = (f32[16,3,64,128]{3,2,1,0:T(8,128)S(1)}, f32[16,3,64,128]{3,2,1,0:T(8,128)S(1)}, f32[16,3,64,128]{3,2,1,0:T(8,128)S(1)}, f32[16,3,64,128]{3,2,1,...) custom-call(f32[16,3,64,128]{3,2,1,0:T(8,128)S(1)} %get-tuple-elemen, ...), custom_call_target="tpu_custom_call" | custom-call | flops 39321600 | bytes 11796480 | tf_op jit(solution)/shard_map/pallas_call | solution.py:329
  11.9 14.5 %collective-permute-done.args_0_ = f32[18,3,32,128]{3,2,1,0:T(8,128)S(1)} collective-permute-done((f32[18,3,32,128]{3,2,1,0:T(8,128)S(1)}, f32[18,3,32,128]{3,2,1,0:T(8,128)S(1)}, u32[]{:S(2)}, u32[]{:S(2)}) %collective-permute-start) | collective-permute-done | bytes 884768 | tf_op jit(solution)/shard_map/ppermute | solution.py:327
  26.4 0.1 collective-permute-start.1
  26.5 1.9 %collective-permute-done.1.args_1_ = f32[10,3,32,128]{3,2,1,0:T(8,128)S(1)} collective-permute-done((f32[10,3,32,128]{3,2,1,0:T(8,128)S(1)}, f32[10,3,32,128]{3,2,1,0:T(8,128)S(1)}, u32[]{:S(2)}, u32[]{:S(2)}) %collective-permute-start.1) | collective-permute-done | bytes 491552 | tf_op jit(solution)/shard_map/ppermute | solution.py:358
  28.4 1.0 %shard_map.70 = (f32[16,3,64,128]{3,2,1,0:T(8,128)S(1)}, f32[16,3,64,128]{3,2,1,0:T(8,128)S(1)}, f32[16,3,64,128]{3,2,1,0:T(8,128)S(1)}, f32[16,3,64,128]{3,2,1,...) custom-call(f32[18,3,32,128]{3,2,1,0:T(8,128)S(1)} %collective-permu, ...), custom_call_target="tpu_custom_call", output_to_operand_aliasing={{0}: (2, {}), {1}: (3, {}), {2}: (4, {}), {3}: (5, {}), {4}... | custom-call | flops 11796480 | bytes 3932160 | tf_op jit(solution)/shard_map/pallas_call | solution.py:344
  29.4 1.2 %collective-permute-done.2.args_0_ = f32[18,3,32,128]{3,2,1,0:T(8,128)S(1)} collective-permute-done((f32[18,3,32,128]{3,2,1,0:T(8,128)S(1)}, f32[18,3,32,128]{3,2,1,0:T(8,128)S(1)}, u32[]{:S(2)}, u32[]{:S(2)}) %collective-permute-start.2) | collective-permute-done | bytes 884768 | tf_op jit(solution)/shard_map/ppermute | solution.py:328
  30.6 0.1 collective-permute-start.3
  30.7 2.0 %shard_map.71 = (f32[16,3,64,128]{3,2,1,0:T(8,128)S(1)}, f32[16,3,64,128]{3,2,1,0:T(8,128)S(1)}, f32[16,3,64,128]{3,2,1,0:T(8,128)S(1)}, f32[16,3,64,128]{3,2,1,...) custom-call(f32[16,3,64,128]{3,2,1,0:T(8,128)S(1)} %get-tuple-elemen, ...), custom_call_target="tpu_custom_call", output_to_operand_aliasing={{0}: (0, {}), {1}: (1, {}), {2}: (2, {}), {3}: (3, {}), {4}... | custom-call | flops 11796480 | bytes 3932160 | tf_op jit(solution)/shard_map/pallas_call | solution.py:344
  32.7 0.0 collective-permute-done.3.args_1_
  32.7 4.0 %shard_map.72 = (f32[16,3,64,128]{3,2,1,0:T(8,128)S(1)}, f32[16,3,64,128]{3,2,1,0:T(8,128)S(1)}, f32[16,3,64,128]{3,2,1,0:T(8,128)S(1)}, f32[16,3,64,128]{3,2,1,...) custom-call(f32[18,3,32,128]{3,2,1,0:T(8,128)S(1)} %collective-permu, ...), custom_call_target="tpu_custom_call", output_to_operand_aliasing={{0}: (2, {}), {1}: (3, {}), {2}: (4, {}), {3}: (5, {}), {4}... | custom-call | flops 11796480 | bytes 3932160 | tf_op jit(solution)/shard_map/pallas_call | solution.py:344
  36.7 0.5 %collective-permute-start.5 = (f32[1,8,16,384]{3,2,1,0:T(8,128)S(1)}, f32[1,8,16,384]{3,2,1,0:T(8,128)S(1)}, u32[]{:S(2)}, u32[]{:S(2)}) collective-permute-start(f32[1,8,16,384]{3,2,1,0:T(8,128)S(1)} %get-tuple-element.135), channel_id=1, source_target_pairs={{0,1},{1,0},{2,3},{3,2},{4,5},{5,4},{6,7},{7,6},{8,9},{9,8},{10,11... | collective-permute-start | bytes 589832 | tf_op jit(solution)/shard_map/ppermute | solution.py:365
  37.2 1.3 %shard_map.73 = (f32[8,64,384]{2,1,0:T(8,128)}, f32[1,8,16,384]{3,2,1,0:T(8,128)S(1)}, f32[1,8,16,384]{3,2,1,0:T(8,128)S(1)}, f32[1,8,16,384]{3,2,1,0:T(8,128)S(1)}) custom-call(f32[3,64,384]{2,1,0:T(8,128)S(1)} %get-tuple-element.106.low, f32[2,64,384]{2,1,0:T(8,128)S(1)} %get-tuple-element.107.mid, f32[3,64,384]{2,1,0:T(8,128)S(1)} %get-tuple-element.125.high, ...), custom_call_target="tpu_custom_call" | custom-call | flops 5898240 | bytes 5898240 | tf_op jit(solution)/shard_map/pallas_call | solution.py:366
  38.6 0.1 collective-permute-start.4
  38.7 0.0 collective-permute-done.5
  38.7 1.6 %collective-permute-start.6 = (f32[8,16,384]{2,1,0:T(8,128)S(1)}, f32[8,16,384]{2,1,0:T(8,128)S(1)}, u32[]{:S(2)}, u32[]{:S(2)}) collective-permute-start(f32[8,16,384]{2,1,0:T(8,128)S(1)} %add_bitcast_fusion), channel_id=1, source_target_pairs={{0,2},{1,3},{2,0},{3,1},{4,6},{5,7},{6,4},{7,5},{8,10},{9,11},{10,... | collective-permute-start | bytes 589832 | tf_op jit(solution)/shard_map/ppermute | solution.py:376
  40.3 0.0 collective-permute-done.4
  40.3 5.8 %collective-permute-done.6 = f32[8,16,384]{2,1,0:T(8,128)S(1)} collective-permute-done((f32[8,16,384]{2,1,0:T(8,128)S(1)}, f32[8,16,384]{2,1,0:T(8,128)S(1)}, u32[]{:S(2)}, u32[]{:S(2)}) %collective-permute-start.6) | collective-permute-done | bytes 196640 | tf_op jit(solution)/shard_map/ppermute | solution.py:376
  46.1 0.7 %bitcast_add_fusion = f32[8,16,384]{2,1,0:T(8,128)} fusion(f32[8,16,384]{2,1,0:T(8,128)S(1)} %collective-permute-done.6, f32[1,8,16,384]{3,2,1,0:T(8,128)S(1)} %get-tuple-element.132, f32[1,8,16,384]{3,2,1,0:T(8,128)S(1)} %collective-permute-done.4), kind=kLoop, calls=%fused_computation | loop fusion | flops 98304 | bytes 786432 | tf_op jit(solution)/shard_map/add | solution.py:381
  (3 shorter events, 0.1 us)
Async XLA Ops:
  0.6 8.2 %copy-start = (f32[8,64,384]{2,1,0:T(8,128)S(1)}, f32[8,64,384]{2,1,0:T(8,128)}, u32[]{:S(2)}) copy-start(f32[8,64,384]{2,1,0:T(8,128)} %p0.3) | copy-start | bytes 2359300
  0.6 8.2 %copy-start.1 = (f32[8,64,384]{2,1,0:T(8,128)S(1)}, f32[8,64,384]{2,1,0:T(8,128)}, u32[]{:S(2)}) copy-start(f32[8,64,384]{2,1,0:T(8,128)} %src.3) | copy-start | bytes 2359300
  0.7 8.2 %copy-start.2 = (f32[8,64,384]{2,1,0:T(8,128)S(1)}, f32[8,64,384]{2,1,0:T(8,128)}, u32[]{:S(2)}) copy-start(f32[8,64,384]{2,1,0:T(8,128)} %obs.3) | copy-start | bytes 2359300
  2.6 23.8 %collective-permute-start = (f32[18,3,32,128]{3,2,1,0:T(8,128)S(1)}, f32[18,3,32,128]{3,2,1,0:T(8,128)S(1)}, u32[]{:S(2)}, u32[]{:S(2)}) collective-permute-start(f32[18,3,32,128]{3,2,1,0:T(8,128)S(1)} %get-tuple-element.69), channel_id=1, source_target_pairs={{0,4},{4,8},{8,12},{1,5},{5,9},{9,13},{2,6},{6,10},{10,14},{3,7},{... | collective-permute-start | bytes 2654216 | tf_op jit(solution)/shard_map/ppermute | solution.py:327
  7.6 23.0 %collective-permute-start.2 = (f32[18,3,32,128]{3,2,1,0:T(8,128)S(1)}, f32[18,3,32,128]{3,2,1,0:T(8,128)S(1)}, u32[]{:S(2)}, u32[]{:S(2)}) collective-permute-start(f32[18,3,32,128]{3,2,1,0:T(8,128)S(1)} %get-tuple-element.103), channel_id=1, source_target_pairs={{4,0},{8,4},{12,8},{5,1},{9,5},{13,9},{6,2},{10,6},{14,10},{7,3},{... | collective-permute-start | bytes 2654216 | tf_op jit(solution)/shard_map/ppermute | solution.py:328
  26.4 1.9 %collective-permute-start.1 = (f32[10,3,32,128]{3,2,1,0:T(8,128)S(1)}, f32[10,3,32,128]{3,2,1,0:T(8,128)S(1)}, u32[]{:S(2)}, u32[]{:S(2)}) collective-permute-start(f32[10,3,32,128]{3,2,1,0:T(8,128)S(1)} %slice.6), channel_id=1, source_target_pairs={{0,1},{1,0},{2,3},{3,2},{4,5},{5,4},{6,7},{7,6},{8,9},{9,8},{10,11... | collective-permute-start | bytes 1474568 | tf_op jit(solution)/shard_map/ppermute | solution.py:358
  30.6 2.1 %collective-permute-start.3 = (f32[10,3,32,128]{3,2,1,0:T(8,128)S(1)}, f32[10,3,32,128]{3,2,1,0:T(8,128)S(1)}, u32[]{:S(2)}, u32[]{:S(2)}) collective-permute-start(f32[10,3,32,128]{3,2,1,0:T(8,128)S(1)} %slice.7), channel_id=1, source_target_pairs={{0,1},{1,0},{2,3},{3,2},{4,5},{5,4},{6,7},{7,6},{8,9},{9,8},{10,11... | collective-permute-start | bytes 1474568 | tf_op jit(solution)/shard_map/ppermute | solution.py:358
  36.7 2.0 %collective-permute-start.5 = (f32[1,8,16,384]{3,2,1,0:T(8,128)S(1)}, f32[1,8,16,384]{3,2,1,0:T(8,128)S(1)}, u32[]{:S(2)}, u32[]{:S(2)}) collective-permute-start(f32[1,8,16,384]{3,2,1,0:T(8,128)S(1)} %get-tuple-element.135), channel_id=1, source_target_pairs={{0,1},{1,0},{2,3},{3,2},{4,5},{5,4},{6,7},{7,6},{8,9},{9,8},{10,11... | collective-permute-start | bytes 589832 | tf_op jit(solution)/shard_map/ppermute | solution.py:365
  38.6 1.7 %collective-permute-start.4 = (f32[1,8,16,384]{3,2,1,0:T(8,128)S(1)}, f32[1,8,16,384]{3,2,1,0:T(8,128)S(1)}, u32[]{:S(2)}, u32[]{:S(2)}) collective-permute-start(f32[1,8,16,384]{3,2,1,0:T(8,128)S(1)} %get-tuple-element.133), channel_id=1, source_target_pairs={{0,1},{1,0},{2,3},{3,2},{4,5},{5,4},{6,7},{7,6},{8,9},{9,8},{10,11... | collective-permute-start | bytes 589832 | tf_op jit(solution)/shard_map/ppermute | solution.py:379
  38.7 7.3 %collective-permute-start.6 = (f32[8,16,384]{2,1,0:T(8,128)S(1)}, f32[8,16,384]{2,1,0:T(8,128)S(1)}, u32[]{:S(2)}, u32[]{:S(2)}) collective-permute-start(f32[8,16,384]{2,1,0:T(8,128)S(1)} %add_bitcast_fusion), channel_id=1, source_target_pairs={{0,2},{1,3},{2,0},{3,1},{4,6},{5,7},{6,4},{7,5},{8,10},{9,11},{10,... | collective-permute-start | bytes 589832 | tf_op jit(solution)/shard_map/ppermute | solution.py:376

commit v5 on v4

--- a/solution.py
+++ b/solution.py
@@ -37,12 +37,22 @@
     return own, [sides[c] + cross(ref, zz, c, r, rows, own[c], sub, zero) for c in range(len(own))]
 
 
-def around_padded(ref, zz, start):
-    own = [ref[zz, c, pl.ds(start, SUB), :] for c in range(ref.shape[1])]
+def around_padded(ref, zz, start, count):
+    sub = lax.broadcasted_iota(jnp.int32, (SUB, LANES), 0)
+    groups = [pl.ds(pl.multiple_of(start + SUB * (q - 1), SUB), SUB) for q in range(count + 2)]
+    tiles = ref.shape[1]
+    own = [[ref[zz, c, g, :] for c in range(tiles)] for g in groups]
+    down = [[pltpu.roll(v, 1, 0) for v in line] for line in own[:-1]]
+    up = [[pltpu.roll(v, SUB - 1, 0) for v in line] for line in own[1:]]
     out = []
-    for c, pair in enumerate(lane_shifts(own)):
-        rest = [ref[zz, c, pl.ds(start + d, SUB), :] for d in (-1, 1)]
-        out.append(pair + tuple(rest) + tuple(ref[zz + d, c, pl.ds(start, SUB), :] for d in (-1, 1)))
+    for q in range(1, count + 1):
+        sides = lane_shifts(own[q])
+        line = []
+        for c in range(tiles):
+            north = jnp.where(sub == 0, down[q - 1][c], down[q][c])
+            south = jnp.where(sub == SUB - 1, up[q][c], up[q - 1][c])
+            line.append(sides[c] + (north, south, ref[zz - 1, c, groups[q], :], ref[zz + 1, c, groups[q], :]))
+        out.append(line)
     return out
 
 
@@ -84,20 +94,25 @@
     def at(r):
         return pl.ds(SUB * r, SUB)
 
-    def first(zz):
-        valid = inside(zz)
+    def coefficients(zz):
+        valid = 0.5 * inside(zz)
         for r in range(rows):
             k, kn = around(K, zz, r, rows)
+            for c in range(tiles):
+                w = [k[c] + v for v in kn[c]]
+                HR[zz, c, at(r), :] = valid / (0.5 + 0.5 * six(w))
+                WL[zz, c, at(r), :] = w[0]
+                WR[zz, c, at(r), :] = w[1]
+
+    def first(zz):
+        for r in range(rows):
             _, pn = around(P0, zz, r, rows)
             for c in range(tiles):
-                w = [k[c] + v for v in kn[c]]
-                rinv = valid / (0.5 + 0.5 * six(w))
-                hr = 0.5 * rinv
+                w = faces(K, WL, WR, zz, c, r, rows)
+                hr = HR[zz, c, at(r), :]
+                rinv = hr + hr
                 sr = SRC[zz, c, at(r), :] * rinv
-                HR[zz, c, at(r), :] = hr
                 SR[zz, c, at(r), :] = sr
-                WL[zz, c, at(r), :] = w[0]
-                WR[zz, c, at(r), :] = w[1]
                 NP0[zz, c, at(r), :] = six(pn[c])
                 P1[zz, c, at(r), :] = sr + weighted(w, pn[c]) * hr
                 U3[zz, c, at(r), :] = OBS[zz, c, at(r), :] * rinv
@@ -133,7 +148,7 @@
                     press(zz)[at(r), pl.ds(c * LANES, LANES)] = p3
                     G[zz, c, at(r), :] = (G[zz, c, at(r), :] + 6.0 * e) + g
 
-    for body, spans in zip((first, second, third), ranges):
+    for body, spans in zip((coefficients, first, second, third), ranges):
         for span in spans:
             lo, hi, *own = span
             lax.fori_loop(lo, hi, lambda zz, _, body=body, own=own: body(zz, *own) or 0, 0)
@@ -207,90 +222,96 @@
 
     lax.fori_loop(HALO, top, clear, 0)
     refs = (K, P0, SRC, OBS, P1, P2, U1, U2, U3, HR, SR, NP0, WL, WR, G, E)
-    ranges = [[(HALO + n, top - n)] for n in (1, 2)] + [[(HALO + 3, top - 3, True)]]
+    ranges = [[(HALO + n, top - n)] for n in (1, 1, 2)] + [[(HALO + 3, top - 3, True)]]
     sweeps(refs, ranges, lambda zz: jnp.float32(1.0), lambda zz: mid.at[zz - HALO - SWEEPS])
 
 
-def side_kernel(low, stages, *args):
-    halos = args[: 2 if 0 in stages else 0]
+def side_kernel(low, stages, parts, *args):
+    halos = args[: len(args) - 2 * FIELDS - (3 in stages) - len(parts) - 1]
     refs = args[len(halos) + FIELDS : len(halos) + 2 * FIELDS]
-    ends = args[len(halos) + 2 * FIELDS :]
+    ends, sems = args[len(halos) + 2 * FIELDS : -1], args[-1]
     K, P0, SRC, OBS = refs[:4]
     nx, depth = K.shape[2], K.shape[0]
     half, top = nx // 2, depth - HALO
     par = lax.axis_index("draw") % 2
 
-    if halos:
-        mine, theirs = halos
-        sems = ends[-1]
-        pairs = [
-            (mine.at[pl.ds(EDGE + h * HALO, HALO)], K.at[pl.ds(0 if low else top, HALO), :, pl.ds(h * half, half)])
-            for h in range(2)
-        ]
-        for half_rows, which in ((mine, par), (theirs, 1 - par)):
+    pairs = []
+    if 0 in stages:
+        for h in range(2):
+            rows = pl.ds(h * half, half)
+            pairs.append((halos[0].at[pl.ds(EDGE + h * HALO, HALO)], K.at[pl.ds(0 if low else top, HALO), :, rows]))
+    if 1 in stages:
+        for half_rows, which in zip(halos[-2:], (par, 1 - par)):
             rows = pl.ds(pl.multiple_of(half * which, half), half)
             first = 0
             for field, width in ((P0, HALO), (SRC, SWEEPS), (OBS, SWEEPS)):
                 planes = pl.ds(HALO - width if low else top, width)
                 pairs.append((half_rows.at[pl.ds(first, width)], field.at[planes, :, rows]))
                 first += width
-        copies = [pltpu.make_async_copy(a, b, sems.at[i]) for i, (a, b) in enumerate(pairs)]
-        for cp in copies:
-            cp.start()
-        for cp in copies:
-            cp.wait()
+    copies = [pltpu.make_async_copy(a, b, sems.at[i]) for i, (a, b) in enumerate(pairs)]
+    for cp in copies:
+        cp.start()
+    for cp in copies:
+        cp.wait()
 
     space, spaces = lax.axis_index("space"), lax.axis_size("space")
     met = jnp.where(space > 0 if low else space + 1 < spaces, 1.0, 0.0).astype(jnp.float32)
     if low:
-        ranges = [[(1, HALO + 1)], [(2, HALO + 2)], [(3, HALO, False), (HALO, HALO + 3, True)]]
-        shift = HALO
+        near, last, shift = (1, HALO + 1), [(3, HALO, False), (HALO, HALO + 3, True)], HALO
+        ranges = [[near], [near], [(2, HALO + 2)], last]
     else:
-        ranges = [[(top - 1, depth - 1)], [(top - 2, depth - 2)], [(top - 3, top, True), (top, depth - 3, False)]]
-        shift = top - 3
+        near, last, shift = (top - 1, depth - 1), [(top - 3, top, True), (top, depth - 3, False)], top - 3
+        ranges = [[near], [near], [(top - 2, depth - 2)], last]
 
     def inside(zz):
         return jnp.where(zz < HALO if low else zz >= top, met, jnp.float32(1.0))
 
     ranges = [spans if n in stages else [] for n, spans in enumerate(ranges)]
     sweeps(refs, ranges, inside, lambda zz: ends[0].at[zz - shift])
-    if not low:
-        gradients(K, P0, refs[6], refs[-2], refs[-1], [(ends[1], 1 - par, 1)])
-
-
-def gradients(K, P0, U1, G, E, parts):
-    tiles, nx, slab = K.shape[1], K.shape[2], K.shape[0] - 2 * HALO
+    gradients(refs, [(out, *part) for out, part in zip(ends[len(ends) - len(parts) :], parts)])
+
+
+def gradients(fields, parts):
+    K, P0, U1, G, E = fields[0], fields[1], fields[6], fields[-2], fields[-1]
+    tiles, nx = K.shape[1], K.shape[2]
     draw, draws = lax.axis_index("draw"), lax.axis_size("draw")
     block, groups = nx // draws, draws // 2
-
-    def plane(z, _):
-        zz = z + HALO
-        for out, parity, first in parts:
+    count = block // SUB
+
+    for out, own, first, z0 in parts:
+        parity = draw % 2 if own else 1 - draw % 2
+
+        def plane(z, _, out=out, first=first, z0=z0, parity=parity):
+            zz = z + z0 + HALO
             for s in range(out.shape[0]):
                 base = (2 * ((draw // 2 + first + s) % groups) + parity) * block
-                for q in range(block // SUB):
-                    start = pl.multiple_of(base + SUB * q, SUB)
-                    v = around_padded(U1, zz, pl.multiple_of(start + SUB, SUB))
-                    w = around_padded(E, zz, pl.multiple_of(start + SUB, SUB))
-                    at = pl.ds(start, SUB)
+                start = pl.multiple_of(base, SUB)
+                v = around_padded(U1, zz, start + SUB, count)
+                w = around_padded(E, zz, start + SUB, count)
+                for q in range(count):
+                    at = pl.ds(pl.multiple_of(start + SUB * q, SUB), SUB)
                     for c in range(tiles):
-                        g = G[zz, c, at, :] + P0[zz, c, at, :] * six(v[c]) + six(w[c])
+                        g = G[zz, c, at, :] + P0[zz, c, at, :] * six(v[q][c]) + six(w[q][c])
                         out[s, z, pl.ds(SUB * q, SUB), pl.ds(c * LANES, LANES)] = 0.5 * K[zz, c, at, :] * g
-        return 0
-
-    lax.fori_loop(0, slab, plane, 0)
-
-
-def rest_kernel(low, mid, high, K, P0, U1, G, E, press, keep_near, keep_far, send_near, sems):
-    slab, nx = press.shape[:2]
-    par = lax.axis_index("draw") % 2
+            return 0
+
+        lax.fori_loop(0, out.shape[1], plane, 0)
+
+
+def far_kernel(z0, *args):
+    gradients(args[:FIELDS], [(args[FIELDS], True, 1, z0)])
+
+
+def rest_kernel(*args):
+    pieces, fields = args[:3], args[3 : 3 + FIELDS]
+    press, keep, sems = args[3 + FIELDS :]
     copies, at = [], 0
-    for ref in (low, mid, high):
+    for ref in pieces:
         copies.append(pltpu.make_async_copy(ref, press.at[pl.ds(at, ref.shape[0])], sems.at[len(copies)]))
         at += ref.shape[0]
     for cp in copies:
         cp.start()
-    gradients(K, P0, U1, G, E, [(keep_far, par, 1), (keep_near, par, 0), (send_near, 1 - par, 0)])
+    gradients(fields, [(keep, True, 0, 0)])
     for cp in copies:
         cp.wait()
 
@@ -310,7 +331,8 @@
     whole = jax.ShapeDtypeStruct((slab, nx, ny), f32)
     mid = jax.ShapeDtypeStruct((slab - 2 * SWEEPS, nx, ny), f32)
     groups = draws // 2
-    near, far = [jax.ShapeDtypeStruct((n, slab, nx // draws, ny), f32) for n in (1, groups - 1)]
+    cut = slab // 2
+    near = jax.ShapeDtypeStruct((1, slab, nx // draws, ny), f32)
     params = pltpu.CompilerParams(vmem_limit_bytes=8 * 2**20)
     cells = slab * nx * ny
 
@@ -337,48 +359,82 @@
     )(K, start_pressure, source, observe)
     fields, centre = (K, *state[:-1]), state[-1]
 
-    def side(low, stages, halos, fields):
-        ends = (jax.ShapeDtypeStruct((SWEEPS, nx, ny), f32),) if 2 in stages else ()
-        ends = ends if low else (*ends, far)
+    def blocks(count, planes):
+        return jax.ShapeDtypeStruct((count, planes, nx // draws, ny), f32)
+
+    def side(low, stages, halos, fields, parts=()):
+        ends = (jax.ShapeDtypeStruct((SWEEPS, nx, ny), f32),) if 3 in stages else ()
+        ends += tuple(blocks(groups - 1 if first else 1, planes) for _, first, _, planes in parts)
         n = len(halos)
         out = pl.pallas_call(
-            functools.partial(side_kernel, low, stages),
+            functools.partial(side_kernel, low, stages, [part[:-1] for part in parts]),
             out_shape=(*kinds, *ends),
             in_specs=[ONCHIP] * (n + FIELDS),
             out_specs=(ONCHIP,) * (FIELDS + len(ends)),
-            scratch_shapes=[pltpu.SemaphoreType.DMA((8,))] if n else [],
+            scratch_shapes=[pltpu.SemaphoreType.DMA((8,))],
             input_output_aliases={n + i: i for i in range(FIELDS)},
             compiler_params=params,
-            cost_estimate=pl.CostEstimate(flops=60 * cells, bytes_accessed=20 * cells, transcendentals=0),
+            cost_estimate=pl.CostEstimate(flops=30 * len(stages) * cells, bytes_accessed=10 * cells, transcendentals=0),
         )(*halos, *fields)
         return out[:FIELDS], *out[FIELDS:]
 
     def swapped(got, fields):
         got, last = lax.optimization_barrier((got, fields[-1]))
-        return (got, lax.ppermute(got[:EDGE], "draw", pair)), (*fields[:-1], last)
-
-    halos, fields = swapped(alo, fields)
-    (fields,) = side(True, (0,), halos, fields)
-    halos, fields = swapped(ahi, fields)
-    fields, low = side(True, (1, 2), (), fields)
-    fields, high, send_far = side(False, (0, 1, 2), halos, fields)
-    got_far = lax.ppermute(send_far, "draw", pair)
-    press, keep_near, keep_far, send_near = pl.pallas_call(
+        return got, lax.ppermute(got[:EDGE], "draw", pair), (*fields[:-1], last)
+
+    def onward(keep, got):
+        return [
+            lax.ppermute(keep[s - 1] + got[s - 1], "draw", [(j, (j + 2 * s) % draws) for j in range(draws)])
+            for s in range(1, groups)
+        ]
+
+    def swap(send):
+        return lax.ppermute(send, "draw", pair)
+
+    def keep_far(z0, planes, fields):
+        return pl.pallas_call(
+            functools.partial(far_kernel, z0),
+            out_shape=blocks(groups - 1, planes),
+            in_specs=[ONCHIP] * FIELDS,
+            out_specs=ONCHIP,
+            compiler_params=params,
+            cost_estimate=pl.CostEstimate(flops=10 * cells, bytes_accessed=10 * cells, transcendentals=0),
+        )(*fields)
+
+    mine, theirs, fields = swapped(alo, fields)
+    (fields,) = side(True, (0,), (mine,), fields)
+    (fields,) = side(True, (1,), (mine, theirs), fields)
+    mine, theirs, fields = swapped(ahi, fields)
+    parts = [(False, 1, 0, cut), (False, 0, 0, cut), (True, 1, 0, cut)]
+    fields, low, send_far, send_near, keep = side(True, (2, 3), (), fields, parts)
+    got_far, near_low = swap(send_far), swap(send_near)
+    (fields,) = side(False, (0, 1), (mine, mine, theirs), fields)
+    got_far, last = lax.optimization_barrier((got_far, fields[-1]))
+    moved_low = onward(keep, got_far)
+    parts = [(False, 1, cut, cut // 2), (False, 1, cut + cut // 2, slab - cut - cut // 2), (False, 0, cut, slab - cut)]
+    fields, high, *send_far, send_near = side(False, (2, 3), (), (*fields[:-1], last), parts)
+    got_far, near_high = [swap(a) for a in send_far], swap(send_near)
+    moved_low, last = lax.optimization_barrier((moved_low, fields[-1]))
+    fields = (*fields[:-1], last)
+    keep = keep_far(cut, slab - cut, fields)
+    sums = [keep[s - 1] + jnp.concatenate([a[s - 1] for a in got_far], axis=0) for s in range(1, groups)]
+    sums, last = lax.optimization_barrier((sums, fields[-1]))
+    fields = (*fields[:-1], last)
+    moved_high = [
+        lax.ppermute(a, "draw", [(j, (j + 2 * s) % draws) for j in range(draws)]) for s, a in enumerate(sums, 1)
+    ]
+    press, keep = pl.pallas_call(
         rest_kernel,
-        out_shape=(whole, near, far, near),
-        in_specs=[ONCHIP] * 8,
-        out_specs=(OFFCHIP,) + (ONCHIP,) * 3,
+        out_shape=(whole, near),
+        in_specs=[ONCHIP] * (3 + FIELDS),
+        out_specs=(OFFCHIP, ONCHIP),
         scratch_shapes=[pltpu.SemaphoreType.DMA((3,))],
         compiler_params=params,
         cost_estimate=pl.CostEstimate(flops=30 * cells, bytes_accessed=30 * cells, transcendentals=0),
-    )(low, centre, high, fields[0], fields[1], fields[6], fields[14], fields[15])
-    moved = [
-        lax.ppermute(keep_far[s - 1] + got_far[s - 1], "draw", [(j, (j + 2 * s) % draws) for j in range(draws)])
-        for s in range(1, groups)
-    ]
-    total = keep_near[0] + lax.ppermute(send_near, "draw", pair)[0]
-    for part_sum in moved:
-        total = total + part_sum
+    )(low, centre, high, *fields)
+    total = keep[0] + jnp.concatenate([near_low[0], near_high[0]], axis=0)
+    for a, b in zip(moved_low, moved_high):
+        total = total + jnp.concatenate([a, b], axis=0)
     return press[None], total
 
 

time: 47 us -> 47.9 us (1.019)
  waiting for transfers between devices: 23.3 us -> 19.9 us
  Pallas kernels: 13.2 us -> 15.7 us
  starting transfers between devices: 8.62 us -> 10.4 us
    ppermute x5 -> x9, waiting for transfers between devices: 7.63 us -> 4.4 us  [the longest x1 3.24 us: local(): lax.ppermute(a, 'draw', [(j, (j + 2 * s) % draws) for j in range(draws)])]
    pallas_call x4 -> x7, Pallas kernels: 8.38 us -> 10.4 us  [the longest x5 9.04 us: side(): pl.pallas_call(functools.partial(side_kernel, low, stages, [part[:-1] for...]
    ppermute x5 -> x9, starting transfers between devices: 2.35 us -> 4.16 us  [the longest x5 1.6 us: swap(): return lax.ppermute(send, 'draw', pair)]
    ppermute x1, waiting for transfers between devices: 14.5 us -> 14.1 us  [local(): alo = lax.ppermute(to_up, 'space', up)]
    pallas_call x1, Pallas kernels: 2.95 us -> 3.43 us  [local(): pl.pallas_call(inner_kernel, out_shape=(*kinds[1:], mid), in_specs=[ONCHI...]
  transfers between devices with their start and end apart: 7 -> 11, of which waited for: 4 -> 4; matrix products, arithmetic and copies ran while one was open for 0% -> 0% of each run, Pallas kernels for 16% -> 29%
where the time goes in v5:
time: 47.9 us; the launch traced here: 47.7 us
  waiting for transfers between devices  19.9 us (42%)
  Pallas kernels  15.7 us (33%)
  starting transfers between devices  10.4 us (22%)
  between operations  0.86 us (2%)
  other arithmetic  0.73 us (2%)
    ppermute x1, waiting for transfers between devices, local(): alo = lax.ppermute(to_up, 'space', up)  14.1 us
    pallas_call x5, Pallas kernels, side(): pl.pallas_call(functools.partial(side_kernel, low, stages, [part[:-1] for...  9.04 us
    ppermute x1, starting transfers between devices, local(): alo = lax.ppermute(to_up, 'space', up)  4.98 us
    pallas_call x1, Pallas kernels, local(): pl.pallas_call(inner_kernel, out_shape=(*kinds[1:], mid), in_specs=[ONCHI...  3.43 us
    ppermute x1, waiting for transfers between devices, local(): lax.ppermute(a, 'draw', [(j, (j + 2 * s) % draws) for j in range(draws)])  3.24 us
    pallas_call x1, Pallas kernels, local(): pl.pallas_call(first_kernel, out_shape=(field, edge, edge), in_specs=[OFF...  1.91 us
    ppermute x5, starting transfers between devices, swap(): return lax.ppermute(send, 'draw', pair)  1.6 us
    ppermute x1, starting transfers between devices, onward(): lax.ppermute(keep[s - 1] + got[s - 1], 'draw', [(j, (j + 2 * s) % draws)...  1.56 us
  transfers between devices with their start and end apart: 11, of which 4 were waited for; matrix products, arithmetic and copies ran while one was open for 0% of the time, Pallas kernels for 29%

profile of v5, /device:TPU:0, one launch (start us, length us, event | category | flops | bytes accessed | tf_op | source)
XLA Modules:
  0.0 47.7 jit_solution(8167420979304421065)
XLA Ops:
  0.6 0.0 copy-start
  0.6 0.0 copy-start.1
  0.7 0.0 copy-start.2
  0.7 1.9 %shard_map.68 = (f32[16,3,64,128]{3,2,1,0:T(8,128)S(1)}, f32[18,3,32,128]{3,2,1,0:T(8,128)S(1)}, f32[18,3,32,128]{3,2,1,0:T(8,128)S(1)}) custom-call(f32[8,64,384]{2,1,0:T(8,128)} %log_perm.1, f32[8,64,384]{2,1,0:T(8,128)} %bitcast.12, f32[8,64,384]{2,1,0:T(8,128)} %p0.3, f32[8,64,384]{2,1,0:T(8,128)} %src.3, f32[8,64,384]{2,1,0:T(8,128)} %obs.3), custom_call_target="tpu_custom_call" | custom-call | flops 196608 | bytes 3932160 | tf_op jit(solution)/shard_map/pallas_call | solution.py:340
  2.6 5.0 %collective-permute-start = (f32[18,3,32,128]{3,2,1,0:T(8,128)S(1)}, f32[18,3,32,128]{3,2,1,0:T(8,128)S(1)}, u32[]{:S(2)}, u32[]{:S(2)}) collective-permute-start(f32[18,3,32,128]{3,2,1,0:T(8,128)S(1)} %get-tuple-element.121), channel_id=1, source_target_pairs={{0,4},{4,8},{8,12},{1,5},{5,9},{9,13},{2,6},{6,10},{10,14},{3,7},{... | collective-permute-start | bytes 2654216 | tf_op jit(solution)/shard_map/ppermute | solution.py:349
  7.6 1.3 %collective-permute-start.2 = (f32[18,3,32,128]{3,2,1,0:T(8,128)S(1)}, f32[18,3,32,128]{3,2,1,0:T(8,128)S(1)}, u32[]{:S(2)}, u32[]{:S(2)}) collective-permute-start(f32[18,3,32,128]{3,2,1,0:T(8,128)S(1)} %get-tuple-element.171), channel_id=1, source_target_pairs={{4,0},{8,4},{12,8},{5,1},{9,5},{13,9},{6,2},{10,6},{14,10},{7,3},{... | collective-permute-start | bytes 2654216 | tf_op jit(solution)/shard_map/ppermute | solution.py:350
  8.9 0.0 copy-done
  8.9 0.0 copy-done.1
  8.9 0.0 copy-done.2
  8.9 3.4 %shard_map.69 = (f32[16,3,64,128]{3,2,1,0:T(8,128)S(1)}, f32[16,3,64,128]{3,2,1,0:T(8,128)S(1)}, f32[16,3,64,128]{3,2,1,0:T(8,128)S(1)}, f32[16,3,64,128]{3,2,1,...) custom-call(f32[16,3,64,128]{3,2,1,0:T(8,128)S(1)} %get-tuple-elemen, ...), custom_call_target="tpu_custom_call" | custom-call | flops 39321600 | bytes 11796480 | tf_op jit(solution)/shard_map/pallas_call | solution.py:351
  12.3 14.1 %collective-permute-done.args_0_ = f32[18,3,32,128]{3,2,1,0:T(8,128)S(1)} collective-permute-done((f32[18,3,32,128]{3,2,1,0:T(8,128)S(1)}, f32[18,3,32,128]{3,2,1,0:T(8,128)S(1)}, u32[]{:S(2)}, u32[]{:S(2)}) %collective-permute-start) | collective-permute-done | bytes 884768 | tf_op jit(solution)/shard_map/ppermute | solution.py:349
  26.4 0.1 collective-permute-start.1
  26.5 0.7 %shard_map.70 = (f32[16,3,64,128]{3,2,1,0:T(8,128)S(1)}, f32[16,3,64,128]{3,2,1,0:T(8,128)S(1)}, f32[16,3,64,128]{3,2,1,0:T(8,128)S(1)}, f32[16,3,64,128]{3,2,1,...) custom-call(f32[18,3,32,128]{3,2,1,0:T(8,128)S(1)} %collective-permu, ...), custom_call_target="tpu_custom_call", output_to_operand_aliasing={{0}: (1, {}), {1}: (2, {}), {2}: (3, {}), {3}: (4, {}), {4}... | custom-call | flops 5898240 | bytes 1966080 | tf_op jit(solution)/shard_map/pallas_call | solution.py:369
  27.2 1.1 %collective-permute-done.1.args_1_ = f32[10,3,32,128]{3,2,1,0:T(8,128)S(1)} collective-permute-done((f32[10,3,32,128]{3,2,1,0:T(8,128)S(1)}, f32[10,3,32,128]{3,2,1,0:T(8,128)S(1)}, u32[]{:S(2)}, u32[]{:S(2)}) %collective-permute-start.1) | collective-permute-done | bytes 491552 | tf_op jit(solution)/shard_map/ppermute | solution.py:383
  28.4 0.8 %shard_map.71 = (f32[16,3,64,128]{3,2,1,0:T(8,128)S(1)}, f32[16,3,64,128]{3,2,1,0:T(8,128)S(1)}, f32[16,3,64,128]{3,2,1,0:T(8,128)S(1)}, f32[16,3,64,128]{3,2,1,...) custom-call(f32[18,3,32,128]{3,2,1,0:T(8,128)S(1)} %collective-permu, ...), custom_call_target="tpu_custom_call", output_to_operand_aliasing={{0}: (2, {}), {1}: (3, {}), {2}: (4, {}), {3}: (5, {}), {4}... | custom-call | flops 5898240 | bytes 1966080 | tf_op jit(solution)/shard_map/pallas_call | solution.py:369
  29.1 1.4 %collective-permute-done.2.args_0_.args_1_ = f32[18,3,32,128]{3,2,1,0:T(8,128)S(1)} collective-permute-done((f32[18,3,32,128]{3,2,1,0:T(8,128)S(1)}, f32[18,3,32,128]{3,2,1,0:T(8,128)S(1)}, u32[]{:S(2)}, u32[]{:S(2)}) %collective-permute-start.2) | collective-permute-done | bytes 884768 | tf_op jit(solution)/shard_map/ppermute | solution.py:350
  30.6 0.1 collective-permute-start.3
  30.7 3.3 %shard_map.72 = (f32[16,3,64,128]{3,2,1,0:T(8,128)S(1)}, f32[16,3,64,128]{3,2,1,0:T(8,128)S(1)}, f32[16,3,64,128]{3,2,1,0:T(8,128)S(1)}, f32[16,3,64,128]{3,2,1,...) custom-call(f32[16,3,64,128]{3,2,1,0:T(8,128)S(1)} %get-tuple-elemen, ...), custom_call_target="tpu_custom_call", output_to_operand_aliasing={{0}: (0, {}), {1}: (1, {}), {2}: (2, {}), {3}: (3, {}), {4}... | custom-call | flops 11796480 | bytes 1966080 | tf_op jit(solution)/shard_map/pallas_call | solution.py:369
  34.0 0.5 %collective-permute-start.4 = (f32[1,4,16,384]{3,2,1,0:T(8,128)S(1)}, f32[1,4,16,384]{3,2,1,0:T(8,128)S(1)}, u32[]{:S(2)}, u32[]{:S(2)}) collective-permute-start(f32[1,4,16,384]{3,2,1,0:T(8,128)S(1)} %get-tuple-element.208), channel_id=1, source_target_pairs={{0,1},{1,0},{2,3},{3,2},{4,5},{5,4},{6,7},{7,6},{8,9},{9,8},{10,11... | collective-permute-start | bytes 294920 | tf_op jit(solution)/shard_map/ppermute | solution.py:392
  34.6 0.0 collective-permute-done.3.args_2_
  34.6 1.4 %shard_map.73 = (f32[16,3,64,128]{3,2,1,0:T(8,128)S(1)}, f32[16,3,64,128]{3,2,1,0:T(8,128)S(1)}, f32[16,3,64,128]{3,2,1,0:T(8,128)S(1)}, f32[16,3,64,128]{3,2,1,...) custom-call(f32[18,3,32,128]{3,2,1,0:T(8,128)S(1)} %collective-permu, ...), custom_call_target="tpu_custom_call", output_to_operand_aliasing={{0}: (3, {}), {1}: (4, {}), {2}: (5, {}), {3}: (6, {}), {4}... | custom-call | flops 11796480 | bytes 1966080 | tf_op jit(solution)/shard_map/pallas_call | solution.py:369
  35.9 0.0 collective-permute-done.4
  36.0 1.6 %collective-permute-start.5 = (f32[4,16,384]{2,1,0:T(8,128)S(1)}, f32[4,16,384]{2,1,0:T(8,128)S(1)}, u32[]{:S(2)}, u32[]{:S(2)}) collective-permute-start(f32[4,16,384]{2,1,0:T(8,128)S(1)} %add_bitcast_fusion), channel_id=1, source_target_pairs={{0,2},{1,3},{2,0},{3,1},{4,6},{5,7},{6,4},{7,5},{8,10},{9,11},{10,... | collective-permute-start | bytes 294920 | tf_op jit(solution)/shard_map/ppermute | solution.py:387
  37.5 2.9 %shard_map.74 = (f32[16,3,64,128]{3,2,1,0:T(8,128)S(1)}, f32[16,3,64,128]{3,2,1,0:T(8,128)S(1)}, f32[16,3,64,128]{3,2,1,0:T(8,128)S(1)}, f32[16,3,64,128]{3,2,1,...) custom-call(f32[16,3,64,128]{3,2,1,0:T(8,128)S(1)} %get-tuple-elemen, ...), custom_call_target="tpu_custom_call", output_to_operand_aliasing={{0}: (0, {}), {1}: (1, {}), {2}: (2, {}), {3}: (3, {}), {4}... | custom-call | flops 11796480 | bytes 1966080 | tf_op jit(solution)/shard_map/pallas_call | solution.py:369
  40.4 0.1 collective-permute-start.6
  40.5 0.5 %collective-permute-start.7 = (f32[1,2,16,384]{3,2,1,0:T(8,128)S(1)}, f32[1,2,16,384]{3,2,1,0:T(8,128)S(1)}, u32[]{:S(2)}, u32[]{:S(2)}) collective-permute-start(f32[1,2,16,384]{3,2,1,0:T(8,128)S(1)} %get-tuple-element.232), channel_id=1, source_target_pairs={{0,1},{1,0},{2,3},{3,2},{4,5},{5,4},{6,7},{7,6},{8,9},{9,8},{10,11... | collective-permute-start | bytes 147464 | tf_op jit(solution)/shard_map/ppermute | solution.py:392
  41.0 0.1 collective-permute-start.8
  41.1 0.4 collective-permute-start.9
  41.5 0.0 collective-permute-done.5
  41.5 0.4 shard_map.75
  41.9 0.0 collective-permute-done.6
  41.9 0.0 collective-permute-done.7
  42.0 0.9 %collective-permute-start.10 = (f32[4,16,384]{2,1,0:T(8,128)S(1)}, f32[4,16,384]{2,1,0:T(8,128)S(1)}, u32[]{:S(2)}, u32[]{:S(2)}) collective-permute-start(f32[4,16,384]{2,1,0:T(8,128)S(1)} %maximum_add_fusion.1), channel_id=1, source_target_pairs={{0,2},{1,3},{2,0},{3,1},{4,6},{5,7},{6,4},{7,5},{8,10},{9,11},{10,... | collective-permute-start | bytes 294920 | tf_op jit(solution)/shard_map/ppermute | solution.py:424
  42.8 0.9 %shard_map.76 = (f32[8,64,384]{2,1,0:T(8,128)}, f32[1,8,16,384]{3,2,1,0:T(8,128)S(1)}) custom-call(f32[3,64,384]{2,1,0:T(8,128)S(1)} %get-tuple-element.174.args_0_, f32[2,64,384]{2,1,0:T(8,128)S(1)} %get-tuple-element.175.args_1_, f32[3,64,384]{2,1,0:T(8,128)S(1)} %get-tuple-element.211.args_2_, f32[16,3,64,128]{3,2,1,0:T(8,128)S(1)} %get-tuple-element.212.args_0_.args_3_, ...), custom_call_target="tpu_custom_call" | custom-call | flops 5898240 | bytes 5898240 | tf_op jit(solution)/shard_map/pallas_call | solution.py:426
  43.7 0.0 collective-permute-done.8
  43.7 0.0 collective-permute-done.9
  43.7 3.2 %collective-permute-done.10 = f32[4,16,384]{2,1,0:T(8,128)S(1)} collective-permute-done((f32[4,16,384]{2,1,0:T(8,128)S(1)}, f32[4,16,384]{2,1,0:T(8,128)S(1)}, u32[]{:S(2)}, u32[]{:S(2)}) %collective-permute-start.10) | collective-permute-done | bytes 98336 | tf_op jit(solution)/shard_map/ppermute | solution.py:424
  47.0 0.7 %fusion = f32[8,16,384]{2,1,0:T(8,128)} fusion(f32[4,16,384]{2,1,0:T(8,128)S(1)} %bitcast.14, f32[4,16,384]{2,1,0:T(8,128)S(1)} %bitcast.13, f32[4,16,384]{2,1,0:T(8,128)S(1)} %collective-permute-done.10, f32[4,16,384]{2,1,0:T(8,128)S(1)} %collective-permute-done.5, f32[1,8,16,384]{3,2,1,0:T(8,128)S(1)} %get-tuple-element.235), kind=kLoop, calls=%fused_computation.1 | loop fusion | flops 196608 | bytes 786432 | tf_op jit(solution)/shard_map/add | solution.py:437
  (4 shorter events, 0.1 us)
Async XLA Ops:
  0.6 8.2 %copy-start = (f32[8,64,384]{2,1,0:T(8,128)S(1)}, f32[8,64,384]{2,1,0:T(8,128)}, u32[]{:S(2)}) copy-start(f32[8,64,384]{2,1,0:T(8,128)} %p0.3) | copy-start | bytes 2359300
  0.6 8.2 %copy-start.1 = (f32[8,64,384]{2,1,0:T(8,128)S(1)}, f32[8,64,384]{2,1,0:T(8,128)}, u32[]{:S(2)}) copy-start(f32[8,64,384]{2,1,0:T(8,128)} %src.3) | copy-start | bytes 2359300
  0.7 8.2 %copy-start.2 = (f32[8,64,384]{2,1,0:T(8,128)S(1)}, f32[8,64,384]{2,1,0:T(8,128)}, u32[]{:S(2)}) copy-start(f32[8,64,384]{2,1,0:T(8,128)} %obs.3) | copy-start | bytes 2359300
  2.6 23.8 %collective-permute-start = (f32[18,3,32,128]{3,2,1,0:T(8,128)S(1)}, f32[18,3,32,128]{3,2,1,0:T(8,128)S(1)}, u32[]{:S(2)}, u32[]{:S(2)}) collective-permute-start(f32[18,3,32,128]{3,2,1,0:T(8,128)S(1)} %get-tuple-element.121), channel_id=1, source_target_pairs={{0,4},{4,8},{8,12},{1,5},{5,9},{9,13},{2,6},{6,10},{10,14},{3,7},{... | collective-permute-start | bytes 2654216 | tf_op jit(solution)/shard_map/ppermute | solution.py:349
  7.6 23.0 %collective-permute-start.2 = (f32[18,3,32,128]{3,2,1,0:T(8,128)S(1)}, f32[18,3,32,128]{3,2,1,0:T(8,128)S(1)}, u32[]{:S(2)}, u32[]{:S(2)}) collective-permute-start(f32[18,3,32,128]{3,2,1,0:T(8,128)S(1)} %get-tuple-element.171), channel_id=1, source_target_pairs={{4,0},{8,4},{12,8},{5,1},{9,5},{13,9},{6,2},{10,6},{14,10},{7,3},{... | collective-permute-start | bytes 2654216 | tf_op jit(solution)/shard_map/ppermute | solution.py:350
  26.4 1.9 %collective-permute-start.1 = (f32[10,3,32,128]{3,2,1,0:T(8,128)S(1)}, f32[10,3,32,128]{3,2,1,0:T(8,128)S(1)}, u32[]{:S(2)}, u32[]{:S(2)}) collective-permute-start(f32[10,3,32,128]{3,2,1,0:T(8,128)S(1)} %slice.6), channel_id=1, source_target_pairs={{0,1},{1,0},{2,3},{3,2},{4,5},{5,4},{6,7},{7,6},{8,9},{9,8},{10,11... | collective-permute-start | bytes 1474568 | tf_op jit(solution)/shard_map/ppermute | solution.py:383
  30.6 3.9 %collective-permute-start.3 = (f32[10,3,32,128]{3,2,1,0:T(8,128)S(1)}, f32[10,3,32,128]{3,2,1,0:T(8,128)S(1)}, u32[]{:S(2)}, u32[]{:S(2)}) collective-permute-start(f32[10,3,32,128]{3,2,1,0:T(8,128)S(1)} %slice.7), channel_id=1, source_target_pairs={{0,1},{1,0},{2,3},{3,2},{4,5},{5,4},{6,7},{7,6},{8,9},{9,8},{10,11... | collective-permute-start | bytes 1474568 | tf_op jit(solution)/shard_map/ppermute | solution.py:383
  34.0 1.9 %collective-permute-start.4 = (f32[1,4,16,384]{3,2,1,0:T(8,128)S(1)}, f32[1,4,16,384]{3,2,1,0:T(8,128)S(1)}, u32[]{:S(2)}, u32[]{:S(2)}) collective-permute-start(f32[1,4,16,384]{3,2,1,0:T(8,128)S(1)} %get-tuple-element.208), channel_id=1, source_target_pairs={{0,1},{1,0},{2,3},{3,2},{4,5},{5,4},{6,7},{7,6},{8,9},{9,8},{10,11... | collective-permute-start | bytes 294920 | tf_op jit(solution)/shard_map/ppermute | solution.py:392
  36.0 5.5 %collective-permute-start.5 = (f32[4,16,384]{2,1,0:T(8,128)S(1)}, f32[4,16,384]{2,1,0:T(8,128)S(1)}, u32[]{:S(2)}, u32[]{:S(2)}) collective-permute-start(f32[4,16,384]{2,1,0:T(8,128)S(1)} %add_bitcast_fusion), channel_id=1, source_target_pairs={{0,2},{1,3},{2,0},{3,1},{4,6},{5,7},{6,4},{7,5},{8,10},{9,11},{10,... | collective-permute-start | bytes 294920 | tf_op jit(solution)/shard_map/ppermute | solution.py:387
  40.4 1.5 %collective-permute-start.6 = (f32[1,2,16,384]{3,2,1,0:T(8,128)S(1)}, f32[1,2,16,384]{3,2,1,0:T(8,128)S(1)}, u32[]{:S(2)}, u32[]{:S(2)}) collective-permute-start(f32[1,2,16,384]{3,2,1,0:T(8,128)S(1)} %get-tuple-element.231), channel_id=1, source_target_pairs={{0,1},{1,0},{2,3},{3,2},{4,5},{5,4},{6,7},{7,6},{8,9},{9,8},{10,11... | collective-permute-start | bytes 147464 | tf_op jit(solution)/shard_map/ppermute | solution.py:392
  40.5 1.4 %collective-permute-start.7 = (f32[1,2,16,384]{3,2,1,0:T(8,128)S(1)}, f32[1,2,16,384]{3,2,1,0:T(8,128)S(1)}, u32[]{:S(2)}, u32[]{:S(2)}) collective-permute-start(f32[1,2,16,384]{3,2,1,0:T(8,128)S(1)} %get-tuple-element.232), channel_id=1, source_target_pairs={{0,1},{1,0},{2,3},{3,2},{4,5},{5,4},{6,7},{7,6},{8,9},{9,8},{10,11... | collective-permute-start | bytes 147464 | tf_op jit(solution)/shard_map/ppermute | solution.py:392
  41.0 2.8 %collective-permute-start.8 = (f32[1,4,16,384]{3,2,1,0:T(8,128)S(1)}, f32[1,4,16,384]{3,2,1,0:T(8,128)S(1)}, u32[]{:S(2)}, u32[]{:S(2)}) collective-permute-start(f32[1,4,16,384]{3,2,1,0:T(8,128)S(1)} %get-tuple-element.236), channel_id=1, source_target_pairs={{0,1},{1,0},{2,3},{3,2},{4,5},{5,4},{6,7},{7,6},{8,9},{9,8},{10,11... | collective-permute-start | bytes 294920 | tf_op jit(solution)/shard_map/ppermute | solution.py:392
  41.1 2.7 %collective-permute-start.9 = (f32[1,4,16,384]{3,2,1,0:T(8,128)S(1)}, f32[1,4,16,384]{3,2,1,0:T(8,128)S(1)}, u32[]{:S(2)}, u32[]{:S(2)}) collective-permute-start(f32[1,4,16,384]{3,2,1,0:T(8,128)S(1)} %get-tuple-element.237), channel_id=1, source_target_pairs={{0,1},{1,0},{2,3},{3,2},{4,5},{5,4},{6,7},{7,6},{8,9},{9,8},{10,11... | collective-permute-start | bytes 294920 | tf_op jit(solution)/shard_map/ppermute | solution.py:392
  42.0 5.0 %collective-permute-start.10 = (f32[4,16,384]{2,1,0:T(8,128)S(1)}, f32[4,16,384]{2,1,0:T(8,128)S(1)}, u32[]{:S(2)}, u32[]{:S(2)}) collective-permute-start(f32[4,16,384]{2,1,0:T(8,128)S(1)} %maximum_add_fusion.1), channel_id=1, source_target_pairs={{0,2},{1,3},{2,0},{3,1},{4,6},{5,7},{6,4},{7,5},{8,10},{9,11},{10,... | collective-permute-start | bytes 294920 | tf_op jit(solution)/shard_map/ppermute | solution.py:424

commit v6 on v5

--- a/solution.py
+++ b/solution.py
@@ -117,6 +117,24 @@
                 P1[zz, c, at(r), :] = sr + weighted(w, pn[c]) * hr
                 U3[zz, c, at(r), :] = OBS[zz, c, at(r), :] * rinv
 
+    def combined(zz):
+        valid = inside(zz)
+        for r in range(rows):
+            k, kn = around(K, zz, r, rows)
+            _, pn = around(P0, zz, r, rows)
+            for c in range(tiles):
+                w = [k[c] + v for v in kn[c]]
+                rinv = valid / (0.5 + 0.5 * six(w))
+                hr = 0.5 * rinv
+                sr = SRC[zz, c, at(r), :] * rinv
+                HR[zz, c, at(r), :] = hr
+                SR[zz, c, at(r), :] = sr
+                WL[zz, c, at(r), :] = w[0]
+                WR[zz, c, at(r), :] = w[1]
+                NP0[zz, c, at(r), :] = six(pn[c])
+                P1[zz, c, at(r), :] = sr + weighted(w, pn[c]) * hr
+                U3[zz, c, at(r), :] = OBS[zz, c, at(r), :] * rinv
+
     def second(zz):
         for r in range(rows):
             _, a = around(P1, zz, r, rows)
@@ -148,7 +166,10 @@
                     press(zz)[at(r), pl.ds(c * LANES, LANES)] = p3
                     G[zz, c, at(r), :] = (G[zz, c, at(r), :] + 6.0 * e) + g
 
-    for body, spans in zip((coefficients, first, second, third), ranges):
+    stages = [coefficients, first, second, third]
+    if ranges[0] and ranges[0] == ranges[1]:
+        stages, ranges = [combined, second, third], ranges[1:]
+    for body, spans in zip(stages, ranges):
         for span in spans:
             lo, hi, *own = span
             lax.fori_loop(lo, hi, lambda zz, _, body=body, own=own: body(zz, *own) or 0, 0)
@@ -280,12 +301,11 @@
 
     for out, own, first, z0 in parts:
         parity = draw % 2 if own else 1 - draw % 2
-
-        def plane(z, _, out=out, first=first, z0=z0, parity=parity):
-            zz = z + z0 + HALO
-            for s in range(out.shape[0]):
-                base = (2 * ((draw // 2 + first + s) % groups) + parity) * block
-                start = pl.multiple_of(base, SUB)
+        for s in range(out.shape[0]):
+            base = (2 * ((draw // 2 + first + s) % groups) + parity) * block
+            start = pl.multiple_of(base, SUB)
+            for z in range(out.shape[1]):
+                zz = z + z0 + HALO
                 v = around_padded(U1, zz, start + SUB, count)
                 w = around_padded(E, zz, start + SUB, count)
                 for q in range(count):
@@ -293,9 +313,6 @@
                     for c in range(tiles):
                         g = G[zz, c, at, :] + P0[zz, c, at, :] * six(v[q][c]) + six(w[q][c])
                         out[s, z, pl.ds(SUB * q, SUB), pl.ds(c * LANES, LANES)] = 0.5 * K[zz, c, at, :] * g
-            return 0
-
-        lax.fori_loop(0, out.shape[1], plane, 0)
 
 
 def far_kernel(z0, *args):
@@ -404,20 +421,21 @@
     mine, theirs, fields = swapped(alo, fields)
     (fields,) = side(True, (0,), (mine,), fields)
     (fields,) = side(True, (1,), (mine, theirs), fields)
+    (fields,) = side(True, (2,), (), fields)
     mine, theirs, fields = swapped(ahi, fields)
     parts = [(False, 1, 0, cut), (False, 0, 0, cut), (True, 1, 0, cut)]
-    fields, low, send_far, send_near, keep = side(True, (2, 3), (), fields, parts)
+    fields, low, send_far, send_near, keep = side(True, (3,), (), fields, parts)
     got_far, near_low = swap(send_far), swap(send_near)
     (fields,) = side(False, (0, 1), (mine, mine, theirs), fields)
-    got_far, last = lax.optimization_barrier((got_far, fields[-1]))
+    got_far, near_low, last = lax.optimization_barrier((got_far, near_low, fields[-1]))
     moved_low = onward(keep, got_far)
-    parts = [(False, 1, cut, cut // 2), (False, 1, cut + cut // 2, slab - cut - cut // 2), (False, 0, cut, slab - cut)]
-    fields, high, *send_far, send_near = side(False, (2, 3), (), (*fields[:-1], last), parts)
-    got_far, near_high = [swap(a) for a in send_far], swap(send_near)
+    parts = [(False, 1, cut, slab - cut), (False, 0, cut, slab - cut)]
+    fields, high, send_far, send_near = side(False, (2, 3), (), (*fields[:-1], last), parts)
+    got_far, near_high = swap(send_far), swap(send_near)
     moved_low, last = lax.optimization_barrier((moved_low, fields[-1]))
     fields = (*fields[:-1], last)
     keep = keep_far(cut, slab - cut, fields)
-    sums = [keep[s - 1] + jnp.concatenate([a[s - 1] for a in got_far], axis=0) for s in range(1, groups)]
+    sums = [keep[s - 1] + got_far[s - 1] for s in range(1, groups)]
     sums, last = lax.optimization_barrier((sums, fields[-1]))
     fields = (*fields[:-1], last)
     moved_high = [

time: 47.9 us -> 45.2 us (0.944)
  Pallas kernels: 15.7 us -> 13.4 us
  waiting for transfers between devices: 19.9 us -> 19.3 us
    pallas_call x5 -> x6, Pallas kernels: 9.04 us -> 7.43 us  [side(): pl.pallas_call(functools.partial(side_kernel, low, stages, [part[:-1] for...]
    ppermute x1, waiting for transfers between devices: 1.43 us -> 0.43 us  [local(): ahi = lax.ppermute(to_down, 'space', down)]
    ppermute x1, waiting for transfers between devices: 3.24 us -> 2.43 us  [local(): lax.ppermute(a, 'draw', [(j, (j + 2 * s) % draws) for j in range(draws)])]
    ppermute x1, starting transfers between devices: 0.86 us -> 1.56 us  [local(): lax.ppermute(a, 'draw', [(j, (j + 2 * s) % draws) for j in range(draws)])]
    ppermute x1, waiting for transfers between devices: 0.01 us -> 0.59 us  [onward(): lax.ppermute(keep[s - 1] + got[s - 1], 'draw', [(j, (j + 2 * s) % draws)...]
    ppermute x1, waiting for transfers between devices: 14.1 us -> 14.5 us  [local(): alo = lax.ppermute(to_up, 'space', up)]
    pallas_call x1, Pallas kernels: 3.43 us -> 2.95 us  [local(): pl.pallas_call(inner_kernel, out_shape=(*kinds[1:], mid), in_specs=[ONCHI...]
    ppermute x5 -> x4, starting transfers between devices: 1.6 us -> 1.19 us  [swap(): return lax.ppermute(send, 'draw', pair)]
  transfers between devices with their start and end apart: 11 -> 10, of which waited for: 4 -> 6; matrix products, arithmetic and copies ran while one was open for 0% -> 0% of each run, Pallas kernels for 29% -> 25%
where the time goes in v6:
time: 45.2 us; the launch traced here: 45.1 us
  waiting for transfers between devices  19.3 us (43%)
  Pallas kernels  13.4 us (30%)
  starting transfers between devices  10.7 us (24%)
  between operations  0.83 us (2%)
  other arithmetic  0.74 us (2%)
    ppermute x1, waiting for transfers between devices, local(): alo = lax.ppermute(to_up, 'space', up)  14.5 us
    pallas_call x6, Pallas kernels, side(): pl.pallas_call(functools.partial(side_kernel, low, stages, [part[:-1] for...  7.43 us
    ppermute x1, starting transfers between devices, local(): alo = lax.ppermute(to_up, 'space', up)  4.98 us
    pallas_call x1, Pallas kernels, local(): pl.pallas_call(inner_kernel, out_shape=(*kinds[1:], mid), in_specs=[ONCHI...  2.95 us
    ppermute x1, waiting for transfers between devices, local(): lax.ppermute(a, 'draw', [(j, (j + 2 * s) % draws) for j in range(draws)])  2.43 us
    pallas_call x1, Pallas kernels, local(): pl.pallas_call(first_kernel, out_shape=(field, edge, edge), in_specs=[OFF...  1.91 us
    ppermute x1, starting transfers between devices, onward(): lax.ppermute(keep[s - 1] + got[s - 1], 'draw', [(j, (j + 2 * s) % draws)...  1.56 us
    ppermute x1, starting transfers between devices, local(): lax.ppermute(a, 'draw', [(j, (j + 2 * s) % draws) for j in range(draws)])  1.56 us
  transfers between devices with their start and end apart: 10, of which 6 were waited for; matrix products, arithmetic and copies ran while one was open for 0% of the time, Pallas kernels for 25%

profile of v6, /device:TPU:0, one launch (start us, length us, event | category | flops | bytes accessed | tf_op | source)
XLA Modules:
  0.0 45.1 jit_solution(11039675659095729111)
XLA Ops:
  0.6 0.0 copy-start
  0.6 0.0 copy-start.1
  0.7 0.0 copy-start.2
  0.7 1.9 %shard_map.68 = (f32[16,3,64,128]{3,2,1,0:T(8,128)S(1)}, f32[18,3,32,128]{3,2,1,0:T(8,128)S(1)}, f32[18,3,32,128]{3,2,1,0:T(8,128)S(1)}) custom-call(f32[8,64,384]{2,1,0:T(8,128)} %log_perm.1, f32[8,64,384]{2,1,0:T(8,128)} %bitcast.10, f32[8,64,384]{2,1,0:T(8,128)} %p0.3, f32[8,64,384]{2,1,0:T(8,128)} %src.3, f32[8,64,384]{2,1,0:T(8,128)} %obs.3), custom_call_target="tpu_custom_call" | custom-call | flops 196608 | bytes 3932160 | tf_op jit(solution)/shard_map/pallas_call | solution.py:357
  2.6 5.0 %collective-permute-start = (f32[18,3,32,128]{3,2,1,0:T(8,128)S(1)}, f32[18,3,32,128]{3,2,1,0:T(8,128)S(1)}, u32[]{:S(2)}, u32[]{:S(2)}) collective-permute-start(f32[18,3,32,128]{3,2,1,0:T(8,128)S(1)} %get-tuple-element.137), channel_id=1, source_target_pairs={{0,4},{4,8},{8,12},{1,5},{5,9},{9,13},{2,6},{6,10},{10,14},{3,7},{... | collective-permute-start | bytes 2654216 | tf_op jit(solution)/shard_map/ppermute | solution.py:366
  7.6 1.3 %collective-permute-start.2 = (f32[18,3,32,128]{3,2,1,0:T(8,128)S(1)}, f32[18,3,32,128]{3,2,1,0:T(8,128)S(1)}, u32[]{:S(2)}, u32[]{:S(2)}) collective-permute-start(f32[18,3,32,128]{3,2,1,0:T(8,128)S(1)} %get-tuple-element.203), channel_id=1, source_target_pairs={{4,0},{8,4},{12,8},{5,1},{9,5},{13,9},{6,2},{10,6},{14,10},{7,3},{... | collective-permute-start | bytes 2654216 | tf_op jit(solution)/shard_map/ppermute | solution.py:367
  8.9 0.0 copy-done
  8.9 0.0 copy-done.1
  8.9 0.0 copy-done.2
  8.9 2.9 %shard_map.69 = (f32[16,3,64,128]{3,2,1,0:T(8,128)S(1)}, f32[16,3,64,128]{3,2,1,0:T(8,128)S(1)}, f32[16,3,64,128]{3,2,1,0:T(8,128)S(1)}, f32[16,3,64,128]{3,2,1,...) custom-call(f32[16,3,64,128]{3,2,1,0:T(8,128)S(1)} %get-tuple-elemen, ...), custom_call_target="tpu_custom_call" | custom-call | flops 39321600 | bytes 11796480 | tf_op jit(solution)/shard_map/pallas_call | solution.py:368
  11.9 14.5 %collective-permute-done.args_0_ = f32[18,3,32,128]{3,2,1,0:T(8,128)S(1)} collective-permute-done((f32[18,3,32,128]{3,2,1,0:T(8,128)S(1)}, f32[18,3,32,128]{3,2,1,0:T(8,128)S(1)}, u32[]{:S(2)}, u32[]{:S(2)}) %collective-permute-start) | collective-permute-done | bytes 884768 | tf_op jit(solution)/shard_map/ppermute | solution.py:366
  26.4 0.1 collective-permute-start.1
  26.5 0.7 %shard_map.70 = (f32[16,3,64,128]{3,2,1,0:T(8,128)S(1)}, f32[16,3,64,128]{3,2,1,0:T(8,128)S(1)}, f32[16,3,64,128]{3,2,1,0:T(8,128)S(1)}, f32[16,3,64,128]{3,2,1,...) custom-call(f32[18,3,32,128]{3,2,1,0:T(8,128)S(1)} %collective-permu, ...), custom_call_target="tpu_custom_call", output_to_operand_aliasing={{0}: (1, {}), {1}: (2, {}), {2}: (3, {}), {3}: (4, {}), {4}... | custom-call | flops 5898240 | bytes 1966080 | tf_op jit(solution)/shard_map/pallas_call | solution.py:386
  27.2 1.1 %collective-permute-done.1.args_1_ = f32[10,3,32,128]{3,2,1,0:T(8,128)S(1)} collective-permute-done((f32[10,3,32,128]{3,2,1,0:T(8,128)S(1)}, f32[10,3,32,128]{3,2,1,0:T(8,128)S(1)}, u32[]{:S(2)}, u32[]{:S(2)}) %collective-permute-start.1) | collective-permute-done | bytes 491552 | tf_op jit(solution)/shard_map/ppermute | solution.py:400
  28.4 0.8 %shard_map.71 = (f32[16,3,64,128]{3,2,1,0:T(8,128)S(1)}, f32[16,3,64,128]{3,2,1,0:T(8,128)S(1)}, f32[16,3,64,128]{3,2,1,0:T(8,128)S(1)}, f32[16,3,64,128]{3,2,1,...) custom-call(f32[18,3,32,128]{3,2,1,0:T(8,128)S(1)} %collective-permu, ...), custom_call_target="tpu_custom_call", output_to_operand_aliasing={{0}: (2, {}), {1}: (3, {}), {2}: (4, {}), {3}: (5, {}), {4}... | custom-call | flops 5898240 | bytes 1966080 | tf_op jit(solution)/shard_map/pallas_call | solution.py:386
  29.1 1.0 %shard_map.72 = (f32[16,3,64,128]{3,2,1,0:T(8,128)S(1)}, f32[16,3,64,128]{3,2,1,0:T(8,128)S(1)}, f32[16,3,64,128]{3,2,1,0:T(8,128)S(1)}, f32[16,3,64,128]{3,2,1,...) custom-call(f32[16,3,64,128]{3,2,1,0:T(8,128)S(1)} %get-tuple-elemen, ...), custom_call_target="tpu_custom_call", output_to_operand_aliasing={{0}: (0, {}), {1}: (1, {}), {2}: (2, {}), {3}: (3, {}), {4}... | custom-call | flops 5898240 | bytes 1966080 | tf_op jit(solution)/shard_map/pallas_call | solution.py:386
  30.1 0.4 collective-permute-done.2.args_0_.args_1_
  30.6 0.1 collective-permute-start.3
  30.7 1.6 %shard_map.73 = (f32[16,3,64,128]{3,2,1,0:T(8,128)S(1)}, f32[16,3,64,128]{3,2,1,0:T(8,128)S(1)}, f32[16,3,64,128]{3,2,1,0:T(8,128)S(1)}, f32[16,3,64,128]{3,2,1,...) custom-call(f32[16,3,64,128]{3,2,1,0:T(8,128)S(1)} %get-tuple-elemen, ...), custom_call_target="tpu_custom_call", output_to_operand_aliasing={{0}: (0, {}), {1}: (1, {}), {2}: (2, {}), {3}: (3, {}), {4}... | custom-call | flops 5898240 | bytes 1966080 | tf_op jit(solution)/shard_map/pallas_call | solution.py:386
  32.3 0.5 %collective-permute-start.4 = (f32[1,4,16,384]{3,2,1,0:T(8,128)S(1)}, f32[1,4,16,384]{3,2,1,0:T(8,128)S(1)}, u32[]{:S(2)}, u32[]{:S(2)}) collective-permute-start(f32[1,4,16,384]{3,2,1,0:T(8,128)S(1)} %get-tuple-element.240), channel_id=1, source_target_pairs={{0,1},{1,0},{2,3},{3,2},{4,5},{5,4},{6,7},{7,6},{8,9},{9,8},{10,11... | collective-permute-start | bytes 294920 | tf_op jit(solution)/shard_map/ppermute | solution.py:409
  32.8 0.1 collective-permute-start.5
  32.9 0.0 collective-permute-done.3.args_2_
  32.9 1.0 %shard_map.74 = (f32[16,3,64,128]{3,2,1,0:T(8,128)S(1)}, f32[16,3,64,128]{3,2,1,0:T(8,128)S(1)}, f32[16,3,64,128]{3,2,1,0:T(8,128)S(1)}, f32[16,3,64,128]{3,2,1,...) custom-call(f32[18,3,32,128]{3,2,1,0:T(8,128)S(1)} %collective-permu, ...), custom_call_target="tpu_custom_call", output_to_operand_aliasing={{0}: (3, {}), {1}: (4, {}), {2}: (5, {}), {3}: (6, {}), {4}... | custom-call | flops 11796480 | bytes 1966080 | tf_op jit(solution)/shard_map/pallas_call | solution.py:386
  34.0 0.0 collective-permute-done.4
  34.0 0.2 collective-permute-done.5
  34.2 1.6 %collective-permute-start.6 = (f32[4,16,384]{2,1,0:T(8,128)S(1)}, f32[4,16,384]{2,1,0:T(8,128)S(1)}, u32[]{:S(2)}, u32[]{:S(2)}) collective-permute-start(f32[4,16,384]{2,1,0:T(8,128)S(1)} %add_bitcast_fusion.1), channel_id=1, source_target_pairs={{0,2},{1,3},{2,0},{3,1},{4,6},{5,7},{6,4},{7,5},{8,10},{9,11},{10,... | collective-permute-start | bytes 294920 | tf_op jit(solution)/shard_map/ppermute | solution.py:404
  35.7 2.3 %shard_map.75 = (f32[16,3,64,128]{3,2,1,0:T(8,128)S(1)}, f32[16,3,64,128]{3,2,1,0:T(8,128)S(1)}, f32[16,3,64,128]{3,2,1,0:T(8,128)S(1)}, f32[16,3,64,128]{3,2,1,...) custom-call(f32[16,3,64,128]{3,2,1,0:T(8,128)S(1)} %get-tuple-elemen, ...), custom_call_target="tpu_custom_call", output_to_operand_aliasing={{0}: (0, {}), {1}: (1, {}), {2}: (2, {}), {3}: (3, {}), {4}... | custom-call | flops 11796480 | bytes 1966080 | tf_op jit(solution)/shard_map/pallas_call | solution.py:386
  38.0 0.1 collective-permute-start.7
  38.1 0.5 %collective-permute-start.8 = (f32[1,4,16,384]{3,2,1,0:T(8,128)S(1)}, f32[1,4,16,384]{3,2,1,0:T(8,128)S(1)}, u32[]{:S(2)}, u32[]{:S(2)}) collective-permute-start(f32[1,4,16,384]{3,2,1,0:T(8,128)S(1)} %get-tuple-element.269), channel_id=1, source_target_pairs={{0,1},{1,0},{2,3},{3,2},{4,5},{5,4},{6,7},{7,6},{8,9},{9,8},{10,11... | collective-permute-start | bytes 294920 | tf_op jit(solution)/shard_map/ppermute | solution.py:409
  38.6 0.6 %collective-permute-done.6 = f32[4,16,384]{2,1,0:T(8,128)S(1)} collective-permute-done((f32[4,16,384]{2,1,0:T(8,128)S(1)}, f32[4,16,384]{2,1,0:T(8,128)S(1)}, u32[]{:S(2)}, u32[]{:S(2)}) %collective-permute-start.6) | collective-permute-done | bytes 98336 | tf_op jit(solution)/shard_map/ppermute | solution.py:404
  39.2 0.2 shard_map.76
  39.4 0.0 collective-permute-done.7
  39.4 1.6 %collective-permute-start.9 = (f32[4,16,384]{2,1,0:T(8,128)S(1)}, f32[4,16,384]{2,1,0:T(8,128)S(1)}, u32[]{:S(2)}, u32[]{:S(2)}) collective-permute-start(f32[4,16,384]{2,1,0:T(8,128)S(1)} %add_bitcast_fusion), channel_id=1, source_target_pairs={{0,2},{1,3},{2,0},{3,1},{4,6},{5,7},{6,4},{7,5},{8,10},{9,11},{10,... | collective-permute-start | bytes 294920 | tf_op jit(solution)/shard_map/ppermute | solution.py:442
  41.0 0.9 %shard_map.77 = (f32[8,64,384]{2,1,0:T(8,128)}, f32[1,8,16,384]{3,2,1,0:T(8,128)S(1)}) custom-call(f32[3,64,384]{2,1,0:T(8,128)S(1)} %get-tuple-element.206.args_0_, f32[2,64,384]{2,1,0:T(8,128)S(1)} %get-tuple-element.207.args_1_, f32[3,64,384]{2,1,0:T(8,128)S(1)} %get-tuple-element.244.args_2_, f32[16,3,64,128]{3,2,1,0:T(8,128)S(1)} %get-tuple-element.245.args_0_.args_3_, ...), custom_call_target="tpu_custom_call" | custom-call | flops 5898240 | bytes 5898240 | tf_op jit(solution)/shard_map/pallas_call | solution.py:444
  41.9 0.0 collective-permute-done.8
  41.9 2.4 %collective-permute-done.9 = f32[4,16,384]{2,1,0:T(8,128)S(1)} collective-permute-done((f32[4,16,384]{2,1,0:T(8,128)S(1)}, f32[4,16,384]{2,1,0:T(8,128)S(1)}, u32[]{:S(2)}, u32[]{:S(2)}) %collective-permute-start.9) | collective-permute-done | bytes 98336 | tf_op jit(solution)/shard_map/ppermute | solution.py:442
  44.3 0.7 %fusion = f32[8,16,384]{2,1,0:T(8,128)} fusion(f32[4,16,384]{2,1,0:T(8,128)S(1)} %bitcast.12, f32[4,16,384]{2,1,0:T(8,128)S(1)} %bitcast.11, f32[4,16,384]{2,1,0:T(8,128)S(1)} %collective-permute-done.9, f32[4,16,384]{2,1,0:T(8,128)S(1)} %collective-permute-done.6, f32[1,8,16,384]{3,2,1,0:T(8,128)S(1)} %get-tuple-element.267), kind=kLoop, calls=%fused_computation.1 | loop fusion | flops 196608 | bytes 786432 | tf_op jit(solution)/shard_map/add | solution.py:455
  (4 shorter events, 0.1 us)
Async XLA Ops:
  0.6 8.2 %copy-start = (f32[8,64,384]{2,1,0:T(8,128)S(1)}, f32[8,64,384]{2,1,0:T(8,128)}, u32[]{:S(2)}) copy-start(f32[8,64,384]{2,1,0:T(8,128)} %p0.3) | copy-start | bytes 2359300
  0.6 8.2 %copy-start.1 = (f32[8,64,384]{2,1,0:T(8,128)S(1)}, f32[8,64,384]{2,1,0:T(8,128)}, u32[]{:S(2)}) copy-start(f32[8,64,384]{2,1,0:T(8,128)} %src.3) | copy-start | bytes 2359300
  0.7 8.2 %copy-start.2 = (f32[8,64,384]{2,1,0:T(8,128)S(1)}, f32[8,64,384]{2,1,0:T(8,128)}, u32[]{:S(2)}) copy-start(f32[8,64,384]{2,1,0:T(8,128)} %obs.3) | copy-start | bytes 2359300
  2.6 23.8 %collective-permute-start = (f32[18,3,32,128]{3,2,1,0:T(8,128)S(1)}, f32[18,3,32,128]{3,2,1,0:T(8,128)S(1)}, u32[]{:S(2)}, u32[]{:S(2)}) collective-permute-start(f32[18,3,32,128]{3,2,1,0:T(8,128)S(1)} %get-tuple-element.137), channel_id=1, source_target_pairs={{0,4},{4,8},{8,12},{1,5},{5,9},{9,13},{2,6},{6,10},{10,14},{3,7},{... | collective-permute-start | bytes 2654216 | tf_op jit(solution)/shard_map/ppermute | solution.py:366
  7.6 23.0 %collective-permute-start.2 = (f32[18,3,32,128]{3,2,1,0:T(8,128)S(1)}, f32[18,3,32,128]{3,2,1,0:T(8,128)S(1)}, u32[]{:S(2)}, u32[]{:S(2)}) collective-permute-start(f32[18,3,32,128]{3,2,1,0:T(8,128)S(1)} %get-tuple-element.203), channel_id=1, source_target_pairs={{4,0},{8,4},{12,8},{5,1},{9,5},{13,9},{6,2},{10,6},{14,10},{7,3},{... | collective-permute-start | bytes 2654216 | tf_op jit(solution)/shard_map/ppermute | solution.py:367
  26.4 1.9 %collective-permute-start.1 = (f32[10,3,32,128]{3,2,1,0:T(8,128)S(1)}, f32[10,3,32,128]{3,2,1,0:T(8,128)S(1)}, u32[]{:S(2)}, u32[]{:S(2)}) collective-permute-start(f32[10,3,32,128]{3,2,1,0:T(8,128)S(1)} %slice.6), channel_id=1, source_target_pairs={{0,1},{1,0},{2,3},{3,2},{4,5},{5,4},{6,7},{7,6},{8,9},{9,8},{10,11... | collective-permute-start | bytes 1474568 | tf_op jit(solution)/shard_map/ppermute | solution.py:400
  30.6 2.3 %collective-permute-start.3 = (f32[10,3,32,128]{3,2,1,0:T(8,128)S(1)}, f32[10,3,32,128]{3,2,1,0:T(8,128)S(1)}, u32[]{:S(2)}, u32[]{:S(2)}) collective-permute-start(f32[10,3,32,128]{3,2,1,0:T(8,128)S(1)} %slice.7), channel_id=1, source_target_pairs={{0,1},{1,0},{2,3},{3,2},{4,5},{5,4},{6,7},{7,6},{8,9},{9,8},{10,11... | collective-permute-start | bytes 1474568 | tf_op jit(solution)/shard_map/ppermute | solution.py:400
  32.3 1.7 %collective-permute-start.4 = (f32[1,4,16,384]{3,2,1,0:T(8,128)S(1)}, f32[1,4,16,384]{3,2,1,0:T(8,128)S(1)}, u32[]{:S(2)}, u32[]{:S(2)}) collective-permute-start(f32[1,4,16,384]{3,2,1,0:T(8,128)S(1)} %get-tuple-element.240), channel_id=1, source_target_pairs={{0,1},{1,0},{2,3},{3,2},{4,5},{5,4},{6,7},{7,6},{8,9},{9,8},{10,11... | collective-permute-start | bytes 294920 | tf_op jit(solution)/shard_map/ppermute | solution.py:409
  32.8 1.3 %collective-permute-start.5 = (f32[1,4,16,384]{3,2,1,0:T(8,128)S(1)}, f32[1,4,16,384]{3,2,1,0:T(8,128)S(1)}, u32[]{:S(2)}, u32[]{:S(2)}) collective-permute-start(f32[1,4,16,384]{3,2,1,0:T(8,128)S(1)} %get-tuple-element.241), channel_id=1, source_target_pairs={{0,1},{1,0},{2,3},{3,2},{4,5},{5,4},{6,7},{7,6},{8,9},{9,8},{10,11... | collective-permute-start | bytes 294920 | tf_op jit(solution)/shard_map/ppermute | solution.py:409
  34.2 5.1 %collective-permute-start.6 = (f32[4,16,384]{2,1,0:T(8,128)S(1)}, f32[4,16,384]{2,1,0:T(8,128)S(1)}, u32[]{:S(2)}, u32[]{:S(2)}) collective-permute-start(f32[4,16,384]{2,1,0:T(8,128)S(1)} %add_bitcast_fusion.1), channel_id=1, source_target_pairs={{0,2},{1,3},{2,0},{3,1},{4,6},{5,7},{6,4},{7,5},{8,10},{9,11},{10,... | collective-permute-start | bytes 294920 | tf_op jit(solution)/shard_map/ppermute | solution.py:404
  38.0 1.4 %collective-permute-start.7 = (f32[1,4,16,384]{3,2,1,0:T(8,128)S(1)}, f32[1,4,16,384]{3,2,1,0:T(8,128)S(1)}, u32[]{:S(2)}, u32[]{:S(2)}) collective-permute-start(f32[1,4,16,384]{3,2,1,0:T(8,128)S(1)} %get-tuple-element.264), channel_id=1, source_target_pairs={{0,1},{1,0},{2,3},{3,2},{4,5},{5,4},{6,7},{7,6},{8,9},{9,8},{10,11... | collective-permute-start | bytes 294920 | tf_op jit(solution)/shard_map/ppermute | solution.py:409
  38.1 3.8 %collective-permute-start.8 = (f32[1,4,16,384]{3,2,1,0:T(8,128)S(1)}, f32[1,4,16,384]{3,2,1,0:T(8,128)S(1)}, u32[]{:S(2)}, u32[]{:S(2)}) collective-permute-start(f32[1,4,16,384]{3,2,1,0:T(8,128)S(1)} %get-tuple-element.269), channel_id=1, source_target_pairs={{0,1},{1,0},{2,3},{3,2},{4,5},{5,4},{6,7},{7,6},{8,9},{9,8},{10,11... | collective-permute-start | bytes 294920 | tf_op jit(solution)/shard_map/ppermute | solution.py:409
  39.4 4.9 %collective-permute-start.9 = (f32[4,16,384]{2,1,0:T(8,128)S(1)}, f32[4,16,384]{2,1,0:T(8,128)S(1)}, u32[]{:S(2)}, u32[]{:S(2)}) collective-permute-start(f32[4,16,384]{2,1,0:T(8,128)S(1)} %add_bitcast_fusion), channel_id=1, source_target_pairs={{0,2},{1,3},{2,0},{3,1},{4,6},{5,7},{6,4},{7,5},{8,10},{9,11},{10,... | collective-permute-start | bytes 294920 | tf_op jit(solution)/shard_map/ppermute | solution.py:442

commit v7 on v6

--- a/solution.py
+++ b/solution.py
@@ -175,7 +175,7 @@
             lax.fori_loop(lo, hi, lambda zz, _, body=body, own=own: body(zz, *own) or 0, 0)
 
 
-def first_kernel(log_perm, noise, p0, src, obs, K, up, down, means, draws, sems):
+def first_kernel(log_perm, noise, p0, src, obs, K, up, down, top, bottom, means, draws, sems):
     slab, nx, ny = log_perm.shape
     tiles, half = ny // LANES, nx // 2
     rows = pl.ds(pl.multiple_of(half * (lax.axis_index("draw") % 2), half), half)
@@ -205,11 +205,10 @@
                 k = jnp.exp(means[z, here, cols] + draws[z, here, cols])
                 K[z + HALO, c, here, :] = k
                 if out is not None:
-                    part, at = divmod(SUB * r, half)
-                    out[EDGE + part * HALO + z - first, c, pl.ds(at, SUB), :] = k
+                    out[z - first, c, here, :] = k
         return 0
 
-    low, high = functools.partial(plane, out=down), functools.partial(plane, out=up, first=slab - HALO)
+    low, high = functools.partial(plane, out=bottom), functools.partial(plane, out=top, first=slab - HALO)
     lax.fori_loop(0, HALO, low, 0)
     lax.fori_loop(HALO, slab - HALO, plane, 0)
     lax.fori_loop(slab - HALO, slab, high, 0)
@@ -257,17 +256,19 @@
     par = lax.axis_index("draw") % 2
 
     pairs = []
-    if 0 in stages:
-        for h in range(2):
-            rows = pl.ds(h * half, half)
-            pairs.append((halos[0].at[pl.ds(EDGE + h * HALO, HALO)], K.at[pl.ds(0 if low else top, HALO), :, rows]))
-    if 1 in stages:
-        for half_rows, which in zip(halos[-2:], (par, 1 - par)):
+    if halos:
+        k, mine, *theirs = halos
+        pairs.append((k, K.at[pl.ds(0 if low else top, HALO)]))
+        for half_rows, which in ((None, par), (theirs, 1 - par)):
             rows = pl.ds(pl.multiple_of(half * which, half), half)
             first = 0
             for field, width in ((P0, HALO), (SRC, SWEEPS), (OBS, SWEEPS)):
                 planes = pl.ds(HALO - width if low else top, width)
-                pairs.append((half_rows.at[pl.ds(first, width)], field.at[planes, :, rows]))
+                if half_rows is None:
+                    ref = mine.at[pl.ds(first, width)]
+                else:
+                    ref = theirs[0] if first == 0 else theirs[1].at[pl.ds(first - HALO, width)]
+                pairs.append((ref, field.at[planes, :, rows]))
                 first += width
     copies = [pltpu.make_async_copy(a, b, sems.at[i]) for i, (a, b) in enumerate(pairs)]
     for cp in copies:
@@ -344,7 +345,8 @@
     field = pltpu.VMEM((depth, tiles, nx, LANES), f32)
     padded = pltpu.VMEM((depth, tiles, nx + 2 * SUB, LANES), f32)
     kinds = [field] * 6 + [padded] + [field] * 8 + [padded]
-    edge = jax.ShapeDtypeStruct((EDGE + 2 * HALO, tiles, half, LANES), f32)
+    edge = jax.ShapeDtypeStruct((EDGE, tiles, half, LANES), f32)
+    rim = jax.ShapeDtypeStruct((HALO, tiles, nx, LANES), f32)
     whole = jax.ShapeDtypeStruct((slab, nx, ny), f32)
     mid = jax.ShapeDtypeStruct((slab - 2 * SWEEPS, nx, ny), f32)
     groups = draws // 2
@@ -354,17 +356,19 @@
     cells = slab * nx * ny
 
     inputs = (log_perm, noise[0], start_pressure, source, observe)
-    K, to_up, to_down = pl.pallas_call(
+    K, to_up, to_down, top, bottom = pl.pallas_call(
         first_kernel,
-        out_shape=(field, edge, edge),
+        out_shape=(field, edge, edge, rim, rim),
         in_specs=[OFFCHIP] * 5,
-        out_specs=(ONCHIP,) * 3,
+        out_specs=(ONCHIP,) * 5,
         scratch_shapes=[pltpu.VMEM((slab, nx, ny), f32)] * 2 + [pltpu.SemaphoreType.DMA((2 + 6 * tiles,))],
         compiler_params=params,
         cost_estimate=pl.CostEstimate(flops=cells, bytes_accessed=20 * cells, transcendentals=cells),
     )(*[pltpu.with_memory_space_constraint(a, pltpu.HBM) for a in inputs])
     alo = lax.ppermute(to_up, "space", up)
     ahi = lax.ppermute(to_down, "space", down)
+    klo = lax.ppermute(top, "space", up)
+    khi = lax.ppermute(bottom, "space", down)
     state = pl.pallas_call(
         inner_kernel,
         out_shape=(*kinds[1:], mid),
@@ -383,6 +387,7 @@
         ends = (jax.ShapeDtypeStruct((SWEEPS, nx, ny), f32),) if 3 in stages else ()
         ends += tuple(blocks(groups - 1 if first else 1, planes) for _, first, _, planes in parts)
         n = len(halos)
+        work = 1 if low else 30 * len(stages) * cells
         out = pl.pallas_call(
             functools.partial(side_kernel, low, stages, [part[:-1] for part in parts]),
             out_shape=(*kinds, *ends),
@@ -391,13 +396,16 @@
             scratch_shapes=[pltpu.SemaphoreType.DMA((8,))],
             input_output_aliases={n + i: i for i in range(FIELDS)},
             compiler_params=params,
-            cost_estimate=pl.CostEstimate(flops=30 * len(stages) * cells, bytes_accessed=10 * cells, transcendentals=0),
+            cost_estimate=pl.CostEstimate(flops=work, bytes_accessed=work, transcendentals=0),
         )(*halos, *fields)
         return out[:FIELDS], *out[FIELDS:]
 
-    def swapped(got, fields):
-        got, last = lax.optimization_barrier((got, fields[-1]))
-        return got, lax.ppermute(got[:EDGE], "draw", pair), (*fields[:-1], last)
+    alo, ahi, last = lax.optimization_barrier((alo, ahi, fields[-1]))
+    fields = (*fields[:-1], last)
+    lower, upper = [
+        (k, mine, *[lax.ppermute(mine[a:b], "draw", pair) for a, b in ((0, HALO), (HALO, EDGE))])
+        for k, mine in ((klo, alo), (khi, ahi))
+    ]
 
     def onward(keep, got):
         return [
@@ -418,15 +426,11 @@
             cost_estimate=pl.CostEstimate(flops=10 * cells, bytes_accessed=10 * cells, transcendentals=0),
         )(*fields)
 
-    mine, theirs, fields = swapped(alo, fields)
-    (fields,) = side(True, (0,), (mine,), fields)
-    (fields,) = side(True, (1,), (mine, theirs), fields)
-    (fields,) = side(True, (2,), (), fields)
-    mine, theirs, fields = swapped(ahi, fields)
+    (fields,) = side(True, (0, 1, 2), lower, fields)
     parts = [(False, 1, 0, cut), (False, 0, 0, cut), (True, 1, 0, cut)]
     fields, low, send_far, send_near, keep = side(True, (3,), (), fields, parts)
     got_far, near_low = swap(send_far), swap(send_near)
-    (fields,) = side(False, (0, 1), (mine, mine, theirs), fields)
+    (fields,) = side(False, (0, 1), upper, fields)
     got_far, near_low, last = lax.optimization_barrier((got_far, near_low, fields[-1]))
     moved_low = onward(keep, got_far)
     parts = [(False, 1, cut, slab - cut), (False, 0, cut, slab - cut)]

time: 45.2 us -> 43.2 us (0.956)
  waiting for transfers between devices: 19.3 us -> 10.9 us
  starting transfers between devices: 10.7 us -> 17.1 us
    ppermute x1, waiting for transfers between devices: 14.5 us -> 1.39 us  [local(): alo = lax.ppermute(to_up, 'space', up)]
    ppermute x2 -> x6, starting transfers between devices: 0.14 us -> 6.58 us  [the longest x1 4.57 us: local(): klo = lax.ppermute(top, 'space', up)]
    ppermute x1, waiting for transfers between devices: 0.43 us -> 4.46 us  [local(): ahi = lax.ppermute(to_down, 'space', down)]
    ppermute x2 -> x6, waiting for transfers between devices: 1.14 us -> 2.02 us  [the longest x1 2.01 us: local(): klo = lax.ppermute(top, 'space', up)]
    pallas_call x6 -> x4, Pallas kernels: 7.43 us -> 7.26 us  [side(): pl.pallas_call(functools.partial(side_kernel, low, stages, [part[:-1] for...]
  transfers between devices with their start and end apart: 10 -> 14, of which waited for: 6 -> 5; matrix products, arithmetic and copies ran while one was open for 0% -> 0% of each run, Pallas kernels for 25% -> 26%
where the time goes in v7:
time: 43.2 us; the launch traced here: 42.9 us
  starting transfers between devices  17.1 us (40%)
  Pallas kernels  13.2 us (31%)
  waiting for transfers between devices  10.9 us (25%)
  between operations  0.86 us (2%)
  other arithmetic  0.74 us (2%)
    pallas_call x4, Pallas kernels, side(): pl.pallas_call(functools.partial(side_kernel, low, stages, [part[:-1] for...  7.26 us
    ppermute x1, starting transfers between devices, local(): alo = lax.ppermute(to_up, 'space', up)  4.96 us
    ppermute x1, starting transfers between devices, local(): klo = lax.ppermute(top, 'space', up)  4.57 us
    ppermute x1, waiting for transfers between devices, local(): ahi = lax.ppermute(to_down, 'space', down)  4.46 us
    pallas_call x1, Pallas kernels, local(): pl.pallas_call(inner_kernel, out_shape=(*kinds[1:], mid), in_specs=[ONCHI...  2.97 us
    ppermute x1, waiting for transfers between devices, local(): lax.ppermute(a, 'draw', [(j, (j + 2 * s) % draws) for j in range(draws)])  2.29 us
    ppermute x1, waiting for transfers between devices, local(): klo = lax.ppermute(top, 'space', up)  2.01 us
    pallas_call x1, Pallas kernels, local(): pl.pallas_call(first_kernel, out_shape=(field, edge, edge, rim, rim), in_...  1.91 us
  transfers between devices with their start and end apart: 14, of which 5 were waited for; matrix products, arithmetic and copies ran while one was open for 0% of the time, Pallas kernels for 26%

profile of v7, /device:TPU:0, one launch (start us, length us, event | category | flops | bytes accessed | tf_op | source)
XLA Modules:
  0.0 42.9 jit_solution(16626567416681168423)
XLA Ops:
  0.6 0.0 copy-start
  0.6 0.0 copy-start.1
  0.7 0.0 copy-start.2
  0.7 1.9 %shard_map.68 = (f32[16,3,64,128]{3,2,1,0:T(8,128)S(1)}, f32[10,3,32,128]{3,2,1,0:T(8,128)S(1)}, f32[10,3,32,128]{3,2,1,0:T(8,128)S(1)}, f32[4,3,64,128]{3,2,1,0:T(8,128)S(1)}, f32[4,3,64,128]{3,2,1,0:T(8,128)S(1)}) custom-call(f32[8,64,384]{2,1,0:T(8,128)} %log_perm.1, f32[8,64,384]{2,1,0:T(8,128)} %bitcast.10, f32[8,64,384]{2,1,0:T(8,128)} %p0.3, ...), custom_call_target="tpu_custom_call" | custom-call | flops 196608 | bytes 3932160 | tf_op jit(solution)/shard_map/pallas_call | solution.py:359
  2.6 5.0 %collective-permute-start.1 = (f32[10,3,32,128]{3,2,1,0:T(8,128)S(1)}, f32[10,3,32,128]{3,2,1,0:T(8,128)S(1)}, u32[]{:S(2)}, u32[]{:S(2)}) collective-permute-start(f32[10,3,32,128]{3,2,1,0:T(8,128)S(1)} %get-tuple-element.107), channel_id=1, source_target_pairs={{0,4},{4,8},{8,12},{1,5},{5,9},{9,13},{2,6},{6,10},{10,14},{3,7},{... | collective-permute-start | bytes 1474568 | tf_op jit(solution)/shard_map/ppermute | solution.py:368
  7.5 1.3 %collective-permute-start.2 = (f32[10,3,32,128]{3,2,1,0:T(8,128)S(1)}, f32[10,3,32,128]{3,2,1,0:T(8,128)S(1)}, u32[]{:S(2)}, u32[]{:S(2)}) collective-permute-start(f32[10,3,32,128]{3,2,1,0:T(8,128)S(1)} %get-tuple-element.108), channel_id=1, source_target_pairs={{4,0},{8,4},{12,8},{5,1},{9,5},{13,9},{6,2},{10,6},{14,10},{7,3},{... | collective-permute-start | bytes 1474568 | tf_op jit(solution)/shard_map/ppermute | solution.py:369
  8.8 4.6 %collective-permute-start = (f32[4,3,64,128]{3,2,1,0:T(8,128)S(1)}, f32[4,3,64,128]{3,2,1,0:T(8,128)S(1)}, u32[]{:S(2)}, u32[]{:S(2)}) collective-permute-start(f32[4,3,64,128]{3,2,1,0:T(8,128)S(1)} %get-tuple-element.106), channel_id=1, source_target_pairs={{0,4},{4,8},{8,12},{1,5},{5,9},{9,13},{2,6},{6,10},{10,14},{3,7},{... | collective-permute-start | bytes 1179656 | tf_op jit(solution)/shard_map/ppermute | solution.py:370
  13.4 1.3 %collective-permute-start.5 = (f32[4,3,64,128]{3,2,1,0:T(8,128)S(1)}, f32[4,3,64,128]{3,2,1,0:T(8,128)S(1)}, u32[]{:S(2)}, u32[]{:S(2)}) collective-permute-start(f32[4,3,64,128]{3,2,1,0:T(8,128)S(1)} %get-tuple-element.145), channel_id=1, source_target_pairs={{4,0},{8,4},{12,8},{5,1},{9,5},{13,9},{6,2},{10,6},{14,10},{7,3},{... | collective-permute-start | bytes 1179656 | tf_op jit(solution)/shard_map/ppermute | solution.py:371
  14.7 0.0 copy-done
  14.7 0.0 copy-done.1
  14.7 0.0 copy-done.2
  14.8 3.0 %shard_map.69 = (f32[16,3,64,128]{3,2,1,0:T(8,128)S(1)}, f32[16,3,64,128]{3,2,1,0:T(8,128)S(1)}, f32[16,3,64,128]{3,2,1,0:T(8,128)S(1)}, f32[16,3,64,128]{3,2,1,...) custom-call(f32[16,3,64,128]{3,2,1,0:T(8,128)S(1)} %get-tuple-elemen, ...), custom_call_target="tpu_custom_call" | custom-call | flops 39321600 | bytes 11796480 | tf_op jit(solution)/shard_map/pallas_call | solution.py:372
  17.7 1.4 %collective-permute-done.1.args_1_ = f32[10,3,32,128]{3,2,1,0:T(8,128)S(1)} collective-permute-done((f32[10,3,32,128]{3,2,1,0:T(8,128)S(1)}, f32[10,3,32,128]{3,2,1,0:T(8,128)S(1)}, u32[]{:S(2)}, u32[]{:S(2)}) %collective-permute-start.1) | collective-permute-done | bytes 491552 | tf_op jit(solution)/shard_map/ppermute | solution.py:368
  19.1 4.5 %collective-permute-done.2.args_1_ = f32[10,3,32,128]{3,2,1,0:T(8,128)S(1)} collective-permute-done((f32[10,3,32,128]{3,2,1,0:T(8,128)S(1)}, f32[10,3,32,128]{3,2,1,0:T(8,128)S(1)}, u32[]{:S(2)}, u32[]{:S(2)}) %collective-permute-start.2) | collective-permute-done | bytes 491552 | tf_op jit(solution)/shard_map/ppermute | solution.py:369
  23.6 0.1 collective-permute-start.4
  23.7 0.6 %collective-permute-start.7 = (f32[6,3,32,128]{3,2,1,0:T(8,128)S(1)}, f32[6,3,32,128]{3,2,1,0:T(8,128)S(1)}, u32[]{:S(2)}, u32[]{:S(2)}) collective-permute-start(f32[6,3,32,128]{3,2,1,0:T(8,128)S(1)} %slice.15), channel_id=1, source_target_pairs={{0,1},{1,0},{2,3},{3,2},{4,5},{5,4},{6,7},{7,6},{8,9},{9,8},{10,11... | collective-permute-start | bytes 884744 | tf_op jit(solution)/shard_map/ppermute | solution.py:406
  24.3 0.1 collective-permute-start.3
  24.4 2.0 %collective-permute-done.args_0_ = f32[4,3,64,128]{3,2,1,0:T(8,128)S(1)} collective-permute-done((f32[4,3,64,128]{3,2,1,0:T(8,128)S(1)}, f32[4,3,64,128]{3,2,1,0:T(8,128)S(1)}, u32[]{:S(2)}, u32[]{:S(2)}) %collective-permute-start) | collective-permute-done | bytes 393248 | tf_op jit(solution)/shard_map/ppermute | solution.py:370
  26.4 0.0 collective-permute-start.6
  26.4 0.0 collective-permute-done.3.args_2_
  26.4 0.0 collective-permute-done.4.args_3_
  26.4 2.1 %shard_map.70 = (f32[16,3,64,128]{3,2,1,0:T(8,128)S(1)}, f32[16,3,64,128]{3,2,1,0:T(8,128)S(1)}, f32[16,3,64,128]{3,2,1,0:T(8,128)S(1)}, f32[16,3,64,128]{3,2,1,...) custom-call(f32[4,3,64,128]{3,2,1,0:T(8,128)S(1)} %collective-permut, ...), custom_call_target="tpu_custom_call", output_to_operand_aliasing={{0}: (4, {}), {1}: (5, {}), {2}: (6, {}), {3}: (7, {}), {4}... | custom-call | flops 1 | bytes 1 | tf_op jit(solution)/shard_map/pallas_call | solution.py:391
  28.5 1.6 %shard_map.71 = (f32[16,3,64,128]{3,2,1,0:T(8,128)S(1)}, f32[16,3,64,128]{3,2,1,0:T(8,128)S(1)}, f32[16,3,64,128]{3,2,1,0:T(8,128)S(1)}, f32[16,3,64,128]{3,2,1,...) custom-call(f32[16,3,64,128]{3,2,1,0:T(8,128)S(1)} %get-tuple-elemen, ...), custom_call_target="tpu_custom_call", output_to_operand_aliasing={{0}: (0, {}), {1}: (1, {}), {2}: (2, {}), {3}: (3, {}), {4}... | custom-call | flops 1 | bytes 1 | tf_op jit(solution)/shard_map/pallas_call | solution.py:391
  30.1 0.5 %collective-permute-start.8 = (f32[1,4,16,384]{3,2,1,0:T(8,128)S(1)}, f32[1,4,16,384]{3,2,1,0:T(8,128)S(1)}, u32[]{:S(2)}, u32[]{:S(2)}) collective-permute-start(f32[1,4,16,384]{3,2,1,0:T(8,128)S(1)} %get-tuple-element.178), channel_id=1, source_target_pairs={{0,1},{1,0},{2,3},{3,2},{4,5},{5,4},{6,7},{7,6},{8,9},{9,8},{10,11... | collective-permute-start | bytes 294920 | tf_op jit(solution)/shard_map/ppermute | solution.py:417
  30.7 0.1 collective-permute-start.9
  30.7 0.0 collective-permute-done.5.args_0_
  30.7 0.0 collective-permute-done.6.args_2_
  30.8 0.0 collective-permute-done.7.args_3_
  30.8 1.2 %shard_map.72 = (f32[16,3,64,128]{3,2,1,0:T(8,128)S(1)}, f32[16,3,64,128]{3,2,1,0:T(8,128)S(1)}, f32[16,3,64,128]{3,2,1,0:T(8,128)S(1)}, f32[16,3,64,128]{3,2,1,...) custom-call(f32[4,3,64,128]{3,2,1,0:T(8,128)S(1)} %collective-permut, ...), custom_call_target="tpu_custom_call", output_to_operand_aliasing={{0}: (4, {}), {1}: (5, {}), {2}: (6, {}), {3}: (7, {}), {4}... | custom-call | flops 11796480 | bytes 11796480 | tf_op jit(solution)/shard_map/pallas_call | solution.py:391
  32.0 0.0 collective-permute-done.8
  32.0 0.0 collective-permute-done.9
  32.0 1.6 %collective-permute-start.10 = (f32[4,16,384]{2,1,0:T(8,128)S(1)}, f32[4,16,384]{2,1,0:T(8,128)S(1)}, u32[]{:S(2)}, u32[]{:S(2)}) collective-permute-start(f32[4,16,384]{2,1,0:T(8,128)S(1)} %add_bitcast_fusion.1), channel_id=1, source_target_pairs={{0,2},{1,3},{2,0},{3,1},{4,6},{5,7},{6,4},{7,5},{8,10},{9,11},{10,... | collective-permute-start | bytes 294920 | tf_op jit(solution)/shard_map/ppermute | solution.py:412
  33.6 2.3 %shard_map.73 = (f32[16,3,64,128]{3,2,1,0:T(8,128)S(1)}, f32[16,3,64,128]{3,2,1,0:T(8,128)S(1)}, f32[16,3,64,128]{3,2,1,0:T(8,128)S(1)}, f32[16,3,64,128]{3,2,1,...) custom-call(f32[16,3,64,128]{3,2,1,0:T(8,128)S(1)} %get-tuple-elemen, ...), custom_call_target="tpu_custom_call", output_to_operand_aliasing={{0}: (0, {}), {1}: (1, {}), {2}: (2, {}), {3}: (3, {}), {4}... | custom-call | flops 11796480 | bytes 11796480 | tf_op jit(solution)/shard_map/pallas_call | solution.py:391
  35.9 0.2 collective-permute-start.11
  36.1 0.3 collective-permute-start.12
  36.5 0.7 %collective-permute-done.10 = f32[4,16,384]{2,1,0:T(8,128)S(1)} collective-permute-done((f32[4,16,384]{2,1,0:T(8,128)S(1)}, f32[4,16,384]{2,1,0:T(8,128)S(1)}, u32[]{:S(2)}, u32[]{:S(2)}) %collective-permute-start.10) | collective-permute-done | bytes 98336 | tf_op jit(solution)/shard_map/ppermute | solution.py:412
  37.2 0.2 shard_map.74
  37.4 0.0 collective-permute-done.11
  37.5 1.6 %collective-permute-start.13 = (f32[4,16,384]{2,1,0:T(8,128)S(1)}, f32[4,16,384]{2,1,0:T(8,128)S(1)}, u32[]{:S(2)}, u32[]{:S(2)}) collective-permute-start(f32[4,16,384]{2,1,0:T(8,128)S(1)} %add_bitcast_fusion), channel_id=1, source_target_pairs={{0,2},{1,3},{2,0},{3,1},{4,6},{5,7},{6,4},{7,5},{8,10},{9,11},{10,... | collective-permute-start | bytes 294920 | tf_op jit(solution)/shard_map/ppermute | solution.py:446
  39.0 0.9 %shard_map.75 = (f32[8,64,384]{2,1,0:T(8,128)}, f32[1,8,16,384]{3,2,1,0:T(8,128)S(1)}) custom-call(f32[3,64,384]{2,1,0:T(8,128)S(1)} %get-tuple-element.143.args_0_, f32[2,64,384]{2,1,0:T(8,128)S(1)} %get-tuple-element.144.args_1_, f32[3,64,384]{2,1,0:T(8,128)S(1)} %get-tuple-element.182.args_2_, f32[16,3,64,128]{3,2,1,0:T(8,128)S(1)} %get-tuple-element.183.args_0_.args_3_, ...), custom_call_target="tpu_custom_call" | custom-call | flops 5898240 | bytes 5898240 | tf_op jit(solution)/shard_map/pallas_call | solution.py:448
  39.9 0.0 collective-permute-done.12
  39.9 2.3 %collective-permute-done.13 = f32[4,16,384]{2,1,0:T(8,128)S(1)} collective-permute-done((f32[4,16,384]{2,1,0:T(8,128)S(1)}, f32[4,16,384]{2,1,0:T(8,128)S(1)}, u32[]{:S(2)}, u32[]{:S(2)}) %collective-permute-start.13) | collective-permute-done | bytes 98336 | tf_op jit(solution)/shard_map/ppermute | solution.py:446
  42.2 0.7 %fusion = f32[8,16,384]{2,1,0:T(8,128)} fusion(f32[4,16,384]{2,1,0:T(8,128)S(1)} %bitcast.12, f32[4,16,384]{2,1,0:T(8,128)S(1)} %bitcast.11, f32[4,16,384]{2,1,0:T(8,128)S(1)} %collective-permute-done.13, f32[4,16,384]{2,1,0:T(8,128)S(1)} %collective-permute-done.10, f32[1,8,16,384]{3,2,1,0:T(8,128)S(1)} %get-tuple-element.205), kind=kLoop, calls=%fused_computation.1 | loop fusion | flops 196608 | bytes 786432 | tf_op jit(solution)/shard_map/add | solution.py:459
  (6 shorter events, 0.1 us)
Async XLA Ops:
  0.6 14.1 %copy-start = (f32[8,64,384]{2,1,0:T(8,128)S(1)}, f32[8,64,384]{2,1,0:T(8,128)}, u32[]{:S(2)}) copy-start(f32[8,64,384]{2,1,0:T(8,128)} %p0.3) | copy-start | bytes 2359300
  0.6 14.1 %copy-start.1 = (f32[8,64,384]{2,1,0:T(8,128)S(1)}, f32[8,64,384]{2,1,0:T(8,128)}, u32[]{:S(2)}) copy-start(f32[8,64,384]{2,1,0:T(8,128)} %src.3) | copy-start | bytes 2359300
  0.7 14.1 %copy-start.2 = (f32[8,64,384]{2,1,0:T(8,128)S(1)}, f32[8,64,384]{2,1,0:T(8,128)}, u32[]{:S(2)}) copy-start(f32[8,64,384]{2,1,0:T(8,128)} %obs.3) | copy-start | bytes 2359300
  2.6 16.5 %collective-permute-start.1 = (f32[10,3,32,128]{3,2,1,0:T(8,128)S(1)}, f32[10,3,32,128]{3,2,1,0:T(8,128)S(1)}, u32[]{:S(2)}, u32[]{:S(2)}) collective-permute-start(f32[10,3,32,128]{3,2,1,0:T(8,128)S(1)} %get-tuple-element.107), channel_id=1, source_target_pairs={{0,4},{4,8},{8,12},{1,5},{5,9},{9,13},{2,6},{6,10},{10,14},{3,7},{... | collective-permute-start | bytes 1474568 | tf_op jit(solution)/shard_map/ppermute | solution.py:368
  7.5 16.0 %collective-permute-start.2 = (f32[10,3,32,128]{3,2,1,0:T(8,128)S(1)}, f32[10,3,32,128]{3,2,1,0:T(8,128)S(1)}, u32[]{:S(2)}, u32[]{:S(2)}) collective-permute-start(f32[10,3,32,128]{3,2,1,0:T(8,128)S(1)} %get-tuple-element.108), channel_id=1, source_target_pairs={{4,0},{8,4},{12,8},{5,1},{9,5},{13,9},{6,2},{10,6},{14,10},{7,3},{... | collective-permute-start | bytes 1474568 | tf_op jit(solution)/shard_map/ppermute | solution.py:369
  8.8 17.6 %collective-permute-start = (f32[4,3,64,128]{3,2,1,0:T(8,128)S(1)}, f32[4,3,64,128]{3,2,1,0:T(8,128)S(1)}, u32[]{:S(2)}, u32[]{:S(2)}) collective-permute-start(f32[4,3,64,128]{3,2,1,0:T(8,128)S(1)} %get-tuple-element.106), channel_id=1, source_target_pairs={{0,4},{4,8},{8,12},{1,5},{5,9},{9,13},{2,6},{6,10},{10,14},{3,7},{... | collective-permute-start | bytes 1179656 | tf_op jit(solution)/shard_map/ppermute | solution.py:370
  13.4 17.3 %collective-permute-start.5 = (f32[4,3,64,128]{3,2,1,0:T(8,128)S(1)}, f32[4,3,64,128]{3,2,1,0:T(8,128)S(1)}, u32[]{:S(2)}, u32[]{:S(2)}) collective-permute-start(f32[4,3,64,128]{3,2,1,0:T(8,128)S(1)} %get-tuple-element.145), channel_id=1, source_target_pairs={{4,0},{8,4},{12,8},{5,1},{9,5},{13,9},{6,2},{10,6},{14,10},{7,3},{... | collective-permute-start | bytes 1179656 | tf_op jit(solution)/shard_map/ppermute | solution.py:371
  23.6 2.8 %collective-permute-start.4 = (f32[6,3,32,128]{3,2,1,0:T(8,128)S(1)}, f32[6,3,32,128]{3,2,1,0:T(8,128)S(1)}, u32[]{:S(2)}, u32[]{:S(2)}) collective-permute-start(f32[6,3,32,128]{3,2,1,0:T(8,128)S(1)} %slice.13), channel_id=1, source_target_pairs={{0,1},{1,0},{2,3},{3,2},{4,5},{5,4},{6,7},{7,6},{8,9},{9,8},{10,11... | collective-permute-start | bytes 884744 | tf_op jit(solution)/shard_map/ppermute | solution.py:406
  23.7 7.0 %collective-permute-start.7 = (f32[6,3,32,128]{3,2,1,0:T(8,128)S(1)}, f32[6,3,32,128]{3,2,1,0:T(8,128)S(1)}, u32[]{:S(2)}, u32[]{:S(2)}) collective-permute-start(f32[6,3,32,128]{3,2,1,0:T(8,128)S(1)} %slice.15), channel_id=1, source_target_pairs={{0,1},{1,0},{2,3},{3,2},{4,5},{5,4},{6,7},{7,6},{8,9},{9,8},{10,11... | collective-permute-start | bytes 884744 | tf_op jit(solution)/shard_map/ppermute | solution.py:406
  24.3 2.1 %collective-permute-start.3 = (f32[4,3,32,128]{3,2,1,0:T(8,128)S(1)}, f32[4,3,32,128]{3,2,1,0:T(8,128)S(1)}, u32[]{:S(2)}, u32[]{:S(2)}) collective-permute-start(f32[4,3,32,128]{3,2,1,0:T(8,128)S(1)} %slice.12), channel_id=1, source_target_pairs={{0,1},{1,0},{2,3},{3,2},{4,5},{5,4},{6,7},{7,6},{8,9},{9,8},{10,11... | collective-permute-start | bytes 589832 | tf_op jit(solution)/shard_map/ppermute | solution.py:406
  26.4 4.4 %collective-permute-start.6 = (f32[4,3,32,128]{3,2,1,0:T(8,128)S(1)}, f32[4,3,32,128]{3,2,1,0:T(8,128)S(1)}, u32[]{:S(2)}, u32[]{:S(2)}) collective-permute-start(f32[4,3,32,128]{3,2,1,0:T(8,128)S(1)} %slice.14), channel_id=1, source_target_pairs={{0,1},{1,0},{2,3},{3,2},{4,5},{5,4},{6,7},{7,6},{8,9},{9,8},{10,11... | collective-permute-start | bytes 589832 | tf_op jit(solution)/shard_map/ppermute | solution.py:406
  30.1 1.9 %collective-permute-start.8 = (f32[1,4,16,384]{3,2,1,0:T(8,128)S(1)}, f32[1,4,16,384]{3,2,1,0:T(8,128)S(1)}, u32[]{:S(2)}, u32[]{:S(2)}) collective-permute-start(f32[1,4,16,384]{3,2,1,0:T(8,128)S(1)} %get-tuple-element.178), channel_id=1, source_target_pairs={{0,1},{1,0},{2,3},{3,2},{4,5},{5,4},{6,7},{7,6},{8,9},{9,8},{10,11... | collective-permute-start | bytes 294920 | tf_op jit(solution)/shard_map/ppermute | solution.py:417
  30.7 1.3 %collective-permute-start.9 = (f32[1,4,16,384]{3,2,1,0:T(8,128)S(1)}, f32[1,4,16,384]{3,2,1,0:T(8,128)S(1)}, u32[]{:S(2)}, u32[]{:S(2)}) collective-permute-start(f32[1,4,16,384]{3,2,1,0:T(8,128)S(1)} %get-tuple-element.179), channel_id=1, source_target_pairs={{0,1},{1,0},{2,3},{3,2},{4,5},{5,4},{6,7},{7,6},{8,9},{9,8},{10,11... | collective-permute-start | bytes 294920 | tf_op jit(solution)/shard_map/ppermute | solution.py:417
  32.0 5.2 %collective-permute-start.10 = (f32[4,16,384]{2,1,0:T(8,128)S(1)}, f32[4,16,384]{2,1,0:T(8,128)S(1)}, u32[]{:S(2)}, u32[]{:S(2)}) collective-permute-start(f32[4,16,384]{2,1,0:T(8,128)S(1)} %add_bitcast_fusion.1), channel_id=1, source_target_pairs={{0,2},{1,3},{2,0},{3,1},{4,6},{5,7},{6,4},{7,5},{8,10},{9,11},{10,... | collective-permute-start | bytes 294920 | tf_op jit(solution)/shard_map/ppermute | solution.py:412
  35.9 1.5 %collective-permute-start.11 = (f32[1,4,16,384]{3,2,1,0:T(8,128)S(1)}, f32[1,4,16,384]{3,2,1,0:T(8,128)S(1)}, u32[]{:S(2)}, u32[]{:S(2)}) collective-permute-start(f32[1,4,16,384]{3,2,1,0:T(8,128)S(1)} %get-tuple-element.202), channel_id=1, source_target_pairs={{0,1},{1,0},{2,3},{3,2},{4,5},{5,4},{6,7},{7,6},{8,9},{9,8},{10,11... | collective-permute-start | bytes 294920 | tf_op jit(solution)/shard_map/ppermute | solution.py:417
  36.1 3.8 %collective-permute-start.12 = (f32[1,4,16,384]{3,2,1,0:T(8,128)S(1)}, f32[1,4,16,384]{3,2,1,0:T(8,128)S(1)}, u32[]{:S(2)}, u32[]{:S(2)}) collective-permute-start(f32[1,4,16,384]{3,2,1,0:T(8,128)S(1)} %get-tuple-element.207), channel_id=1, source_target_pairs={{0,1},{1,0},{2,3},{3,2},{4,5},{5,4},{6,7},{7,6},{8,9},{9,8},{10,11... | collective-permute-start | bytes 294920 | tf_op jit(solution)/shard_map/ppermute | solution.py:417
  37.5 4.8 %collective-permute-start.13 = (f32[4,16,384]{2,1,0:T(8,128)S(1)}, f32[4,16,384]{2,1,0:T(8,128)S(1)}, u32[]{:S(2)}, u32[]{:S(2)}) collective-permute-start(f32[4,16,384]{2,1,0:T(8,128)S(1)} %add_bitcast_fusion), channel_id=1, source_target_pairs={{0,2},{1,3},{2,0},{3,1},{4,6},{5,7},{6,4},{7,5},{8,10},{9,11},{10,... | collective-permute-start | bytes 294920 | tf_op jit(solution)/shard_map/ppermute | solution.py:446

commit v8 on v7

--- a/solution.py
+++ b/solution.py
@@ -9,7 +9,8 @@
 
 SWEEPS = 3
 HALO = SWEEPS + 1
-EDGE = HALO + 2 * SWEEPS
+SLOTS = HALO // 2
+EDGE = SLOTS + 2 * SWEEPS
 FIELDS = 16
 LANES = 128
 SUB = 8
@@ -178,7 +179,9 @@
 def first_kernel(log_perm, noise, p0, src, obs, K, up, down, top, bottom, means, draws, sems):
     slab, nx, ny = log_perm.shape
     tiles, half = ny // LANES, nx // 2
-    rows = pl.ds(pl.multiple_of(half * (lax.axis_index("draw") % 2), half), half)
+    draw, quarter = lax.axis_index("draw"), half // 2
+    rows = pl.ds(pl.multiple_of(half * (draw % 2), half), half)
+    few = pl.ds(pl.multiple_of(half * (draw % 2) + quarter * (draw // 2 % 2), quarter), quarter)
     copies = []
 
     def copy(src_ref, dst_ref):
@@ -188,11 +191,15 @@
     copy(noise, draws)
     for c in range(tiles):
         cols = pl.ds(c * LANES, LANES)
-        at = 0
-        for ref, width in ((p0, HALO), (src, SWEEPS), (obs, SWEEPS)):
-            for start, out in ((slab - width, up), (0, down)):
-                copy(ref.at[pl.ds(start, width), rows, cols], out.at[pl.ds(at, width), c])
-            at += width
+        for start, out in ((slab - HALO, up), (0, down)):
+            for h in range(2):
+                planes = pl.ds(start + h * SLOTS, SLOTS)
+                copy(p0.at[planes, few, cols], out.at[pl.ds(0, SLOTS), c, pl.ds(h * quarter, quarter)])
+        at = SLOTS
+        for ref in (src, obs):
+            for start, out in ((slab - SWEEPS, up), (0, down)):
+                copy(ref.at[pl.ds(start, SWEEPS), rows, cols], out.at[pl.ds(at, SWEEPS), c])
+            at += SWEEPS
     for cp in copies:
         cp.start()
     for cp in copies[:2]:
@@ -257,19 +264,21 @@
 
     pairs = []
     if halos:
-        k, mine, *theirs = halos
+        k, mine, beside, theirs, theirs_beside, theirs_rest = halos
         pairs.append((k, K.at[pl.ds(0 if low else top, HALO)]))
-        for half_rows, which in ((None, par), (theirs, 1 - par)):
+        quarter, across = half // 2, lax.axis_index("draw") // 2 % 2
+        pieces = ((mine, par, across), (beside, par, 1 - across), (theirs, 1 - par, across))
+        for ref, which, part in (*pieces, (theirs_beside, 1 - par, 1 - across)):
+            slots = pl.ds(0 if low or ref is mine else SLOTS, SLOTS)
+            rows = pl.ds(pl.multiple_of(half * which + quarter * part, quarter), quarter)
+            for h in range(2):
+                planes = pl.ds((0 if low else top) + h * SLOTS, SLOTS)
+                pairs.append((ref.at[slots, :, pl.ds(h * quarter, quarter)], P0.at[planes, :, rows]))
+        for ref, which, first in ((mine, par, SLOTS), (theirs_rest, 1 - par, 0)):
             rows = pl.ds(pl.multiple_of(half * which, half), half)
-            first = 0
-            for field, width in ((P0, HALO), (SRC, SWEEPS), (OBS, SWEEPS)):
-                planes = pl.ds(HALO - width if low else top, width)
-                if half_rows is None:
-                    ref = mine.at[pl.ds(first, width)]
-                else:
-                    ref = theirs[0] if first == 0 else theirs[1].at[pl.ds(first - HALO, width)]
-                pairs.append((ref, field.at[planes, :, rows]))
-                first += width
+            planes = pl.ds(HALO - SWEEPS if low else top, SWEEPS)
+            for n, field in enumerate((SRC, OBS)):
+                pairs.append((ref.at[pl.ds(first + n * SWEEPS, SWEEPS)], field.at[planes, :, rows]))
     copies = [pltpu.make_async_copy(a, b, sems.at[i]) for i, (a, b) in enumerate(pairs)]
     for cp in copies:
         cp.start()
@@ -361,7 +370,7 @@
         out_shape=(field, edge, edge, rim, rim),
         in_specs=[OFFCHIP] * 5,
         out_specs=(ONCHIP,) * 5,
-        scratch_shapes=[pltpu.VMEM((slab, nx, ny), f32)] * 2 + [pltpu.SemaphoreType.DMA((2 + 6 * tiles,))],
+        scratch_shapes=[pltpu.VMEM((slab, nx, ny), f32)] * 2 + [pltpu.SemaphoreType.DMA((2 + 8 * tiles,))],
         compiler_params=params,
         cost_estimate=pl.CostEstimate(flops=cells, bytes_accessed=20 * cells, transcendentals=cells),
     )(*[pltpu.with_memory_space_constraint(a, pltpu.HBM) for a in inputs])
@@ -393,7 +402,7 @@
             out_shape=(*kinds, *ends),
             in_specs=[ONCHIP] * (n + FIELDS),
             out_specs=(ONCHIP,) * (FIELDS + len(ends)),
-            scratch_shapes=[pltpu.SemaphoreType.DMA((8,))],
+            scratch_shapes=[pltpu.SemaphoreType.DMA((13,))],
             input_output_aliases={n + i: i for i in range(FIELDS)},
             compiler_params=params,
             cost_estimate=pl.CostEstimate(flops=work, bytes_accessed=work, transcendentals=0),
@@ -402,10 +411,11 @@
 
     alo, ahi, last = lax.optimization_barrier((alo, ahi, fields[-1]))
     fields = (*fields[:-1], last)
-    lower, upper = [
-        (k, mine, *[lax.ppermute(mine[a:b], "draw", pair) for a, b in ((0, HALO), (HALO, EDGE))])
-        for k, mine in ((klo, alo), (khi, ahi))
-    ]
+    own = jnp.concatenate([alo[:SLOTS], ahi[:SLOTS]], axis=0)
+    beside = lax.ppermute(own, "draw", [(i, i ^ 2) for i in range(draws)])
+    from_core = [lax.ppermute(a, "draw", pair) for a in (own, beside)]
+    lower = (klo, alo, beside, *from_core, lax.ppermute(alo[SLOTS:], "draw", pair))
+    upper = (khi, ahi, beside, *from_core, lax.ppermute(ahi[SLOTS:], "draw", pair))
 
     def onward(keep, got):
         return [

time: 43.2 us -> 44.8 us (1.037)
  waiting for transfers between devices: 10.9 us -> 12.4 us
    ppermute x4 -> x5, waiting for transfers between devices: 0.01 us -> 2.93 us  [the longest x1 1.49 us: local(): beside = lax.ppermute(own, 'draw', [(i, i ^ 2) for i in range(draws)])]
    ppermute x4 -> x5, starting transfers between devices: 0.71 us -> 2.19 us  [the longest x1 1.56 us: local(): beside = lax.ppermute(own, 'draw', [(i, i ^ 2) for i in range(draws)])]
    ppermute x1, waiting for transfers between devices: 4.46 us -> 2.99 us  [local(): ahi = lax.ppermute(to_down, 'space', down)]
    ppermute x1, waiting for transfers between devices: 2.01 us -> 0.7 us  [local(): klo = lax.ppermute(top, 'space', up)]
    ppermute x1, waiting for transfers between devices: 0.01 us -> 1.26 us  [local(): khi = lax.ppermute(bottom, 'space', down)]
    ppermute x1, starting transfers between devices: 1.56 us -> 0.6 us  [onward(): lax.ppermute(keep[s - 1] + got[s - 1], 'draw', [(j, (j + 2 * s) % draws)...]
    ppermute x1, waiting for transfers between devices: 1.39 us -> 0.59 us  [local(): alo = lax.ppermute(to_up, 'space', up)]
    ppermute x1, starting transfers between devices: 1.56 us -> 1.02 us  [local(): lax.ppermute(a, 'draw', [(j, (j + 2 * s) % draws) for j in range(draws)])]
  transfers between devices with their start and end apart: 14 -> 15, of which waited for: 5 -> 8; matrix products, arithmetic and copies ran while one was open for 0% -> 0% of each run, Pallas kernels for 26% -> 26%
where the time goes in v8:
time: 44.8 us; the launch traced here: 44.6 us
  starting transfers between devices  17 us (38%)
  Pallas kernels  13.5 us (30%)
  waiting for transfers between devices  12.4 us (28%)
  between operations  0.88 us (2%)
  other arithmetic  0.75 us (2%)
    pallas_call x4, Pallas kernels, side(): pl.pallas_call(functools.partial(side_kernel, low, stages, [part[:-1] for...  7.42 us
    ppermute x1, starting transfers between devices, local(): alo = lax.ppermute(to_up, 'space', up)  4.95 us
    ppermute x1, starting transfers between devices, local(): klo = lax.ppermute(top, 'space', up)  4.57 us
    ppermute x1, waiting for transfers between devices, local(): ahi = lax.ppermute(to_down, 'space', down)  2.99 us
    pallas_call x1, Pallas kernels, local(): pl.pallas_call(inner_kernel, out_shape=(*kinds[1:], mid), in_specs=[ONCHI...  2.97 us
    ppermute x1, waiting for transfers between devices, local(): lax.ppermute(a, 'draw', [(j, (j + 2 * s) % draws) for j in range(draws)])  2.74 us
    pallas_call x1, Pallas kernels, local(): pl.pallas_call(first_kernel, out_shape=(field, edge, edge, rim, rim), in_...  1.97 us
    ppermute x1, starting transfers between devices, local(): beside = lax.ppermute(own, 'draw', [(i, i ^ 2) for i in range(draws)])  1.56 us
  transfers between devices with their start and end apart: 15, of which 8 were waited for; matrix products, arithmetic and copies ran while one was open for 0% of the time, Pallas kernels for 26%

profile of v8, /device:TPU:0, one launch (start us, length us, event | category | flops | bytes accessed | tf_op | source)
XLA Modules:
  0.0 44.6 jit_solution(18108718765282528965)
XLA Ops:
  0.6 0.0 copy-start
  0.6 0.0 copy-start.1
  0.7 0.0 copy-start.2
  0.7 2.0 %shard_map.68 = (f32[16,3,64,128]{3,2,1,0:T(8,128)S(1)}, f32[8,3,32,128]{3,2,1,0:T(8,128)S(1)}, f32[8,3,32,128]{3,2,1,0:T(8,128)S(1)}, f32[4,3,64,128]{3,2,1,0:T(8,128)S(1)}, f32[4,3,64,128]{3,2,1,0:T(8,128)S(1)}) custom-call(f32[8,64,384]{2,1,0:T(8,128)} %log_perm.1, f32[8,64,384]{2,1,0:T(8,128)} %bitcast.10, f32[8,64,384]{2,1,0:T(8,128)} %p0.3, ...), custom_call_target="tpu_custom_call" | custom-call | flops 196608 | bytes 3932160 | tf_op jit(solution)/shard_map/pallas_call | solution.py:368
  2.6 5.0 %collective-permute-start.1 = (f32[8,3,32,128]{3,2,1,0:T(8,128)S(1)}, f32[8,3,32,128]{3,2,1,0:T(8,128)S(1)}, u32[]{:S(2)}, u32[]{:S(2)}) collective-permute-start(f32[8,3,32,128]{3,2,1,0:T(8,128)S(1)} %get-tuple-element.107), channel_id=1, source_target_pairs={{0,4},{4,8},{8,12},{1,5},{5,9},{9,13},{2,6},{6,10},{10,14},{3,7},{... | collective-permute-start | bytes 1179656 | tf_op jit(solution)/shard_map/ppermute | solution.py:377
  7.6 1.3 %collective-permute-start.2 = (f32[8,3,32,128]{3,2,1,0:T(8,128)S(1)}, f32[8,3,32,128]{3,2,1,0:T(8,128)S(1)}, u32[]{:S(2)}, u32[]{:S(2)}) collective-permute-start(f32[8,3,32,128]{3,2,1,0:T(8,128)S(1)} %get-tuple-element.108), channel_id=1, source_target_pairs={{4,0},{8,4},{12,8},{5,1},{9,5},{13,9},{6,2},{10,6},{14,10},{7,3},{... | collective-permute-start | bytes 1179656 | tf_op jit(solution)/shard_map/ppermute | solution.py:378
  8.9 4.6 %collective-permute-start = (f32[4,3,64,128]{3,2,1,0:T(8,128)S(1)}, f32[4,3,64,128]{3,2,1,0:T(8,128)S(1)}, u32[]{:S(2)}, u32[]{:S(2)}) collective-permute-start(f32[4,3,64,128]{3,2,1,0:T(8,128)S(1)} %get-tuple-element.106), channel_id=1, source_target_pairs={{0,4},{4,8},{8,12},{1,5},{5,9},{9,13},{2,6},{6,10},{10,14},{3,7},{... | collective-permute-start | bytes 1179656 | tf_op jit(solution)/shard_map/ppermute | solution.py:379
  13.5 0.0 copy-done
  13.5 0.0 copy-done.1
  13.5 0.0 copy-done.2
  13.5 3.0 %shard_map.69 = (f32[16,3,64,128]{3,2,1,0:T(8,128)S(1)}, f32[16,3,64,128]{3,2,1,0:T(8,128)S(1)}, f32[16,3,64,128]{3,2,1,0:T(8,128)S(1)}, f32[16,3,64,128]{3,2,1,...) custom-call(f32[16,3,64,128]{3,2,1,0:T(8,128)S(1)} %get-tuple-elemen, ...), custom_call_target="tpu_custom_call" | custom-call | flops 39321600 | bytes 11796480 | tf_op jit(solution)/shard_map/pallas_call | solution.py:381
  16.5 0.6 %collective-permute-done.1.args_1_ = f32[8,3,32,128]{3,2,1,0:T(8,128)S(1)} collective-permute-done((f32[8,3,32,128]{3,2,1,0:T(8,128)S(1)}, f32[8,3,32,128]{3,2,1,0:T(8,128)S(1)}, u32[]{:S(2)}, u32[]{:S(2)}) %collective-permute-start.1) | collective-permute-done | bytes 393248 | tf_op jit(solution)/shard_map/ppermute | solution.py:377
  17.1 3.0 %collective-permute-done.2.args_1_ = f32[8,3,32,128]{3,2,1,0:T(8,128)S(1)} collective-permute-done((f32[8,3,32,128]{3,2,1,0:T(8,128)S(1)}, f32[8,3,32,128]{3,2,1,0:T(8,128)S(1)}, u32[]{:S(2)}, u32[]{:S(2)}) %collective-permute-start.2) | collective-permute-done | bytes 393248 | tf_op jit(solution)/shard_map/ppermute | solution.py:378
  20.1 1.6 %collective-permute-start.3 = (f32[4,3,32,128]{3,2,1,0:T(8,128)S(1)}, f32[4,3,32,128]{3,2,1,0:T(8,128)S(1)}, u32[]{:S(2)}, u32[]{:S(2)}) collective-permute-start(f32[4,3,32,128]{3,2,1,0:T(8,128)S(1)} %pad_maximum_fusion), channel_id=1, source_target_pairs={{0,2},{1,3},{2,0},{3,1},{4,6},{5,7},{6,4},{7,5},{8,10},{9,11},{10,... | collective-permute-start | bytes 589832 | tf_op jit(solution)/shard_map/ppermute | solution.py:415
  21.7 1.3 %collective-permute-start.7 = (f32[4,3,64,128]{3,2,1,0:T(8,128)S(1)}, f32[4,3,64,128]{3,2,1,0:T(8,128)S(1)}, u32[]{:S(2)}, u32[]{:S(2)}) collective-permute-start(f32[4,3,64,128]{3,2,1,0:T(8,128)S(1)} %get-tuple-element.146), channel_id=1, source_target_pairs={{4,0},{8,4},{12,8},{5,1},{9,5},{13,9},{6,2},{10,6},{14,10},{7,3},{... | collective-permute-start | bytes 1179656 | tf_op jit(solution)/shard_map/ppermute | solution.py:380
  23.0 0.1 collective-permute-start.6
  23.1 0.6 %collective-permute-start.8 = (f32[6,3,32,128]{3,2,1,0:T(8,128)S(1)}, f32[6,3,32,128]{3,2,1,0:T(8,128)S(1)}, u32[]{:S(2)}, u32[]{:S(2)}) collective-permute-start(f32[6,3,32,128]{3,2,1,0:T(8,128)S(1)} %slice.15), channel_id=1, source_target_pairs={{0,1},{1,0},{2,3},{3,2},{4,5},{5,4},{6,7},{7,6},{8,9},{9,8},{10,11... | collective-permute-start | bytes 884744 | tf_op jit(solution)/shard_map/ppermute | solution.py:418
  23.7 0.7 %collective-permute-done.args_0_ = f32[4,3,64,128]{3,2,1,0:T(8,128)S(1)} collective-permute-done((f32[4,3,64,128]{3,2,1,0:T(8,128)S(1)}, f32[4,3,64,128]{3,2,1,0:T(8,128)S(1)}, u32[]{:S(2)}, u32[]{:S(2)}) %collective-permute-start) | collective-permute-done | bytes 393248 | tf_op jit(solution)/shard_map/ppermute | solution.py:379
  24.4 0.0 collective-permute-start.4
  24.4 1.5 %collective-permute-done.3.args_2_ = f32[4,3,32,128]{3,2,1,0:T(8,128)S(1)} collective-permute-done((f32[4,3,32,128]{3,2,1,0:T(8,128)S(1)}, f32[4,3,32,128]{3,2,1,0:T(8,128)S(1)}, u32[]{:S(2)}, u32[]{:S(2)}) %collective-permute-start.3) | collective-permute-done | bytes 196640 | tf_op jit(solution)/shard_map/ppermute | solution.py:415
  25.9 0.0 collective-permute-start.5
  25.9 0.0 collective-permute-done.4.args_3_
  25.9 0.0 collective-permute-done.6.args_5_
  25.9 1.4 %collective-permute-done.5.args_4_ = f32[4,3,32,128]{3,2,1,0:T(8,128)S(1)} collective-permute-done((f32[4,3,32,128]{3,2,1,0:T(8,128)S(1)}, f32[4,3,32,128]{3,2,1,0:T(8,128)S(1)}, u32[]{:S(2)}, u32[]{:S(2)}) %collective-permute-start.5) | collective-permute-done | bytes 196640 | tf_op jit(solution)/shard_map/ppermute | solution.py:416
  27.3 2.1 %shard_map.70 = (f32[16,3,64,128]{3,2,1,0:T(8,128)S(1)}, f32[16,3,64,128]{3,2,1,0:T(8,128)S(1)}, f32[16,3,64,128]{3,2,1,0:T(8,128)S(1)}, f32[16,3,64,128]{3,2,1,...) custom-call(f32[4,3,64,128]{3,2,1,0:T(8,128)S(1)} %collective-permut, ...), custom_call_target="tpu_custom_call", output_to_operand_aliasing={{0}: (6, {}), {1}: (7, {}), {2}: (8, {}), {3}: (9, {}), {4}... | custom-call | flops 1 | bytes 1 | tf_op jit(solution)/shard_map/pallas_call | solution.py:400
  29.4 1.6 %shard_map.71 = (f32[16,3,64,128]{3,2,1,0:T(8,128)S(1)}, f32[16,3,64,128]{3,2,1,0:T(8,128)S(1)}, f32[16,3,64,128]{3,2,1,0:T(8,128)S(1)}, f32[16,3,64,128]{3,2,1,...) custom-call(f32[16,3,64,128]{3,2,1,0:T(8,128)S(1)} %get-tuple-elemen, ...), custom_call_target="tpu_custom_call", output_to_operand_aliasing={{0}: (0, {}), {1}: (1, {}), {2}: (2, {}), {3}: (3, {}), {4}... | custom-call | flops 1 | bytes 1 | tf_op jit(solution)/shard_map/pallas_call | solution.py:400
  31.1 0.2 collective-permute-start.10
  31.3 0.4 collective-permute-start.9
  31.7 1.3 %collective-permute-done.7.args_0_ = f32[4,3,64,128]{3,2,1,0:T(8,128)S(1)} collective-permute-done((f32[4,3,64,128]{3,2,1,0:T(8,128)S(1)}, f32[4,3,64,128]{3,2,1,0:T(8,128)S(1)}, u32[]{:S(2)}, u32[]{:S(2)}) %collective-permute-start.7) | collective-permute-done | bytes 393248 | tf_op jit(solution)/shard_map/ppermute | solution.py:380
  32.9 0.0 collective-permute-done.8.args_5_
  32.9 1.3 %shard_map.72 = (f32[16,3,64,128]{3,2,1,0:T(8,128)S(1)}, f32[16,3,64,128]{3,2,1,0:T(8,128)S(1)}, f32[16,3,64,128]{3,2,1,0:T(8,128)S(1)}, f32[16,3,64,128]{3,2,1,...) custom-call(f32[4,3,64,128]{3,2,1,0:T(8,128)S(1)} %collective-permut, ...), custom_call_target="tpu_custom_call", output_to_operand_aliasing={{0}: (6, {}), {1}: (7, {}), {2}: (8, {}), {3}: (9, {}), {4}... | custom-call | flops 11796480 | bytes 11796480 | tf_op jit(solution)/shard_map/pallas_call | solution.py:400
  34.2 0.0 collective-permute-done.10
  34.2 0.0 collective-permute-done.9
  34.3 0.6 %collective-permute-start.11 = (f32[4,16,384]{2,1,0:T(8,128)S(1)}, f32[4,16,384]{2,1,0:T(8,128)S(1)}, u32[]{:S(2)}, u32[]{:S(2)}) collective-permute-start(f32[4,16,384]{2,1,0:T(8,128)S(1)} %add_bitcast_fusion.1), channel_id=1, source_target_pairs={{0,2},{1,3},{2,0},{3,1},{4,6},{5,7},{6,4},{7,5},{8,10},{9,11},{10,... | collective-permute-start | bytes 294920 | tf_op jit(solution)/shard_map/ppermute | solution.py:422
  34.9 2.4 %shard_map.73 = (f32[16,3,64,128]{3,2,1,0:T(8,128)S(1)}, f32[16,3,64,128]{3,2,1,0:T(8,128)S(1)}, f32[16,3,64,128]{3,2,1,0:T(8,128)S(1)}, f32[16,3,64,128]{3,2,1,...) custom-call(f32[16,3,64,128]{3,2,1,0:T(8,128)S(1)} %get-tuple-elemen, ...), custom_call_target="tpu_custom_call", output_to_operand_aliasing={{0}: (0, {}), {1}: (1, {}), {2}: (2, {}), {3}: (3, {}), {4}... | custom-call | flops 11796480 | bytes 11796480 | tf_op jit(solution)/shard_map/pallas_call | solution.py:400
  37.2 0.1 collective-permute-start.12
  37.3 0.5 %collective-permute-start.13 = (f32[1,4,16,384]{3,2,1,0:T(8,128)S(1)}, f32[1,4,16,384]{3,2,1,0:T(8,128)S(1)}, u32[]{:S(2)}, u32[]{:S(2)}) collective-permute-start(f32[1,4,16,384]{3,2,1,0:T(8,128)S(1)} %get-tuple-element.207), channel_id=1, source_target_pairs={{0,1},{1,0},{2,3},{3,2},{4,5},{5,4},{6,7},{7,6},{8,9},{9,8},{10,11... | collective-permute-start | bytes 294920 | tf_op jit(solution)/shard_map/ppermute | solution.py:427
  37.8 1.1 %collective-permute-done.11 = f32[4,16,384]{2,1,0:T(8,128)S(1)} collective-permute-done((f32[4,16,384]{2,1,0:T(8,128)S(1)}, f32[4,16,384]{2,1,0:T(8,128)S(1)}, u32[]{:S(2)}, u32[]{:S(2)}) %collective-permute-start.11) | collective-permute-done | bytes 98336 | tf_op jit(solution)/shard_map/ppermute | solution.py:422
  38.9 0.2 shard_map.74
  39.1 0.0 collective-permute-done.12
  39.2 1.0 %collective-permute-start.14 = (f32[4,16,384]{2,1,0:T(8,128)S(1)}, f32[4,16,384]{2,1,0:T(8,128)S(1)}, u32[]{:S(2)}, u32[]{:S(2)}) collective-permute-start(f32[4,16,384]{2,1,0:T(8,128)S(1)} %add_bitcast_fusion), channel_id=1, source_target_pairs={{0,2},{1,3},{2,0},{3,1},{4,6},{5,7},{6,4},{7,5},{8,10},{9,11},{10,... | collective-permute-start | bytes 294920 | tf_op jit(solution)/shard_map/ppermute | solution.py:456
  40.2 0.9 %shard_map.75 = (f32[8,64,384]{2,1,0:T(8,128)}, f32[1,8,16,384]{3,2,1,0:T(8,128)S(1)}) custom-call(f32[3,64,384]{2,1,0:T(8,128)S(1)} %get-tuple-element.144.args_0_, f32[2,64,384]{2,1,0:T(8,128)S(1)} %get-tuple-element.145.args_1_, f32[3,64,384]{2,1,0:T(8,128)S(1)} %get-tuple-element.182.args_2_, f32[16,3,64,128]{3,2,1,0:T(8,128)S(1)} %get-tuple-element.183.args_0_.args_3_, ...), custom_call_target="tpu_custom_call" | custom-call | flops 5898240 | bytes 5898240 | tf_op jit(solution)/shard_map/pallas_call | solution.py:458
  41.1 0.0 collective-permute-done.13
  41.1 2.7 %collective-permute-done.14 = f32[4,16,384]{2,1,0:T(8,128)S(1)} collective-permute-done((f32[4,16,384]{2,1,0:T(8,128)S(1)}, f32[4,16,384]{2,1,0:T(8,128)S(1)}, u32[]{:S(2)}, u32[]{:S(2)}) %collective-permute-start.14) | collective-permute-done | bytes 98336 | tf_op jit(solution)/shard_map/ppermute | solution.py:456
  43.8 0.7 %fusion = f32[8,16,384]{2,1,0:T(8,128)} fusion(f32[4,16,384]{2,1,0:T(8,128)S(1)} %bitcast.12, f32[4,16,384]{2,1,0:T(8,128)S(1)} %bitcast.11, f32[4,16,384]{2,1,0:T(8,128)S(1)} %collective-permute-done.14, f32[4,16,384]{2,1,0:T(8,128)S(1)} %collective-permute-done.11, f32[1,8,16,384]{3,2,1,0:T(8,128)S(1)} %get-tuple-element.205), kind=kLoop, calls=%fused_computation.2 | loop fusion | flops 196608 | bytes 786432 | tf_op jit(solution)/shard_map/add | solution.py:469
  (7 shorter events, 0.1 us)
Async XLA Ops:
  0.6 12.8 %copy-start = (f32[8,64,384]{2,1,0:T(8,128)S(1)}, f32[8,64,384]{2,1,0:T(8,128)}, u32[]{:S(2)}) copy-start(f32[8,64,384]{2,1,0:T(8,128)} %p0.3) | copy-start | bytes 2359300
  0.6 12.8 %copy-start.1 = (f32[8,64,384]{2,1,0:T(8,128)S(1)}, f32[8,64,384]{2,1,0:T(8,128)}, u32[]{:S(2)}) copy-start(f32[8,64,384]{2,1,0:T(8,128)} %src.3) | copy-start | bytes 2359300
  0.7 12.8 %copy-start.2 = (f32[8,64,384]{2,1,0:T(8,128)S(1)}, f32[8,64,384]{2,1,0:T(8,128)}, u32[]{:S(2)}) copy-start(f32[8,64,384]{2,1,0:T(8,128)} %obs.3) | copy-start | bytes 2359300
  2.6 14.4 %collective-permute-start.1 = (f32[8,3,32,128]{3,2,1,0:T(8,128)S(1)}, f32[8,3,32,128]{3,2,1,0:T(8,128)S(1)}, u32[]{:S(2)}, u32[]{:S(2)}) collective-permute-start(f32[8,3,32,128]{3,2,1,0:T(8,128)S(1)} %get-tuple-element.107), channel_id=1, source_target_pairs={{0,4},{4,8},{8,12},{1,5},{5,9},{9,13},{2,6},{6,10},{10,14},{3,7},{... | collective-permute-start | bytes 1179656 | tf_op jit(solution)/shard_map/ppermute | solution.py:377
  7.6 12.5 %collective-permute-start.2 = (f32[8,3,32,128]{3,2,1,0:T(8,128)S(1)}, f32[8,3,32,128]{3,2,1,0:T(8,128)S(1)}, u32[]{:S(2)}, u32[]{:S(2)}) collective-permute-start(f32[8,3,32,128]{3,2,1,0:T(8,128)S(1)} %get-tuple-element.108), channel_id=1, source_target_pairs={{4,0},{8,4},{12,8},{5,1},{9,5},{13,9},{6,2},{10,6},{14,10},{7,3},{... | collective-permute-start | bytes 1179656 | tf_op jit(solution)/shard_map/ppermute | solution.py:378
  8.9 15.5 %collective-permute-start = (f32[4,3,64,128]{3,2,1,0:T(8,128)S(1)}, f32[4,3,64,128]{3,2,1,0:T(8,128)S(1)}, u32[]{:S(2)}, u32[]{:S(2)}) collective-permute-start(f32[4,3,64,128]{3,2,1,0:T(8,128)S(1)} %get-tuple-element.106), channel_id=1, source_target_pairs={{0,4},{4,8},{8,12},{1,5},{5,9},{9,13},{2,6},{6,10},{10,14},{3,7},{... | collective-permute-start | bytes 1179656 | tf_op jit(solution)/shard_map/ppermute | solution.py:379
  20.1 5.7 %collective-permute-start.3 = (f32[4,3,32,128]{3,2,1,0:T(8,128)S(1)}, f32[4,3,32,128]{3,2,1,0:T(8,128)S(1)}, u32[]{:S(2)}, u32[]{:S(2)}) collective-permute-start(f32[4,3,32,128]{3,2,1,0:T(8,128)S(1)} %pad_maximum_fusion), channel_id=1, source_target_pairs={{0,2},{1,3},{2,0},{3,1},{4,6},{5,7},{6,4},{7,5},{8,10},{9,11},{10,... | collective-permute-start | bytes 589832 | tf_op jit(solution)/shard_map/ppermute | solution.py:415
  21.7 11.3 %collective-permute-start.7 = (f32[4,3,64,128]{3,2,1,0:T(8,128)S(1)}, f32[4,3,64,128]{3,2,1,0:T(8,128)S(1)}, u32[]{:S(2)}, u32[]{:S(2)}) collective-permute-start(f32[4,3,64,128]{3,2,1,0:T(8,128)S(1)} %get-tuple-element.146), channel_id=1, source_target_pairs={{4,0},{8,4},{12,8},{5,1},{9,5},{13,9},{6,2},{10,6},{14,10},{7,3},{... | collective-permute-start | bytes 1179656 | tf_op jit(solution)/shard_map/ppermute | solution.py:380
  23.0 2.9 %collective-permute-start.6 = (f32[6,3,32,128]{3,2,1,0:T(8,128)S(1)}, f32[6,3,32,128]{3,2,1,0:T(8,128)S(1)}, u32[]{:S(2)}, u32[]{:S(2)}) collective-permute-start(f32[6,3,32,128]{3,2,1,0:T(8,128)S(1)} %slice.14), channel_id=1, source_target_pairs={{0,1},{1,0},{2,3},{3,2},{4,5},{5,4},{6,7},{7,6},{8,9},{9,8},{10,11... | collective-permute-start | bytes 884744 | tf_op jit(solution)/shard_map/ppermute | solution.py:417
  23.1 9.8 %collective-permute-start.8 = (f32[6,3,32,128]{3,2,1,0:T(8,128)S(1)}, f32[6,3,32,128]{3,2,1,0:T(8,128)S(1)}, u32[]{:S(2)}, u32[]{:S(2)}) collective-permute-start(f32[6,3,32,128]{3,2,1,0:T(8,128)S(1)} %slice.15), channel_id=1, source_target_pairs={{0,1},{1,0},{2,3},{3,2},{4,5},{5,4},{6,7},{7,6},{8,9},{9,8},{10,11... | collective-permute-start | bytes 884744 | tf_op jit(solution)/shard_map/ppermute | solution.py:418
  24.4 1.5 %collective-permute-start.4 = (f32[4,3,32,128]{3,2,1,0:T(8,128)S(1)}, f32[4,3,32,128]{3,2,1,0:T(8,128)S(1)}, u32[]{:S(2)}, u32[]{:S(2)}) collective-permute-start(f32[4,3,32,128]{3,2,1,0:T(8,128)S(1)} %pad_maximum_fusion), channel_id=1, source_target_pairs={{0,1},{1,0},{2,3},{3,2},{4,5},{5,4},{6,7},{7,6},{8,9},{9,8},{10,11... | collective-permute-start | bytes 589832 | tf_op jit(solution)/shard_map/ppermute | solution.py:416
  25.9 1.4 %collective-permute-start.5 = (f32[4,3,32,128]{3,2,1,0:T(8,128)S(1)}, f32[4,3,32,128]{3,2,1,0:T(8,128)S(1)}, u32[]{:S(2)}, u32[]{:S(2)}) collective-permute-start(f32[4,3,32,128]{3,2,1,0:T(8,128)S(1)} %collective-permute-done.3.args_2_), channel_id=1, source_target_pairs={{0,1},{1,0},{2,3},{3,2},{4,5},{5,4},{6,7},{7,6},{8,9},{9,8},{10,11... | collective-permute-start | bytes 589832 | tf_op jit(solution)/shard_map/ppermute | solution.py:416
  31.1 3.1 %collective-permute-start.10 = (f32[1,4,16,384]{3,2,1,0:T(8,128)S(1)}, f32[1,4,16,384]{3,2,1,0:T(8,128)S(1)}, u32[]{:S(2)}, u32[]{:S(2)}) collective-permute-start(f32[1,4,16,384]{3,2,1,0:T(8,128)S(1)} %get-tuple-element.179), channel_id=1, source_target_pairs={{0,1},{1,0},{2,3},{3,2},{4,5},{5,4},{6,7},{7,6},{8,9},{9,8},{10,11... | collective-permute-start | bytes 294920 | tf_op jit(solution)/shard_map/ppermute | solution.py:427
  31.3 2.9 %collective-permute-start.9 = (f32[1,4,16,384]{3,2,1,0:T(8,128)S(1)}, f32[1,4,16,384]{3,2,1,0:T(8,128)S(1)}, u32[]{:S(2)}, u32[]{:S(2)}) collective-permute-start(f32[1,4,16,384]{3,2,1,0:T(8,128)S(1)} %get-tuple-element.178), channel_id=1, source_target_pairs={{0,1},{1,0},{2,3},{3,2},{4,5},{5,4},{6,7},{7,6},{8,9},{9,8},{10,11... | collective-permute-start | bytes 294920 | tf_op jit(solution)/shard_map/ppermute | solution.py:427
  34.3 4.7 %collective-permute-start.11 = (f32[4,16,384]{2,1,0:T(8,128)S(1)}, f32[4,16,384]{2,1,0:T(8,128)S(1)}, u32[]{:S(2)}, u32[]{:S(2)}) collective-permute-start(f32[4,16,384]{2,1,0:T(8,128)S(1)} %add_bitcast_fusion.1), channel_id=1, source_target_pairs={{0,2},{1,3},{2,0},{3,1},{4,6},{5,7},{6,4},{7,5},{8,10},{9,11},{10,... | collective-permute-start | bytes 294920 | tf_op jit(solution)/shard_map/ppermute | solution.py:422
  37.2 1.9 %collective-permute-start.12 = (f32[1,4,16,384]{3,2,1,0:T(8,128)S(1)}, f32[1,4,16,384]{3,2,1,0:T(8,128)S(1)}, u32[]{:S(2)}, u32[]{:S(2)}) collective-permute-start(f32[1,4,16,384]{3,2,1,0:T(8,128)S(1)} %get-tuple-element.202), channel_id=1, source_target_pairs={{0,1},{1,0},{2,3},{3,2},{4,5},{5,4},{6,7},{7,6},{8,9},{9,8},{10,11... | collective-permute-start | bytes 294920 | tf_op jit(solution)/shard_map/ppermute | solution.py:427
  37.3 3.8 %collective-permute-start.13 = (f32[1,4,16,384]{3,2,1,0:T(8,128)S(1)}, f32[1,4,16,384]{3,2,1,0:T(8,128)S(1)}, u32[]{:S(2)}, u32[]{:S(2)}) collective-permute-start(f32[1,4,16,384]{3,2,1,0:T(8,128)S(1)} %get-tuple-element.207), channel_id=1, source_target_pairs={{0,1},{1,0},{2,3},{3,2},{4,5},{5,4},{6,7},{7,6},{8,9},{9,8},{10,11... | collective-permute-start | bytes 294920 | tf_op jit(solution)/shard_map/ppermute | solution.py:427
  39.2 4.7 %collective-permute-start.14 = (f32[4,16,384]{2,1,0:T(8,128)S(1)}, f32[4,16,384]{2,1,0:T(8,128)S(1)}, u32[]{:S(2)}, u32[]{:S(2)}) collective-permute-start(f32[4,16,384]{2,1,0:T(8,128)S(1)} %add_bitcast_fusion), channel_id=1, source_target_pairs={{0,2},{1,3},{2,0},{3,1},{4,6},{5,7},{6,4},{7,5},{8,10},{9,11},{10,... | collective-permute-start | bytes 294920 | tf_op jit(solution)/shard_map/ppermute | solution.py:456

commit v9 on v7

--- a/solution.py
+++ b/solution.py
@@ -246,30 +246,36 @@
     sweeps(refs, ranges, lambda zz: jnp.float32(1.0), lambda zz: mid.at[zz - HALO - SWEEPS])
 
 
+def fill_kernel(low, *args):
+    mine, theirs, rest = args[:3]
+    P0, SRC, OBS, sems = args[-4:]
+    nx, depth = P0.shape[2], P0.shape[0]
+    half, par = nx // 2, lax.axis_index("draw") % 2
+    pairs = []
+    for which, start, sweeps_from in ((par, mine, mine.at[pl.ds(HALO, 2 * SWEEPS)]), (1 - par, theirs, rest)):
+        rows = pl.ds(pl.multiple_of(half * which, half), half)
+        planes = pl.ds(0 if low else depth - HALO, HALO)
+        pairs.append((start.at[pl.ds(0, HALO)], P0.at[planes, :, rows]))
+        planes = pl.ds(HALO - SWEEPS if low else depth - HALO, SWEEPS)
+        for n, field in enumerate((SRC, OBS)):
+            pairs.append((sweeps_from.at[pl.ds(n * SWEEPS, SWEEPS)], field.at[planes, :, rows]))
+    copies = [pltpu.make_async_copy(a, b, sems.at[i]) for i, (a, b) in enumerate(pairs)]
+    for cp in copies:
+        cp.start()
+    for cp in copies:
+        cp.wait()
+
+
 def side_kernel(low, stages, parts, *args):
     halos = args[: len(args) - 2 * FIELDS - (3 in stages) - len(parts) - 1]
     refs = args[len(halos) + FIELDS : len(halos) + 2 * FIELDS]
     ends, sems = args[len(halos) + 2 * FIELDS : -1], args[-1]
-    K, P0, SRC, OBS = refs[:4]
-    nx, depth = K.shape[2], K.shape[0]
-    half, top = nx // 2, depth - HALO
-    par = lax.axis_index("draw") % 2
+    K, depth = refs[0], refs[0].shape[0]
+    top = depth - HALO
 
     pairs = []
     if halos:
-        k, mine, *theirs = halos
-        pairs.append((k, K.at[pl.ds(0 if low else top, HALO)]))
-        for half_rows, which in ((None, par), (theirs, 1 - par)):
-            rows = pl.ds(pl.multiple_of(half * which, half), half)
-            first = 0
-            for field, width in ((P0, HALO), (SRC, SWEEPS), (OBS, SWEEPS)):
-                planes = pl.ds(HALO - width if low else top, width)
-                if half_rows is None:
-                    ref = mine.at[pl.ds(first, width)]
-                else:
-                    ref = theirs[0] if first == 0 else theirs[1].at[pl.ds(first - HALO, width)]
-                pairs.append((ref, field.at[planes, :, rows]))
-                first += width
+        pairs.append((halos[0], K.at[pl.ds(0 if low else top, HALO)]))
     copies = [pltpu.make_async_copy(a, b, sems.at[i]) for i, (a, b) in enumerate(pairs)]
     for cp in copies:
         cp.start()
@@ -393,7 +399,7 @@
             out_shape=(*kinds, *ends),
             in_specs=[ONCHIP] * (n + FIELDS),
             out_specs=(ONCHIP,) * (FIELDS + len(ends)),
-            scratch_shapes=[pltpu.SemaphoreType.DMA((8,))],
+            scratch_shapes=[pltpu.SemaphoreType.DMA((1,))],
             input_output_aliases={n + i: i for i in range(FIELDS)},
             compiler_params=params,
             cost_estimate=pl.CostEstimate(flops=work, bytes_accessed=work, transcendentals=0),
@@ -403,9 +409,21 @@
     alo, ahi, last = lax.optimization_barrier((alo, ahi, fields[-1]))
     fields = (*fields[:-1], last)
     lower, upper = [
-        (k, mine, *[lax.ppermute(mine[a:b], "draw", pair) for a, b in ((0, HALO), (HALO, EDGE))])
-        for k, mine in ((klo, alo), (khi, ahi))
+        (mine, *[lax.ppermute(mine[a:b], "draw", pair) for a, b in ((0, HALO), (HALO, EDGE))]) for mine in (alo, ahi)
     ]
+
+    def fill(low, pieces, fields):
+        out = pl.pallas_call(
+            functools.partial(fill_kernel, low),
+            out_shape=kinds[1:4],
+            in_specs=[ONCHIP] * 6,
+            out_specs=(ONCHIP,) * 3,
+            scratch_shapes=[pltpu.SemaphoreType.DMA((6,))],
+            input_output_aliases={3 + i: i for i in range(3)},
+            compiler_params=params,
+            cost_estimate=pl.CostEstimate(flops=1, bytes_accessed=1, transcendentals=0),
+        )(*pieces, *fields[1:4])
+        return (fields[0], *out, *fields[4:])
 
     def onward(keep, got):
         return [
@@ -426,11 +444,15 @@
             cost_estimate=pl.CostEstimate(flops=10 * cells, bytes_accessed=10 * cells, transcendentals=0),
         )(*fields)
 
-    (fields,) = side(True, (0, 1, 2), lower, fields)
+    fields = fill(True, lower, fields)
+    (fields,) = side(True, (0, 1, 2), (klo,), fields)
+    khi, last = lax.optimization_barrier((khi, fields[-1]))
+    fields = (*fields[:-1], last)
     parts = [(False, 1, 0, cut), (False, 0, 0, cut), (True, 1, 0, cut)]
     fields, low, send_far, send_near, keep = side(True, (3,), (), fields, parts)
     got_far, near_low = swap(send_far), swap(send_near)
-    (fields,) = side(False, (0, 1), upper, fields)
+    fields = fill(False, upper, fields)
+    (fields,) = side(False, (0, 1), (khi,), fields)
     got_far, near_low, last = lax.optimization_barrier((got_far, near_low, fields[-1]))
     moved_low = onward(keep, got_far)
     parts = [(False, 1, cut, slab - cut), (False, 0, cut, slab - cut)]

time: 43.2 us -> 44.7 us (1.035)
  waiting for transfers between devices: 10.9 us -> 13 us
  Pallas kernels: 13.2 us -> 12.6 us
    ppermute x1, waiting for transfers between devices: 0.01 us -> 2.33 us  [local(): khi = lax.ppermute(bottom, 'space', down)]
    ppermute x1, waiting for transfers between devices: 2.01 us -> 0.66 us  [local(): klo = lax.ppermute(top, 'space', up)]
    ppermute x4, waiting for transfers between devices: 0.01 us -> 1 us  [local(): lax.ppermute(mine[a:b], 'draw', pair)]
    pallas_call x4, Pallas kernels: 7.26 us -> 6.31 us  [side(): pl.pallas_call(functools.partial(side_kernel, low, stages, [part[:-1] for...]
  transfers between devices with their start and end apart: 14 -> 14, of which waited for: 5 -> 8; matrix products, arithmetic and copies ran while one was open for 0% -> 0% of each run, Pallas kernels for 26% -> 24%
where the time goes in v9:
time: 44.7 us; the launch traced here: 44.5 us
  starting transfers between devices  17.2 us (38%)
  waiting for transfers between devices  13 us (29%)
  Pallas kernels  12.6 us (28%)
  between operations  0.88 us (2%)
  other arithmetic  0.73 us (2%)
    pallas_call x4, Pallas kernels, side(): pl.pallas_call(functools.partial(side_kernel, low, stages, [part[:-1] for...  6.31 us
    ppermute x1, starting transfers between devices, local(): alo = lax.ppermute(to_up, 'space', up)  4.96 us
    ppermute x1, starting transfers between devices, local(): klo = lax.ppermute(top, 'space', up)  4.57 us
    ppermute x1, waiting for transfers between devices, local(): ahi = lax.ppermute(to_down, 'space', down)  4.46 us
    pallas_call x1, Pallas kernels, local(): pl.pallas_call(inner_kernel, out_shape=(*kinds[1:], mid), in_specs=[ONCHI...  2.86 us
    ppermute x1, waiting for transfers between devices, local(): lax.ppermute(a, 'draw', [(j, (j + 2 * s) % draws) for j in range(draws)])  2.43 us
    ppermute x1, waiting for transfers between devices, local(): khi = lax.ppermute(bottom, 'space', down)  2.33 us
    pallas_call x1, Pallas kernels, local(): pl.pallas_call(first_kernel, out_shape=(field, edge, edge, rim, rim), in_...  1.91 us
  transfers between devices with their start and end apart: 14, of which 8 were waited for; matrix products, arithmetic and copies ran while one was open for 0% of the time, Pallas kernels for 24%

profile of v9, /device:TPU:0, one launch (start us, length us, event | category | flops | bytes accessed | tf_op | source)
XLA Modules:
  0.0 44.5 jit_solution(45728288663397741)
XLA Ops:
  0.6 0.0 copy-start
  0.6 0.0 copy-start.1
  0.7 0.0 copy-start.2
  0.7 1.9 %shard_map.68 = (f32[16,3,64,128]{3,2,1,0:T(8,128)S(1)}, f32[10,3,32,128]{3,2,1,0:T(8,128)S(1)}, f32[10,3,32,128]{3,2,1,0:T(8,128)S(1)}, f32[4,3,64,128]{3,2,1,0:T(8,128)S(1)}, f32[4,3,64,128]{3,2,1,0:T(8,128)S(1)}) custom-call(f32[8,64,384]{2,1,0:T(8,128)} %log_perm.1, f32[8,64,384]{2,1,0:T(8,128)} %bitcast.10, f32[8,64,384]{2,1,0:T(8,128)} %p0.3, ...), custom_call_target="tpu_custom_call" | custom-call | flops 196608 | bytes 3932160 | tf_op jit(solution)/shard_map/pallas_call | solution.py:365
  2.6 5.0 %collective-permute-start.1 = (f32[10,3,32,128]{3,2,1,0:T(8,128)S(1)}, f32[10,3,32,128]{3,2,1,0:T(8,128)S(1)}, u32[]{:S(2)}, u32[]{:S(2)}) collective-permute-start(f32[10,3,32,128]{3,2,1,0:T(8,128)S(1)} %get-tuple-element.116), channel_id=1, source_target_pairs={{0,4},{4,8},{8,12},{1,5},{5,9},{9,13},{2,6},{6,10},{10,14},{3,7},{... | collective-permute-start | bytes 1474568 | tf_op jit(solution)/shard_map/ppermute | solution.py:374
  7.5 1.3 %collective-permute-start.2 = (f32[10,3,32,128]{3,2,1,0:T(8,128)S(1)}, f32[10,3,32,128]{3,2,1,0:T(8,128)S(1)}, u32[]{:S(2)}, u32[]{:S(2)}) collective-permute-start(f32[10,3,32,128]{3,2,1,0:T(8,128)S(1)} %get-tuple-element.117), channel_id=1, source_target_pairs={{4,0},{8,4},{12,8},{5,1},{9,5},{13,9},{6,2},{10,6},{14,10},{7,3},{... | collective-permute-start | bytes 1474568 | tf_op jit(solution)/shard_map/ppermute | solution.py:375
  8.8 4.6 %collective-permute-start = (f32[4,3,64,128]{3,2,1,0:T(8,128)S(1)}, f32[4,3,64,128]{3,2,1,0:T(8,128)S(1)}, u32[]{:S(2)}, u32[]{:S(2)}) collective-permute-start(f32[4,3,64,128]{3,2,1,0:T(8,128)S(1)} %get-tuple-element.114), channel_id=1, source_target_pairs={{0,4},{4,8},{8,12},{1,5},{5,9},{9,13},{2,6},{6,10},{10,14},{3,7},{... | collective-permute-start | bytes 1179656 | tf_op jit(solution)/shard_map/ppermute | solution.py:376
  13.4 1.3 %collective-permute-start.5 = (f32[4,3,64,128]{3,2,1,0:T(8,128)S(1)}, f32[4,3,64,128]{3,2,1,0:T(8,128)S(1)}, u32[]{:S(2)}, u32[]{:S(2)}) collective-permute-start(f32[4,3,64,128]{3,2,1,0:T(8,128)S(1)} %get-tuple-element.153), channel_id=1, source_target_pairs={{4,0},{8,4},{12,8},{5,1},{9,5},{13,9},{6,2},{10,6},{14,10},{7,3},{... | collective-permute-start | bytes 1179656 | tf_op jit(solution)/shard_map/ppermute | solution.py:377
  14.7 0.0 copy-done
  14.7 0.0 copy-done.1
  14.7 0.0 copy-done.2
  14.8 2.9 %shard_map.69 = (f32[16,3,64,128]{3,2,1,0:T(8,128)S(1)}, f32[16,3,64,128]{3,2,1,0:T(8,128)S(1)}, f32[16,3,64,128]{3,2,1,0:T(8,128)S(1)}, f32[16,3,64,128]{3,2,1,...) custom-call(f32[16,3,64,128]{3,2,1,0:T(8,128)S(1)} %get-tuple-elemen, ...), custom_call_target="tpu_custom_call" | custom-call | flops 39321600 | bytes 11796480 | tf_op jit(solution)/shard_map/pallas_call | solution.py:378
  17.6 1.5 %collective-permute-done.1.args_0_ = f32[10,3,32,128]{3,2,1,0:T(8,128)S(1)} collective-permute-done((f32[10,3,32,128]{3,2,1,0:T(8,128)S(1)}, f32[10,3,32,128]{3,2,1,0:T(8,128)S(1)}, u32[]{:S(2)}, u32[]{:S(2)}) %collective-permute-start.1) | collective-permute-done | bytes 491552 | tf_op jit(solution)/shard_map/ppermute | solution.py:374
  19.1 4.5 %collective-permute-done.2.args_0_ = f32[10,3,32,128]{3,2,1,0:T(8,128)S(1)} collective-permute-done((f32[10,3,32,128]{3,2,1,0:T(8,128)S(1)}, f32[10,3,32,128]{3,2,1,0:T(8,128)S(1)}, u32[]{:S(2)}, u32[]{:S(2)}) %collective-permute-start.2) | collective-permute-done | bytes 491552 | tf_op jit(solution)/shard_map/ppermute | solution.py:375
  23.6 0.1 collective-permute-start.3
  23.7 0.6 %collective-permute-start.4 = (f32[6,3,32,128]{3,2,1,0:T(8,128)S(1)}, f32[6,3,32,128]{3,2,1,0:T(8,128)S(1)}, u32[]{:S(2)}, u32[]{:S(2)}) collective-permute-start(f32[6,3,32,128]{3,2,1,0:T(8,128)S(1)} %slice.13), channel_id=1, source_target_pairs={{0,1},{1,0},{2,3},{3,2},{4,5},{5,4},{6,7},{7,6},{8,9},{9,8},{10,11... | collective-permute-start | bytes 884744 | tf_op jit(solution)/shard_map/ppermute | solution.py:412
  24.3 0.1 collective-permute-start.7
  24.4 0.7 %collective-permute-done.3.args_1_ = f32[4,3,32,128]{3,2,1,0:T(8,128)S(1)} collective-permute-done((f32[4,3,32,128]{3,2,1,0:T(8,128)S(1)}, f32[4,3,32,128]{3,2,1,0:T(8,128)S(1)}, u32[]{:S(2)}, u32[]{:S(2)}) %collective-permute-start.3) | collective-permute-done | bytes 196640 | tf_op jit(solution)/shard_map/ppermute | solution.py:412
  25.1 0.1 collective-permute-start.6
  25.2 0.3 collective-permute-done.4.args_2_
  25.5 0.2 shard_map.70
  25.7 0.7 %collective-permute-done.args_0_ = f32[4,3,64,128]{3,2,1,0:T(8,128)S(1)} collective-permute-done((f32[4,3,64,128]{3,2,1,0:T(8,128)S(1)}, f32[4,3,64,128]{3,2,1,0:T(8,128)S(1)}, u32[]{:S(2)}, u32[]{:S(2)}) %collective-permute-start) | collective-permute-done | bytes 393248 | tf_op jit(solution)/shard_map/ppermute | solution.py:376
  26.4 1.8 %shard_map.71 = (f32[16,3,64,128]{3,2,1,0:T(8,128)S(1)}, f32[16,3,64,128]{3,2,1,0:T(8,128)S(1)}, f32[16,3,64,128]{3,2,1,0:T(8,128)S(1)}, f32[16,3,64,128]{3,2,1,...) custom-call(f32[4,3,64,128]{3,2,1,0:T(8,128)S(1)} %collective-permut, ...), custom_call_target="tpu_custom_call", output_to_operand_aliasing={{0}: (1, {}), {1}: (2, {}), {2}: (3, {}), {3}: (4, {}), {4}... | custom-call | flops 1 | bytes 1 | tf_op jit(solution)/shard_map/pallas_call | solution.py:397
  28.2 2.3 %collective-permute-done.5.args_0_ = f32[4,3,64,128]{3,2,1,0:T(8,128)S(1)} collective-permute-done((f32[4,3,64,128]{3,2,1,0:T(8,128)S(1)}, f32[4,3,64,128]{3,2,1,0:T(8,128)S(1)}, u32[]{:S(2)}, u32[]{:S(2)}) %collective-permute-start.5) | collective-permute-done | bytes 393248 | tf_op jit(solution)/shard_map/ppermute | solution.py:377
  30.5 1.4 %shard_map.72 = (f32[16,3,64,128]{3,2,1,0:T(8,128)S(1)}, f32[16,3,64,128]{3,2,1,0:T(8,128)S(1)}, f32[16,3,64,128]{3,2,1,0:T(8,128)S(1)}, f32[16,3,64,128]{3,2,1,...) custom-call(f32[16,3,64,128]{3,2,1,0:T(8,128)S(1)} %get-tuple-elemen, ...), custom_call_target="tpu_custom_call", output_to_operand_aliasing={{0}: (0, {}), {1}: (1, {}), {2}: (2, {}), {3}: (3, {}), {4}... | custom-call | flops 1 | bytes 1 | tf_op jit(solution)/shard_map/pallas_call | solution.py:397
  32.0 0.1 collective-permute-start.8
  32.0 0.5 %collective-permute-start.9 = (f32[1,4,16,384]{3,2,1,0:T(8,128)S(1)}, f32[1,4,16,384]{3,2,1,0:T(8,128)S(1)}, u32[]{:S(2)}, u32[]{:S(2)}) collective-permute-start(f32[1,4,16,384]{3,2,1,0:T(8,128)S(1)} %get-tuple-element.195), channel_id=1, source_target_pairs={{0,1},{1,0},{2,3},{3,2},{4,5},{5,4},{6,7},{7,6},{8,9},{9,8},{10,11... | collective-permute-start | bytes 294920 | tf_op jit(solution)/shard_map/ppermute | solution.py:435
  32.5 0.0 collective-permute-done.6.args_1_
  32.5 0.0 collective-permute-done.7.args_2_
  32.5 0.2 shard_map.73
  32.8 1.0 %shard_map.74 = (f32[16,3,64,128]{3,2,1,0:T(8,128)S(1)}, f32[16,3,64,128]{3,2,1,0:T(8,128)S(1)}, f32[16,3,64,128]{3,2,1,0:T(8,128)S(1)}, f32[16,3,64,128]{3,2,1,...) custom-call(f32[4,3,64,128]{3,2,1,0:T(8,128)S(1)} %collective-permut, ...), custom_call_target="tpu_custom_call", output_to_operand_aliasing={{0}: (1, {}), {1}: (2, {}), {2}: (3, {}), {3}: (4, {}), {4}... | custom-call | flops 11796480 | bytes 11796480 | tf_op jit(solution)/shard_map/pallas_call | solution.py:397
  33.8 0.0 collective-permute-done.8
  33.8 0.0 collective-permute-done.9
  33.8 1.6 %collective-permute-start.10 = (f32[4,16,384]{2,1,0:T(8,128)S(1)}, f32[4,16,384]{2,1,0:T(8,128)S(1)}, u32[]{:S(2)}, u32[]{:S(2)}) collective-permute-start(f32[4,16,384]{2,1,0:T(8,128)S(1)} %add_bitcast_fusion.1), channel_id=1, source_target_pairs={{0,2},{1,3},{2,0},{3,1},{4,6},{5,7},{6,4},{7,5},{8,10},{9,11},{10,... | collective-permute-start | bytes 294920 | tf_op jit(solution)/shard_map/ppermute | solution.py:430
  35.4 2.1 %shard_map.75 = (f32[16,3,64,128]{3,2,1,0:T(8,128)S(1)}, f32[16,3,64,128]{3,2,1,0:T(8,128)S(1)}, f32[16,3,64,128]{3,2,1,0:T(8,128)S(1)}, f32[16,3,64,128]{3,2,1,...) custom-call(f32[16,3,64,128]{3,2,1,0:T(8,128)S(1)} %get-tuple-elemen, ...), custom_call_target="tpu_custom_call", output_to_operand_aliasing={{0}: (0, {}), {1}: (1, {}), {2}: (2, {}), {3}: (3, {}), {4}... | custom-call | flops 11796480 | bytes 11796480 | tf_op jit(solution)/shard_map/pallas_call | solution.py:397
  37.5 0.1 collective-permute-start.11
  37.6 0.5 %collective-permute-start.12 = (f32[1,4,16,384]{3,2,1,0:T(8,128)S(1)}, f32[1,4,16,384]{3,2,1,0:T(8,128)S(1)}, u32[]{:S(2)}, u32[]{:S(2)}) collective-permute-start(f32[1,4,16,384]{3,2,1,0:T(8,128)S(1)} %get-tuple-element.223), channel_id=1, source_target_pairs={{0,1},{1,0},{2,3},{3,2},{4,5},{5,4},{6,7},{7,6},{8,9},{9,8},{10,11... | collective-permute-start | bytes 294920 | tf_op jit(solution)/shard_map/ppermute | solution.py:435
  38.1 0.6 %collective-permute-done.10 = f32[4,16,384]{2,1,0:T(8,128)S(1)} collective-permute-done((f32[4,16,384]{2,1,0:T(8,128)S(1)}, f32[4,16,384]{2,1,0:T(8,128)S(1)}, u32[]{:S(2)}, u32[]{:S(2)}) %collective-permute-start.10) | collective-permute-done | bytes 98336 | tf_op jit(solution)/shard_map/ppermute | solution.py:430
  38.6 0.2 shard_map.76
  38.8 0.0 collective-permute-done.11
  38.9 1.6 %collective-permute-start.13 = (f32[4,16,384]{2,1,0:T(8,128)S(1)}, f32[4,16,384]{2,1,0:T(8,128)S(1)}, u32[]{:S(2)}, u32[]{:S(2)}) collective-permute-start(f32[4,16,384]{2,1,0:T(8,128)S(1)} %add_bitcast_fusion), channel_id=1, source_target_pairs={{0,2},{1,3},{2,0},{3,1},{4,6},{5,7},{6,4},{7,5},{8,10},{9,11},{10,... | collective-permute-start | bytes 294920 | tf_op jit(solution)/shard_map/ppermute | solution.py:468
  40.4 0.9 %shard_map.77 = (f32[8,64,384]{2,1,0:T(8,128)}, f32[1,8,16,384]{3,2,1,0:T(8,128)S(1)}) custom-call(f32[3,64,384]{2,1,0:T(8,128)S(1)} %get-tuple-element.156.args_0_, f32[2,64,384]{2,1,0:T(8,128)S(1)} %get-tuple-element.157.args_1_, f32[3,64,384]{2,1,0:T(8,128)S(1)} %get-tuple-element.198.args_2_, f32[16,3,64,128]{3,2,1,0:T(8,128)S(1)} %get-tuple-element.199.args_0_.args_3_, ...), custom_call_target="tpu_custom_call" | custom-call | flops 5898240 | bytes 5898240 | tf_op jit(solution)/shard_map/pallas_call | solution.py:470
  41.3 0.0 collective-permute-done.12
  41.3 2.4 %collective-permute-done.13 = f32[4,16,384]{2,1,0:T(8,128)S(1)} collective-permute-done((f32[4,16,384]{2,1,0:T(8,128)S(1)}, f32[4,16,384]{2,1,0:T(8,128)S(1)}, u32[]{:S(2)}, u32[]{:S(2)}) %collective-permute-start.13) | collective-permute-done | bytes 98336 | tf_op jit(solution)/shard_map/ppermute | solution.py:468
  43.8 0.7 %fusion = f32[8,16,384]{2,1,0:T(8,128)} fusion(f32[4,16,384]{2,1,0:T(8,128)S(1)} %bitcast.12, f32[4,16,384]{2,1,0:T(8,128)S(1)} %bitcast.11, f32[4,16,384]{2,1,0:T(8,128)S(1)} %collective-permute-done.13, f32[4,16,384]{2,1,0:T(8,128)S(1)} %collective-permute-done.10, f32[1,8,16,384]{3,2,1,0:T(8,128)S(1)} %get-tuple-element.221), kind=kLoop, calls=%fused_computation.1 | loop fusion | flops 196608 | bytes 786432 | tf_op jit(solution)/shard_map/add | solution.py:481
  (6 shorter events, 0.1 us)
Async XLA Ops:
  0.6 14.1 %copy-start = (f32[8,64,384]{2,1,0:T(8,128)S(1)}, f32[8,64,384]{2,1,0:T(8,128)}, u32[]{:S(2)}) copy-start(f32[8,64,384]{2,1,0:T(8,128)} %p0.3) | copy-start | bytes 2359300
  0.6 14.1 %copy-start.1 = (f32[8,64,384]{2,1,0:T(8,128)S(1)}, f32[8,64,384]{2,1,0:T(8,128)}, u32[]{:S(2)}) copy-start(f32[8,64,384]{2,1,0:T(8,128)} %src.3) | copy-start | bytes 2359300
  0.7 14.1 %copy-start.2 = (f32[8,64,384]{2,1,0:T(8,128)S(1)}, f32[8,64,384]{2,1,0:T(8,128)}, u32[]{:S(2)}) copy-start(f32[8,64,384]{2,1,0:T(8,128)} %obs.3) | copy-start | bytes 2359300
  2.6 16.5 %collective-permute-start.1 = (f32[10,3,32,128]{3,2,1,0:T(8,128)S(1)}, f32[10,3,32,128]{3,2,1,0:T(8,128)S(1)}, u32[]{:S(2)}, u32[]{:S(2)}) collective-permute-start(f32[10,3,32,128]{3,2,1,0:T(8,128)S(1)} %get-tuple-element.116), channel_id=1, source_target_pairs={{0,4},{4,8},{8,12},{1,5},{5,9},{9,13},{2,6},{6,10},{10,14},{3,7},{... | collective-permute-start | bytes 1474568 | tf_op jit(solution)/shard_map/ppermute | solution.py:374
  7.5 16.0 %collective-permute-start.2 = (f32[10,3,32,128]{3,2,1,0:T(8,128)S(1)}, f32[10,3,32,128]{3,2,1,0:T(8,128)S(1)}, u32[]{:S(2)}, u32[]{:S(2)}) collective-permute-start(f32[10,3,32,128]{3,2,1,0:T(8,128)S(1)} %get-tuple-element.117), channel_id=1, source_target_pairs={{4,0},{8,4},{12,8},{5,1},{9,5},{13,9},{6,2},{10,6},{14,10},{7,3},{... | collective-permute-start | bytes 1474568 | tf_op jit(solution)/shard_map/ppermute | solution.py:375
  8.8 17.6 %collective-permute-start = (f32[4,3,64,128]{3,2,1,0:T(8,128)S(1)}, f32[4,3,64,128]{3,2,1,0:T(8,128)S(1)}, u32[]{:S(2)}, u32[]{:S(2)}) collective-permute-start(f32[4,3,64,128]{3,2,1,0:T(8,128)S(1)} %get-tuple-element.114), channel_id=1, source_target_pairs={{0,4},{4,8},{8,12},{1,5},{5,9},{9,13},{2,6},{6,10},{10,14},{3,7},{... | collective-permute-start | bytes 1179656 | tf_op jit(solution)/shard_map/ppermute | solution.py:376
  13.4 17.1 %collective-permute-start.5 = (f32[4,3,64,128]{3,2,1,0:T(8,128)S(1)}, f32[4,3,64,128]{3,2,1,0:T(8,128)S(1)}, u32[]{:S(2)}, u32[]{:S(2)}) collective-permute-start(f32[4,3,64,128]{3,2,1,0:T(8,128)S(1)} %get-tuple-element.153), channel_id=1, source_target_pairs={{4,0},{8,4},{12,8},{5,1},{9,5},{13,9},{6,2},{10,6},{14,10},{7,3},{... | collective-permute-start | bytes 1179656 | tf_op jit(solution)/shard_map/ppermute | solution.py:377
  23.6 1.5 %collective-permute-start.3 = (f32[4,3,32,128]{3,2,1,0:T(8,128)S(1)}, f32[4,3,32,128]{3,2,1,0:T(8,128)S(1)}, u32[]{:S(2)}, u32[]{:S(2)}) collective-permute-start(f32[4,3,32,128]{3,2,1,0:T(8,128)S(1)} %slice.12), channel_id=1, source_target_pairs={{0,1},{1,0},{2,3},{3,2},{4,5},{5,4},{6,7},{7,6},{8,9},{9,8},{10,11... | collective-permute-start | bytes 589832 | tf_op jit(solution)/shard_map/ppermute | solution.py:412
  23.7 1.8 %collective-permute-start.4 = (f32[6,3,32,128]{3,2,1,0:T(8,128)S(1)}, f32[6,3,32,128]{3,2,1,0:T(8,128)S(1)}, u32[]{:S(2)}, u32[]{:S(2)}) collective-permute-start(f32[6,3,32,128]{3,2,1,0:T(8,128)S(1)} %slice.13), channel_id=1, source_target_pairs={{0,1},{1,0},{2,3},{3,2},{4,5},{5,4},{6,7},{7,6},{8,9},{9,8},{10,11... | collective-permute-start | bytes 884744 | tf_op jit(solution)/shard_map/ppermute | solution.py:412
  24.3 8.2 %collective-permute-start.7 = (f32[6,3,32,128]{3,2,1,0:T(8,128)S(1)}, f32[6,3,32,128]{3,2,1,0:T(8,128)S(1)}, u32[]{:S(2)}, u32[]{:S(2)}) collective-permute-start(f32[6,3,32,128]{3,2,1,0:T(8,128)S(1)} %slice.15), channel_id=1, source_target_pairs={{0,1},{1,0},{2,3},{3,2},{4,5},{5,4},{6,7},{7,6},{8,9},{9,8},{10,11... | collective-permute-start | bytes 884744 | tf_op jit(solution)/shard_map/ppermute | solution.py:412
  25.1 7.4 %collective-permute-start.6 = (f32[4,3,32,128]{3,2,1,0:T(8,128)S(1)}, f32[4,3,32,128]{3,2,1,0:T(8,128)S(1)}, u32[]{:S(2)}, u32[]{:S(2)}) collective-permute-start(f32[4,3,32,128]{3,2,1,0:T(8,128)S(1)} %slice.14), channel_id=1, source_target_pairs={{0,1},{1,0},{2,3},{3,2},{4,5},{5,4},{6,7},{7,6},{8,9},{9,8},{10,11... | collective-permute-start | bytes 589832 | tf_op jit(solution)/shard_map/ppermute | solution.py:412
  32.0 1.8 %collective-permute-start.8 = (f32[1,4,16,384]{3,2,1,0:T(8,128)S(1)}, f32[1,4,16,384]{3,2,1,0:T(8,128)S(1)}, u32[]{:S(2)}, u32[]{:S(2)}) collective-permute-start(f32[1,4,16,384]{3,2,1,0:T(8,128)S(1)} %get-tuple-element.194), channel_id=1, source_target_pairs={{0,1},{1,0},{2,3},{3,2},{4,5},{5,4},{6,7},{7,6},{8,9},{9,8},{10,11... | collective-permute-start | bytes 294920 | tf_op jit(solution)/shard_map/ppermute | solution.py:435
  32.0 1.7 %collective-permute-start.9 = (f32[1,4,16,384]{3,2,1,0:T(8,128)S(1)}, f32[1,4,16,384]{3,2,1,0:T(8,128)S(1)}, u32[]{:S(2)}, u32[]{:S(2)}) collective-permute-start(f32[1,4,16,384]{3,2,1,0:T(8,128)S(1)} %get-tuple-element.195), channel_id=1, source_target_pairs={{0,1},{1,0},{2,3},{3,2},{4,5},{5,4},{6,7},{7,6},{8,9},{9,8},{10,11... | collective-permute-start | bytes 294920 | tf_op jit(solution)/shard_map/ppermute | solution.py:435
  33.8 4.8 %collective-permute-start.10 = (f32[4,16,384]{2,1,0:T(8,128)S(1)}, f32[4,16,384]{2,1,0:T(8,128)S(1)}, u32[]{:S(2)}, u32[]{:S(2)}) collective-permute-start(f32[4,16,384]{2,1,0:T(8,128)S(1)} %add_bitcast_fusion.1), channel_id=1, source_target_pairs={{0,2},{1,3},{2,0},{3,1},{4,6},{5,7},{6,4},{7,5},{8,10},{9,11},{10,... | collective-permute-start | bytes 294920 | tf_op jit(solution)/shard_map/ppermute | solution.py:430
  37.5 1.4 %collective-permute-start.11 = (f32[1,4,16,384]{3,2,1,0:T(8,128)S(1)}, f32[1,4,16,384]{3,2,1,0:T(8,128)S(1)}, u32[]{:S(2)}, u32[]{:S(2)}) collective-permute-start(f32[1,4,16,384]{3,2,1,0:T(8,128)S(1)} %get-tuple-element.218), channel_id=1, source_target_pairs={{0,1},{1,0},{2,3},{3,2},{4,5},{5,4},{6,7},{7,6},{8,9},{9,8},{10,11... | collective-permute-start | bytes 294920 | tf_op jit(solution)/shard_map/ppermute | solution.py:435
  37.6 3.8 %collective-permute-start.12 = (f32[1,4,16,384]{3,2,1,0:T(8,128)S(1)}, f32[1,4,16,384]{3,2,1,0:T(8,128)S(1)}, u32[]{:S(2)}, u32[]{:S(2)}) collective-permute-start(f32[1,4,16,384]{3,2,1,0:T(8,128)S(1)} %get-tuple-element.223), channel_id=1, source_target_pairs={{0,1},{1,0},{2,3},{3,2},{4,5},{5,4},{6,7},{7,6},{8,9},{9,8},{10,11... | collective-permute-start | bytes 294920 | tf_op jit(solution)/shard_map/ppermute | solution.py:435
  38.9 4.9 %collective-permute-start.13 = (f32[4,16,384]{2,1,0:T(8,128)S(1)}, f32[4,16,384]{2,1,0:T(8,128)S(1)}, u32[]{:S(2)}, u32[]{:S(2)}) collective-permute-start(f32[4,16,384]{2,1,0:T(8,128)S(1)} %add_bitcast_fusion), channel_id=1, source_target_pairs={{0,2},{1,3},{2,0},{3,1},{4,6},{5,7},{6,4},{7,5},{8,10},{9,11},{10,... | collective-permute-start | bytes 294920 | tf_op jit(solution)/shard_map/ppermute | solution.py:468

commit v10 on v7

--- a/solution.py
+++ b/solution.py
@@ -175,32 +175,38 @@
             lax.fori_loop(lo, hi, lambda zz, _, body=body, own=own: body(zz, *own) or 0, 0)
 
 
-def first_kernel(log_perm, noise, p0, src, obs, K, up, down, top, bottom, means, draws, sems):
-    slab, nx, ny = log_perm.shape
-    tiles, half = ny // LANES, nx // 2
+def edges_kernel(p0, src, obs, up, down, sems):
+    slab, nx, ny = p0.shape
+    half = nx // 2
     rows = pl.ds(pl.multiple_of(half * (lax.axis_index("draw") % 2), half), half)
     copies = []
-
-    def copy(src_ref, dst_ref):
-        copies.append(pltpu.make_async_copy(src_ref, dst_ref, sems.at[len(copies)]))
-
-    copy(log_perm, means)
-    copy(noise, draws)
-    for c in range(tiles):
+    for c in range(ny // LANES):
         cols = pl.ds(c * LANES, LANES)
         at = 0
         for ref, width in ((p0, HALO), (src, SWEEPS), (obs, SWEEPS)):
             for start, out in ((slab - width, up), (0, down)):
-                copy(ref.at[pl.ds(start, width), rows, cols], out.at[pl.ds(at, width), c])
+                pair = (ref.at[pl.ds(start, width), rows, cols], out.at[pl.ds(at, width), c])
+                copies.append(pltpu.make_async_copy(*pair, sems.at[len(copies)]))
             at += width
     for cp in copies:
         cp.start()
-    for cp in copies[:2]:
+    for cp in copies:
+        cp.wait()
+
+
+def conduct_kernel(log_perm, noise, K, top, bottom, means, draws, sems):
+    slab, nx, ny = log_perm.shape
+    copies = [
+        pltpu.make_async_copy(a, b, sems.at[i]) for i, (a, b) in enumerate(((log_perm, means), (noise, draws)))
+    ]
+    for cp in copies:
+        cp.start()
+    for cp in copies:
         cp.wait()
 
     def plane(z, _, out=None, first=0):
         for r in range(nx // SUB):
-            for c in range(tiles):
+            for c in range(ny // LANES):
                 here, cols = pl.ds(SUB * r, SUB), pl.ds(c * LANES, LANES)
                 k = jnp.exp(means[z, here, cols] + draws[z, here, cols])
                 K[z + HALO, c, here, :] = k
@@ -212,8 +218,6 @@
     lax.fori_loop(0, HALO, low, 0)
     lax.fori_loop(HALO, slab - HALO, plane, 0)
     lax.fori_loop(slab - HALO, slab, high, 0)
-    for cp in copies[2:]:
-        cp.wait()
 
 
 def inner_kernel(K, p0, src, obs, P0, SRC, OBS, P1, P2, U1, U2, U3, HR, SR, NP0, WL, WR, G, E, mid, sems):
@@ -355,16 +359,27 @@
     params = pltpu.CompilerParams(vmem_limit_bytes=8 * 2**20)
     cells = slab * nx * ny
 
-    inputs = (log_perm, noise[0], start_pressure, source, observe)
-    K, to_up, to_down, top, bottom = pl.pallas_call(
-        first_kernel,
-        out_shape=(field, edge, edge, rim, rim),
-        in_specs=[OFFCHIP] * 5,
-        out_specs=(ONCHIP,) * 5,
-        scratch_shapes=[pltpu.VMEM((slab, nx, ny), f32)] * 2 + [pltpu.SemaphoreType.DMA((2 + 6 * tiles,))],
+    def offchip(*arrays):
+        return [pltpu.with_memory_space_constraint(a, pltpu.HBM) for a in arrays]
+
+    to_up, to_down = pl.pallas_call(
+        edges_kernel,
+        out_shape=(edge, edge),
+        in_specs=[OFFCHIP] * 3,
+        out_specs=(ONCHIP,) * 2,
+        scratch_shapes=[pltpu.SemaphoreType.DMA((6 * tiles,))],
         compiler_params=params,
-        cost_estimate=pl.CostEstimate(flops=cells, bytes_accessed=20 * cells, transcendentals=cells),
-    )(*[pltpu.with_memory_space_constraint(a, pltpu.HBM) for a in inputs])
+        cost_estimate=pl.CostEstimate(flops=1, bytes_accessed=1, transcendentals=0),
+    )(*offchip(start_pressure, source, observe))
+    K, top, bottom = pl.pallas_call(
+        conduct_kernel,
+        out_shape=(field, rim, rim),
+        in_specs=[OFFCHIP] * 2,
+        out_specs=(ONCHIP,) * 3,
+        scratch_shapes=[pltpu.VMEM((slab, nx, ny), f32)] * 2 + [pltpu.SemaphoreType.DMA((2,))],
+        compiler_params=params,
+        cost_estimate=pl.CostEstimate(flops=1, bytes_accessed=1, transcendentals=0),
+    )(*offchip(log_perm, noise[0]))
     alo = lax.ppermute(to_up, "space", up)
     ahi = lax.ppermute(to_down, "space", down)
     klo = lax.ppermute(top, "space", up)

time: 43.2 us -> 42.5 us (0.984)
  waiting for transfers between devices: 10.9 us -> 9.53 us
  Pallas kernels: 13.2 us -> 13.9 us
    ppermute x1, waiting for transfers between devices: 1.39 us -> 0.01 us  [local(): alo = lax.ppermute(to_up, 'space', up)]
    pallas_call x1 -> x2, Pallas kernels: 1.91 us -> 3.09 us  [the longest x1 1.57 us: local(): pl.pallas_call(conduct_kernel, out_shape=(field, rim, rim), in_specs=[OFF...]
  transfers between devices with their start and end apart: 14 -> 14, of which waited for: 5 -> 4; matrix products, arithmetic and copies ran while one was open for 0% -> 0% of each run, Pallas kernels for 26% -> 29%
where the time goes in v10:
time: 42.5 us; the launch traced here: 42.3 us
  starting transfers between devices  17.1 us (40%)
  Pallas kernels  13.9 us (33%)
  waiting for transfers between devices  9.53 us (22%)
  between operations  0.87 us (2%)
  other arithmetic  0.73 us (2%)
    pallas_call x4, Pallas kernels, side(): pl.pallas_call(functools.partial(side_kernel, low, stages, [part[:-1] for...  6.91 us
    ppermute x1, starting transfers between devices, local(): alo = lax.ppermute(to_up, 'space', up)  4.96 us
    ppermute x1, starting transfers between devices, local(): klo = lax.ppermute(top, 'space', up)  4.57 us
    ppermute x1, waiting for transfers between devices, local(): ahi = lax.ppermute(to_down, 'space', down)  4.38 us
    pallas_call x1, Pallas kernels, local(): pl.pallas_call(inner_kernel, out_shape=(*kinds[1:], mid), in_specs=[ONCHI...  2.86 us
    ppermute x1, waiting for transfers between devices, local(): lax.ppermute(a, 'draw', [(j, (j + 2 * s) % draws) for j in range(draws)])  2.2 us
    ppermute x1, waiting for transfers between devices, local(): klo = lax.ppermute(top, 'space', up)  2.01 us
    pallas_call x1, Pallas kernels, local(): pl.pallas_call(conduct_kernel, out_shape=(field, rim, rim), in_specs=[OFF...  1.57 us
  transfers between devices with their start and end apart: 14, of which 4 were waited for; matrix products, arithmetic and copies ran while one was open for 0% of the time, Pallas kernels for 29%

profile of v10, /device:TPU:0, one launch (start us, length us, event | category | flops | bytes accessed | tf_op | source)
XLA Modules:
  0.0 42.3 jit_solution(13423864191789833700)
XLA Ops:
  0.6 0.0 copy-start.1
  0.6 0.0 copy-start
  0.7 0.0 copy-start.2
  0.7 1.5 %shard_map.69 = (f32[10,3,32,128]{3,2,1,0:T(8,128)S(1)}, f32[10,3,32,128]{3,2,1,0:T(8,128)S(1)}) custom-call(f32[8,64,384]{2,1,0:T(8,128)} %p0.3, f32[8,64,384]{2,1,0:T(8,128)} %src.3, f32[8,64,384]{2,1,0:T(8,128)} %obs.3), custom_call_target="tpu_custom_call" | custom-call | flops 1 | bytes 1 | tf_op jit(solution)/shard_map/pallas_call | solution.py:365
  2.2 5.0 %collective-permute-start.1 = (f32[10,3,32,128]{3,2,1,0:T(8,128)S(1)}, f32[10,3,32,128]{3,2,1,0:T(8,128)S(1)}, u32[]{:S(2)}, u32[]{:S(2)}) collective-permute-start(f32[10,3,32,128]{3,2,1,0:T(8,128)S(1)} %get-tuple-element.107), channel_id=1, source_target_pairs={{0,4},{4,8},{8,12},{1,5},{5,9},{9,13},{2,6},{6,10},{10,14},{3,7},{... | collective-permute-start | bytes 1474568 | tf_op jit(solution)/shard_map/ppermute | solution.py:383
  7.2 1.3 %collective-permute-start.2 = (f32[10,3,32,128]{3,2,1,0:T(8,128)S(1)}, f32[10,3,32,128]{3,2,1,0:T(8,128)S(1)}, u32[]{:S(2)}, u32[]{:S(2)}) collective-permute-start(f32[10,3,32,128]{3,2,1,0:T(8,128)S(1)} %get-tuple-element.108), channel_id=1, source_target_pairs={{4,0},{8,4},{12,8},{5,1},{9,5},{13,9},{6,2},{10,6},{14,10},{7,3},{... | collective-permute-start | bytes 1474568 | tf_op jit(solution)/shard_map/ppermute | solution.py:384
  8.5 1.6 %shard_map.68 = (f32[16,3,64,128]{3,2,1,0:T(8,128)S(1)}, f32[4,3,64,128]{3,2,1,0:T(8,128)S(1)}, f32[4,3,64,128]{3,2,1,0:T(8,128)S(1)}) custom-call(f32[8,64,384]{2,1,0:T(8,128)} %log_perm.1, f32[8,64,384]{2,1,0:T(8,128)} %bitcast.10), custom_call_target="tpu_custom_call" | custom-call | flops 1 | bytes 1 | tf_op jit(solution)/shard_map/pallas_call | solution.py:374
  10.0 4.6 %collective-permute-start = (f32[4,3,64,128]{3,2,1,0:T(8,128)S(1)}, f32[4,3,64,128]{3,2,1,0:T(8,128)S(1)}, u32[]{:S(2)}, u32[]{:S(2)}) collective-permute-start(f32[4,3,64,128]{3,2,1,0:T(8,128)S(1)} %get-tuple-element.106), channel_id=1, source_target_pairs={{0,4},{4,8},{8,12},{1,5},{5,9},{9,13},{2,6},{6,10},{10,14},{3,7},{... | collective-permute-start | bytes 1179656 | tf_op jit(solution)/shard_map/ppermute | solution.py:385
  14.6 1.3 %collective-permute-start.5 = (f32[4,3,64,128]{3,2,1,0:T(8,128)S(1)}, f32[4,3,64,128]{3,2,1,0:T(8,128)S(1)}, u32[]{:S(2)}, u32[]{:S(2)}) collective-permute-start(f32[4,3,64,128]{3,2,1,0:T(8,128)S(1)} %get-tuple-element.145), channel_id=1, source_target_pairs={{4,0},{8,4},{12,8},{5,1},{9,5},{13,9},{6,2},{10,6},{14,10},{7,3},{... | collective-permute-start | bytes 1179656 | tf_op jit(solution)/shard_map/ppermute | solution.py:386
  15.9 0.0 copy-done.1
  15.9 0.0 copy-done
  15.9 0.0 copy-done.2
  15.9 2.9 %shard_map.70 = (f32[16,3,64,128]{3,2,1,0:T(8,128)S(1)}, f32[16,3,64,128]{3,2,1,0:T(8,128)S(1)}, f32[16,3,64,128]{3,2,1,0:T(8,128)S(1)}, f32[16,3,64,128]{3,2,1,...) custom-call(f32[16,3,64,128]{3,2,1,0:T(8,128)S(1)} %get-tuple-elemen, ...), custom_call_target="tpu_custom_call" | custom-call | flops 39321600 | bytes 11796480 | tf_op jit(solution)/shard_map/pallas_call | solution.py:387
  18.8 0.0 collective-permute-done.1.args_1_
  18.8 4.4 %collective-permute-done.2.args_1_ = f32[10,3,32,128]{3,2,1,0:T(8,128)S(1)} collective-permute-done((f32[10,3,32,128]{3,2,1,0:T(8,128)S(1)}, f32[10,3,32,128]{3,2,1,0:T(8,128)S(1)}, u32[]{:S(2)}, u32[]{:S(2)}) %collective-permute-start.2) | collective-permute-done | bytes 491552 | tf_op jit(solution)/shard_map/ppermute | solution.py:384
  23.2 0.1 collective-permute-start.4
  23.3 0.6 %collective-permute-start.7 = (f32[6,3,32,128]{3,2,1,0:T(8,128)S(1)}, f32[6,3,32,128]{3,2,1,0:T(8,128)S(1)}, u32[]{:S(2)}, u32[]{:S(2)}) collective-permute-start(f32[6,3,32,128]{3,2,1,0:T(8,128)S(1)} %slice.15), channel_id=1, source_target_pairs={{0,1},{1,0},{2,3},{3,2},{4,5},{5,4},{6,7},{7,6},{8,9},{9,8},{10,11... | collective-permute-start | bytes 884744 | tf_op jit(solution)/shard_map/ppermute | solution.py:421
  23.9 0.1 collective-permute-start.3
  24.0 2.0 %collective-permute-done.args_0_ = f32[4,3,64,128]{3,2,1,0:T(8,128)S(1)} collective-permute-done((f32[4,3,64,128]{3,2,1,0:T(8,128)S(1)}, f32[4,3,64,128]{3,2,1,0:T(8,128)S(1)}, u32[]{:S(2)}, u32[]{:S(2)}) %collective-permute-start) | collective-permute-done | bytes 393248 | tf_op jit(solution)/shard_map/ppermute | solution.py:385
  26.0 0.0 collective-permute-start.6
  26.0 0.0 collective-permute-done.3.args_2_
  26.0 0.0 collective-permute-done.4.args_3_
  26.0 2.1 %shard_map.71 = (f32[16,3,64,128]{3,2,1,0:T(8,128)S(1)}, f32[16,3,64,128]{3,2,1,0:T(8,128)S(1)}, f32[16,3,64,128]{3,2,1,0:T(8,128)S(1)}, f32[16,3,64,128]{3,2,1,...) custom-call(f32[4,3,64,128]{3,2,1,0:T(8,128)S(1)} %collective-permut, ...), custom_call_target="tpu_custom_call", output_to_operand_aliasing={{0}: (4, {}), {1}: (5, {}), {2}: (6, {}), {3}: (7, {}), {4}... | custom-call | flops 1 | bytes 1 | tf_op jit(solution)/shard_map/pallas_call | solution.py:406
  28.1 1.5 %shard_map.72 = (f32[16,3,64,128]{3,2,1,0:T(8,128)S(1)}, f32[16,3,64,128]{3,2,1,0:T(8,128)S(1)}, f32[16,3,64,128]{3,2,1,0:T(8,128)S(1)}, f32[16,3,64,128]{3,2,1,...) custom-call(f32[16,3,64,128]{3,2,1,0:T(8,128)S(1)} %get-tuple-elemen, ...), custom_call_target="tpu_custom_call", output_to_operand_aliasing={{0}: (0, {}), {1}: (1, {}), {2}: (2, {}), {3}: (3, {}), {4}... | custom-call | flops 1 | bytes 1 | tf_op jit(solution)/shard_map/pallas_call | solution.py:406
  29.6 0.5 %collective-permute-start.8 = (f32[1,4,16,384]{3,2,1,0:T(8,128)S(1)}, f32[1,4,16,384]{3,2,1,0:T(8,128)S(1)}, u32[]{:S(2)}, u32[]{:S(2)}) collective-permute-start(f32[1,4,16,384]{3,2,1,0:T(8,128)S(1)} %get-tuple-element.178), channel_id=1, source_target_pairs={{0,1},{1,0},{2,3},{3,2},{4,5},{5,4},{6,7},{7,6},{8,9},{9,8},{10,11... | collective-permute-start | bytes 294920 | tf_op jit(solution)/shard_map/ppermute | solution.py:432
  30.1 0.1 collective-permute-start.9
  30.2 0.0 collective-permute-done.5.args_0_
  30.2 0.0 collective-permute-done.6.args_2_
  30.2 0.0 collective-permute-done.7.args_3_
  30.2 1.2 %shard_map.73 = (f32[16,3,64,128]{3,2,1,0:T(8,128)S(1)}, f32[16,3,64,128]{3,2,1,0:T(8,128)S(1)}, f32[16,3,64,128]{3,2,1,0:T(8,128)S(1)}, f32[16,3,64,128]{3,2,1,...) custom-call(f32[4,3,64,128]{3,2,1,0:T(8,128)S(1)} %collective-permut, ...), custom_call_target="tpu_custom_call", output_to_operand_aliasing={{0}: (4, {}), {1}: (5, {}), {2}: (6, {}), {3}: (7, {}), {4}... | custom-call | flops 11796480 | bytes 11796480 | tf_op jit(solution)/shard_map/pallas_call | solution.py:406
  31.4 0.0 collective-permute-done.8
  31.4 0.0 collective-permute-done.9
  31.5 1.6 %collective-permute-start.10 = (f32[4,16,384]{2,1,0:T(8,128)S(1)}, f32[4,16,384]{2,1,0:T(8,128)S(1)}, u32[]{:S(2)}, u32[]{:S(2)}) collective-permute-start(f32[4,16,384]{2,1,0:T(8,128)S(1)} %add_bitcast_fusion.1), channel_id=1, source_target_pairs={{0,2},{1,3},{2,0},{3,1},{4,6},{5,7},{6,4},{7,5},{8,10},{9,11},{10,... | collective-permute-start | bytes 294920 | tf_op jit(solution)/shard_map/ppermute | solution.py:427
  33.0 2.2 %shard_map.74 = (f32[16,3,64,128]{3,2,1,0:T(8,128)S(1)}, f32[16,3,64,128]{3,2,1,0:T(8,128)S(1)}, f32[16,3,64,128]{3,2,1,0:T(8,128)S(1)}, f32[16,3,64,128]{3,2,1,...) custom-call(f32[16,3,64,128]{3,2,1,0:T(8,128)S(1)} %get-tuple-elemen, ...), custom_call_target="tpu_custom_call", output_to_operand_aliasing={{0}: (0, {}), {1}: (1, {}), {2}: (2, {}), {3}: (3, {}), {4}... | custom-call | flops 11796480 | bytes 11796480 | tf_op jit(solution)/shard_map/pallas_call | solution.py:406
  35.2 0.2 collective-permute-start.11
  35.4 0.4 collective-permute-start.12
  35.8 0.9 %collective-permute-done.10 = f32[4,16,384]{2,1,0:T(8,128)S(1)} collective-permute-done((f32[4,16,384]{2,1,0:T(8,128)S(1)}, f32[4,16,384]{2,1,0:T(8,128)S(1)}, u32[]{:S(2)}, u32[]{:S(2)}) %collective-permute-start.10) | collective-permute-done | bytes 98336 | tf_op jit(solution)/shard_map/ppermute | solution.py:427
  36.7 0.2 shard_map.75
  36.9 0.0 collective-permute-done.11
  36.9 1.6 %collective-permute-start.13 = (f32[4,16,384]{2,1,0:T(8,128)S(1)}, f32[4,16,384]{2,1,0:T(8,128)S(1)}, u32[]{:S(2)}, u32[]{:S(2)}) collective-permute-start(f32[4,16,384]{2,1,0:T(8,128)S(1)} %add_bitcast_fusion), channel_id=1, source_target_pairs={{0,2},{1,3},{2,0},{3,1},{4,6},{5,7},{6,4},{7,5},{8,10},{9,11},{10,... | collective-permute-start | bytes 294920 | tf_op jit(solution)/shard_map/ppermute | solution.py:461
  38.4 0.9 %shard_map.76 = (f32[8,64,384]{2,1,0:T(8,128)}, f32[1,8,16,384]{3,2,1,0:T(8,128)S(1)}) custom-call(f32[3,64,384]{2,1,0:T(8,128)S(1)} %get-tuple-element.143.args_0_, f32[2,64,384]{2,1,0:T(8,128)S(1)} %get-tuple-element.144.args_1_, f32[3,64,384]{2,1,0:T(8,128)S(1)} %get-tuple-element.182.args_2_, f32[16,3,64,128]{3,2,1,0:T(8,128)S(1)} %get-tuple-element.183.args_0_.args_3_, ...), custom_call_target="tpu_custom_call" | custom-call | flops 5898240 | bytes 5898240 | tf_op jit(solution)/shard_map/pallas_call | solution.py:463
  39.4 0.0 collective-permute-done.12
  39.4 2.2 %collective-permute-done.13 = f32[4,16,384]{2,1,0:T(8,128)S(1)} collective-permute-done((f32[4,16,384]{2,1,0:T(8,128)S(1)}, f32[4,16,384]{2,1,0:T(8,128)S(1)}, u32[]{:S(2)}, u32[]{:S(2)}) %collective-permute-start.13) | collective-permute-done | bytes 98336 | tf_op jit(solution)/shard_map/ppermute | solution.py:461
  41.6 0.7 %fusion = f32[8,16,384]{2,1,0:T(8,128)} fusion(f32[4,16,384]{2,1,0:T(8,128)S(1)} %bitcast.12, f32[4,16,384]{2,1,0:T(8,128)S(1)} %bitcast.11, f32[4,16,384]{2,1,0:T(8,128)S(1)} %collective-permute-done.13, f32[4,16,384]{2,1,0:T(8,128)S(1)} %collective-permute-done.10, f32[1,8,16,384]{3,2,1,0:T(8,128)S(1)} %get-tuple-element.205), kind=kLoop, calls=%fused_computation.1 | loop fusion | flops 196608 | bytes 786432 | tf_op jit(solution)/shard_map/add | solution.py:474
  (6 shorter events, 0.1 us)
Async XLA Ops:
  0.6 15.3 %copy-start.1 = (f32[8,64,384]{2,1,0:T(8,128)S(1)}, f32[8,64,384]{2,1,0:T(8,128)}, u32[]{:S(2)}) copy-start(f32[8,64,384]{2,1,0:T(8,128)} %src.3) | copy-start | bytes 2359300
  0.6 15.3 %copy-start = (f32[8,64,384]{2,1,0:T(8,128)S(1)}, f32[8,64,384]{2,1,0:T(8,128)}, u32[]{:S(2)}) copy-start(f32[8,64,384]{2,1,0:T(8,128)} %p0.3) | copy-start | bytes 2359300
  0.7 15.3 %copy-start.2 = (f32[8,64,384]{2,1,0:T(8,128)S(1)}, f32[8,64,384]{2,1,0:T(8,128)}, u32[]{:S(2)}) copy-start(f32[8,64,384]{2,1,0:T(8,128)} %obs.3) | copy-start | bytes 2359300
  2.2 16.6 %collective-permute-start.1 = (f32[10,3,32,128]{3,2,1,0:T(8,128)S(1)}, f32[10,3,32,128]{3,2,1,0:T(8,128)S(1)}, u32[]{:S(2)}, u32[]{:S(2)}) collective-permute-start(f32[10,3,32,128]{3,2,1,0:T(8,128)S(1)} %get-tuple-element.107), channel_id=1, source_target_pairs={{0,4},{4,8},{8,12},{1,5},{5,9},{9,13},{2,6},{6,10},{10,14},{3,7},{... | collective-permute-start | bytes 1474568 | tf_op jit(solution)/shard_map/ppermute | solution.py:383
  7.2 16.0 %collective-permute-start.2 = (f32[10,3,32,128]{3,2,1,0:T(8,128)S(1)}, f32[10,3,32,128]{3,2,1,0:T(8,128)S(1)}, u32[]{:S(2)}, u32[]{:S(2)}) collective-permute-start(f32[10,3,32,128]{3,2,1,0:T(8,128)S(1)} %get-tuple-element.108), channel_id=1, source_target_pairs={{4,0},{8,4},{12,8},{5,1},{9,5},{13,9},{6,2},{10,6},{14,10},{7,3},{... | collective-permute-start | bytes 1474568 | tf_op jit(solution)/shard_map/ppermute | solution.py:384
  10.0 16.0 %collective-permute-start = (f32[4,3,64,128]{3,2,1,0:T(8,128)S(1)}, f32[4,3,64,128]{3,2,1,0:T(8,128)S(1)}, u32[]{:S(2)}, u32[]{:S(2)}) collective-permute-start(f32[4,3,64,128]{3,2,1,0:T(8,128)S(1)} %get-tuple-element.106), channel_id=1, source_target_pairs={{0,4},{4,8},{8,12},{1,5},{5,9},{9,13},{2,6},{6,10},{10,14},{3,7},{... | collective-permute-start | bytes 1179656 | tf_op jit(solution)/shard_map/ppermute | solution.py:385
  14.6 15.6 %collective-permute-start.5 = (f32[4,3,64,128]{3,2,1,0:T(8,128)S(1)}, f32[4,3,64,128]{3,2,1,0:T(8,128)S(1)}, u32[]{:S(2)}, u32[]{:S(2)}) collective-permute-start(f32[4,3,64,128]{3,2,1,0:T(8,128)S(1)} %get-tuple-element.145), channel_id=1, source_target_pairs={{4,0},{8,4},{12,8},{5,1},{9,5},{13,9},{6,2},{10,6},{14,10},{7,3},{... | collective-permute-start | bytes 1179656 | tf_op jit(solution)/shard_map/ppermute | solution.py:386
  23.2 2.8 %collective-permute-start.4 = (f32[6,3,32,128]{3,2,1,0:T(8,128)S(1)}, f32[6,3,32,128]{3,2,1,0:T(8,128)S(1)}, u32[]{:S(2)}, u32[]{:S(2)}) collective-permute-start(f32[6,3,32,128]{3,2,1,0:T(8,128)S(1)} %slice.13), channel_id=1, source_target_pairs={{0,1},{1,0},{2,3},{3,2},{4,5},{5,4},{6,7},{7,6},{8,9},{9,8},{10,11... | collective-permute-start | bytes 884744 | tf_op jit(solution)/shard_map/ppermute | solution.py:421
  23.3 6.9 %collective-permute-start.7 = (f32[6,3,32,128]{3,2,1,0:T(8,128)S(1)}, f32[6,3,32,128]{3,2,1,0:T(8,128)S(1)}, u32[]{:S(2)}, u32[]{:S(2)}) collective-permute-start(f32[6,3,32,128]{3,2,1,0:T(8,128)S(1)} %slice.15), channel_id=1, source_target_pairs={{0,1},{1,0},{2,3},{3,2},{4,5},{5,4},{6,7},{7,6},{8,9},{9,8},{10,11... | collective-permute-start | bytes 884744 | tf_op jit(solution)/shard_map/ppermute | solution.py:421
  23.9 2.1 %collective-permute-start.3 = (f32[4,3,32,128]{3,2,1,0:T(8,128)S(1)}, f32[4,3,32,128]{3,2,1,0:T(8,128)S(1)}, u32[]{:S(2)}, u32[]{:S(2)}) collective-permute-start(f32[4,3,32,128]{3,2,1,0:T(8,128)S(1)} %slice.12), channel_id=1, source_target_pairs={{0,1},{1,0},{2,3},{3,2},{4,5},{5,4},{6,7},{7,6},{8,9},{9,8},{10,11... | collective-permute-start | bytes 589832 | tf_op jit(solution)/shard_map/ppermute | solution.py:421
  26.0 4.2 %collective-permute-start.6 = (f32[4,3,32,128]{3,2,1,0:T(8,128)S(1)}, f32[4,3,32,128]{3,2,1,0:T(8,128)S(1)}, u32[]{:S(2)}, u32[]{:S(2)}) collective-permute-start(f32[4,3,32,128]{3,2,1,0:T(8,128)S(1)} %slice.14), channel_id=1, source_target_pairs={{0,1},{1,0},{2,3},{3,2},{4,5},{5,4},{6,7},{7,6},{8,9},{9,8},{10,11... | collective-permute-start | bytes 589832 | tf_op jit(solution)/shard_map/ppermute | solution.py:421
  29.6 1.9 %collective-permute-start.8 = (f32[1,4,16,384]{3,2,1,0:T(8,128)S(1)}, f32[1,4,16,384]{3,2,1,0:T(8,128)S(1)}, u32[]{:S(2)}, u32[]{:S(2)}) collective-permute-start(f32[1,4,16,384]{3,2,1,0:T(8,128)S(1)} %get-tuple-element.178), channel_id=1, source_target_pairs={{0,1},{1,0},{2,3},{3,2},{4,5},{5,4},{6,7},{7,6},{8,9},{9,8},{10,11... | collective-permute-start | bytes 294920 | tf_op jit(solution)/shard_map/ppermute | solution.py:432
  30.1 1.3 %collective-permute-start.9 = (f32[1,4,16,384]{3,2,1,0:T(8,128)S(1)}, f32[1,4,16,384]{3,2,1,0:T(8,128)S(1)}, u32[]{:S(2)}, u32[]{:S(2)}) collective-permute-start(f32[1,4,16,384]{3,2,1,0:T(8,128)S(1)} %get-tuple-element.179), channel_id=1, source_target_pairs={{0,1},{1,0},{2,3},{3,2},{4,5},{5,4},{6,7},{7,6},{8,9},{9,8},{10,11... | collective-permute-start | bytes 294920 | tf_op jit(solution)/shard_map/ppermute | solution.py:432
  31.5 5.2 %collective-permute-start.10 = (f32[4,16,384]{2,1,0:T(8,128)S(1)}, f32[4,16,384]{2,1,0:T(8,128)S(1)}, u32[]{:S(2)}, u32[]{:S(2)}) collective-permute-start(f32[4,16,384]{2,1,0:T(8,128)S(1)} %add_bitcast_fusion.1), channel_id=1, source_target_pairs={{0,2},{1,3},{2,0},{3,1},{4,6},{5,7},{6,4},{7,5},{8,10},{9,11},{10,... | collective-permute-start | bytes 294920 | tf_op jit(solution)/shard_map/ppermute | solution.py:427
  35.2 1.7 %collective-permute-start.11 = (f32[1,4,16,384]{3,2,1,0:T(8,128)S(1)}, f32[1,4,16,384]{3,2,1,0:T(8,128)S(1)}, u32[]{:S(2)}, u32[]{:S(2)}) collective-permute-start(f32[1,4,16,384]{3,2,1,0:T(8,128)S(1)} %get-tuple-element.202), channel_id=1, source_target_pairs={{0,1},{1,0},{2,3},{3,2},{4,5},{5,4},{6,7},{7,6},{8,9},{9,8},{10,11... | collective-permute-start | bytes 294920 | tf_op jit(solution)/shard_map/ppermute | solution.py:432
  35.4 4.0 %collective-permute-start.12 = (f32[1,4,16,384]{3,2,1,0:T(8,128)S(1)}, f32[1,4,16,384]{3,2,1,0:T(8,128)S(1)}, u32[]{:S(2)}, u32[]{:S(2)}) collective-permute-start(f32[1,4,16,384]{3,2,1,0:T(8,128)S(1)} %get-tuple-element.207), channel_id=1, source_target_pairs={{0,1},{1,0},{2,3},{3,2},{4,5},{5,4},{6,7},{7,6},{8,9},{9,8},{10,11... | collective-permute-start | bytes 294920 | tf_op jit(solution)/shard_map/ppermute | solution.py:432
  36.9 4.7 %collective-permute-start.13 = (f32[4,16,384]{2,1,0:T(8,128)S(1)}, f32[4,16,384]{2,1,0:T(8,128)S(1)}, u32[]{:S(2)}, u32[]{:S(2)}) collective-permute-start(f32[4,16,384]{2,1,0:T(8,128)S(1)} %add_bitcast_fusion), channel_id=1, source_target_pairs={{0,2},{1,3},{2,0},{3,1},{4,6},{5,7},{6,4},{7,5},{8,10},{9,11},{10,... | collective-permute-start | bytes 294920 | tf_op jit(solution)/shard_map/ppermute | solution.py:461

commit v11 on v10

--- a/solution.py
+++ b/solution.py
@@ -172,7 +172,7 @@
     for body, spans in zip(stages, ranges):
         for span in spans:
             lo, hi, *own = span
-            lax.fori_loop(lo, hi, lambda zz, _, body=body, own=own: body(zz, *own) or 0, 0)
+            lax.fori_loop(lo, hi, lambda zz, _, body=body, own=own: body(zz, *own) or 0, 0, unroll=hi - lo <= HALO)
 
 
 def edges_kernel(p0, src, obs, up, down, sems):

time: 42.5 us -> 42.1 us (level)
  Pallas kernels: 13.9 us -> 13.2 us
    pallas_call x4, Pallas kernels: 6.91 us -> 6.3 us  [side(): pl.pallas_call(functools.partial(side_kernel, low, stages, [part[:-1] for...]
  transfers between devices with their start and end apart: 14 -> 14, of which waited for: 4 -> 5; matrix products, arithmetic and copies ran while one was open for 0% -> 0% of each run, Pallas kernels for 29% -> 28%
where the time goes in v11:
time: 42.1 us; the launch traced here: 41.9 us
  starting transfers between devices  17.1 us (41%)
  Pallas kernels  13.2 us (31%)
  waiting for transfers between devices  9.85 us (23%)
  between operations  0.87 us (2%)
  other arithmetic  0.73 us (2%)
    pallas_call x4, Pallas kernels, side(): pl.pallas_call(functools.partial(side_kernel, low, stages, [part[:-1] for...  6.3 us
    ppermute x1, starting transfers between devices, local(): alo = lax.ppermute(to_up, 'space', up)  4.96 us
    ppermute x1, starting transfers between devices, local(): klo = lax.ppermute(top, 'space', up)  4.57 us
    ppermute x1, waiting for transfers between devices, local(): ahi = lax.ppermute(to_down, 'space', down)  4.46 us
    pallas_call x1, Pallas kernels, local(): pl.pallas_call(inner_kernel, out_shape=(*kinds[1:], mid), in_specs=[ONCHI...  2.76 us
    ppermute x1, waiting for transfers between devices, local(): lax.ppermute(a, 'draw', [(j, (j + 2 * s) % draws) for j in range(draws)])  2.28 us
    ppermute x1, waiting for transfers between devices, local(): klo = lax.ppermute(top, 'space', up)  2.01 us
    pallas_call x1, Pallas kernels, local(): pl.pallas_call(conduct_kernel, out_shape=(field, rim, rim), in_specs=[OFF...  1.57 us
  transfers between devices with their start and end apart: 14, of which 5 were waited for; matrix products, arithmetic and copies ran while one was open for 0% of the time, Pallas kernels for 28%

profile of v11, /device:TPU:0, one launch (start us, length us, event | category | flops | bytes accessed | tf_op | source)
XLA Modules:
  0.0 41.9 jit_solution(9176140921709769876)
XLA Ops:
  0.6 0.0 copy-start.1
  0.6 0.0 copy-start
  0.7 0.0 copy-start.2
  0.7 1.5 %shard_map.69 = (f32[10,3,32,128]{3,2,1,0:T(8,128)S(1)}, f32[10,3,32,128]{3,2,1,0:T(8,128)S(1)}) custom-call(f32[8,64,384]{2,1,0:T(8,128)} %p0.3, f32[8,64,384]{2,1,0:T(8,128)} %src.3, f32[8,64,384]{2,1,0:T(8,128)} %obs.3), custom_call_target="tpu_custom_call" | custom-call | flops 1 | bytes 1 | tf_op jit(solution)/shard_map/pallas_call | solution.py:365
  2.2 5.0 %collective-permute-start.1 = (f32[10,3,32,128]{3,2,1,0:T(8,128)S(1)}, f32[10,3,32,128]{3,2,1,0:T(8,128)S(1)}, u32[]{:S(2)}, u32[]{:S(2)}) collective-permute-start(f32[10,3,32,128]{3,2,1,0:T(8,128)S(1)} %get-tuple-element.107), channel_id=1, source_target_pairs={{0,4},{4,8},{8,12},{1,5},{5,9},{9,13},{2,6},{6,10},{10,14},{3,7},{... | collective-permute-start | bytes 1474568 | tf_op jit(solution)/shard_map/ppermute | solution.py:383
  7.2 1.3 %collective-permute-start.2 = (f32[10,3,32,128]{3,2,1,0:T(8,128)S(1)}, f32[10,3,32,128]{3,2,1,0:T(8,128)S(1)}, u32[]{:S(2)}, u32[]{:S(2)}) collective-permute-start(f32[10,3,32,128]{3,2,1,0:T(8,128)S(1)} %get-tuple-element.108), channel_id=1, source_target_pairs={{4,0},{8,4},{12,8},{5,1},{9,5},{13,9},{6,2},{10,6},{14,10},{7,3},{... | collective-permute-start | bytes 1474568 | tf_op jit(solution)/shard_map/ppermute | solution.py:384
  8.5 1.6 %shard_map.68 = (f32[16,3,64,128]{3,2,1,0:T(8,128)S(1)}, f32[4,3,64,128]{3,2,1,0:T(8,128)S(1)}, f32[4,3,64,128]{3,2,1,0:T(8,128)S(1)}) custom-call(f32[8,64,384]{2,1,0:T(8,128)} %log_perm.1, f32[8,64,384]{2,1,0:T(8,128)} %bitcast.10), custom_call_target="tpu_custom_call" | custom-call | flops 1 | bytes 1 | tf_op jit(solution)/shard_map/pallas_call | solution.py:374
  10.0 4.6 %collective-permute-start = (f32[4,3,64,128]{3,2,1,0:T(8,128)S(1)}, f32[4,3,64,128]{3,2,1,0:T(8,128)S(1)}, u32[]{:S(2)}, u32[]{:S(2)}) collective-permute-start(f32[4,3,64,128]{3,2,1,0:T(8,128)S(1)} %get-tuple-element.106), channel_id=1, source_target_pairs={{0,4},{4,8},{8,12},{1,5},{5,9},{9,13},{2,6},{6,10},{10,14},{3,7},{... | collective-permute-start | bytes 1179656 | tf_op jit(solution)/shard_map/ppermute | solution.py:385
  14.6 1.3 %collective-permute-start.5 = (f32[4,3,64,128]{3,2,1,0:T(8,128)S(1)}, f32[4,3,64,128]{3,2,1,0:T(8,128)S(1)}, u32[]{:S(2)}, u32[]{:S(2)}) collective-permute-start(f32[4,3,64,128]{3,2,1,0:T(8,128)S(1)} %get-tuple-element.145), channel_id=1, source_target_pairs={{4,0},{8,4},{12,8},{5,1},{9,5},{13,9},{6,2},{10,6},{14,10},{7,3},{... | collective-permute-start | bytes 1179656 | tf_op jit(solution)/shard_map/ppermute | solution.py:386
  15.9 0.0 copy-done.1
  15.9 0.0 copy-done
  15.9 0.0 copy-done.2
  15.9 2.8 %shard_map.70 = (f32[16,3,64,128]{3,2,1,0:T(8,128)S(1)}, f32[16,3,64,128]{3,2,1,0:T(8,128)S(1)}, f32[16,3,64,128]{3,2,1,0:T(8,128)S(1)}, f32[16,3,64,128]{3,2,1,...) custom-call(f32[16,3,64,128]{3,2,1,0:T(8,128)S(1)} %get-tuple-elemen, ...), custom_call_target="tpu_custom_call" | custom-call | flops 39321600 | bytes 11796480 | tf_op jit(solution)/shard_map/pallas_call | solution.py:387
  18.7 0.0 collective-permute-done.1.args_1_
  18.7 4.5 %collective-permute-done.2.args_1_ = f32[10,3,32,128]{3,2,1,0:T(8,128)S(1)} collective-permute-done((f32[10,3,32,128]{3,2,1,0:T(8,128)S(1)}, f32[10,3,32,128]{3,2,1,0:T(8,128)S(1)}, u32[]{:S(2)}, u32[]{:S(2)}) %collective-permute-start.2) | collective-permute-done | bytes 491552 | tf_op jit(solution)/shard_map/ppermute | solution.py:384
  23.2 0.1 collective-permute-start.4
  23.3 0.6 %collective-permute-start.7 = (f32[6,3,32,128]{3,2,1,0:T(8,128)S(1)}, f32[6,3,32,128]{3,2,1,0:T(8,128)S(1)}, u32[]{:S(2)}, u32[]{:S(2)}) collective-permute-start(f32[6,3,32,128]{3,2,1,0:T(8,128)S(1)} %slice.15), channel_id=1, source_target_pairs={{0,1},{1,0},{2,3},{3,2},{4,5},{5,4},{6,7},{7,6},{8,9},{9,8},{10,11... | collective-permute-start | bytes 884744 | tf_op jit(solution)/shard_map/ppermute | solution.py:421
  23.9 0.1 collective-permute-start.3
  24.0 2.0 %collective-permute-done.args_0_ = f32[4,3,64,128]{3,2,1,0:T(8,128)S(1)} collective-permute-done((f32[4,3,64,128]{3,2,1,0:T(8,128)S(1)}, f32[4,3,64,128]{3,2,1,0:T(8,128)S(1)}, u32[]{:S(2)}, u32[]{:S(2)}) %collective-permute-start) | collective-permute-done | bytes 393248 | tf_op jit(solution)/shard_map/ppermute | solution.py:385
  26.0 0.0 collective-permute-start.6
  26.0 0.0 collective-permute-done.3.args_2_
  26.0 0.0 collective-permute-done.4.args_3_
  26.0 1.9 %shard_map.71 = (f32[16,3,64,128]{3,2,1,0:T(8,128)S(1)}, f32[16,3,64,128]{3,2,1,0:T(8,128)S(1)}, f32[16,3,64,128]{3,2,1,0:T(8,128)S(1)}, f32[16,3,64,128]{3,2,1,...) custom-call(f32[4,3,64,128]{3,2,1,0:T(8,128)S(1)} %collective-permut, ...), custom_call_target="tpu_custom_call", output_to_operand_aliasing={{0}: (4, {}), {1}: (5, {}), {2}: (6, {}), {3}: (7, {}), {4}... | custom-call | flops 1 | bytes 1 | tf_op jit(solution)/shard_map/pallas_call | solution.py:406
  27.9 1.4 %shard_map.72 = (f32[16,3,64,128]{3,2,1,0:T(8,128)S(1)}, f32[16,3,64,128]{3,2,1,0:T(8,128)S(1)}, f32[16,3,64,128]{3,2,1,0:T(8,128)S(1)}, f32[16,3,64,128]{3,2,1,...) custom-call(f32[16,3,64,128]{3,2,1,0:T(8,128)S(1)} %get-tuple-elemen, ...), custom_call_target="tpu_custom_call", output_to_operand_aliasing={{0}: (0, {}), {1}: (1, {}), {2}: (2, {}), {3}: (3, {}), {4}... | custom-call | flops 1 | bytes 1 | tf_op jit(solution)/shard_map/pallas_call | solution.py:406
  29.2 0.5 %collective-permute-start.8 = (f32[1,4,16,384]{3,2,1,0:T(8,128)S(1)}, f32[1,4,16,384]{3,2,1,0:T(8,128)S(1)}, u32[]{:S(2)}, u32[]{:S(2)}) collective-permute-start(f32[1,4,16,384]{3,2,1,0:T(8,128)S(1)} %get-tuple-element.178), channel_id=1, source_target_pairs={{0,1},{1,0},{2,3},{3,2},{4,5},{5,4},{6,7},{7,6},{8,9},{9,8},{10,11... | collective-permute-start | bytes 294920 | tf_op jit(solution)/shard_map/ppermute | solution.py:432
  29.8 0.1 collective-permute-start.9
  29.9 0.3 collective-permute-done.5.args_0_
  30.2 0.0 collective-permute-done.6.args_2_
  30.2 0.0 collective-permute-done.7.args_3_
  30.2 1.0 %shard_map.73 = (f32[16,3,64,128]{3,2,1,0:T(8,128)S(1)}, f32[16,3,64,128]{3,2,1,0:T(8,128)S(1)}, f32[16,3,64,128]{3,2,1,0:T(8,128)S(1)}, f32[16,3,64,128]{3,2,1,...) custom-call(f32[4,3,64,128]{3,2,1,0:T(8,128)S(1)} %collective-permut, ...), custom_call_target="tpu_custom_call", output_to_operand_aliasing={{0}: (4, {}), {1}: (5, {}), {2}: (6, {}), {3}: (7, {}), {4}... | custom-call | flops 11796480 | bytes 11796480 | tf_op jit(solution)/shard_map/pallas_call | solution.py:406
  31.2 0.0 collective-permute-done.8
  31.2 0.0 collective-permute-done.9
  31.3 1.6 %collective-permute-start.10 = (f32[4,16,384]{2,1,0:T(8,128)S(1)}, f32[4,16,384]{2,1,0:T(8,128)S(1)}, u32[]{:S(2)}, u32[]{:S(2)}) collective-permute-start(f32[4,16,384]{2,1,0:T(8,128)S(1)} %add_bitcast_fusion.1), channel_id=1, source_target_pairs={{0,2},{1,3},{2,0},{3,1},{4,6},{5,7},{6,4},{7,5},{8,10},{9,11},{10,... | collective-permute-start | bytes 294920 | tf_op jit(solution)/shard_map/ppermute | solution.py:427
  32.8 2.1 %shard_map.74 = (f32[16,3,64,128]{3,2,1,0:T(8,128)S(1)}, f32[16,3,64,128]{3,2,1,0:T(8,128)S(1)}, f32[16,3,64,128]{3,2,1,0:T(8,128)S(1)}, f32[16,3,64,128]{3,2,1,...) custom-call(f32[16,3,64,128]{3,2,1,0:T(8,128)S(1)} %get-tuple-elemen, ...), custom_call_target="tpu_custom_call", output_to_operand_aliasing={{0}: (0, {}), {1}: (1, {}), {2}: (2, {}), {3}: (3, {}), {4}... | custom-call | flops 11796480 | bytes 11796480 | tf_op jit(solution)/shard_map/pallas_call | solution.py:406
  34.9 0.1 collective-permute-start.11
  34.9 0.5 %collective-permute-start.12 = (f32[1,4,16,384]{3,2,1,0:T(8,128)S(1)}, f32[1,4,16,384]{3,2,1,0:T(8,128)S(1)}, u32[]{:S(2)}, u32[]{:S(2)}) collective-permute-start(f32[1,4,16,384]{3,2,1,0:T(8,128)S(1)} %get-tuple-element.207), channel_id=1, source_target_pairs={{0,1},{1,0},{2,3},{3,2},{4,5},{5,4},{6,7},{7,6},{8,9},{9,8},{10,11... | collective-permute-start | bytes 294920 | tf_op jit(solution)/shard_map/ppermute | solution.py:432
  35.4 0.8 %collective-permute-done.10 = f32[4,16,384]{2,1,0:T(8,128)S(1)} collective-permute-done((f32[4,16,384]{2,1,0:T(8,128)S(1)}, f32[4,16,384]{2,1,0:T(8,128)S(1)}, u32[]{:S(2)}, u32[]{:S(2)}) %collective-permute-start.10) | collective-permute-done | bytes 98336 | tf_op jit(solution)/shard_map/ppermute | solution.py:427
  36.2 0.2 shard_map.75
  36.4 0.0 collective-permute-done.11
  36.4 1.6 %collective-permute-start.13 = (f32[4,16,384]{2,1,0:T(8,128)S(1)}, f32[4,16,384]{2,1,0:T(8,128)S(1)}, u32[]{:S(2)}, u32[]{:S(2)}) collective-permute-start(f32[4,16,384]{2,1,0:T(8,128)S(1)} %add_bitcast_fusion), channel_id=1, source_target_pairs={{0,2},{1,3},{2,0},{3,1},{4,6},{5,7},{6,4},{7,5},{8,10},{9,11},{10,... | collective-permute-start | bytes 294920 | tf_op jit(solution)/shard_map/ppermute | solution.py:461
  38.0 0.9 %shard_map.76 = (f32[8,64,384]{2,1,0:T(8,128)}, f32[1,8,16,384]{3,2,1,0:T(8,128)S(1)}) custom-call(f32[3,64,384]{2,1,0:T(8,128)S(1)} %get-tuple-element.143.args_0_, f32[2,64,384]{2,1,0:T(8,128)S(1)} %get-tuple-element.144.args_1_, f32[3,64,384]{2,1,0:T(8,128)S(1)} %get-tuple-element.182.args_2_, f32[16,3,64,128]{3,2,1,0:T(8,128)S(1)} %get-tuple-element.183.args_0_.args_3_, ...), custom_call_target="tpu_custom_call" | custom-call | flops 5898240 | bytes 5898240 | tf_op jit(solution)/shard_map/pallas_call | solution.py:463
  38.9 0.0 collective-permute-done.12
  38.9 2.3 %collective-permute-done.13 = f32[4,16,384]{2,1,0:T(8,128)S(1)} collective-permute-done((f32[4,16,384]{2,1,0:T(8,128)S(1)}, f32[4,16,384]{2,1,0:T(8,128)S(1)}, u32[]{:S(2)}, u32[]{:S(2)}) %collective-permute-start.13) | collective-permute-done | bytes 98336 | tf_op jit(solution)/shard_map/ppermute | solution.py:461
  41.2 0.7 %fusion = f32[8,16,384]{2,1,0:T(8,128)} fusion(f32[4,16,384]{2,1,0:T(8,128)S(1)} %bitcast.12, f32[4,16,384]{2,1,0:T(8,128)S(1)} %bitcast.11, f32[4,16,384]{2,1,0:T(8,128)S(1)} %collective-permute-done.13, f32[4,16,384]{2,1,0:T(8,128)S(1)} %collective-permute-done.10, f32[1,8,16,384]{3,2,1,0:T(8,128)S(1)} %get-tuple-element.205), kind=kLoop, calls=%fused_computation.1 | loop fusion | flops 196608 | bytes 786432 | tf_op jit(solution)/shard_map/add | solution.py:474
  (6 shorter events, 0.1 us)
Async XLA Ops:
  0.6 15.3 %copy-start.1 = (f32[8,64,384]{2,1,0:T(8,128)S(1)}, f32[8,64,384]{2,1,0:T(8,128)}, u32[]{:S(2)}) copy-start(f32[8,64,384]{2,1,0:T(8,128)} %src.3) | copy-start | bytes 2359300
  0.6 15.3 %copy-start = (f32[8,64,384]{2,1,0:T(8,128)S(1)}, f32[8,64,384]{2,1,0:T(8,128)}, u32[]{:S(2)}) copy-start(f32[8,64,384]{2,1,0:T(8,128)} %p0.3) | copy-start | bytes 2359300
  0.7 15.3 %copy-start.2 = (f32[8,64,384]{2,1,0:T(8,128)S(1)}, f32[8,64,384]{2,1,0:T(8,128)}, u32[]{:S(2)}) copy-start(f32[8,64,384]{2,1,0:T(8,128)} %obs.3) | copy-start | bytes 2359300
  2.2 16.5 %collective-permute-start.1 = (f32[10,3,32,128]{3,2,1,0:T(8,128)S(1)}, f32[10,3,32,128]{3,2,1,0:T(8,128)S(1)}, u32[]{:S(2)}, u32[]{:S(2)}) collective-permute-start(f32[10,3,32,128]{3,2,1,0:T(8,128)S(1)} %get-tuple-element.107), channel_id=1, source_target_pairs={{0,4},{4,8},{8,12},{1,5},{5,9},{9,13},{2,6},{6,10},{10,14},{3,7},{... | collective-permute-start | bytes 1474568 | tf_op jit(solution)/shard_map/ppermute | solution.py:383
  7.2 16.0 %collective-permute-start.2 = (f32[10,3,32,128]{3,2,1,0:T(8,128)S(1)}, f32[10,3,32,128]{3,2,1,0:T(8,128)S(1)}, u32[]{:S(2)}, u32[]{:S(2)}) collective-permute-start(f32[10,3,32,128]{3,2,1,0:T(8,128)S(1)} %get-tuple-element.108), channel_id=1, source_target_pairs={{4,0},{8,4},{12,8},{5,1},{9,5},{13,9},{6,2},{10,6},{14,10},{7,3},{... | collective-permute-start | bytes 1474568 | tf_op jit(solution)/shard_map/ppermute | solution.py:384
  10.0 16.0 %collective-permute-start = (f32[4,3,64,128]{3,2,1,0:T(8,128)S(1)}, f32[4,3,64,128]{3,2,1,0:T(8,128)S(1)}, u32[]{:S(2)}, u32[]{:S(2)}) collective-permute-start(f32[4,3,64,128]{3,2,1,0:T(8,128)S(1)} %get-tuple-element.106), channel_id=1, source_target_pairs={{0,4},{4,8},{8,12},{1,5},{5,9},{9,13},{2,6},{6,10},{10,14},{3,7},{... | collective-permute-start | bytes 1179656 | tf_op jit(solution)/shard_map/ppermute | solution.py:385
  14.6 15.5 %collective-permute-start.5 = (f32[4,3,64,128]{3,2,1,0:T(8,128)S(1)}, f32[4,3,64,128]{3,2,1,0:T(8,128)S(1)}, u32[]{:S(2)}, u32[]{:S(2)}) collective-permute-start(f32[4,3,64,128]{3,2,1,0:T(8,128)S(1)} %get-tuple-element.145), channel_id=1, source_target_pairs={{4,0},{8,4},{12,8},{5,1},{9,5},{13,9},{6,2},{10,6},{14,10},{7,3},{... | collective-permute-start | bytes 1179656 | tf_op jit(solution)/shard_map/ppermute | solution.py:386
  23.2 2.8 %collective-permute-start.4 = (f32[6,3,32,128]{3,2,1,0:T(8,128)S(1)}, f32[6,3,32,128]{3,2,1,0:T(8,128)S(1)}, u32[]{:S(2)}, u32[]{:S(2)}) collective-permute-start(f32[6,3,32,128]{3,2,1,0:T(8,128)S(1)} %slice.13), channel_id=1, source_target_pairs={{0,1},{1,0},{2,3},{3,2},{4,5},{5,4},{6,7},{7,6},{8,9},{9,8},{10,11... | collective-permute-start | bytes 884744 | tf_op jit(solution)/shard_map/ppermute | solution.py:421
  23.3 6.8 %collective-permute-start.7 = (f32[6,3,32,128]{3,2,1,0:T(8,128)S(1)}, f32[6,3,32,128]{3,2,1,0:T(8,128)S(1)}, u32[]{:S(2)}, u32[]{:S(2)}) collective-permute-start(f32[6,3,32,128]{3,2,1,0:T(8,128)S(1)} %slice.15), channel_id=1, source_target_pairs={{0,1},{1,0},{2,3},{3,2},{4,5},{5,4},{6,7},{7,6},{8,9},{9,8},{10,11... | collective-permute-start | bytes 884744 | tf_op jit(solution)/shard_map/ppermute | solution.py:421
  23.9 2.1 %collective-permute-start.3 = (f32[4,3,32,128]{3,2,1,0:T(8,128)S(1)}, f32[4,3,32,128]{3,2,1,0:T(8,128)S(1)}, u32[]{:S(2)}, u32[]{:S(2)}) collective-permute-start(f32[4,3,32,128]{3,2,1,0:T(8,128)S(1)} %slice.12), channel_id=1, source_target_pairs={{0,1},{1,0},{2,3},{3,2},{4,5},{5,4},{6,7},{7,6},{8,9},{9,8},{10,11... | collective-permute-start | bytes 589832 | tf_op jit(solution)/shard_map/ppermute | solution.py:421
  26.0 4.1 %collective-permute-start.6 = (f32[4,3,32,128]{3,2,1,0:T(8,128)S(1)}, f32[4,3,32,128]{3,2,1,0:T(8,128)S(1)}, u32[]{:S(2)}, u32[]{:S(2)}) collective-permute-start(f32[4,3,32,128]{3,2,1,0:T(8,128)S(1)} %slice.14), channel_id=1, source_target_pairs={{0,1},{1,0},{2,3},{3,2},{4,5},{5,4},{6,7},{7,6},{8,9},{9,8},{10,11... | collective-permute-start | bytes 589832 | tf_op jit(solution)/shard_map/ppermute | solution.py:421
  29.2 2.0 %collective-permute-start.8 = (f32[1,4,16,384]{3,2,1,0:T(8,128)S(1)}, f32[1,4,16,384]{3,2,1,0:T(8,128)S(1)}, u32[]{:S(2)}, u32[]{:S(2)}) collective-permute-start(f32[1,4,16,384]{3,2,1,0:T(8,128)S(1)} %get-tuple-element.178), channel_id=1, source_target_pairs={{0,1},{1,0},{2,3},{3,2},{4,5},{5,4},{6,7},{7,6},{8,9},{9,8},{10,11... | collective-permute-start | bytes 294920 | tf_op jit(solution)/shard_map/ppermute | solution.py:432
  29.8 1.4 %collective-permute-start.9 = (f32[1,4,16,384]{3,2,1,0:T(8,128)S(1)}, f32[1,4,16,384]{3,2,1,0:T(8,128)S(1)}, u32[]{:S(2)}, u32[]{:S(2)}) collective-permute-start(f32[1,4,16,384]{3,2,1,0:T(8,128)S(1)} %get-tuple-element.179), channel_id=1, source_target_pairs={{0,1},{1,0},{2,3},{3,2},{4,5},{5,4},{6,7},{7,6},{8,9},{9,8},{10,11... | collective-permute-start | bytes 294920 | tf_op jit(solution)/shard_map/ppermute | solution.py:432
  31.3 4.9 %collective-permute-start.10 = (f32[4,16,384]{2,1,0:T(8,128)S(1)}, f32[4,16,384]{2,1,0:T(8,128)S(1)}, u32[]{:S(2)}, u32[]{:S(2)}) collective-permute-start(f32[4,16,384]{2,1,0:T(8,128)S(1)} %add_bitcast_fusion.1), channel_id=1, source_target_pairs={{0,2},{1,3},{2,0},{3,1},{4,6},{5,7},{6,4},{7,5},{8,10},{9,11},{10,... | collective-permute-start | bytes 294920 | tf_op jit(solution)/shard_map/ppermute | solution.py:427
  34.9 1.5 %collective-permute-start.11 = (f32[1,4,16,384]{3,2,1,0:T(8,128)S(1)}, f32[1,4,16,384]{3,2,1,0:T(8,128)S(1)}, u32[]{:S(2)}, u32[]{:S(2)}) collective-permute-start(f32[1,4,16,384]{3,2,1,0:T(8,128)S(1)} %get-tuple-element.202), channel_id=1, source_target_pairs={{0,1},{1,0},{2,3},{3,2},{4,5},{5,4},{6,7},{7,6},{8,9},{9,8},{10,11... | collective-permute-start | bytes 294920 | tf_op jit(solution)/shard_map/ppermute | solution.py:432
  34.9 3.9 %collective-permute-start.12 = (f32[1,4,16,384]{3,2,1,0:T(8,128)S(1)}, f32[1,4,16,384]{3,2,1,0:T(8,128)S(1)}, u32[]{:S(2)}, u32[]{:S(2)}) collective-permute-start(f32[1,4,16,384]{3,2,1,0:T(8,128)S(1)} %get-tuple-element.207), channel_id=1, source_target_pairs={{0,1},{1,0},{2,3},{3,2},{4,5},{5,4},{6,7},{7,6},{8,9},{9,8},{10,11... | collective-permute-start | bytes 294920 | tf_op jit(solution)/shard_map/ppermute | solution.py:432
  36.4 4.8 %collective-permute-start.13 = (f32[4,16,384]{2,1,0:T(8,128)S(1)}, f32[4,16,384]{2,1,0:T(8,128)S(1)}, u32[]{:S(2)}, u32[]{:S(2)}) collective-permute-start(f32[4,16,384]{2,1,0:T(8,128)S(1)} %add_bitcast_fusion), channel_id=1, source_target_pairs={{0,2},{1,3},{2,0},{3,1},{4,6},{5,7},{6,4},{7,5},{8,10},{9,11},{10,... | collective-permute-start | bytes 294920 | tf_op jit(solution)/shard_map/ppermute | solution.py:461
